TPU v7x, 32 devices: a whole 2x2x4 slice. The times are simulated.
32 devices in a mesh: seq: 8 (over z, x), chan: 4 (over y, core).
Axes of the slice: x: 2, y: 2, z: 4, core: 2. Of those that a mesh axis runs over, the one named last changes fastest.
Arguments:
- tokens: bfloat16 [4, 512, 1024], P(None, 'chan', 'seq'), may hold values from -6 to 6
- lengths: int32 [4, 1], replicated, may hold values from 256 to 1024, as said below
- ln_gain: float32 [512], P('chan'), may hold values from 0.5 to 1.5
- ln_bias: float32 [512], P('chan'), may hold values from -4 to 4
- b_coef: float32 [2, 512, 64], P(None, 'chan'), may hold values from -0.75 to 0.75
- e_coef: float32 [2, 512, 64], P(None, 'chan'), may hold values from -0.75 to 0.75
- c_coef: float32 [2, 512, 64], P(None, 'chan'), may hold values from -0.875 to 0.875
- skip_gain: float32 [512], P('chan'), may hold values from 0.5 to 1.5
- decay_rate: float32 [512, 64], P('chan'), may hold values from 0.0001953125 to 0.05
- rotation: float32 [512, 64], P('chan'), may hold values from -3.140625 to 3.140625
- w_value: bfloat16 [512, 512], P(None, 'chan'), may hold values from -0.5 to 0.5
- w_gate: bfloat16 [512, 512], P(None, 'chan'), may hold values from -0.25 to 0.25
- bias_value: float32 [512], P('chan'), may hold values from -4 to 4
- bias_gate: float32 [512], P('chan'), may hold values from -4 to 4
- out_cotangent: bfloat16 [4, 512, 1024], P(None, 'chan', 'seq'), may hold values from -6 to 6
Outputs:
- out: bfloat16 [4, 512, 1024], P(None, 'chan', 'seq')
- input_grad: float32 [4, 512, 1024], P(None, 'chan', 'seq')
- d_ln_gain: float32 [512], P('chan')
- d_ln_bias: float32 [512], P('chan')
- d_b_coef: float32 [2, 512, 64], P(None, 'chan')
- d_e_coef: float32 [2, 512, 64], P(None, 'chan')
- d_c_coef: float32 [2, 512, 64], P(None, 'chan')
- d_skip_gain: float32 [512], P('chan')
- d_w_value: float32 [512, 512], P('seq', 'chan')
- d_w_gate: float32 [512, 512], P('seq', 'chan')
- d_bias_value: float32 [512], P('chan')
- d_bias_gate: float32 [512], P('chan')
Inputs may be any that keep to these rules, and one draw needn't show every extreme that they name: `lengths`: in every draw the sequence of one micro-batch, which one drawn from the seed, fills its whole slot of 1024.
All inputs are finite; a program needn't handle non-finite values.
Results may differ from a plain program's by a relative error of at most 0.005.
The roundings to bfloat16 on the way count: a program that leaves them out, or rounds other values in their place, can miss the bound.
Values may be sent and summed in bfloat16 or wider, within the bound.
No kernel may reach another device: no remote copies, remote signals or barrier semaphores. Data moves between devices by JAX's collectives and lax.ppermute only.
A program may use at most 192 MiB of HBM per device.

v0:
```python
import math

import jax
import jax.numpy as jnp
from jax import lax
from jax.sharding import PartitionSpec as P

SLOT_MAX = 4096


highest = lax.Precision.HIGHEST
epsilon = 1e-05


def passed_along(array, axis, by):
    peers = lax.axis_size(axis)
    pairs = [(i, i + by) for i in range(peers) if 0 <= i + by < peers]
    return lax.ppermute(array, axis, pairs)


def prefix(part, axis, combine, identity, reverse):
    count = lax.axis_size(axis)
    place = lax.axis_index(axis)
    ahead = count - 1 - place if reverse else place
    gathered = jax.tree.map(lambda a: lax.all_gather(a, axis), part)
    state = jax.tree.map(lambda a, e: jnp.zeros_like(a) + jnp.asarray(e, a.dtype), part, identity)

    def one(lap, state):
        source = count - 1 - lap if reverse else lap
        return combine(
            state, jax.tree.map(lambda a: lax.dynamic_index_in_dim(a, source, 0, False), gathered)
        )

    return lax.fori_loop(0, ahead, one, state)


def complex_mul(left_re, left_im, right_re, right_im):
    return (left_re * right_re - left_im * right_im, left_re * right_im + left_im * right_re)


def times_conj(left_re, left_im, right_re, right_im):
    return (left_re * right_re + left_im * right_im, left_im * right_re - left_re * right_im)


def chain_join(earlier, latter):
    decay_re, decay_im = complex_mul(earlier[0], earlier[1], latter[0], latter[1])
    carry_re, carry_im = complex_mul(latter[0], latter[1], earlier[2], earlier[3])
    return (decay_re, decay_im, carry_re + latter[2], carry_im + latter[3])


def power_table(decay_rate, rotation, exponents):
    magnitude = jnp.exp(-decay_rate[None] * exponents[:, None, None])
    turned = rotation[None] * exponents[:, None, None]
    return (magnitude * jnp.cos(turned), magnitude * jnp.sin(turned))


def gelu_slope(pre_act):
    cumulative = 0.5 * (1.0 + jax.scipy.special.erf(pre_act / math.sqrt(2.0)))
    density = jnp.exp(-0.5 * pre_act * pre_act) / math.sqrt(2.0 * math.pi)
    return cumulative + pre_act * density


def shards(
    tokens,
    lengths,
    ln_gain,
    ln_bias,
    b_coef,
    e_coef,
    c_coef,
    skip_gain,
    decay_rate,
    rotation,
    w_value,
    w_gate,
    bias_value,
    bias_gate,
    out_cotangent,
):
    tok_rows = jnp.transpose(tokens, (0, 2, 1))
    cot_rows = jnp.transpose(out_cotangent, (0, 2, 1))
    local_rows = tok_rows.shape[1]
    chan_width = tok_rows.shape[2]
    mode_count = decay_rate.shape[1]
    full_width = w_value.shape[0]
    seq_devices = lax.axis_size("seq")
    seq_rank = lax.axis_index("seq")
    slot_len = min(SLOT_MAX, local_rows * seq_devices)
    block_len = math.gcd(local_rows, 64)
    block_count = local_rows // block_len
    first_row = seq_rank * local_rows
    carries = (first_row % slot_len != 0).astype(jnp.float32)
    slot_index = first_row // slot_len
    slot_lengths = lax.dynamic_index_in_dim(lengths, slot_index, 1, keepdims=False)
    positions = first_row % slot_len + jnp.arange(local_rows, dtype=jnp.int32)
    live_rows = (positions[None, :] < slot_lengths[:, None]).astype(jnp.float32)
    exponents = jnp.arange(block_len + 1, dtype=jnp.float32)
    pow_re, pow_im = power_table(decay_rate, rotation, exponents)
    head_re, head_im = (pow_re[:block_len], pow_im[:block_len])
    tail_re, tail_im = (pow_re[block_len - 1 :: -1], pow_im[block_len - 1 :: -1])
    next_re, next_im = (pow_re[1:], pow_im[1:])
    jump_re, jump_im = (pow_re[block_len], pow_im[block_len])
    span_steps = jnp.arange(block_count + 1, dtype=jnp.float32) * block_len
    far_re, far_im = power_table(decay_rate, rotation, span_steps)
    whole_re, whole_im = (far_re[block_count], far_im[block_count])
    lag_index = jnp.arange(block_len, dtype=jnp.int32)
    lag_table = (
        lag_index[:, None, None] - lag_index[None, :, None] == lag_index[None, None, :]
    ).astype(jnp.float32)
    cb_re, cb_im = complex_mul(c_coef[0], c_coef[1], b_coef[0], b_coef[1])
    ce_re, ce_im = complex_mul(c_coef[0], c_coef[1], e_coef[0], e_coef[1])
    kernel_u = jnp.einsum("hn,khn->hk", cb_re, head_re, precision=highest) - jnp.einsum(
        "hn,khn->hk", cb_im, head_im, precision=highest
    )
    kernel_v = jnp.einsum("hn,khn->hk", ce_re, head_re, precision=highest) - jnp.einsum(
        "hn,khn->hk", ce_im, head_im, precision=highest
    )
    toeplitz_u = jnp.einsum("tjk,hk->htj", lag_table, kernel_u, precision=highest)
    toeplitz_v = jnp.einsum("tjk,hk->htj", lag_table, kernel_v, precision=highest)
    out_re, out_im = complex_mul(c_coef[0][None], c_coef[1][None], next_re, next_im)
    unit_decay = jnp.ones((chan_width, mode_count), jnp.float32)
    nothing = jnp.zeros((chan_width, mode_count), jnp.float32)
    fold_rows = (w_value, w_gate)
    out_parts = []
    grad_parts = []
    grad_list = None
    for micro_at in range(tok_rows.shape[0]):
        tok_group = tok_rows[micro_at : micro_at + 1]
        group_size = tok_group.shape[0]
        x_full = tok_group.astype(jnp.float32)
        row_sums = lax.psum((jnp.sum(x_full, axis=-1), jnp.sum(x_full * x_full, axis=-1)), "chan")
        row_mean = row_sums[0] / full_width
        row_var = row_sums[1] / full_width - row_mean * row_mean
        inv_std = lax.rsqrt(row_var + epsilon)[..., None]
        x_hat = (x_full - row_mean[..., None]) * inv_std
        live_cols = live_rows[micro_at : micro_at + 1][..., None]
        u_in = live_cols * (x_hat * ln_gain + ln_bias)
        before = passed_along(u_in[:, -1, :], "seq", 1) * carries
        u_prev = jnp.concatenate([before[:, None, :], u_in[:, :-1, :]], axis=1)
        v_in = u_in * u_prev
        u_blocks = u_in.reshape(group_size, block_count, block_len, chan_width)
        v_blocks = v_in.reshape(group_size, block_count, block_len, chan_width)
        y_local = jnp.einsum(
            "htj,mbjh->mbth", toeplitz_u, u_blocks, precision=highest
        ) + jnp.einsum("htj,mbjh->mbth", toeplitz_v, v_blocks, precision=highest)
        uq_re = jnp.einsum("jhn,mbjh->bmhn", tail_re, u_blocks, precision=highest)
        uq_im = jnp.einsum("jhn,mbjh->bmhn", tail_im, u_blocks, precision=highest)
        vq_re = jnp.einsum("jhn,mbjh->bmhn", tail_re, v_blocks, precision=highest)
        vq_im = jnp.einsum("jhn,mbjh->bmhn", tail_im, v_blocks, precision=highest)
        bu_re, bu_im = complex_mul(b_coef[0], b_coef[1], uq_re, uq_im)
        ev_re, ev_im = complex_mul(e_coef[0], e_coef[1], vq_re, vq_im)

        def advance(carried, inputs):
            moved_re, moved_im = complex_mul(jump_re, jump_im, carried[0], carried[1])
            return ((moved_re + inputs[0], moved_im + inputs[1]), carried)

        zero_state = jnp.zeros((group_size, chan_width, mode_count), jnp.float32)
        (end_re, end_im), (start_re, start_im) = lax.scan(
            advance, (zero_state, zero_state), (bu_re + ev_re, bu_im + ev_im)
        )
        chained = prefix(
            (carries * whole_re, carries * whole_im, end_re, end_im),
            "seq",
            chain_join,
            (unit_decay, nothing, zero_state, zero_state),
            False,
        )
        init_re = carries * chained[2]
        init_im = carries * chained[3]
        lift_re, lift_im = complex_mul(
            far_re[:block_count, None], far_im[:block_count, None], init_re[None], init_im[None]
        )
        state_re = start_re + lift_re
        state_im = start_im + lift_im
        y_cross = jnp.einsum("thn,bmhn->mbth", out_re, state_re, precision=highest) - jnp.einsum(
            "thn,bmhn->mbth", out_im, state_im, precision=highest
        )
        pre_act = (y_local + y_cross).reshape(group_size, local_rows, chan_width) + skip_gain * u_in
        act_low = jax.nn.gelu(pre_act, approximate=False).astype(jnp.bfloat16)
        grad_out = live_cols * cot_rows[micro_at : micro_at + 1].astype(jnp.float32)
        act_full = lax.all_gather(act_low, "chan", axis=2, tiled=True)
        value_out = (
            jnp.einsum("mrc,cd->mrd", act_full, w_value, preferred_element_type=jnp.float32)
            + bias_value
        )
        gate_pre = (
            jnp.einsum("mrc,cd->mrd", act_full, w_gate, preferred_element_type=jnp.float32)
            + bias_gate
        )
        gate_sig = jax.nn.sigmoid(gate_pre)
        out_group = (live_cols * (x_full + value_out * gate_sig)).astype(jnp.bfloat16)
        d_value = (grad_out * gate_sig).astype(jnp.bfloat16)
        d_gate = (grad_out * value_out * gate_sig * (1.0 - gate_sig)).astype(jnp.bfloat16)
        grad_wv = jnp.einsum("mrc,mrd->cd", act_full, d_value, preferred_element_type=jnp.float32)
        grad_wg = jnp.einsum("mrc,mrd->cd", act_full, d_gate, preferred_element_type=jnp.float32)
        grad_bv = jnp.sum(d_value.astype(jnp.float32), axis=(0, 1))
        grad_bg = jnp.sum(d_gate.astype(jnp.float32), axis=(0, 1))
        flat_value = d_value.reshape(group_size * local_rows, chan_width)
        flat_gate = d_gate.reshape(group_size * local_rows, chan_width)
        rows_value = fold_rows[0]
        rows_gate = fold_rows[1]
        summed_term = lax.psum_scatter(
            jnp.einsum("ch,rh->cr", rows_value, flat_value, preferred_element_type=jnp.float32)
            + jnp.einsum("ch,rh->cr", rows_gate, flat_gate, preferred_element_type=jnp.float32),
            "chan",
            scatter_dimension=0,
            tiled=True,
        )
        d_act = summed_term.T.reshape(group_size, local_rows, chan_width)
        d_pre = d_act * gelu_slope(pre_act)
        dy_blocks = d_pre.reshape(group_size, block_count, block_len, chan_width)
        du_local = jnp.einsum("htj,mbth->mbjh", toeplitz_u, dy_blocks, precision=highest)
        dv_local = jnp.einsum("htj,mbth->mbjh", toeplitz_v, dy_blocks, precision=highest)
        outer_u = jnp.einsum("mbth,mbjh->htj", dy_blocks, u_blocks, precision=highest)
        outer_v = jnp.einsum("mbth,mbjh->htj", dy_blocks, v_blocks, precision=highest)
        corr_u = jnp.einsum("htj,tjk->hk", outer_u, lag_table, precision=highest)
        corr_v = jnp.einsum("htj,tjk->hk", outer_v, lag_table, precision=highest)
        dcb_re = jnp.einsum("hk,khn->hn", corr_u, head_re, precision=highest)
        dcb_im = -jnp.einsum("hk,khn->hn", corr_u, head_im, precision=highest)
        dce_re = jnp.einsum("hk,khn->hn", corr_v, head_re, precision=highest)
        dce_im = -jnp.einsum("hk,khn->hn", corr_v, head_im, precision=highest)
        yd_re = jnp.einsum("mbth,thn->bmhn", dy_blocks, next_re, precision=highest)
        yd_im = jnp.einsum("mbth,thn->bmhn", dy_blocks, next_im, precision=highest)
        cy_re, cy_im = complex_mul(c_coef[0], c_coef[1], yd_re, yd_im)
        sy_re, sy_im = complex_mul(state_re, state_im, yd_re, yd_im)

        def retreat(adjoint, inputs):
            moved_re, moved_im = complex_mul(jump_re, -jump_im, adjoint[0], adjoint[1])
            return ((inputs[0] + moved_re, inputs[1] + moved_im), adjoint)

        (first_re, first_im), (after_re, after_im) = lax.scan(
            retreat, (zero_state, zero_state), (cy_re, -cy_im), reverse=True
        )
        returned = prefix(
            (carries * whole_re, -carries * whole_im, carries * first_re, carries * first_im),
            "seq",
            chain_join,
            (unit_decay, nothing, zero_state, zero_state),
            True,
        )
        back_re, back_im = complex_mul(
            far_re[block_count - 1 :: -1, None],
            -far_im[block_count - 1 :: -1, None],
            returned[2][None],
            returned[3][None],
        )
        adj_re = after_re + back_re
        adj_im = after_im + back_im
        hb_re, hb_im = times_conj(adj_re, adj_im, b_coef[0], b_coef[1])
        he_re, he_im = times_conj(adj_re, adj_im, e_coef[0], e_coef[1])
        du_state = jnp.einsum("jhn,bmhn->mbjh", tail_re, hb_re, precision=highest) + jnp.einsum(
            "jhn,bmhn->mbjh", tail_im, hb_im, precision=highest
        )
        dv_state = jnp.einsum("jhn,bmhn->mbjh", tail_re, he_re, precision=highest) + jnp.einsum(
            "jhn,bmhn->mbjh", tail_im, he_im, precision=highest
        )
        d_v = (dv_local + dv_state).reshape(group_size, local_rows, chan_width)
        d_u_prev = d_v * u_in
        after_row = passed_along(carries * d_u_prev[:, 0, :], "seq", -1)
        d_u = (
            skip_gain * d_pre
            + (du_local + du_state).reshape(group_size, local_rows, chan_width)
            + d_v * u_prev
        )
        d_u = d_u + jnp.concatenate([d_u_prev[:, 1:, :], after_row[:, None, :]], axis=1)
        sb_re, sb_im = times_conj(adj_re, adj_im, uq_re, uq_im)
        se_re, se_im = times_conj(adj_re, adj_im, vq_re, vq_im)
        gb_re, gb_im = times_conj(dcb_re, dcb_im, c_coef[0], c_coef[1])
        ge_re, ge_im = times_conj(dce_re, dce_im, c_coef[0], c_coef[1])
        gcb_re, gcb_im = times_conj(dcb_re, dcb_im, b_coef[0], b_coef[1])
        gce_re, gce_im = times_conj(dce_re, dce_im, e_coef[0], e_coef[1])
        grad_b = jnp.stack(
            [gb_re + jnp.sum(sb_re, axis=(0, 1)), gb_im + jnp.sum(sb_im, axis=(0, 1))]
        )
        grad_e = jnp.stack(
            [ge_re + jnp.sum(se_re, axis=(0, 1)), ge_im + jnp.sum(se_im, axis=(0, 1))]
        )
        grad_c = jnp.stack(
            [
                gcb_re + gce_re + jnp.sum(sy_re, axis=(0, 1)),
                gcb_im + gce_im - jnp.sum(sy_im, axis=(0, 1)),
            ]
        )
        grad_skip = jnp.sum(d_pre * u_in, axis=(0, 1))
        d_q = live_cols * d_u
        grad_gain = jnp.sum(d_q * x_hat, axis=(0, 1))
        grad_bias = jnp.sum(d_q, axis=(0, 1))
        d_hat = d_q * ln_gain
        hat_sums = lax.psum((jnp.sum(d_hat, axis=-1), jnp.sum(d_hat * x_hat, axis=-1)), "chan")
        d_input = grad_out + inv_std * (
            d_hat
            - hat_sums[0][..., None] / full_width
            - x_hat * hat_sums[1][..., None] / full_width
        )
        result_one = (
            out_group,
            d_input,
            (
                grad_gain,
                grad_bias,
                grad_b,
                grad_e,
                grad_c,
                grad_skip,
                grad_wv,
                grad_wg,
                grad_bv,
                grad_bg,
            ),
        )
        out_parts.append(result_one[0])
        grad_parts.append(result_one[1])
        grad_list = (
            result_one[2] if grad_list is None else jax.tree.map(jnp.add, grad_list, result_one[2])
        )
    out_all = jnp.concatenate(out_parts, axis=0)
    d_all = jnp.concatenate(grad_parts, axis=0)
    summed_small = lax.psum(
        (
            grad_list[0],
            grad_list[1],
            grad_list[2],
            grad_list[3],
            grad_list[4],
            grad_list[5],
            grad_list[8],
            grad_list[9],
        ),
        "seq",
    )
    summed_weights = (
        lax.psum_scatter(grad_list[6], "seq", scatter_dimension=0, tiled=True),
        lax.psum_scatter(grad_list[7], "seq", scatter_dimension=0, tiled=True),
    )
    out_chan = jnp.transpose(out_all, (0, 2, 1))
    grad_chan = jnp.transpose(d_all, (0, 2, 1))
    return (
        out_chan,
        grad_chan,
        summed_small[0],
        summed_small[1],
        summed_small[2],
        summed_small[3],
        summed_small[4],
        summed_small[5],
        summed_weights[0],
        summed_weights[1],
        summed_small[6],
        summed_small[7],
    )


def solution(mesh):
    placed = (
        P(None, "chan", "seq"),
        P(),
        P("chan"),
        P("chan"),
        P(None, "chan", None),
        P(None, "chan", None),
        P(None, "chan", None),
        P("chan"),
        P("chan", None),
        P("chan", None),
        P(None, "chan"),
        P(None, "chan"),
        P("chan"),
        P("chan"),
        P(None, "chan", "seq"),
    )
    return jax.shard_map(
        shards,
        mesh=mesh,
        in_specs=placed,
        out_specs=(
            P(None, "chan", "seq"),
            P(None, "chan", "seq"),
            P("chan"),
            P("chan"),
            P(None, "chan", None),
            P(None, "chan", None),
            P(None, "chan", None),
            P("chan"),
            P("seq", "chan"),
            P("seq", "chan"),
            P("chan"),
            P("chan"),
        ),
        check_vma=False,
    )
```

profile of v0, /device:TPU:0, one launch (start us, length us, event | category | flops | bytes accessed | tf_op | source)
XLA Modules:
  0.0 1735.3 jit_solution(5925272037041665480)
XLA Ops:
  10.3 8.3 all-reduce.4
  31.5 17.1 cosine_multiply_fusion
  92.7 8.3 fusion.430
  101.1 8.3 fusion.450
  117.7 9.2 fusion.466
  134.2 8.3 fusion.428
  142.5 8.6 fusion.448
  151.7 30.9 %all_gather.146 = f32[8,128,64]{1,2,0:T(8,128)S(1)} all-gather(f32[1,128,64]{1,2,0:T(8,128)S(1)} %slice_multiply_fusion), channel_id=1, replica_groups=mesh['seq'=8,'chan'=4] {'seq'}, dimensions={0}, use_global_device_ids=true | all-gather | bytes 294912 | tf_op jit(solution)/shard_map/all_gather | solution.py:25
  183.2 30.8 %all_gather.147 = f32[8,128,64]{1,2,0:T(8,128)S(1)} all-gather(f32[1,128,64]{1,2,0:T(8,128)S(1)} %get-tuple-element.3285), channel_id=1, replica_groups=mesh['seq'=8,'chan'=4] {'seq'}, dimensions={0}, use_global_device_ids=true | all-gather | bytes 294912 | tf_op jit(solution)/shard_map/all_gather | solution.py:25
  247.8 30.9 %all-gather = f32[8,128,64]{1,2,0:T(8,128)S(1)} all-gather(f32[1,128,64]{1,2,0:T(8,128)S(1)} %copy.649), channel_id=2, replica_groups=mesh['seq'=8,'chan'=4] {'seq'}, dimensions={0}, use_global_device_ids=true | all-gather | bytes 294912 | tf_op jit(solution)/shard_map/all_gather | solution.py:25
  278.8 32.9 %all-gather.1 = f32[8,128,64]{1,2,0:T(8,128)} all-gather(f32[1,128,64]{1,2,0:T(8,128)S(1)} %copy.650), channel_id=3, replica_groups=mesh['seq'=8,'chan'=4] {'seq'}, dimensions={0}, use_global_device_ids=true | all-gather | bytes 294912 | tf_op jit(solution)/shard_map/all_gather | solution.py:25
  316.6 34.4 %all-gather.2 = f32[8,128,64]{1,2,0:T(8,128)S(1)} all-gather(f32[1,128,64]{1,2,0:T(8,128)S(1)} %copy.678), channel_id=4, replica_groups=mesh['seq'=8,'chan'=4] {'seq'}, dimensions={0}, use_global_device_ids=true | all-gather | bytes 294912 | tf_op jit(solution)/shard_map/all_gather | solution.py:25
  351.1 30.8 %all-gather.3 = f32[8,128,64]{1,2,0:T(8,128)S(1)} all-gather(f32[1,128,64]{1,2,0:T(8,128)S(1)} %copy.679), channel_id=5, replica_groups=mesh['seq'=8,'chan'=4] {'seq'}, dimensions={0}, use_global_device_ids=true | all-gather | bytes 294912 | tf_op jit(solution)/shard_map/all_gather | solution.py:25
  383.3 8.6 fusion.55
  391.9 8.3 fusion.471
  407.0 8.5 fusion.52
  415.8 8.4 fusion.477
  424.3 8.3 fusion.51
  448.1 32.5 %all_gather.168 = f32[8,128,64]{1,2,0:T(8,128)S(1)} all-gather(f32[1,128,64]{1,2,0:T(8,128)S(1)} %copy-done.174), channel_id=1, replica_groups=mesh['seq'=8,'chan'=4] {'seq'}, dimensions={0}, use_global_device_ids=true | all-gather | bytes 294912 | tf_op jit(solution)/shard_map/all_gather | solution.py:25
  489.1 16.4 reduce-scatter.9.cloned.1.call-done
  552.7 8.4 fusion.498
  583.3 8.6 fusion.499
  614.1 8.3 fusion.502
  644.8 8.6 fusion.503
  655.9 30.9 %all-gather.8 = f32[8,128,64]{1,2,0:T(8,128)S(1)} all-gather(f32[1,128,64]{1,2,0:T(8,128)S(1)} %broadcast_multiply_fusion.7), channel_id=10, replica_groups=mesh['seq'=8,'chan'=4] {'seq'}, dimensions={0}, use_global_device_ids=true | all-gather | bytes 294912 | tf_op jit(solution)/shard_map/all_gather | solution.py:25
  686.9 30.7 %all-gather.9 = f32[8,128,64]{1,2,0:T(8,128)S(1)} all-gather(f32[1,128,64]{1,2,0:T(8,128)S(1)} %broadcast_multiply_fusion.6), channel_id=11, replica_groups=mesh['seq'=8,'chan'=4] {'seq'}, dimensions={0}, use_global_device_ids=true | all-gather | bytes 294912 | tf_op jit(solution)/shard_map/all_gather | solution.py:25
  726.2 30.9 %all-gather.10 = f32[8,128,64]{1,2,0:T(8,128)S(1)} all-gather(f32[1,128,64]{1,2,0:T(8,128)S(1)} %broadcast_multiply_fusion.5), channel_id=12, replica_groups=mesh['seq'=8,'chan'=4] {'seq'}, dimensions={0}, use_global_device_ids=true | all-gather | bytes 294912 | tf_op jit(solution)/shard_map/all_gather | solution.py:25
  757.1 30.7 %all-gather.11 = f32[8,128,64]{1,2,0:T(8,128)S(1)} all-gather(f32[1,128,64]{1,2,0:T(8,128)S(1)} %broadcast_multiply_fusion.4), channel_id=13, replica_groups=mesh['seq'=8,'chan'=4] {'seq'}, dimensions={0}, use_global_device_ids=true | all-gather | bytes 294912 | tf_op jit(solution)/shard_map/all_gather | solution.py:25
  793.0 8.3 fusion.491
  801.5 8.4 fusion.41
  810.9 8.3 fusion.493
  819.4 8.3 fusion.37
  831.5 8.5 fusion.490
  842.1 8.3 fusion.492
  856.6 8.7 fusion.43
  865.5 7.6 fusion.39
  887.3 8.5 fusion.478
  976.6 32.9 %all-gather.4 = f32[8,128,64]{1,2,0:T(8,128)} all-gather(f32[1,128,64]{1,2,0:T(8,128)S(1)} %copy.707), channel_id=6, replica_groups=mesh['seq'=8,'chan'=4] {'seq'}, dimensions={0}, use_global_device_ids=true | all-gather | bytes 294912 | tf_op jit(solution)/shard_map/all_gather | solution.py:25
  1009.6 32.8 %all-gather.5 = f32[8,128,64]{1,2,0:T(8,128)} all-gather(f32[1,128,64]{1,2,0:T(8,128)S(1)} %copy.708), channel_id=7, replica_groups=mesh['seq'=8,'chan'=4] {'seq'}, dimensions={0}, use_global_device_ids=true | all-gather | bytes 294912 | tf_op jit(solution)/shard_map/all_gather | solution.py:25
  1048.8 37.0 %all-gather.6 = f32[8,128,64]{1,2,0:T(8,128)} all-gather(f32[1,128,64]{1,2,0:T(8,128)S(1)} %copy.736), channel_id=8, replica_groups=mesh['seq'=8,'chan'=4] {'seq'}, dimensions={0}, use_global_device_ids=true | all-gather | bytes 294912 | tf_op jit(solution)/shard_map/all_gather | solution.py:25
  1085.8 32.9 %all-gather.7 = f32[8,128,64]{1,2,0:T(8,128)} all-gather(f32[1,128,64]{1,2,0:T(8,128)S(1)} %copy.737), channel_id=9, replica_groups=mesh['seq'=8,'chan'=4] {'seq'}, dimensions={0}, use_global_device_ids=true | all-gather | bytes 294912 | tf_op jit(solution)/shard_map/all_gather | solution.py:25
  1120.1 8.5 fusion.483
  1128.7 8.3 fusion.48
  1137.2 8.3 fusion.46
  1145.7 8.3 fusion.489
  1154.2 8.5 fusion.45
  1206.7 22.5 %reduce-scatter.11.cloned.1.call-done = f32[128,128]{0,1:T(8,128)} async-done(((f32[512,128]{0,1:T(8,128)}), f32[128,128]{0,1:T(8,128)}) %reduce-scatter.11.cloned.1.call-update) | async-done | bytes 65552 | tf_op jit(solution)/shard_map/reduce_scatter | solution.py:202
  1254.7 8.4 fusion.505
  1285.2 8.4 fusion.500
  1315.8 8.6 fusion.504
  1346.6 8.4 fusion.501
  1379.6 31.3 %all-gather.14 = f32[8,128,64]{1,2,0:T(8,128)S(1)} all-gather(f32[1,128,64]{1,2,0:T(8,128)S(1)} %broadcast_multiply_fusion.1), channel_id=16, replica_groups=mesh['seq'=8,'chan'=4] {'seq'}, dimensions={0}, use_global_device_ids=true | all-gather | bytes 294912 | tf_op jit(solution)/shard_map/all_gather | solution.py:25
  1411.0 30.7 %all-gather.15 = f32[8,128,64]{1,2,0:T(8,128)S(1)} all-gather(f32[1,128,64]{1,2,0:T(8,128)S(1)} %broadcast_multiply_fusion), channel_id=17, replica_groups=mesh['seq'=8,'chan'=4] {'seq'}, dimensions={0}, use_global_device_ids=true | all-gather | bytes 294912 | tf_op jit(solution)/shard_map/all_gather | solution.py:25
  1448.7 31.0 %all-gather.12 = f32[8,128,64]{1,2,0:T(8,128)S(1)} all-gather(f32[1,128,64]{1,2,0:T(8,128)S(1)} %broadcast_multiply_fusion.3), channel_id=14, replica_groups=mesh['seq'=8,'chan'=4] {'seq'}, dimensions={0}, use_global_device_ids=true | all-gather | bytes 294912 | tf_op jit(solution)/shard_map/all_gather | solution.py:25
  1479.8 30.7 %all-gather.13 = f32[8,128,64]{1,2,0:T(8,128)S(1)} all-gather(f32[1,128,64]{1,2,0:T(8,128)S(1)} %broadcast_multiply_fusion.2), channel_id=15, replica_groups=mesh['seq'=8,'chan'=4] {'seq'}, dimensions={0}, use_global_device_ids=true | all-gather | bytes 294912 | tf_op jit(solution)/shard_map/all_gather | solution.py:25
  1552.5 8.5 fusion.497
  1561.2 8.3 fusion.29
  1569.8 8.4 fusion.495
  1578.3 8.3 fusion.33
  1588.4 8.3 fusion.494
  1598.3 8.5 fusion.496
  1607.1 8.5 fusion.35
  1631.5 20.9 %all-reduce = (f32[128]{0:T(128)}, f32[128]{0:T(128)}, f32[128]{0:T(128)}, f32[128]{0:T(128)}, f32[128]{0:T(128)}) all-reduce(f32[128]{0:T(128)S(1)} %add_add_fusion.4, f32[128]{0:T(128)S(1)} %add_add_fusion.3, f32[128]{0:T(128)S(1)} %add_add_fusion.2, f32[128]{0:T(128)S(1)} %add_add_fusion.1, ...), channel_id=1, replica_groups=mesh['seq'=8,'chan'=4] {'seq'}, use_global_device_ids=true, to_apply=%region_72.73 | all-reduce | flops 640 | bytes 5120 | tf_op jit(solution)/shard_map/psum | solution.py:318
  1663.6 64.5 %reduce-scatter.17.cloned.1.call-done = f32[64,128]{1,0:T(8,128)} async-done(((f32[512,128]{1,0:T(8,128)}), f32[64,128]{1,0:T(8,128)}) %reduce-scatter.17.cloned.1.call-update) | async-done | bytes 32784 | tf_op jit(solution)/shard_map/reduce_scatter | solution.py:333
  (1220 shorter events, 651.1 us)
Async XLA Ops:
  7.2 437.2 %copy-start = (bf16[512,128]{1,0:T(8,128)(2,1)S(1)}, bf16[512,128]{1,0:T(8,128)(2,1)}, u32[]{:S(2)}) copy-start(bf16[512,128]{1,0:T(8,128)(2,1)} %param.58) | copy-start | bytes 393220
  7.2 481.9 %reduce-scatter.7.cloned.1.call-start = ((), (), s32[]{:S(2)}) async-start(), calls=%async_computation.6 | async-start | bytes 327680 | tf_op jit(solution)/shard_map/reduce_scatter | solution.py:202
  19.5 205.2 %copy-start.58 = (f32[1,128,128]{2,1,0:T(8,128)}, f32[1,128,128]{2,1,0:T(8,128)S(1)}, u32[]{:S(2)}) copy-start(f32[1,128,128]{2,1,0:T(8,128)S(1)} %get-tuple-element.3214) | copy-start | bytes 196612
  19.5 205.2 %copy-start.60 = (f32[1,128,128]{2,1,0:T(8,128)}, f32[1,128,128]{2,1,0:T(8,128)S(1)}, u32[]{:S(2)}) copy-start(f32[1,128,128]{2,1,0:T(8,128)S(1)} %get-tuple-element.3215) | copy-start | bytes 196612
  20.1 203.4 %collective-permute-start = (f32[1,128]{1,0:T(1,128)}, f32[1,128]{1,0:T(1,128)}, u32[]{:S(2)}, u32[]{:S(2)}) collective-permute-start(f32[1,128]{1,0:T(1,128)} %slice_bitcast_fusion.3), channel_id=1, source_target_pairs={{0,4},{4,8},{8,12},{12,16},{16,20},{20,24},{24,28},{1,5},{5,9},{9,... | collective-permute-start | bytes 1544 | tf_op jit(solution)/shard_map/ppermute | solution.py:18
  24.5 199.6 %collective-permute-start.1 = (f32[1,128]{1,0:T(1,128)}, f32[1,128]{1,0:T(1,128)}, u32[]{:S(2)}, u32[]{:S(2)}) collective-permute-start(f32[1,128]{1,0:T(1,128)} %slice_bitcast_fusion.2), channel_id=1, source_target_pairs={{0,4},{4,8},{8,12},{12,16},{16,20},{20,24},{24,28},{1,5},{5,9},{9,... | collective-permute-start | bytes 1544 | tf_op jit(solution)/shard_map/ppermute | solution.py:18
  29.7 63.0 %copy-start.35 = (f32[1,128,64]{2,1,0:T(8,128)}, f32[1,128,64]{2,1,0:T(8,128)S(1)}, u32[]{:S(2)}) copy-start(f32[1,128,64]{2,1,0:T(8,128)S(1)} %copy.1042) | copy-start | bytes 98308
  29.8 62.9 %copy-start.37 = (f32[1,128,64]{2,1,0:T(8,128)}, f32[1,128,64]{2,1,0:T(8,128)S(1)}, u32[]{:S(2)}) copy-start(f32[1,128,64]{2,1,0:T(8,128)S(1)} %copy.1041) | copy-start | bytes 98308
  92.2 154.3 %copy-start.64 = (f32[128,64]{0,1:T(8,128)}, f32[128,64]{0,1:T(8,128)S(1)}, u32[]{:S(2)}) copy-start(f32[128,64]{0,1:T(8,128)S(1)} %get-tuple-element.3297) | copy-start | bytes 98308
  92.2 154.3 %copy-start.67 = (f32[128,64]{0,1:T(8,128)}, f32[128,64]{0,1:T(8,128)S(1)}, u32[]{:S(2)}) copy-start(f32[128,64]{0,1:T(8,128)S(1)} %get-tuple-element.3320) | copy-start | bytes 98308
  151.6 329.0 %copy-start.39 = (f32[3,128,64]{1,2,0:T(8,128)}, f32[3,128,64]{1,2,0:T(8,128)S(1)}, u32[]{:S(2)}) copy-start(f32[3,128,64]{1,2,0:T(8,128)S(1)} %get-tuple-element.3286) | copy-start | bytes 294916
  151.6 329.6 %copy-start.41 = (f32[3,128,64]{1,2,0:T(8,128)}, f32[3,128,64]{1,2,0:T(8,128)S(1)}, u32[]{:S(2)}) copy-start(f32[3,128,64]{1,2,0:T(8,128)S(1)} %get-tuple-element.3287) | copy-start | bytes 294916
  246.5 65.2 %copy-start.105 = (f32[128,2,64]{0,2,1:T(8,128)}, f32[128,2,64]{0,2,1:T(8,128)S(1)}, u32[]{:S(2)}) copy-start(f32[128,2,64]{0,2,1:T(8,128)S(1)} %copy.671) | copy-start | bytes 196612
  247.7 66.7 %copy-start.148 = (f32[2,1,128,64]{2,3,0,1:T(8,128)}, f32[2,1,128,64]{2,3,0,1:T(8,128)S(1)}, u32[]{:S(2)}) copy-start(f32[2,1,128,64]{2,3,0,1:T(8,128)S(1)} %get-tuple-element.1752) | copy-start | bytes 196612
  247.7 66.7 %copy-start.150 = (f32[2,1,128,64]{2,3,0,1:T(8,128)}, f32[2,1,128,64]{2,3,0,1:T(8,128)S(1)}, u32[]{:S(2)}) copy-start(f32[2,1,128,64]{2,3,0,1:T(8,128)S(1)} %get-tuple-element.1757) | copy-start | bytes 196612
  316.5 65.5 %copy-start.149 = (f32[2,1,128,64]{2,3,0,1:T(8,128)S(1)}, f32[2,1,128,64]{2,3,0,1:T(8,128)}, u32[]{:S(2)}) copy-start(f32[2,1,128,64]{2,3,0,1:T(8,128)} %copy-done.148) | copy-start | bytes 196612
  316.6 65.5 %copy-start.151 = (f32[2,1,128,64]{2,3,0,1:T(8,128)S(1)}, f32[2,1,128,64]{2,3,0,1:T(8,128)}, u32[]{:S(2)}) copy-start(f32[2,1,128,64]{2,3,0,1:T(8,128)} %copy-done.150) | copy-start | bytes 196612
  316.6 66.7 %copy-start.130 = (f32[128,2,64]{2,1,0:T(2,128)S(1)}, f32[128,2,64]{2,1,0:T(2,128)}, u32[]{:S(2)}) copy-start(f32[128,2,64]{2,1,0:T(2,128)} %fusion.466) | copy-start | bytes 196612
  383.0 41.1 %copy-start.112 = (f32[2,1,128,64]{2,3,0,1:T(8,128)}, f32[2,1,128,64]{2,3,0,1:T(8,128)S(1)}, u32[]{:S(2)}) copy-start(f32[2,1,128,64]{2,3,0,1:T(8,128)S(1)} %get-tuple-element.3189) | copy-start | bytes 196612
  444.0 63.2 %copy-start.33 = (bf16[1,128,512]{2,1,0:T(8,128)(2,1)}, bf16[1,128,512]{2,1,0:T(8,128)(2,1)S(1)}, u32[]{:S(2)}) copy-start(bf16[1,128,512]{2,1,0:T(8,128)(2,1)S(1)} %all_gather.157) | copy-start | bytes 393220
  448.0 57.5 %reduce-scatter.9.cloned.1.call-start = ((), (), s32[]{:S(2)}) async-start(), calls=%async_computation.7 | async-start | bytes 327680 | tf_op jit(solution)/shard_map/reduce_scatter | solution.py:202
  484.8 722.0 %reduce-scatter.13.cloned.1.call-start = ((), (), s32[]{:S(2)}) async-start(), calls=%async_computation.9 | async-start | bytes 327680 | tf_op jit(solution)/shard_map/reduce_scatter | solution.py:202
  655.3 67.7 %copy-start.111 = (f32[2,1,128,64]{2,3,0,1:T(8,128)S(1)}, f32[2,1,128,64]{2,3,0,1:T(8,128)}, u32[]{:S(2)}) copy-start(f32[2,1,128,64]{2,3,0,1:T(8,128)} %copy-done.110) | copy-start | bytes 196612
  655.3 69.3 %copy-start.29 = (f32[1,128,64]{2,1,0:T(8,128)S(1)}, f32[1,128,64]{2,1,0:T(8,128)}, u32[]{:S(2)}) copy-start(f32[1,128,64]{2,1,0:T(8,128)} %custom-call.10) | copy-start | bytes 98308
  655.3 69.3 %copy-start.30 = (f32[1,128,64]{2,1,0:T(8,128)S(1)}, f32[1,128,64]{2,1,0:T(8,128)}, u32[]{:S(2)}) copy-start(f32[1,128,64]{2,1,0:T(8,128)} %custom-call.11) | copy-start | bytes 98308
  725.5 64.5 %copy-start.175 = (f32[128,64]{0,1:T(8,128)S(1)}, f32[128,64]{0,1:T(8,128)}, u32[]{:S(2)}) copy-start(f32[128,64]{0,1:T(8,128)} %copy.769) | copy-start | bytes 98308
  725.5 66.6 %copy-start.65 = (f32[128,64]{0,1:T(8,128)S(1)}, f32[128,64]{0,1:T(8,128)}, u32[]{:S(2)}) copy-start(f32[128,64]{0,1:T(8,128)} %copy-done.64) | copy-start | bytes 98308
  725.6 66.6 %copy-start.68 = (f32[128,64]{0,1:T(8,128)S(1)}, f32[128,64]{0,1:T(8,128)}, u32[]{:S(2)}) copy-start(f32[128,64]{0,1:T(8,128)} %copy-done.67) | copy-start | bytes 98308
  725.6 66.6 %copy-start.71 = (f32[128,64]{0,1:T(8,128)S(1)}, f32[128,64]{0,1:T(8,128)}, u32[]{:S(2)}) copy-start(f32[128,64]{0,1:T(8,128)} %get-tuple-element.3321) | copy-start | bytes 98308
  830.1 47.9 %collective-permute-start.4 = (f32[1,128]{1,0:T(1,128)}, f32[1,128]{1,0:T(1,128)}, u32[]{:S(2)}, u32[]{:S(2)}) collective-permute-start(f32[1,128]{1,0:T(1,128)} %fusion.411), channel_id=1, source_target_pairs={{4,0},{8,4},{12,8},{16,12},{20,16},{24,20},{28,24},{5,1},{9,5},{13... | collective-permute-start | bytes 1544 | tf_op jit(solution)/shard_map/ppermute | solution.py:18
  840.7 37.3 %collective-permute-start.5 = (f32[1,128]{1,0:T(1,128)}, f32[1,128]{1,0:T(1,128)}, u32[]{:S(2)}, u32[]{:S(2)}) collective-permute-start(f32[1,128]{1,0:T(1,128)} %fusion.410), channel_id=1, source_target_pairs={{4,0},{8,4},{12,8},{16,12},{20,16},{24,20},{28,24},{5,1},{9,5},{13... | collective-permute-start | bytes 1544 | tf_op jit(solution)/shard_map/ppermute | solution.py:18
  886.9 48.9 %copy-start.194 = (f32[128]{0:T(128)}, f32[128]{0:T(128)S(1)}, u32[]{:S(2)}) copy-start(f32[128]{0:T(128)S(1)} %get-tuple-element.3304) | copy-start | bytes 1540
  886.9 48.9 %copy-start.197 = (f32[128]{0:T(128)}, f32[128]{0:T(128)S(1)}, u32[]{:S(2)}) copy-start(f32[128]{0:T(128)S(1)} %get-tuple-element.3305) | copy-start | bytes 1540
  886.9 48.9 %copy-start.200 = (f32[128]{0:T(128)}, f32[128]{0:T(128)S(1)}, u32[]{:S(2)}) copy-start(f32[128]{0:T(128)S(1)} %get-tuple-element.3306) | copy-start | bytes 1540
  886.9 48.9 %copy-start.203 = (f32[128]{0:T(128)}, f32[128]{0:T(128)S(1)}, u32[]{:S(2)}) copy-start(f32[128]{0:T(128)S(1)} %get-tuple-element.3307) | copy-start | bytes 1540
  887.2 48.7 %copy-start.51 = (f32[1,128,128]{2,1,0:T(8,128)}, f32[1,128,128]{2,1,0:T(8,128)S(1)}, u32[]{:S(2)}) copy-start(f32[1,128,128]{2,1,0:T(8,128)S(1)} %get-tuple-element.3208) | copy-start | bytes 196612
  887.2 48.7 %copy-start.53 = (f32[1,128,128]{2,1,0:T(8,128)}, f32[1,128,128]{2,1,0:T(8,128)S(1)}, u32[]{:S(2)}) copy-start(f32[1,128,128]{2,1,0:T(8,128)S(1)} %get-tuple-element.3209) | copy-start | bytes 196612
  922.1 13.0 collective-permute-start.2
  927.8 7.3 collective-permute-start.3
  933.3 38.2 %copy-start.95 = (f32[128,2,64]{0,2,1:T(8,128)}, f32[128,2,64]{0,2,1:T(8,128)S(1)}, u32[]{:S(2)}) copy-start(f32[128,2,64]{0,2,1:T(8,128)S(1)} %copy.696) | copy-start | bytes 196612
  976.6 68.5 %copy-start.25 = (f32[1,128,64]{2,1,0:T(8,128)S(1)}, f32[1,128,64]{2,1,0:T(8,128)}, u32[]{:S(2)}) copy-start(f32[1,128,64]{2,1,0:T(8,128)} %custom-call.6) | copy-start | bytes 98308
  976.6 68.5 %copy-start.26 = (f32[1,128,64]{2,1,0:T(8,128)S(1)}, f32[1,128,64]{2,1,0:T(8,128)}, u32[]{:S(2)}) copy-start(f32[1,128,64]{2,1,0:T(8,128)} %custom-call.7) | copy-start | bytes 98308
  976.6 68.5 %copy-start.77 = (f32[2,1,128,64]{2,3,0,1:T(8,128)S(1)}, f32[2,1,128,64]{2,3,0,1:T(8,128)}, u32[]{:S(2)}) copy-start(f32[2,1,128,64]{2,3,0,1:T(8,128)} %get-tuple-element.4665) | copy-start | bytes 196612
  1048.7 70.3 %copy-start.40 = (f32[3,128,64]{1,2,0:T(8,128)S(1)}, f32[3,128,64]{1,2,0:T(8,128)}, u32[]{:S(2)}) copy-start(f32[3,128,64]{1,2,0:T(8,128)} %copy-done.39) | copy-start | bytes 294916
  1048.7 70.3 %copy-start.42 = (f32[3,128,64]{1,2,0:T(8,128)S(1)}, f32[3,128,64]{1,2,0:T(8,128)}, u32[]{:S(2)}) copy-start(f32[3,128,64]{1,2,0:T(8,128)} %copy-done.41) | copy-start | bytes 294916
  1178.8 50.4 %reduce-scatter.11.cloned.1.call-start = ((), (), s32[]{:S(2)}) async-start(), calls=%async_computation.8 | async-start | bytes 327680 | tf_op jit(solution)/shard_map/reduce_scatter | solution.py:202
  1197.6 454.8 %all-reduce.7.cloned.1.call-start = ((), (), s32[]{:S(2)}) async-start(), calls=%async_computation.12 | async-start | bytes 786432 | tf_op jit(solution)/shard_map/psum | solution.py:318
  1379.0 67.2 %copy-start.134 = (f32[128,64,2]{1,2,0:T(2,128)S(1)}, f32[128,64,2]{1,2,0:T(2,128)}, u32[]{:S(2)}) copy-start(f32[128,64,2]{1,2,0:T(2,128)} %fusion.2) | copy-start | bytes 196612
  1379.0 67.2 %copy-start.74 = (f32[128,64]{0,1:T(8,128)S(1)}, f32[128,64]{0,1:T(8,128)}, u32[]{:S(2)}) copy-start(f32[128,64]{0,1:T(8,128)} %get-tuple-element.3288) | copy-start | bytes 98308
  1379.0 67.2 %copy-start.76 = (f32[128,64]{0,1:T(8,128)S(1)}, f32[128,64]{0,1:T(8,128)}, u32[]{:S(2)}) copy-start(f32[128,64]{0,1:T(8,128)} %get-tuple-element.3289) | copy-start | bytes 98308
  1379.0 67.2 %copy-start.114 = (f32[2,1,128,64]{2,3,0,1:T(8,128)S(1)}, f32[2,1,128,64]{2,3,0,1:T(8,128)}, u32[]{:S(2)}) copy-start(f32[2,1,128,64]{2,3,0,1:T(8,128)} %copy-done.113) | copy-start | bytes 196612
  1379.0 67.2 %copy-start.116 = (f32[2,1,128,64]{2,3,0,1:T(8,128)S(1)}, f32[2,1,128,64]{2,3,0,1:T(8,128)}, u32[]{:S(2)}) copy-start(f32[2,1,128,64]{2,3,0,1:T(8,128)} %copy-done.115) | copy-start | bytes 196612
  1448.6 75.4 %copy-start.44 = (f32[1,128,64]{2,1,0:T(8,128)S(1)}, f32[1,128,64]{2,1,0:T(8,128)}, u32[]{:S(2)}) copy-start(f32[1,128,64]{2,1,0:T(8,128)} %copy-done.43) | copy-start | bytes 98308
  1448.6 75.4 %copy-start.46 = (f32[1,128,64]{2,1,0:T(8,128)S(1)}, f32[1,128,64]{2,1,0:T(8,128)}, u32[]{:S(2)}) copy-start(f32[1,128,64]{2,1,0:T(8,128)} %copy-done.45) | copy-start | bytes 98308
  1448.6 75.4 %copy-start.48 = (f32[1,128,64]{2,1,0:T(8,128)S(1)}, f32[1,128,64]{2,1,0:T(8,128)}, u32[]{:S(2)}) copy-start(f32[1,128,64]{2,1,0:T(8,128)} %copy-done.47) | copy-start | bytes 98308
  1448.6 75.4 %copy-start.50 = (f32[1,128,64]{2,1,0:T(8,128)S(1)}, f32[1,128,64]{2,1,0:T(8,128)}, u32[]{:S(2)}) copy-start(f32[1,128,64]{2,1,0:T(8,128)} %copy-done.49) | copy-start | bytes 98308
  1448.6 75.4 %copy-start.79 = (f32[128,1,64]{2,1,0:T(1,128)S(1)}, f32[128,1,64]{2,1,0:T(1,128)}, u32[]{:S(2)}) copy-start(f32[128,1,64]{2,1,0:T(1,128)} %fusion.438) | copy-start | bytes 98308
  1448.6 75.4 %copy-start.80 = (f32[128,1,64]{2,1,0:T(1,128)S(1)}, f32[128,1,64]{2,1,0:T(1,128)}, u32[]{:S(2)}) copy-start(f32[128,1,64]{2,1,0:T(1,128)} %fusion.418) | copy-start | bytes 98308
  1448.6 75.4 %copy-start.83 = (f32[128,1,64]{2,1,0:T(1,128)S(1)}, f32[128,1,64]{2,1,0:T(1,128)}, u32[]{:S(2)}) copy-start(f32[128,1,64]{2,1,0:T(1,128)} %fusion.446) | copy-start | bytes 98308
  1448.6 75.4 %copy-start.84 = (f32[128,1,64]{2,1,0:T(1,128)S(1)}, f32[128,1,64]{2,1,0:T(1,128)}, u32[]{:S(2)}) copy-start(f32[128,1,64]{2,1,0:T(1,128)} %fusion.426) | copy-start | bytes 98308
  1530.8 132.8 %reduce-scatter.15.cloned.1.call-start = ((), (), s32[]{:S(2)}) async-start(), calls=%async_computation.10 | async-start | bytes 294912 | tf_op jit(solution)/shard_map/reduce_scatter | solution.py:332
  1531.8 196.3 %reduce-scatter.17.cloned.1.call-start = ((), (), s32[]{:S(2)}) async-start(), calls=%async_computation.11 | async-start | bytes 294912 | tf_op jit(solution)/shard_map/reduce_scatter | solution.py:333
  1587.0 36.4 %collective-permute-start.6 = (f32[1,128]{1,0:T(1,128)S(1)}, f32[1,128]{1,0:T(1,128)S(1)}, u32[]{:S(2)}, u32[]{:S(2)}) collective-permute-start(f32[1,128]{1,0:T(1,128)S(1)} %fusion.409), channel_id=1, source_target_pairs={{4,0},{8,4},{12,8},{16,12},{20,16},{24,20},{28,24},{5,1},{9,5},{13... | collective-permute-start | bytes 1544 | tf_op jit(solution)/shard_map/ppermute | solution.py:18
  1596.9 26.5 %collective-permute-start.7 = (f32[1,128]{1,0:T(1,128)S(1)}, f32[1,128]{1,0:T(1,128)S(1)}, u32[]{:S(2)}, u32[]{:S(2)}) collective-permute-start(f32[1,128]{1,0:T(1,128)S(1)} %fusion.408), channel_id=1, source_target_pairs={{4,0},{8,4},{12,8},{16,12},{20,16},{24,20},{28,24},{5,1},{9,5},{13... | collective-permute-start | bytes 1544 | tf_op jit(solution)/shard_map/ppermute | solution.py:18
  (214 other events, 3028.8 us)
Sparse Core Ops, SparseCore 0:
  448.1 22.3 reduce-scatter.6
  484.9 20.5 reduce-scatter.8
  1179.0 27.7 reduce-scatter.12
  1209.2 20.0 reduce-scatter.10
  1530.9 68.2 all-reduce.6
  1603.3 60.2 reduce-scatter.14
  1667.8 60.2 reduce-scatter.16
where the time goes:
time: 1750 us; the launch traced here: 1740 us
  matrix products  687 us (39%)
  blocking collectives  669 us (38%)
  local copies, waits for them, and re-layouts  157 us (9%)
  waiting for transfers between devices  112 us (6%)
  other arithmetic  64.8 us (4%)
  starting transfers between devices  23.4 us (1%)
  between operations  19.1 us (1%)
    all_gather x19, blocking collectives, prefix(): gathered = jax.tree.map(lambda a: lax.all_gather(a, axis), part)  606 us
    reduce_scatter x1, waiting for transfers between devices, shards(): lax.psum_scatter(grad_list[7], 'seq', scatter_dimension=0, tiled=True)  64.5 us
    reduce_scatter x4, waiting for transfers between devices, shards(): lax.psum_scatter(jnp.einsum('ch,rh->cr', rows_value, flat_value, preferre...  40.7 us
  transfers between devices with their start and end apart: 15, of which 5 were waited for; matrix products, arithmetic and copies ran while one was open for 18% of the time, Pallas kernels for 0%

commit v1 on v0

v1 whole, which is shorter than its diff:
```python
import functools
import math

import jax
import jax.numpy as jnp
from jax import lax
from jax.experimental import pallas as pl
from jax.experimental.pallas import tpu as pltpu
from jax.sharding import PartitionSpec as P

f32 = jnp.float32
bf16 = jnp.bfloat16
epsilon = 1e-05
NN = (((1,), (0,)), ((), ()))
NT = (((1,), (1,)), ((), ()))
TN = (((0,), (0,)), ((), ()))


def mm(left, right, dims=NN):
    return lax.dot_general(left, right, dims, preferred_element_type=f32)


def split(x):
    high = x.astype(bf16)
    return high, (x - high.astype(f32)).astype(bf16)


def swap(x, half):
    return pltpu.roll(x, half, axis=x.ndim - 1)


def lanes(shape):
    return lax.broadcasted_iota(jnp.int32, shape, len(shape) - 1)


def pair(z, half):
    low = lanes(z.shape) < half
    turned = swap(z, half)
    return jnp.where(low, z, turned), jnp.where(low, -turned, z)


def cmul(x, z, half):
    return x * z[0] + swap(x, half) * z[1]


def normal_cdf(y):
    return 0.5 * (1.0 + lax.erf(y * (1.0 / math.sqrt(2.0))))


def live_rows(lens_ref, micros, chunks, width):
    shape = (chunks, width)
    at = lax.broadcasted_iota(jnp.int32, shape, 0) * width + lanes(shape)
    rows = [(at < lens_ref[m, 0]).astype(f32) for m in range(micros)]
    return jnp.concatenate(rows, axis=0)


def channel_rows(ref, channel, micros, chunks, chans):
    rows = [
        ref[pl.ds(m * chans + channel, chunks, stride=micros * chans), :] for m in range(micros)
    ]
    return jnp.concatenate(rows, axis=0)


def shift_chunks(x, by, micros, chunks):
    cube = x.reshape(micros, chunks, x.shape[-1])
    place = lax.broadcasted_iota(jnp.int32, cube.shape, 1)
    if by > 0:
        moved = jnp.where(place >= by, pltpu.roll(cube, by, axis=1), 0.0)
    else:
        moved = jnp.where(place < chunks + by, pltpu.roll(cube, chunks + by, axis=1), 0.0)
    return moved.reshape(x.shape)


def previous(u, micros, chunks):
    turned = pltpu.roll(u, 1, axis=1)
    return jnp.where(lanes(u.shape) == 0, shift_chunks(turned, 1, micros, chunks), turned)


def following(u, micros, chunks):
    width = u.shape[1]
    turned = pltpu.roll(u, width - 1, axis=1)
    return jnp.where(
        lanes(u.shape) == width - 1, shift_chunks(turned, -1, micros, chunks), turned
    )


def mode_rows(ref, base, chans, half):
    if len(ref.shape) == 3:
        return jnp.concatenate(
            [ref[0, pl.ds(base, chans), :], ref[1, pl.ds(base, chans), :]], axis=1
        )
    part = ref[pl.ds(base, chans), :]
    return jnp.concatenate([part, part], axis=1)


def forward_kernel(
    micros,
    chunks,
    chans,
    group,
    rank_ref,
    lens_ref,
    gain_ref,
    bias_ref,
    skip_ref,
    b_ref,
    e_ref,
    c_ref,
    decay_ref,
    turn_ref,
    xhat_ref,
    act_ref,
    y_ref,
    uq_ref,
    vq_ref,
    st_ref,
    th_ref,
    tl_ref,
    dh_ref,
    dl_ref,
    ph_ref,
    pl_ref,
    jump_ref,
    rise,
    fall,
    consts,
    jumps,
    act_keep,
):
    width = xhat_ref.shape[1]
    half = decay_ref.shape[1]
    base = rank_ref[0] * chans
    levels = int(math.log2(width)) - 3
    spans = int(math.log2(chunks))

    @pl.when(pl.program_id(0) == 0)
    def _():
        decay = mode_rows(decay_ref, base, chans, half)
        turn = mode_rows(turn_ref, base, chans, half)
        b = mode_rows(b_ref, base, chans, half)
        e = mode_rows(e_ref, base, chans, half)
        c = mode_rows(c_ref, base, chans, half)
        low = lanes(decay.shape) < half
        size = jnp.exp(-decay)
        turned = jnp.where(low, jnp.cos(turn), jnp.sin(turn))
        a = size * turned
        inverse = jnp.exp(decay) * jnp.where(low, turned, -turned)
        a_pair = pair(a, half)
        power = jnp.where(low, 1.0, 0.0)
        fall[pl.ds(7 * chans, chans), :] = power
        power = a
        for k in range(8):
            rise[pl.ds(k * chans, chans), :] = power
            if k < 7:
                fall[pl.ds((6 - k) * chans, chans), :] = power
                power = cmul(power, a_pair, half)
        sign = jnp.where(low, 1.0, -1.0)
        c_pair = pair(c, half)
        ca = cmul(inverse, c_pair, half)
        b_pair = pair(b, half)
        e_pair = pair(e, half)
        consts[0] = b_pair[0]
        consts[1] = b_pair[1]
        consts[2] = e_pair[0]
        consts[3] = e_pair[1]
        consts[4] = c_pair[0]
        consts[5] = c_pair[1]
        consts[6] = cmul(ca, b_pair, half) * sign
        consts[7] = cmul(ca, e_pair, half) * sign
        for k in range(levels):
            power_pair = pair(power, half)
            consts[8 + 2 * k] = power_pair[0]
            consts[9 + 2 * k] = power_pair[1]
            power = cmul(power, power_pair, half)
        for k in range(spans):
            power_pair = pair(power, half)
            jumps[2 * k] = power_pair[0]
            jumps[2 * k + 1] = power_pair[1]
            power = cmul(power, power_pair, half)
        jump_ref[...] = jumps[...]

    live = live_rows(lens_ref, micros, chunks, width)
    rows = micros * chunks
    for g in range(group):
        channel = pl.program_id(0) * group + g

        def const(k):
            return consts[k, pl.ds(channel, 1), :]

        def jump(k):
            return (jumps[2 * k, pl.ds(channel, 1), :], jumps[2 * k + 1, pl.ds(channel, 1), :])

        up = rise[pl.ds(channel, 8, stride=chans), :]
        down = fall[pl.ds(channel, 8, stride=chans), :]
        for k in range(levels):
            step = (const(8 + 2 * k), const(9 + 2 * k))
            up = jnp.concatenate([up, cmul(up, step, half)], axis=0)
            down = jnp.concatenate([cmul(down, step, half), down], axis=0)
        up_hi, up_lo = split(up)
        down_hi, down_lo = split(down)
        ph_ref[g] = up_hi
        pl_ref[g] = up_lo
        dh_ref[g] = down_hi
        dl_ref[g] = down_lo
        row = lax.broadcasted_iota(jnp.int32, (8, width), 0)
        coefs = jnp.where(row == 0, const(6), jnp.where(row == 1, const(7), 0.0))
        coef_hi = coefs.astype(bf16).astype(f32)
        coef_both = jnp.concatenate([coef_hi, coefs - coef_hi], axis=0).astype(bf16)
        taps = mm(coef_both, up_hi, NT) + mm(coef_both, up_lo, NT)
        taps = taps[:8] + taps[8:]
        shape = (width, width)
        ahead = lanes(shape) >= lax.broadcasted_iota(jnp.int32, shape, 0)
        toeplitz = []
        for k in range(2):
            spread = jnp.broadcast_to(taps[k : k + 1], shape)
            spread = pltpu.roll(spread, 0, axis=1, stride=1, stride_axis=0)
            toeplitz.append(jnp.where(ahead, spread, 0.0))
        t_hi, t_lo = split(jnp.concatenate(toeplitz, axis=0))
        th_ref[g] = t_hi
        tl_ref[g] = t_lo

        at = base + channel
        x_hat = channel_rows(xhat_ref, channel, micros, chunks, chans)
        u = live * (x_hat * gain_ref[at] + bias_ref[at])
        v = u * previous(u, micros, chunks)
        uv_hi, uv_lo = split(jnp.concatenate([u, v], axis=0))
        q = mm(jnp.concatenate([uv_hi, uv_lo], axis=0), down_hi)
        q = q[: 2 * rows] + q[2 * rows :] + mm(uv_hi, down_lo)
        uq, vq = q[:rows], q[rows:]
        uq_ref[g] = uq
        vq_ref[g] = vq
        wide_hi = jnp.concatenate([uv_hi[:rows], uv_hi[rows:]], axis=1)
        wide_lo = jnp.concatenate([uv_lo[:rows], uv_lo[rows:]], axis=1)
        y = mm(jnp.concatenate([wide_hi, wide_lo], axis=0), t_hi)
        y = y[:rows] + y[rows:] + mm(wide_hi, t_lo)
        state = cmul(uq, (const(0), const(1)), half) + cmul(vq, (const(2), const(3)), half)
        for k in range(spans):
            state = state + cmul(shift_chunks(state, 2**k, micros, chunks), jump(k), half)
        start = shift_chunks(state, 1, micros, chunks)
        st_ref[g] = start
        sent = cmul(start, (const(4), const(5)), half)
        sent = jnp.where(lanes(sent.shape) < half, sent, -sent)
        sent_hi, sent_lo = split(sent)
        cross = mm(jnp.concatenate([sent_hi, sent_lo], axis=0), up_hi, NT)
        y = y + cross[:rows] + cross[rows:] + mm(sent_hi, up_lo, NT) + skip_ref[at] * u
        y_ref[g] = y
        act = y * normal_cdf(y)
        for m in range(micros):
            act_keep[pl.ds(m * chunks * chans + channel, chunks, stride=chans), :] = act[
                m * chunks : (m + 1) * chunks
            ]

    @pl.when(pl.program_id(0) == pl.num_programs(0) - 1)
    def _():
        act_ref[...] = act_keep[...].astype(bf16)


def backward_kernel(
    micros,
    chunks,
    chans,
    group,
    rank_ref,
    lens_ref,
    gain_ref,
    bias_ref,
    skip_ref,
    b_ref,
    e_ref,
    c_ref,
    xhat_ref,
    dact_ref,
    y_ref,
    uq_ref,
    vq_ref,
    st_ref,
    th_ref,
    tl_ref,
    dh_ref,
    dl_ref,
    ph_ref,
    pl_ref,
    jump_ref,
    dh_out,
    gb_ref,
    ge_ref,
    gc_ref,
    gs_ref,
    gg_ref,
    gn_ref,
    consts,
):
    width = xhat_ref.shape[1]
    half = b_ref.shape[2]
    base = rank_ref[0] * chans
    spans = int(math.log2(chunks))

    @pl.when(pl.program_id(0) == 0)
    def _():
        for k, ref in enumerate((b_ref, e_ref, c_ref)):
            both = pair(mode_rows(ref, base, chans, half), half)
            consts[2 * k] = both[0]
            consts[2 * k + 1] = both[1]

    live = live_rows(lens_ref, micros, chunks, width)
    rows = micros * chunks
    shape = (width, width)
    sub = lax.broadcasted_iota(jnp.int32, shape, 0)
    mirror = (lanes(shape) + sub == width - 1).astype(f32).astype(bf16)
    ahead = lanes(shape) >= sub
    for g in range(group):
        channel = pl.program_id(0) * group + g

        def const(k):
            return (consts[2 * k, pl.ds(channel, 1), :], consts[2 * k + 1, pl.ds(channel, 1), :])

        def jump(k):
            return (
                jump_ref[2 * k, pl.ds(channel, 1), :],
                jump_ref[2 * k + 1, pl.ds(channel, 1), :],
            )

        at = base + channel
        gain = gain_ref[at]
        x_hat = channel_rows(xhat_ref, channel, micros, chunks, chans)
        u = live * (x_hat * gain + bias_ref[at])
        u_prev = previous(u, micros, chunks)
        v = u * u_prev
        y = y_ref[g]
        d_act = dact_ref[pl.ds(channel, rows, stride=chans), :]
        density = jnp.exp(-0.5 * y * y) * (1.0 / math.sqrt(2.0 * math.pi))
        d_y = d_act * (normal_cdf(y) + y * density)
        dy_hi, dy_lo = split(d_y)
        dy_both = jnp.concatenate([dy_hi, dy_lo], axis=0)
        up_hi = ph_ref[g]
        down_hi = dh_ref[g]
        down_lo = dl_ref[g]
        t_hi = th_ref[g]
        t_lo = tl_ref[g]
        first = mm(dy_both, jnp.concatenate([up_hi, mirror], axis=1))
        yd = first[:rows, :width] + first[rows:, :width] + mm(dy_hi, pl_ref[g])
        back_hi = first[:rows, width:].astype(bf16)
        back_lo = first[rows:, width:].astype(bf16)
        duv = mm(dy_both, t_hi, NT)
        duv = duv[:rows] + duv[rows:] + mm(dy_hi, t_lo, NT)
        d_u, d_v = duv[:, :width], duv[:, width:]

        wide_hi, wide_lo = split(jnp.concatenate([u, v], axis=1))
        outer = mm(
            jnp.concatenate([back_hi, back_lo, back_hi], axis=0),
            jnp.concatenate([wide_hi, wide_hi, wide_lo], axis=0),
            TN,
        )
        sums = []
        for k in range(2):
            turned = pltpu.roll(
                outer[:, k * width : (k + 1) * width], 0, axis=1, stride=1, stride_axis=0
            )
            sums.append(jnp.sum(jnp.where(ahead, turned, 0.0), axis=0, keepdims=True))
        row = lax.broadcasted_iota(jnp.int32, (8, width), 0)
        lags = jnp.where(row == 0, sums[0], jnp.where(row == 1, sums[1], 0.0))
        lag_hi = lags.astype(bf16).astype(f32)
        lag_both = jnp.concatenate([lag_hi, lags - lag_hi], axis=0).astype(bf16)
        tops = mm(lag_both, down_hi) + mm(lag_both, down_lo)
        tops = tops[:8] + tops[8:]
        top_u, top_v = tops[0:1], tops[1:2]

        adj = cmul(yd, const(2), half)
        for k in range(spans):
            adj = adj + cmul(shift_chunks(adj, -(2**k), micros, chunks), jump(k), half)
        adj = shift_chunks(adj, -1, micros, chunks)
        sent = jnp.concatenate([cmul(adj, const(0), half), cmul(adj, const(1), half)], axis=0)
        sent = jnp.where(lanes(sent.shape) < half, sent, -sent)
        sent_hi, sent_lo = split(sent)
        cross = mm(jnp.concatenate([sent_hi, sent_lo], axis=0), down_hi, NT)
        cross = cross[: 2 * rows] + cross[2 * rows :] + mm(sent_hi, down_lo, NT)
        d_v = d_v + cross[rows:]
        d_u = d_u + cross[:rows] + skip_ref[at] * d_y + d_v * u_prev
        d_u = d_u + following(d_v * u, micros, chunks)

        def total(x):
            return jnp.sum(x, axis=0, keepdims=True)

        adj_pair = pair(adj, half)
        flip = jnp.where(lanes((1, width)) < half, 1.0, -1.0)
        gb_ref[pl.ds(channel, 1), :] = flip * (
            cmul(top_u, const(2), half) + total(cmul(uq_ref[g], adj_pair, half))
        )
        ge_ref[pl.ds(channel, 1), :] = flip * (
            cmul(top_v, const(2), half) + total(cmul(vq_ref[g], adj_pair, half))
        )
        gc_ref[pl.ds(channel, 1), :] = flip * (
            cmul(top_u, const(0), half)
            + cmul(top_v, const(1), half)
            + total(cmul(st_ref[g], pair(yd, half), half))
        )
        gs_ref[pl.ds(channel, 1), :] = total(d_y * u)
        d_q = live * d_u
        gg_ref[pl.ds(channel, 1), :] = total(d_q * x_hat)
        gn_ref[pl.ds(channel, 1), :] = total(d_q)
        d_h = d_q * gain
        for m in range(micros):
            dh_out[pl.ds(m * chans + channel, chunks, stride=micros * chans), :] = d_h[
                m * chunks : (m + 1) * chunks
            ]


def project_kernel(
    width,
    place_ref,
    lens_ref,
    act_ref,
    xc_ref,
    wv_ref,
    wg_ref,
    bias_ref,
    out_ref,
    dact_ref,
):
    peers, _, chans, rows = xc_ref.shape
    full = peers * chans
    x = xc_ref[:, 0].reshape(full, rows).astype(f32)
    cot = xc_ref[:, 1].reshape(full, rows).astype(f32)
    start = place_ref[1] * rows
    at = place_ref[0] * width + lax.rem(start, width) + lanes((1, rows))
    live = (at < lens_ref[start // width, 0]).astype(f32)
    act = act_ref[...]
    wv = wv_ref[...]
    wg = wg_ref[...]
    value = mm(wv, act, TN) + bias_ref[:, 0:1]
    gate = jax.nn.sigmoid(mm(wg, act, TN) + bias_ref[:, 1:2])
    g = live * cot
    d_value = (g * gate).astype(bf16)
    d_gate = (g * value * gate * (1.0 - gate)).astype(bf16)
    out = (live * (x + value * gate)).astype(bf16)
    out_ref[:, 0] = out.reshape(peers, chans, rows)
    out_ref[:, 1] = d_value.reshape(peers, chans, rows)
    out_ref[:, 2] = d_gate.reshape(peers, chans, rows)
    dact_ref[...] = mm(wv, d_value) + mm(wg, d_gate)


def smem():
    return pl.BlockSpec(memory_space=pltpu.SMEM)


def whole(shape):
    return pl.BlockSpec(shape, lambda i: (0,) * len(shape))


def piece(shape):
    return pl.BlockSpec(shape, lambda i: (i,) + (0,) * (len(shape) - 1))


def shards(
    tokens,
    lengths,
    ln_gain,
    ln_bias,
    b_coef,
    e_coef,
    c_coef,
    skip_gain,
    decay_rate,
    rotation,
    w_value,
    w_gate,
    bias_value,
    bias_gate,
    out_cotangent,
):
    micros, wide, width = tokens.shape
    modes = decay_rate.shape[1]
    full = w_value.shape[0]
    seqs = lax.axis_size("seq")
    peers = lax.axis_size("chan")
    seq_rank = lax.axis_index("seq").astype(jnp.int32)
    chan_rank = lax.axis_index("chan").astype(jnp.int32)
    chans = wide // seqs
    rows = micros * seqs
    own = micros * width // peers
    parts = width // own
    both = ("chan", "seq")
    group = min(4, chans)
    steps = chans // group

    def to_own(x):
        return x.reshape(micros, -1, parts, own).transpose(0, 2, 1, 3).reshape(peers, -1, own)

    def from_own(x):
        return x.reshape(micros, parts, -1, own).transpose(0, 2, 1, 3).reshape(micros, -1, width)

    xc = jnp.stack([to_own(tokens), to_own(out_cotangent)], axis=1)
    xc = lax.all_to_all(xc, "chan", 0, 0, tiled=True)
    weights = lax.all_gather(jnp.stack([w_value, w_gate]), "chan", axis=2, tiled=True)

    x_full = tokens.astype(f32)
    part_mean = jnp.mean(x_full, axis=1)
    part_square = jnp.sum(jnp.square(x_full - part_mean[:, None, :]), axis=1)
    biases = jnp.stack([bias_value, bias_gate])
    stats = lax.all_gather(
        jnp.concatenate([part_mean, part_square, jnp.pad(biases, ((0, 0), (0, width - wide)))]),
        "chan",
    )
    means = stats[:, :micros]
    row_mean = jnp.mean(means, axis=0)
    row_var = (
        jnp.sum(stats[:, micros : 2 * micros], axis=0)
        + wide * jnp.sum(jnp.square(means - row_mean), axis=0)
    ) / full
    inv_std = lax.rsqrt(row_var + epsilon)
    x_hat = (x_full - row_mean[:, None, :]) * inv_std[:, None, :]
    bias_cols = stats[:, 2 * micros :, :wide].transpose(0, 2, 1).reshape(full, 2)

    x_mine = lax.all_to_all(
        x_hat.reshape(micros, seqs, chans, width).transpose(1, 0, 2, 3),
        "seq",
        0,
        0,
        tiled=True,
    ).reshape(seqs * micros * chans, width)

    rank = seq_rank.reshape(1)
    levels = int(math.log2(width)) - 3
    spans = int(math.log2(seqs))
    lane = 2 * modes
    kept = [
        jax.ShapeDtypeStruct((chans, rows, width), f32),
        jax.ShapeDtypeStruct((chans, rows, lane), f32),
        jax.ShapeDtypeStruct((chans, rows, lane), f32),
        jax.ShapeDtypeStruct((chans, rows, lane), f32),
        jax.ShapeDtypeStruct((chans, 2 * width, width), bf16),
        jax.ShapeDtypeStruct((chans, 2 * width, width), bf16),
        jax.ShapeDtypeStruct((chans, width, lane), bf16),
        jax.ShapeDtypeStruct((chans, width, lane), bf16),
        jax.ShapeDtypeStruct((chans, width, lane), bf16),
        jax.ShapeDtypeStruct((chans, width, lane), bf16),
    ]
    kept_specs = [piece((group,) + k.shape[1:]) for k in kept]
    jump_shape = (2 * spans, chans, lane)
    limits = pltpu.CompilerParams(vmem_limit_bytes=48 * 1024 * 1024)
    act, *saved = pl.pallas_call(
        functools.partial(forward_kernel, micros, seqs, chans, group),
        grid=(steps,),
        in_specs=[smem()] * 5
        + [whole(b_coef.shape)] * 3
        + [whole(decay_rate.shape)] * 2
        + [whole(x_mine.shape)],
        out_specs=[whole((rows * chans, width))] + kept_specs + [whole(jump_shape)],
        out_shape=[jax.ShapeDtypeStruct((rows * chans, width), bf16)]
        + kept
        + [jax.ShapeDtypeStruct(jump_shape, f32)],
        scratch_shapes=[
            pltpu.VMEM((8 * chans, lane), f32),
            pltpu.VMEM((8 * chans, lane), f32),
            pltpu.VMEM((8 + 2 * levels, chans, lane), f32),
            pltpu.VMEM(jump_shape, f32),
            pltpu.VMEM((rows * chans, width), f32),
        ],
        compiler_params=limits,
        name="mixer_forward",
    )(
        rank,
        lengths,
        ln_gain,
        ln_bias,
        skip_gain,
        b_coef,
        e_coef,
        c_coef,
        decay_rate,
        rotation,
        x_mine,
    )

    act = (
        act.reshape(micros, seqs, chans, parts, own)
        .transpose(0, 3, 1, 2, 4)
        .reshape(peers * seqs, chans, own)
    )
    act = lax.all_to_all(act, both, 0, 0, tiled=True).reshape(full, own)
    place = jnp.stack([seq_rank, chan_rank])
    sent, d_act = pl.pallas_call(
        functools.partial(project_kernel, width),
        in_specs=[smem()] * 2 + [pl.BlockSpec(memory_space=pltpu.VMEM)] * 5,
        out_specs=[pl.BlockSpec(memory_space=pltpu.VMEM)] * 2,
        out_shape=[
            jax.ShapeDtypeStruct((peers, 3, wide, own), bf16),
            jax.ShapeDtypeStruct((full, own), f32),
        ],
        compiler_params=limits,
        name="project",
    )(place, lengths, act, xc, weights[0], weights[1], bias_cols)

    d_act = lax.all_to_all(
        d_act.reshape(peers * seqs, chans, own), both, 0, 0, tiled=True
    )
    d_act = (
        d_act.reshape(micros, parts, seqs, chans, own)
        .transpose(0, 2, 3, 1, 4)
        .reshape(rows * chans, width)
    )
    small = jax.ShapeDtypeStruct((chans, lane), f32)
    d_hat_mine, *grads = pl.pallas_call(
        functools.partial(backward_kernel, micros, seqs, chans, group),
        grid=(steps,),
        in_specs=[smem()] * 5
        + [whole(b_coef.shape)] * 3
        + [whole(x_mine.shape)] * 2
        + kept_specs
        + [whole(jump_shape)],
        out_specs=[whole(x_mine.shape)] + [whole(small.shape)] * 6,
        out_shape=[jax.ShapeDtypeStruct(x_mine.shape, f32)] + [small] * 6,
        scratch_shapes=[pltpu.VMEM((6, chans, lane), f32)],
        compiler_params=limits,
        name="mixer_backward",
    )(
        rank,
        lengths,
        ln_gain,
        ln_bias,
        skip_gain,
        b_coef,
        e_coef,
        c_coef,
        x_mine,
        d_act,
        *saved,
    )

    sent = lax.all_to_all(sent, "chan", 0, 0, tiled=True)
    out = from_own(sent[:, 0])
    act_all = lax.all_gather(act, "chan")
    d_both = sent[:, 1:].reshape(peers, 2 * wide, own)
    grad_w = jnp.einsum("pkr,pdr->kd", act_all, d_both, preferred_element_type=f32)
    grad_bias = jnp.sum(sent[:, 1:].astype(f32), axis=(0, 3)).reshape(1, 2, wide)
    grad_w = grad_w.reshape(seqs, full // seqs, 2, wide).transpose(0, 2, 1, 3)

    sums = jnp.stack([jnp.sum(g, axis=1) for g in grads[3:]])
    shared = jnp.concatenate(
        [
            jnp.stack(grads[:3]).reshape(-1),
            sums.reshape(-1),
            grad_bias.reshape(-1),
        ]
    )
    pad = -shared.shape[0] % width
    shared = jnp.pad(shared, (0, pad)).reshape(1, -1, width)
    tail = jnp.concatenate(
        [
            d_hat_mine.reshape(seqs, micros * chans, width),
            jnp.broadcast_to(shared, (seqs,) + shared.shape[1:]),
            grad_w.reshape(seqs, -1, width),
        ],
        axis=1,
    )
    tail = lax.all_to_all(tail, "seq", 0, 0, tiled=True)
    cut = micros * chans
    d_hat = (
        tail[:, :cut]
        .reshape(seqs, micros, chans, width)
        .transpose(1, 0, 2, 3)
        .reshape(micros, wide, width)
    )
    last = cut + shared.shape[1]
    got = tail[:, cut:last].reshape(seqs, -1)
    modes_end = 3 * chans * lane
    got_modes = (
        got[:, :modes_end]
        .reshape(seqs, 3, chans, 2, modes)
        .transpose(1, 3, 0, 2, 4)
        .reshape(3, 2, wide, modes)
    )
    got_sums = (
        got[:, modes_end : modes_end + 3 * chans]
        .reshape(seqs, 3, chans)
        .transpose(1, 0, 2)
        .reshape(3, wide)
    )
    bias_at = modes_end + 3 * chans
    got_bias = jnp.sum(got[:, bias_at : bias_at + 2 * wide].reshape(seqs, 2, wide), axis=0)
    got_w = jnp.sum(tail[:, last:], axis=0).reshape(2, full // seqs, wide)

    own_sums = lax.all_gather(
        jnp.concatenate([jnp.sum(d_hat, axis=1), jnp.sum(d_hat * x_hat, axis=1)]), "chan"
    )
    hat_sums = jnp.sum(own_sums, axis=0) / full
    positions = seq_rank * width + jnp.arange(width, dtype=jnp.int32)
    live = (positions[None, :] < lengths).astype(f32)
    d_input = live[:, None, :] * out_cotangent.astype(f32) + inv_std[:, None, :] * (
        d_hat - hat_sums[:micros, None, :] - x_hat * hat_sums[micros:, None, :]
    )
    return (
        out,
        d_input,
        got_sums[1],
        got_sums[2],
        got_modes[0],
        got_modes[1],
        got_modes[2],
        got_sums[0],
        got_w[0],
        got_w[1],
        got_bias[0],
        got_bias[1],
    )


def solution(mesh):
    chan = P("chan")
    modes = P(None, "chan", None)
    table = P("chan", None)
    weight = P(None, "chan")
    rows = P(None, "chan", "seq")
    spread = P("seq", "chan")
    return jax.shard_map(
        shards,
        mesh=mesh,
        in_specs=(
            rows,
            P(),
            chan,
            chan,
            modes,
            modes,
            modes,
            chan,
            table,
            table,
            weight,
            weight,
            chan,
            chan,
            rows,
        ),
        out_specs=(
            rows,
            rows,
            chan,
            chan,
            modes,
            modes,
            modes,
            chan,
            spread,
            spread,
            chan,
            chan,
        ),
        check_vma=False,
    )
```

time: 1750 us -> 177 us (0.10)
  matrix products: 687 us -> 2.18 us
  blocking collectives: 669 us -> 30.6 us
  local copies, waits for them, and re-layouts: 157 us -> 35.3 us
  waiting for transfers between devices: 112 us -> 38.4 us
  other arithmetic: 64.8 us -> 7.67 us
  Pallas kernels: 0 us -> 25.3 us
    dot_general x126 -> x1, matrix products: 687 us -> 2.18 us  [shards(): jnp.einsum('pkr,pdr->kd', act_all, d_both, preferred_element_type=f32)]
    all_gather x23 -> x3, blocking collectives: 628 us -> 20.8 us  [the longest x1 9.44 us: shards(): act_all = lax.all_gather(act, 'chan')]
    reduce_scatter x6 -> x0, waiting for transfers between devices: 112 us -> none  [the longest x1 64.5 us: shards(): lax.psum_scatter(grad_list[7], 'seq', scatter_dimension=0, tiled=True)]
    dot_general x38 -> x0, local copies, waits for them, and re-layouts: 67.5 us -> none  [the longest x4 21.4 us: shards(): jnp.einsum('mbth,mbjh->htj', dy_blocks, v_blocks, precision=highest)]
    psum x4 -> x0, blocking collectives: 41.8 us -> none  [the longest x1 20.9 us: shards(): lax.psum((grad_list[0], grad_list[1], grad_list[2], grad_list[3], grad_li...]
    all_to_all x0 -> x5, waiting for transfers between devices: none -> 38.4 us  [the longest x1 23.3 us: shards(): tail = lax.all_to_all(tail, 'seq', 0, 0, tiled=True)]
    mul x33 -> x1, other arithmetic: 28.7 us -> 0.03 us  [shards(): x_hat = (x_full - row_mean[:, None, :]) * inv_std[:, None, :]]
    pallas_call x0 -> x3, Pallas kernels: none -> 25.3 us  [the longest x1 13.7 us: shards(): pl.pallas_call(functools.partial(forward_kernel, micros, seqs, chans, gro...]
  transfers between devices with their start and end apart: 15 -> 6, of which waited for: 5 -> 3; matrix products, arithmetic and copies ran while one was open for 18% -> 5% of each run, Pallas kernels for 0% -> 8%
where the time goes in v1:
time: 177 us; the launch traced here: 176 us
  waiting for transfers between devices  38.4 us (22%)
  local copies, waits for them, and re-layouts  35.3 us (20%)
  blocking collectives  30.6 us (17%)
  Pallas kernels  25.3 us (14%)
  starting transfers between devices  22.1 us (12%)
  between operations  14.4 us (8%)
  other arithmetic  7.67 us (4%)
  matrix products  2.18 us (1%)
    unnamed x114, local copies, waits for them, and re-layouts  28 us
    all_to_all x1, waiting for transfers between devices, shards(): tail = lax.all_to_all(tail, 'seq', 0, 0, tiled=True)  23.3 us
    pallas_call x1, Pallas kernels, shards(): pl.pallas_call(functools.partial(forward_kernel, micros, seqs, chans, gro...  13.7 us
    all_to_all x1, blocking collectives, shards(): sent = lax.all_to_all(sent, 'chan', 0, 0, tiled=True)  9.84 us
    pallas_call x1, Pallas kernels, shards(): pl.pallas_call(functools.partial(backward_kernel, micros, seqs, chans, gr...  9.74 us
    all_gather x1, blocking collectives, shards(): act_all = lax.all_gather(act, 'chan')  9.44 us
    all_to_all x1, waiting for transfers between devices, shards(): lax.all_to_all(x_hat.reshape(micros, seqs, chans, width).transpose(1, 0,...  8.68 us
    all_to_all x1, waiting for transfers between devices, shards(): act = lax.all_to_all(act, both, 0, 0, tiled=True).reshape(full, own)  6.44 us
  transfers between devices with their start and end apart: 6, of which 3 were waited for; matrix products, arithmetic and copies ran while one was open for 5% of the time, Pallas kernels for 8%

profile of v1, /device:TPU:0, one launch (start us, length us, event | category | flops | bytes accessed | tf_op | source)
XLA Modules:
  0.0 176.0 jit_solution(7083330160207237817)
XLA Ops:
  7.2 1.7 pad_maximum_fusion.2
  9.0 0.9 copy-done.33
  10.0 0.6 copy-done.50
  10.6 6.2 %all-gather.2 = f32[4,10,128]{2,1,0:T(8,128)S(1)} all-gather(f32[1,10,128]{2,1,0:T(8,128)S(1)} %maximum_bitcast_fusion), channel_id=2, replica_groups=mesh['seq'=8,'chan'=4] {'chan'}, dimensions={0}, use_global_device_ids=true | all-gather | bytes 25600 | tf_op jit(solution)/shard_map/all_gather | solution.py:500
  16.9 0.6 copy-done.41
  18.0 0.7 copy.180
  18.8 6.4 %all-to-all-start = ((f32[8,4,16,128]{3,2,1,0:T(8,128)}), f32[8,4,16,128]{3,2,1,0:T(8,128)S(1)}, u32[]{:S(2)}, u32[]{:S(2)}) async-start(f32[8,4,16,128]{3,2,1,0:T(8,128)} %bitcast.85), calls=%async_computation | async-start | bytes 524288 | tf_op jit(solution)/shard_map/all_to_all | solution.py:514
  25.1 0.7 pad_maximum_fusion.1
  25.9 8.7 %all-to-all-done = f32[8,4,16,128]{3,2,1,0:T(8,128)S(1)} async-done(((f32[8,4,16,128]{3,2,1,0:T(8,128)}), f32[8,4,16,128]{3,2,1,0:T(8,128)S(1)}, u32[]{:S(2)}, u32[]{:S(2)}) %all-to-all-start) | async-done | bytes 262176 | tf_op jit(solution)/shard_map/all_to_all | solution.py:514
  34.5 3.5 %all-to-all-start.2 = ((bf16[4,2,128,128]{3,2,1,0:T(8,128)(2,1)}), bf16[4,2,128,128]{3,2,1,0:T(8,128)(2,1)S(1)}, u32[]{:S(2)}, u32[]{:S(2)}) async-start(bf16[4,2,128,128]{3,2,1,0:T(8,128)(2,1)} %pad_maximum_fusion.1), calls=%async_computation.2 | async-start | bytes 524288 | tf_op jit(solution)/shard_map/all_to_all | solution.py:493
  38.1 0.6 copy-done.48
  38.9 0.7 copy-done.46
  39.7 0.7 copy-done.38
  40.6 0.7 copy-done.39
  41.4 0.7 copy-done.40
  42.5 0.7 copy-done.28
  43.2 13.7 %mixer_forward.1 = (bf16[512,128]{1,0:T(8,128)(2,1)}, f32[16,32,128]{2,1,0:T(8,128)S(1)}, f32[16,32,128]{2,1,0:T(8,128)S(1)}, f32[16,32,128]{2,1,0:T(8,128)S(1)}...) custom-call(s32[1]{0:T(128)} %bitcast.rank_ref, ...), custom_call_target="tpu_custom_call" | custom-call | tf_op jit(solution)/shard_map/mixer_forward/pallas_call | solution.py:541
  56.8 0.8 copy-done
  57.6 0.8 copy-done.2
  58.4 0.8 copy-done.4
  59.2 0.8 copy-done.6
  60.0 0.7 copy-done.9
  60.7 0.7 copy-done.11
  61.5 0.7 copy-done.13
  62.1 0.7 copy-done.15
  62.9 0.6 copy-done.17
  63.5 4.1 %all-to-all-start.1 = ((bf16[32,16,128]{2,1,0:T(8,128)(2,1)}), bf16[32,16,128]{2,1,0:T(8,128)(2,1)S(1)}, u32[]{:S(2)}, u32[]{:S(2)}) async-start(bf16[32,16,128]{2,1,0:T(8,128)(2,1)} %bitcast.8), calls=%async_computation.1 | async-start | bytes 262144 | tf_op jit(solution)/shard_map/all_to_all | solution.py:580
  67.6 1.3 slice_bitcast_fusion
  68.9 6.4 %all-to-all-done.1 = bf16[32,16,128]{2,1,0:T(8,128)(2,1)S(1)} async-done(((bf16[32,16,128]{2,1,0:T(8,128)(2,1)}), bf16[32,16,128]{2,1,0:T(8,128)(2,1)S(1)}, u32[]{:S(2)}, u32[]{:S(2)}) %all-to-all-start.1) | async-done | bytes 131104 | tf_op jit(solution)/shard_map/all_to_all | solution.py:580
  75.3 1.9 %project.1 = (bf16[4,3,128,128]{3,2,1,0:T(8,128)(2,1)S(1)}, f32[512,128]{1,0:T(8,128)S(1)}) custom-call(s32[2]{0:T(128)S(1)} %pad_add_fusion.place_ref, s32[4,1]{1,0:T(4,128)S(1)} %copy.143.lens_ref, bf16[512,128]{1,0:T(8,128)(2,1)S(1)} %bitcast.89, bf16[4,2,128,128]{3,2,1,0:T(8,128)(2,1)S(1)} %all-to-all-done.2.xc_ref, ...), custom_call_target="tpu_custom_call" | custom-call | tf_op jit(solution)/shard_map/project/pallas_call | solution.py:582
  77.2 9.8 %all_to_all.30 = bf16[4,3,128,128]{3,2,1,0:T(8,128)(2,1)S(1)} all-to-all(bf16[4,3,128,128]{3,2,1,0:T(8,128)(2,1)S(1)} %get-tuple-element.34), channel_id=1, replica_groups=mesh['seq'=8,'chan'=4] {'chan'}, dimensions={0} | all-to-all | bytes 786432 | tf_op jit(solution)/shard_map/all_to_all | solution.py:630
  87.1 2.6 %all-to-all-start.4 = ((f32[32,16,128]{2,1,0:T(8,128)}), f32[32,16,128]{2,1,0:T(8,128)S(1)}, u32[]{:S(2)}, u32[]{:S(2)}) async-start(f32[32,16,128]{2,1,0:T(8,128)} %bitcast.93), calls=%async_computation.4 | async-start | bytes 524288 | tf_op jit(solution)/shard_map/all_to_all | solution.py:594
  89.7 9.4 %all_gather.21 = bf16[4,512,128]{2,1,0:T(8,128)(2,1)S(1)} all-gather(bf16[1,512,128]{2,1,0:T(8,128)(2,1)S(1)} %bitcast.90), channel_id=1, replica_groups=mesh['seq'=8,'chan'=4] {'chan'}, dimensions={0}, use_global_device_ids=true | all-gather | bytes 655360 | tf_op jit(solution)/shard_map/all_gather | solution.py:632
  99.1 0.7 convert_reduce_fusion
  99.8 2.2 %fusion = f32[8,64,2,128,1]{3,1,4,2,0:T(8,128)} fusion(bf16[8,64,4,128,1]{3,1,0,2,4:T(8,128)(2,1)S(1)} %bitcast.106, bf16[4,3,128,128]{3,2,1,0:T(8,128)(2,1)} %copy-done.35), kind=kOutput, calls=%fused_computation.4 | convolution fusion | flops 134217728 | bytes 1310720 | tf_op jit(solution)/shard_map/pkr,pdr->kd/dot_general | solution.py:634
  102.0 0.6 copy-done.30
  102.7 1.0 copy-done.5
  103.7 1.0 copy-done.7
  104.7 0.9 copy-done.12
  105.7 0.9 copy-done.14
  106.6 0.9 copy-done.16
  107.6 0.8 copy-done.18
  108.4 9.7 %mixer_backward.1 = (f32[512,128]{1,0:T(8,128)S(1)}, f32[16,128]{1,0:T(8,128)S(1)}, f32[16,128]{1,0:T(8,128)S(1)}, f32[16,128]{1,0:T(8,128)S(1)}, f32[16,128]{1,...) custom-call(s32[1]{0:T(128)} %bitcast.rank_ref, s32[4,1]{1,0:T(4,128)S(1)} %copy.143.lens_ref, ...), custom_call_target="tpu_custom_call" | custom-call | tf_op jit(solution)/shard_map/mixer_backward/pallas_call | solution.py:603
  118.2 0.6 copy-done.19
  118.7 0.6 copy-done.21
  119.3 0.6 copy-done.22
  119.9 0.6 copy-done.24
  120.5 0.6 copy-done.26
  121.1 0.8 reduce_sum.131
  122.9 0.7 copy-done.47
  123.7 2.1 %pad_maximum_fusion = f32[8,243,128]{2,1,0:T(8,128)} fusion(f32[8,128,128]{2,1,0:T(8,128)} %bitcast.111, f32[8,51,128]{2,1,0:T(8,128)S(1)} %broadcast_in_dim.5, f32[8,64,128]{2,1,0:T(8,128)S(1)} %bitcast.94), kind=kLoop, calls=%fused_computation | loop fusion | flops 497664 | bytes 1990656 | tf_op jit(solution)/shard_map/concatenate | solution.py:648
  125.8 5.5 %all-to-all-start.5 = ((f32[8,243,128]{2,1,0:T(8,128)}), f32[8,243,128]{2,1,0:T(8,128)S(1)}, u32[]{:S(2)}, u32[]{:S(2)}) async-start(f32[8,243,128]{2,1,0:T(8,128)} %pad_maximum_fusion), calls=%async_computation.5 | async-start | bytes 2031616 | tf_op jit(solution)/shard_map/all_to_all | solution.py:656
  131.3 0.6 copy-done.49
  132.0 1.6 slice_bitcast_fusion.3
  133.6 23.3 %all-to-all-done.5 = f32[8,243,128]{2,1,0:T(8,128)S(1)} async-done(((f32[8,243,128]{2,1,0:T(8,128)}), f32[8,243,128]{2,1,0:T(8,128)S(1)}, u32[]{:S(2)}, u32[]{:S(2)}) %all-to-all-start.5) | async-done | bytes 995360 | tf_op jit(solution)/shard_map/all_to_all | solution.py:656
  157.2 0.6 fusion.12
  158.8 0.6 squeeze.35
  159.3 0.6 squeeze.31
  159.9 0.6 squeeze.30
  160.5 5.2 %all-gather.1 = f32[32,128]{1,0:T(8,128)S(1)} all-gather(f32[8,128]{1,0:T(8,128)S(1)} %pad_maximum_fusion.4), channel_id=3, replica_groups=mesh['seq'=8,'chan'=4] {'chan'}, dimensions={0}, use_global_device_ids=true | all-gather | bytes 20480 | tf_op jit(solution)/shard_map/all_gather | solution.py:683
  166.1 0.7 copy.157
  166.8 0.7 copy.156
  167.5 0.7 copy.155
  168.4 0.8 fusion.8
  (124 shorter events, 4.6 us)
Async XLA Ops:
  7.2 60.4 %all-gather.5.cloned.1.call-start = ((), (), s32[]{:S(2)}) async-start(), calls=%async_computation.6 | async-start | bytes 1310720 | tf_op jit(solution)/shard_map/all_gather | solution.py:494
  8.9 0.9 copy-start.33
  9.9 0.7 copy-start.50
  10.0 0.7 copy-start.51
  16.8 0.6 copy-start.41
  17.4 0.6 copy-start.43
  18.7 6.4 %copy-start.36 = (bf16[4,128,128]{2,1,0:T(8,128)(2,1)S(1)}, bf16[4,128,128]{2,1,0:T(8,128)(2,1)}, u32[]{:S(2)}) copy-start(bf16[4,128,128]{2,1,0:T(8,128)(2,1)} %param.29) | copy-start | bytes 393220
  18.8 15.8 %all-to-all-start = ((f32[8,4,16,128]{3,2,1,0:T(8,128)}), f32[8,4,16,128]{3,2,1,0:T(8,128)S(1)}, u32[]{:S(2)}, u32[]{:S(2)}) async-start(f32[8,4,16,128]{3,2,1,0:T(8,128)} %bitcast.85), calls=%async_computation | async-start | bytes 524288 | tf_op jit(solution)/shard_map/all_to_all | solution.py:514
  34.5 4.3 %copy-start.45 = (f32[128,64]{0,1:T(8,128)S(1)}, f32[128,64]{0,1:T(8,128)}, u32[]{:S(2)}) copy-start(f32[128,64]{0,1:T(8,128)} %param.23) | copy-start | bytes 98308
  34.5 29.0 %all-to-all-start.2 = ((bf16[4,2,128,128]{3,2,1,0:T(8,128)(2,1)}), bf16[4,2,128,128]{3,2,1,0:T(8,128)(2,1)S(1)}, u32[]{:S(2)}, u32[]{:S(2)}) async-start(bf16[4,2,128,128]{3,2,1,0:T(8,128)(2,1)} %pad_maximum_fusion.1), calls=%async_computation.2 | async-start | bytes 524288 | tf_op jit(solution)/shard_map/all_to_all | solution.py:493
  38.1 0.7 copy-start.48
  38.9 0.8 copy-start.46
  39.6 0.8 copy-start.38
  40.4 0.8 copy-start.39
  41.3 0.8 copy-start.40
  42.5 0.7 copy-start.28
  42.5 0.7 copy-start.29
  42.5 0.7 copy-start.31
  56.8 0.8 copy-start
  57.6 0.8 copy-start.2
  58.4 0.8 copy-start.4
  59.2 0.8 copy-start.6
  60.0 0.7 copy-start.9
  60.7 0.7 copy-start.11
  61.5 0.7 copy-start.13
  62.1 0.7 copy-start.15
  62.9 0.6 copy-start.17
  63.5 11.8 %all-to-all-start.1 = ((bf16[32,16,128]{2,1,0:T(8,128)(2,1)}), bf16[32,16,128]{2,1,0:T(8,128)(2,1)S(1)}, u32[]{:S(2)}, u32[]{:S(2)}) async-start(bf16[32,16,128]{2,1,0:T(8,128)(2,1)} %bitcast.8), calls=%async_computation.1 | async-start | bytes 262144 | tf_op jit(solution)/shard_map/all_to_all | solution.py:580
  77.2 9.8 %copy-start.8 = (f32[512,128]{1,0:T(8,128)}, f32[512,128]{1,0:T(8,128)S(1)}, u32[]{:S(2)}) copy-start(f32[512,128]{1,0:T(8,128)S(1)} %get-tuple-element.35) | copy-start | bytes 786436
  87.1 12.0 %copy-start.35 = (bf16[4,3,128,128]{3,2,1,0:T(8,128)(2,1)}, bf16[4,3,128,128]{3,2,1,0:T(8,128)(2,1)S(1)}, u32[]{:S(2)}) copy-start(bf16[4,3,128,128]{3,2,1,0:T(8,128)(2,1)S(1)} %all_to_all.30) | copy-start | bytes 1179652
  87.1 14.9 %all-to-all-start.4 = ((f32[32,16,128]{2,1,0:T(8,128)}), f32[32,16,128]{2,1,0:T(8,128)S(1)}, u32[]{:S(2)}, u32[]{:S(2)}) async-start(f32[32,16,128]{2,1,0:T(8,128)} %bitcast.93), calls=%async_computation.4 | async-start | bytes 524288 | tf_op jit(solution)/shard_map/all_to_all | solution.py:594
  99.8 2.2 %copy-start.1 = (bf16[16,128,128]{2,1,0:T(8,128)(2,1)S(1)}, bf16[16,128,128]{2,1,0:T(8,128)(2,1)}, u32[]{:S(2)}) copy-start(bf16[16,128,128]{2,1,0:T(8,128)(2,1)} %copy-done) | copy-start | bytes 1572868
  99.8 2.2 %copy-start.3 = (bf16[16,128,128]{2,1,0:T(8,128)(2,1)S(1)}, bf16[16,128,128]{2,1,0:T(8,128)(2,1)}, u32[]{:S(2)}) copy-start(bf16[16,128,128]{2,1,0:T(8,128)(2,1)} %copy-done.2) | copy-start | bytes 1572868
  99.8 2.2 %copy-start.10 = (f32[16,32,128]{2,1,0:T(8,128)S(1)}, f32[16,32,128]{2,1,0:T(8,128)}, u32[]{:S(2)}) copy-start(f32[16,32,128]{2,1,0:T(8,128)} %copy-done.9) | copy-start | bytes 786436
  102.0 0.7 copy-start.30
  102.0 0.7 copy-start.32
  102.7 1.0 copy-start.5
  103.7 1.0 copy-start.7
  104.7 0.9 copy-start.12
  105.7 0.9 copy-start.14
  106.6 0.9 copy-start.16
  107.6 0.8 copy-start.18
  118.1 0.6 copy-start.19
  118.7 0.6 copy-start.21
  119.3 0.6 copy-start.22
  119.9 0.6 copy-start.24
  120.5 0.6 copy-start.26
  121.1 0.8 copy-start.20
  122.1 0.7 copy-start.27
  122.2 0.7 copy-start.23
  122.2 0.7 copy-start.25
  122.9 0.7 copy-start.47
  125.8 31.1 %all-to-all-start.5 = ((f32[8,243,128]{2,1,0:T(8,128)}), f32[8,243,128]{2,1,0:T(8,128)S(1)}, u32[]{:S(2)}, u32[]{:S(2)}) async-start(f32[8,243,128]{2,1,0:T(8,128)} %pad_maximum_fusion), calls=%async_computation.5 | async-start | bytes 2031616 | tf_op jit(solution)/shard_map/all_to_all | solution.py:656
  131.3 0.7 copy-start.49
  157.2 1.2 copy-start.44
  157.2 1.2 copy-start.34
  157.9 0.7 copy-start.42
  167.5 0.9 copy-start.37
Sparse Core Ops, SparseCore 0:
  9.6 19.5 all-gather.4

commit v2 on v1

v2 whole, which is shorter than its diff:
```python
import functools
import math

import jax
import jax.numpy as jnp
from jax import lax
from jax.experimental import pallas as pl
from jax.experimental.pallas import tpu as pltpu
from jax.sharding import PartitionSpec as P

f32 = jnp.float32
bf16 = jnp.bfloat16
epsilon = 1e-05
NN = (((1,), (0,)), ((), ()))
NT = (((1,), (1,)), ((), ()))
TN = (((0,), (0,)), ((), ()))


def mm(left, right, dims=NN):
    return lax.dot_general(left, right, dims, preferred_element_type=f32)


def split(x):
    high = x.astype(bf16)
    return high, (x - high.astype(f32)).astype(bf16)


def swap(x, half):
    return pltpu.roll(x, half, axis=x.ndim - 1)


def lanes(shape):
    return lax.broadcasted_iota(jnp.int32, shape, len(shape) - 1)


def pair(z, half):
    low = lanes(z.shape) < half
    turned = swap(z, half)
    return jnp.where(low, z, turned), jnp.where(low, -turned, z)


def cmul(x, z, half):
    return x * z[0] + swap(x, half) * z[1]


def normal_cdf(y):
    return 0.5 * (1.0 + lax.erf(y * (1.0 / math.sqrt(2.0))))


def live_rows(lens_ref, micros, chunks, width):
    shape = (chunks, width)
    at = lax.broadcasted_iota(jnp.int32, shape, 0) * width + lanes(shape)
    rows = [(at < lens_ref[m, 0]).astype(f32) for m in range(micros)]
    return jnp.concatenate(rows, axis=0)


def channel_rows(ref, channel, micros, chunks, chans):
    rows = [
        ref[pl.ds(m * chans + channel, chunks, stride=micros * chans), :] for m in range(micros)
    ]
    return jnp.concatenate(rows, axis=0)


def shift_chunks(x, by, micros, chunks):
    cube = x.reshape(micros, chunks, x.shape[-1])
    place = lax.broadcasted_iota(jnp.int32, cube.shape, 1)
    if by > 0:
        moved = jnp.where(place >= by, pltpu.roll(cube, by, axis=1), 0.0)
    else:
        moved = jnp.where(place < chunks + by, pltpu.roll(cube, chunks + by, axis=1), 0.0)
    return moved.reshape(x.shape)


def previous(u, micros, chunks):
    turned = pltpu.roll(u, 1, axis=1)
    return jnp.where(lanes(u.shape) == 0, shift_chunks(turned, 1, micros, chunks), turned)


def following(u, micros, chunks):
    width = u.shape[1]
    turned = pltpu.roll(u, width - 1, axis=1)
    return jnp.where(
        lanes(u.shape) == width - 1, shift_chunks(turned, -1, micros, chunks), turned
    )


def gather_kernel(rank_ref, cot_ref, wv_ref, wg_ref, bv_ref, bg_ref, *outs):
    peers, wide, _ = cot_ref.shape
    full = wv_ref.shape[0]
    pieces = []
    for value in (bv_ref[...], bg_ref[...]):
        for _ in range(3):
            high = value.astype(bf16).astype(f32)
            pieces.append(high)
            value = value - high
    pieces.append(jnp.zeros((10, wide), f32))
    biases = jnp.concatenate(pieces, axis=0).astype(bf16)
    for k, out in enumerate(outs):
        out[pl.ds(0, wide), :] = cot_ref[rank_ref[0] ^ k]
        out[pl.ds(wide, full), :] = wv_ref[...]
        out[pl.ds(wide + full, full), :] = wg_ref[...]
        out[pl.ds(wide + 2 * full, 16), :] = biases


def stats_kernel(tokens_ref, out_ref):
    micros, wide, width = tokens_ref.shape
    x = tokens_ref[...].astype(f32)
    mean = jnp.sum(x, axis=1) * (1.0 / wide)
    out_ref[pl.ds(0, micros), :] = mean
    out_ref[pl.ds(micros, micros), :] = jnp.sum(jnp.square(x - mean[:, None, :]), axis=1)


def normal_kernel(seqs, tokens_ref, stats_ref, xhat_ref, norm_ref):
    micros, wide, width = tokens_ref.shape
    peers = stats_ref.shape[0]
    chans = wide // seqs
    means = stats_ref[:, :micros]
    mean = jnp.sum(means, axis=0) * (1.0 / peers)
    square = jnp.sum(stats_ref[:, micros:], axis=0)
    square = square + wide * jnp.sum(jnp.square(means - mean[None]), axis=0)
    inverse = lax.rsqrt(square * (1.0 / (peers * wide)) + epsilon)
    norm_ref[pl.ds(0, micros), :] = mean
    norm_ref[pl.ds(micros, micros), :] = inverse
    for m in range(micros):
        x = tokens_ref[m].astype(f32)
        x_hat = (x - mean[m : m + 1]) * inverse[m : m + 1]
        xhat_ref[:, m] = x_hat.reshape(seqs, chans, width)


def table_kernel(
    chans,
    seqs,
    width,
    rank_ref,
    b_ref,
    e_ref,
    c_ref,
    decay_ref,
    turn_ref,
    tab_ref,
    const_ref,
    turned_keep,
    rise,
    fall,
    steps,
):
    half = decay_ref.shape[0]
    base = rank_ref[0] * chans
    levels = int(math.log2(width)) - 3
    spans = int(math.log2(seqs))
    group = tab_ref.shape[0]

    def own(value):
        turned_keep[...] = value.T
        return turned_keep[pl.ds(base, chans), :]

    @pl.when(pl.program_id(0) == 0)
    def _():
        b = own(b_ref[...].reshape(2 * half, -1))
        e = own(e_ref[...].reshape(2 * half, -1))
        c = own(c_ref[...].reshape(2 * half, -1))
        mixed = own(jnp.concatenate([decay_ref[...], turn_ref[...]], axis=0))
        low = lanes(mixed.shape) < half
        other = swap(mixed, half)
        decay = jnp.where(low, mixed, other)
        turn = jnp.where(low, other, mixed)
        turned = jnp.where(low, jnp.cos(turn), jnp.sin(turn))
        a = jnp.exp(-decay) * turned
        inverse = jnp.exp(decay) * jnp.where(low, turned, -turned)
        a_pair = pair(a, half)
        fall[pl.ds(7 * chans, chans), :] = jnp.where(low, 1.0, 0.0)
        power = a
        for k in range(8):
            rise[pl.ds(k * chans, chans), :] = power
            if k < 7:
                fall[pl.ds((6 - k) * chans, chans), :] = power
                power = cmul(power, a_pair, half)
        sign = jnp.where(low, 1.0, -1.0)
        pairs = [pair(z, half) for z in (b, e, c)]
        for k in range(3):
            const_ref[2 * k] = pairs[k][0]
            const_ref[2 * k + 1] = pairs[k][1]
        ca = cmul(inverse, pairs[2], half)
        steps[0] = cmul(ca, pairs[0], half) * sign
        steps[1] = cmul(ca, pairs[1], half) * sign
        for k in range(levels):
            power_pair = pair(power, half)
            steps[2 + 2 * k] = power_pair[0]
            steps[3 + 2 * k] = power_pair[1]
            power = cmul(power, power_pair, half)
        for k in range(spans):
            power_pair = pair(power, half)
            const_ref[6 + 2 * k] = power_pair[0]
            const_ref[7 + 2 * k] = power_pair[1]
            power = cmul(power, power_pair, half)

    for g in range(group):
        channel = pl.program_id(0) * group + g

        def step(k):
            return steps[k, pl.ds(channel, 1), :]

        up = rise[pl.ds(channel, 8, stride=chans), :]
        down = fall[pl.ds(channel, 8, stride=chans), :]
        for k in range(levels):
            by = (step(2 + 2 * k), step(3 + 2 * k))
            up = jnp.concatenate([up, cmul(up, by, half)], axis=0)
            down = jnp.concatenate([cmul(down, by, half), down], axis=0)
        up_hi, up_lo = split(up)
        down_hi, down_lo = split(down)
        row = lax.broadcasted_iota(jnp.int32, (8, width), 0)
        coefs = jnp.where(row == 0, step(0), jnp.where(row == 1, step(1), 0.0))
        coef_hi = coefs.astype(bf16).astype(f32)
        coef_both = jnp.concatenate([coef_hi, coefs - coef_hi], axis=0).astype(bf16)
        taps = mm(coef_both, up_hi, NT) + mm(coef_both, up_lo, NT)
        taps = taps[:8] + taps[8:]
        shape = (width, width)
        ahead = lanes(shape) >= lax.broadcasted_iota(jnp.int32, shape, 0)
        for k in range(2):
            spread = jnp.broadcast_to(taps[k : k + 1], shape)
            spread = pltpu.roll(spread, 0, axis=1, stride=1, stride_axis=0)
            t_hi, t_lo = split(jnp.where(ahead, spread, 0.0))
            tab_ref[g, pl.ds(k * width, width), :] = t_hi
            tab_ref[g, pl.ds((2 + k) * width, width), :] = t_lo
        for k, value in enumerate((down_hi, down_lo, up_hi, up_lo)):
            tab_ref[g, pl.ds((4 + k) * width, width), :] = value


def forward_kernel(
    micros,
    chunks,
    chans,
    group,
    rank_ref,
    lens_ref,
    gain_ref,
    bias_ref,
    skip_ref,
    xhat_ref,
    tab_ref,
    const_ref,
    act_ref,
    kept_ref,
    act_keep,
):
    width = xhat_ref.shape[1]
    half = const_ref.shape[2] // 2
    base = rank_ref[0] * chans
    spans = int(math.log2(chunks))
    live = live_rows(lens_ref, micros, chunks, width)
    rows = micros * chunks
    for g in range(group):
        channel = pl.program_id(0) * group + g

        def const(k):
            return (
                const_ref[2 * k, pl.ds(channel, 1), :],
                const_ref[2 * k + 1, pl.ds(channel, 1), :],
            )

        t_hi = tab_ref[g, : 2 * width]
        t_lo = tab_ref[g, 2 * width : 4 * width]
        down_hi, down_lo, up_hi, up_lo = [
            tab_ref[g, k * width : (k + 1) * width] for k in range(4, 8)
        ]
        at = base + channel
        x_hat = channel_rows(xhat_ref, channel, micros, chunks, chans)
        u = live * (x_hat * gain_ref[at] + bias_ref[at])
        v = u * previous(u, micros, chunks)
        uv_hi, uv_lo = split(jnp.concatenate([u, v], axis=0))
        q = mm(jnp.concatenate([uv_hi, uv_lo], axis=0), down_hi)
        q = q[: 2 * rows] + q[2 * rows :] + mm(uv_hi, down_lo)
        uq, vq = q[:rows], q[rows:]
        wide_hi = jnp.concatenate([uv_hi[:rows], uv_hi[rows:]], axis=1)
        wide_lo = jnp.concatenate([uv_lo[:rows], uv_lo[rows:]], axis=1)
        y = mm(jnp.concatenate([wide_hi, wide_lo], axis=0), t_hi)
        y = y[:rows] + y[rows:] + mm(wide_hi, t_lo)
        state = cmul(uq, const(0), half) + cmul(vq, const(1), half)
        for k in range(spans):
            state = state + cmul(shift_chunks(state, 2**k, micros, chunks), const(3 + k), half)
        start = shift_chunks(state, 1, micros, chunks)
        sent = cmul(start, const(2), half)
        sent = jnp.where(lanes(sent.shape) < half, sent, -sent)
        sent_hi, sent_lo = split(sent)
        cross = mm(jnp.concatenate([sent_hi, sent_lo], axis=0), up_hi, NT)
        y = y + cross[:rows] + cross[rows:] + mm(sent_hi, up_lo, NT) + skip_ref[at] * u
        for k, value in enumerate((y, uq, vq, start)):
            kept_ref[g, pl.ds(k * rows, rows), :] = value
        act = y * normal_cdf(y)
        for m in range(micros):
            act_keep[pl.ds(m * chunks * chans + channel, chunks, stride=chans), :] = act[
                m * chunks : (m + 1) * chunks
            ]

    @pl.when(pl.program_id(0) == pl.num_programs(0) - 1)
    def _():
        act_ref[...] = act_keep[...].astype(bf16)


def backward_kernel(
    micros,
    chunks,
    chans,
    group,
    rank_ref,
    lens_ref,
    gain_ref,
    bias_ref,
    skip_ref,
    xhat_ref,
    dact_ref,
    tab_ref,
    const_ref,
    kept_ref,
    weights_ref,
    out_ref,
    sums_keep,
    modes_keep,
    head,
):
    width = xhat_ref.shape[1]
    half = const_ref.shape[2] // 2
    base = rank_ref[0] * chans
    spans = int(math.log2(chunks))
    live = live_rows(lens_ref, micros, chunks, width)
    rows = micros * chunks
    stride = head.shape[0] // chunks
    shape = (width, width)
    sub = lax.broadcasted_iota(jnp.int32, shape, 0)
    mirror = (lanes(shape) + sub == width - 1).astype(f32).astype(bf16)
    ahead = lanes(shape) >= sub
    for g in range(group):
        channel = pl.program_id(0) * group + g

        def const(k):
            return (
                const_ref[2 * k, pl.ds(channel, 1), :],
                const_ref[2 * k + 1, pl.ds(channel, 1), :],
            )

        t_hi = tab_ref[g, : 2 * width]
        t_lo = tab_ref[g, 2 * width : 4 * width]
        down_hi, down_lo, up_hi, up_lo = [
            tab_ref[g, k * width : (k + 1) * width] for k in range(4, 8)
        ]
        y, uq, vq, start = [kept_ref[g, pl.ds(k * rows, rows), :] for k in range(4)]
        at = base + channel
        gain = gain_ref[at]
        x_hat = channel_rows(xhat_ref, channel, micros, chunks, chans)
        u = live * (x_hat * gain + bias_ref[at])
        u_prev = previous(u, micros, chunks)
        v = u * u_prev
        d_act = dact_ref[pl.ds(channel, rows, stride=chans), :]
        density = jnp.exp(-0.5 * y * y) * (1.0 / math.sqrt(2.0 * math.pi))
        d_y = d_act * (normal_cdf(y) + y * density)
        dy_hi, dy_lo = split(d_y)
        dy_both = jnp.concatenate([dy_hi, dy_lo], axis=0)
        first = mm(dy_both, jnp.concatenate([up_hi, mirror], axis=1))
        yd = first[:rows, :width] + first[rows:, :width] + mm(dy_hi, up_lo)
        back_hi = first[:rows, width:].astype(bf16)
        back_lo = first[rows:, width:].astype(bf16)
        duv = mm(dy_both, t_hi, NT)
        duv = duv[:rows] + duv[rows:] + mm(dy_hi, t_lo, NT)
        d_u, d_v = duv[:, :width], duv[:, width:]

        wide_hi, wide_lo = split(jnp.concatenate([u, v], axis=1))
        outer = mm(
            jnp.concatenate([back_hi, back_lo, back_hi], axis=0),
            jnp.concatenate([wide_hi, wide_hi, wide_lo], axis=0),
            TN,
        )
        sums = []
        for k in range(2):
            turned = pltpu.roll(
                outer[:, k * width : (k + 1) * width], 0, axis=1, stride=1, stride_axis=0
            )
            sums.append(jnp.sum(jnp.where(ahead, turned, 0.0), axis=0, keepdims=True))
        row = lax.broadcasted_iota(jnp.int32, (8, width), 0)
        lags = jnp.where(row == 0, sums[0], jnp.where(row == 1, sums[1], 0.0))
        lag_hi = lags.astype(bf16).astype(f32)
        lag_both = jnp.concatenate([lag_hi, lags - lag_hi], axis=0).astype(bf16)
        tops = mm(lag_both, down_hi) + mm(lag_both, down_lo)
        tops = tops[:8] + tops[8:]
        top_u, top_v = tops[0:1], tops[1:2]

        adj = cmul(yd, const(2), half)
        for k in range(spans):
            adj = adj + cmul(shift_chunks(adj, -(2**k), micros, chunks), const(3 + k), half)
        adj = shift_chunks(adj, -1, micros, chunks)
        sent = jnp.concatenate([cmul(adj, const(0), half), cmul(adj, const(1), half)], axis=0)
        sent = jnp.where(lanes(sent.shape) < half, sent, -sent)
        sent_hi, sent_lo = split(sent)
        cross = mm(jnp.concatenate([sent_hi, sent_lo], axis=0), down_hi, NT)
        cross = cross[: 2 * rows] + cross[2 * rows :] + mm(sent_hi, down_lo, NT)
        d_v = d_v + cross[rows:]
        d_u = d_u + cross[:rows] + skip_ref[at] * d_y + d_v * u_prev
        d_u = d_u + following(d_v * u, micros, chunks)

        def total(x):
            return jnp.sum(x, axis=0, keepdims=True)

        adj_pair = pair(adj, half)
        flip = jnp.where(lanes((1, 2 * half)) < half, 1.0, -1.0)
        modes_keep[pl.ds(channel, 1), :] = flip * (
            cmul(top_u, const(2), half) + total(cmul(uq, adj_pair, half))
        )
        modes_keep[pl.ds(chans + channel, 1), :] = flip * (
            cmul(top_v, const(2), half) + total(cmul(vq, adj_pair, half))
        )
        modes_keep[pl.ds(2 * chans + channel, 1), :] = flip * (
            cmul(top_u, const(0), half)
            + cmul(top_v, const(1), half)
            + total(cmul(start, pair(yd, half), half))
        )
        d_q = live * d_u
        for k, value in enumerate((d_y * u, d_q * x_hat, d_q)):
            sums_keep[pl.ds(k * chans + channel, 1), :] = total(value)
        d_h = d_q * gain
        for m in range(micros):
            head[pl.ds(m * chans + channel, chunks, stride=stride), :] = d_h[
                m * chunks : (m + 1) * chunks
            ]

    @pl.when(pl.program_id(0) == pl.num_programs(0) - 1)
    def _():
        sums = jnp.sum(sums_keep[...].T, axis=0, keepdims=True)
        modes = modes_keep[...]
        modes_hi = modes.astype(bf16).astype(f32)
        sums_hi = sums.astype(bf16).astype(f32)
        cut = micros * chans
        count, wide = weights_ref.shape[1:]
        bias = weights_ref[chunks, pl.ds(0, 16), :].astype(f32)
        for k in range(chunks):
            at = k * stride + cut
            head[pl.ds(at, 3 * chans), :] = modes_hi
            head[pl.ds(at + 3 * chans, 3 * chans), :] = modes - modes_hi
            head[pl.ds(at + 6 * chans, 1), pl.ds(0, 3 * chans)] = sums_hi
            head[pl.ds(at + 6 * chans + 1, 1), pl.ds(0, 3 * chans)] = sums - sums_hi
            for j in range(4):
                head[pl.ds(at + 6 * chans + 2 + j, 1), pl.ds(0, wide)] = bias[4 * j : 4 * j + 1]
            out_ref[k, pl.ds(0, stride), :] = head[pl.ds(k * stride, stride), :].astype(bf16)
            out_ref[k, pl.ds(stride, count), pl.ds(0, wide)] = weights_ref[k]


def project_kernel(width, place_ref, lens_ref, act_ref, *refs):
    dact_ref = refs[-1]
    full, rows = act_ref.shape
    peers = len(refs) - 1
    wide = full // peers
    start = place_ref[1] * rows
    at = place_ref[0] * width + lax.rem(start, width) + lanes((1, rows))
    live = (at < lens_ref[start // width, 0]).astype(f32)
    act = act_ref[...]
    d_act = None
    for ref in refs[:-1]:
        g = live * ref[pl.ds(0, wide), :].astype(f32)
        wv = ref[pl.ds(wide, full), :]
        wg = ref[pl.ds(wide + full, full), :]
        bias = ref[pl.ds(wide + 2 * full, 16), :].astype(f32).T
        both = mm(jnp.concatenate([wv, wg], axis=1), act, TN)
        value = both[:wide] + (bias[:, 0:1] + bias[:, 1:2] + bias[:, 2:3])
        gate = jax.nn.sigmoid(both[wide:] + (bias[:, 3:4] + bias[:, 4:5] + bias[:, 5:6]))
        d_value = (g * gate).astype(bf16)
        d_gate = (g * value * gate * (1.0 - gate)).astype(bf16)
        part = mm(wv, d_value) + mm(wg, d_gate)
        d_act = part if d_act is None else d_act + part
    dact_ref[...] = d_act


def output_kernel(
    seqs,
    rank_ref,
    lens_ref,
    order_ref,
    tokens_ref,
    cot_ref,
    wv_ref,
    wg_ref,
    bv_ref,
    bg_ref,
    *refs,
):
    acts_in, (out_ref, grad_ref) = refs[:-2], refs[-2:]
    micros, wide, width = tokens_ref.shape
    full = wv_ref.shape[0]
    at = rank_ref[0] * width + lanes((1, width))
    weights = jnp.concatenate([wv_ref[...], wg_ref[...]], axis=1)
    bias = jnp.concatenate([bv_ref[...], bg_ref[...]], axis=1)
    bias = jnp.broadcast_to(bias, (8, 2 * wide)).T[:, 0:1]
    acts, grads = [], []
    for k in range(micros):
        m = order_ref[k]
        live = (at < lens_ref[m, 0]).astype(f32)
        act = acts_in[k][...]
        both = mm(weights, act, TN) + bias
        value = both[:wide]
        gate = jax.nn.sigmoid(both[wide:])
        out_ref[m] = (live * (tokens_ref[m].astype(f32) + value * gate)).astype(bf16)
        g = live * cot_ref[m].astype(f32)
        d_value = (g * gate).astype(bf16)
        d_gate = (g * value * gate * (1.0 - gate)).astype(bf16)
        acts.append(act)
        grads.append(jnp.concatenate([d_value, d_gate], axis=0))
    grads = jnp.concatenate(grads, axis=1)
    grad_w = mm(jnp.concatenate(acts, axis=1), grads, NT)
    ones = jnp.ones((8, grads.shape[1]), bf16)
    grad_b = mm(ones, grads, NT)
    count = full // seqs
    for k in range(seqs):
        part = grad_w[k * count : (k + 1) * count]
        grad_ref[k, pl.ds(0, count), :] = part[:, :wide].astype(bf16)
        grad_ref[k, pl.ds(count, count), :] = part[:, wide:].astype(bf16)
    high, low = split(jnp.concatenate([grad_b[:4, :wide], grad_b[:4, wide:]], axis=0))
    grad_ref[seqs, pl.ds(0, 16), :] = jnp.concatenate([high, low], axis=0)


def normal(tokens_ref, norm_ref, m):
    micros = tokens_ref.shape[0]
    return (tokens_ref[m].astype(f32) - norm_ref[m : m + 1]) * norm_ref[
        micros + m : micros + m + 1
    ]


def sums_kernel(got_ref, tokens_ref, norm_ref, out_ref, head_ref):
    micros, wide, width = tokens_ref.shape
    seqs, stride, _ = head_ref.shape
    chans = wide // seqs
    head_ref[...] = got_ref[:, pl.ds(0, stride), :].astype(f32)
    for m in range(micros):
        d_hat = head_ref[:, pl.ds(m * chans, chans), :].reshape(wide, width)
        x_hat = normal(tokens_ref, norm_ref, m)
        out_ref[pl.ds(m, 1), :] = jnp.sum(d_hat, axis=0, keepdims=True)
        out_ref[pl.ds(micros + m, 1), :] = jnp.sum(d_hat * x_hat, axis=0, keepdims=True)


def final_kernel(
    rank_ref,
    lens_ref,
    got_ref,
    head_ref,
    hat_ref,
    tokens_ref,
    cot_ref,
    norm_ref,
    d_in_ref,
    b_ref,
    e_ref,
    c_ref,
    skip_ref,
    gain_ref,
    norm_bias_ref,
    wv_ref,
    wg_ref,
    bv_ref,
    bg_ref,
):
    micros, wide, width = tokens_ref.shape
    seqs, stride, _ = head_ref.shape
    peers = hat_ref.shape[0]
    chans = wide // seqs
    hat = jnp.sum(hat_ref[...], axis=0) * (1.0 / (peers * wide))
    at = rank_ref[0] * width + lanes((1, width))
    for m in range(micros):
        live = (at < lens_ref[m, 0]).astype(f32)
        d_hat = head_ref[:, pl.ds(m * chans, chans), :].reshape(wide, width)
        x_hat = normal(tokens_ref, norm_ref, m)
        inside = d_hat - hat[m : m + 1] - x_hat * hat[micros + m : micros + m + 1]
        d_in_ref[m] = (
            live * cot_ref[m].astype(f32) + norm_ref[micros + m : micros + m + 1] * inside
        )
    cut = micros * chans
    for k, ref in enumerate((b_ref, e_ref, c_ref)):
        modes = (
            head_ref[:, pl.ds(cut + k * chans, chans), :]
            + head_ref[:, pl.ds(cut + (3 + k) * chans, chans), :]
        )
        ref[...] = modes.reshape(wide, -1).T.reshape(ref.shape)
    place = lanes((1, wide)) // chans
    last = cut + 6 * chans
    for k, ref in enumerate((skip_ref, gain_ref, norm_bias_ref)):
        line = jnp.zeros((1, wide), f32)
        for s in range(seqs):
            own = head_ref[s, pl.ds(last, 1), :] + head_ref[s, pl.ds(last + 1, 1), :]
            own = pltpu.roll(own, (s - k) * chans % own.shape[1], axis=1)[:, :wide]
            line = jnp.where(place == s, own, line)
        ref[...] = line
    count = wv_ref.shape[0]
    for k, ref in enumerate((wv_ref, wg_ref)):
        parts = got_ref[:, pl.ds(stride + k * count, count), pl.ds(0, wide)]
        ref[...] = jnp.sum(parts.astype(f32), axis=0)
    for k, ref in enumerate((bv_ref, bg_ref)):
        line = jnp.zeros((1, wide), f32)
        for s in range(seqs):
            line = line + head_ref[s, pl.ds(last + 2 + k, 1), pl.ds(0, wide)]
            line = line + head_ref[s, pl.ds(last + 4 + k, 1), pl.ds(0, wide)]
        ref[...] = line


def smem():
    return pl.BlockSpec(memory_space=pltpu.SMEM)


def vmem():
    return pl.BlockSpec(memory_space=pltpu.VMEM)


def whole(shape):
    return pl.BlockSpec(shape, lambda i: (0,) * len(shape))


def piece(shape):
    return pl.BlockSpec(shape, lambda i: (i,) + (0,) * (len(shape) - 1))


def shape_of(shape, kind=f32):
    return jax.ShapeDtypeStruct(shape, kind)


def kernel_call(kernel, name, scalars, arrays, outs, micros_of_time, limit=8, **more):
    ins = [smem()] * len(scalars) + [vmem()] * len(arrays)
    return pl.pallas_call(
        kernel,
        in_specs=ins,
        out_specs=[vmem()] * len(outs),
        out_shape=outs,
        compiler_params=pltpu.CompilerParams(vmem_limit_bytes=limit * 1024 * 1024),
        cost_estimate=cost(micros_of_time),
        name=name,
        **more,
    )(*scalars, *arrays)


def cost(micros_of_time):
    return pl.CostEstimate(
        flops=int(micros_of_time * 1e9), bytes_accessed=int(micros_of_time * 3e6), transcendentals=0
    )


def shards(
    tokens,
    lengths,
    ln_gain,
    ln_bias,
    b_coef,
    e_coef,
    c_coef,
    skip_gain,
    decay_rate,
    rotation,
    w_value,
    w_gate,
    bias_value,
    bias_gate,
    out_cotangent,
):
    micros, wide, width = tokens.shape
    modes = decay_rate.shape[1]
    full = w_value.shape[0]
    seqs = lax.axis_size("seq")
    peers = lax.axis_size("chan")
    seq_rank = lax.axis_index("seq").astype(jnp.int32)
    chan_rank = lax.axis_index("chan").astype(jnp.int32)
    chans = wide // seqs
    rows = micros * seqs
    own = micros * width // peers
    parts = width // own
    both = ("chan", "seq")
    group = min(4, chans)
    steps = chans // group
    lane = 2 * modes
    spans = int(math.log2(seqs))
    levels = int(math.log2(width)) - 3
    rank = seq_rank.reshape(1)
    place = jnp.stack([seq_rank, chan_rank])
    bias_rows = (bias_value.reshape(1, wide), bias_gate.reshape(1, wide))

    def exchange(x, axis):
        return lax.all_to_all(x, axis, 0, 0, tiled=True)

    def cross(x, by):
        return lax.ppermute(x, "chan", [(i, i ^ by) for i in range(peers)])

    (part_stats,) = kernel_call(
        stats_kernel, "stats", (), (tokens,), [shape_of((2 * micros, width))], 1
    )
    stats = lax.all_gather(part_stats, "chan")
    x_hat, norm = kernel_call(
        functools.partial(normal_kernel, seqs),
        "normal",
        (),
        (tokens, stats),
        [shape_of((seqs, micros, chans, width)), shape_of((2 * micros, width))],
        1,
    )

    x_mine = exchange(x_hat, "seq").reshape(seqs * micros * chans, width)

    cot, wv, wg, _ = lax.optimization_barrier((out_cotangent, w_value, w_gate, norm))
    cot_own = cot.reshape(micros, wide, parts, own).transpose(0, 2, 1, 3).reshape(peers, wide, own)
    weights = kernel_call(
        gather_kernel,
        "weights",
        (chan_rank.reshape(1),),
        (cot_own, wv, wg) + bias_rows,
        [shape_of((wide + 2 * full + 16, own), bf16)] * peers,
        1,
    )
    weights = [weights[0]] + [cross(weights[k], k) for k in range(1, peers)]

    turned = [jnp.transpose(z, (0, 2, 1)) for z in (b_coef, e_coef, c_coef)]
    tables = shape_of((chans, 8 * width, lane), bf16)
    consts = shape_of((6 + 2 * spans, chans, lane))
    tab, const = pl.pallas_call(
        functools.partial(table_kernel, chans, seqs, width),
        grid=(steps,),
        in_specs=[smem()]
        + [whole(turned[0].shape)] * 3
        + [whole(decay_rate.T.shape)] * 2,
        out_specs=[piece((group,) + tables.shape[1:]), whole(consts.shape)],
        out_shape=[tables, consts],
        scratch_shapes=[
            pltpu.VMEM((wide, lane), f32),
            pltpu.VMEM((8 * chans, lane), f32),
            pltpu.VMEM((8 * chans, lane), f32),
            pltpu.VMEM((2 + 2 * levels, chans, lane), f32),
        ],
        compiler_params=pltpu.CompilerParams(vmem_limit_bytes=12 * 1024 * 1024),
        cost_estimate=cost(4),
        name="tables",
    )(rank, *turned, decay_rate.T, rotation.T)
    tab = pltpu.with_memory_space_constraint(tab, pltpu.HBM)

    kept = shape_of((chans, 4 * rows, lane))
    act, saved = pl.pallas_call(
        functools.partial(forward_kernel, micros, seqs, chans, group),
        grid=(steps,),
        in_specs=[smem()] * 5
        + [whole(x_mine.shape), piece((group,) + tables.shape[1:]), whole(consts.shape)],
        out_specs=[whole((rows * chans, width)), piece((group,) + kept.shape[1:])],
        out_shape=[shape_of((rows * chans, width), bf16), kept],
        scratch_shapes=[pltpu.VMEM((rows * chans, width), f32)],
        compiler_params=pltpu.CompilerParams(vmem_limit_bytes=12 * 1024 * 1024),
        cost_estimate=cost(8),
        name="mixer_forward",
    )(rank, lengths, ln_gain, ln_bias, skip_gain, x_mine, tab, const)

    act = (
        act.reshape(micros, seqs, chans, parts, own)
        .transpose(0, 3, 1, 2, 4)
        .reshape(peers * seqs, chans, own)
    )
    act = exchange(act, both).reshape(full, own)
    (d_act,) = kernel_call(
        functools.partial(project_kernel, width),
        "project",
        (place, lengths),
        (act, *weights),
        [shape_of((full, own))],
        2,
        limit=12,
    )

    act, d_act = lax.optimization_barrier((act, d_act))
    acts = [act] + [cross(act, k) for k in range(1, peers)]
    if parts == 1:
        order = chan_rank ^ jnp.arange(peers, dtype=jnp.int32)
    else:
        stacked = jnp.stack(acts)[chan_rank ^ jnp.arange(peers, dtype=jnp.int32)]
        stacked = stacked.reshape(micros, parts, full, own).transpose(0, 2, 1, 3)
        stacked = stacked.reshape(micros, full, width)
        acts = [stacked[m] for m in range(micros)]
        order = jnp.arange(micros, dtype=jnp.int32)

    d_act = exchange(d_act.reshape(peers * seqs, chans, own), both)
    d_act = (
        d_act.reshape(micros, parts, seqs, chans, own)
        .transpose(0, 2, 3, 1, 4)
        .reshape(rows * chans, width)
    )
    count = full // seqs
    out, grad_w = kernel_call(
        functools.partial(output_kernel, seqs),
        "output",
        (rank, lengths, order),
        (tokens, out_cotangent, w_value, w_gate) + bias_rows + tuple(acts),
        [shape_of(tokens.shape, bf16), shape_of((seqs + 1, 2 * count, wide), bf16)],
        3,
        limit=12,
    )

    stride = -(-((micros + 6) * chans + 6) // 16) * 16
    send = shape_of((seqs, stride + 2 * count, width), bf16)
    d_hat = pl.pallas_call(
        functools.partial(backward_kernel, micros, seqs, chans, group),
        grid=(steps,),
        in_specs=[smem()] * 5
        + [whole(x_mine.shape)] * 2
        + [
            piece((group,) + tables.shape[1:]),
            whole(consts.shape),
            piece((group,) + kept.shape[1:]),
            whole(grad_w.shape),
        ],
        out_specs=whole(send.shape),
        out_shape=send,
        scratch_shapes=[pltpu.VMEM((3 * chans, lane), f32)] * 2
        + [pltpu.VMEM((seqs * stride, width), f32)],
        compiler_params=pltpu.CompilerParams(vmem_limit_bytes=16 * 1024 * 1024),
        cost_estimate=cost(9),
        name="mixer_backward",
    )(rank, lengths, ln_gain, ln_bias, skip_gain, x_mine, d_act, tab, const, saved, grad_w)
    got = exchange(d_hat, "seq")
    own_sums, head = kernel_call(
        sums_kernel,
        "sums",
        (),
        (got, tokens, norm),
        [shape_of((2 * micros, width)), shape_of((seqs, stride, width))],
        1,
    )
    hat_sums = lax.all_gather(own_sums, "chan")
    mode_grad = shape_of((2, modes, wide))
    d_input, d_b, d_e, d_c, d_skip, d_gain, d_bias, d_wv, d_wg, d_bv, d_bg = kernel_call(
        final_kernel,
        "final",
        (rank, lengths),
        (got, head, hat_sums, tokens, out_cotangent, norm),
        [shape_of(tokens.shape)]
        + [mode_grad] * 3
        + [shape_of((1, wide))] * 3
        + [shape_of((count, wide))] * 2
        + [shape_of((1, wide))] * 2,
        2,
    )
    d_b, d_e, d_c = [jnp.transpose(z, (0, 2, 1)) for z in (d_b, d_e, d_c)]
    d_skip, d_gain, d_bias, d_bv, d_bg = [
        z.reshape(wide) for z in (d_skip, d_gain, d_bias, d_bv, d_bg)
    ]
    return (out, d_input, d_gain, d_bias, d_b, d_e, d_c, d_skip, d_wv, d_wg, d_bv, d_bg)


def solution(mesh):
    chan = P("chan")
    modes = P(None, "chan", None)
    table = P("chan", None)
    weight = P(None, "chan")
    rows = P(None, "chan", "seq")
    spread = P("seq", "chan")
    return jax.shard_map(
        shards,
        mesh=mesh,
        in_specs=(
            rows,
            P(),
            chan,
            chan,
            modes,
            modes,
            modes,
            chan,
            table,
            table,
            weight,
            weight,
            chan,
            chan,
            rows,
        ),
        out_specs=(
            rows,
            rows,
            chan,
            chan,
            modes,
            modes,
            modes,
            chan,
            spread,
            spread,
            chan,
            chan,
        ),
        check_vma=False,
    )
```

time: 177 us -> 105 us (0.59)
  local copies, waits for them, and re-layouts: 35.3 us -> 4.11 us
  waiting for transfers between devices: 38.4 us -> 17.4 us
  between operations: 14.4 us -> 0.87 us
  other arithmetic: 7.67 us -> 0.08 us
  Pallas kernels: 25.3 us -> 29.6 us
  starting transfers between devices: 22.1 us -> 18.4 us
  blocking collectives: 30.6 us -> 34.2 us
  matrix products: 2.18 us -> 0 us
    all_to_all x5 -> x3, waiting for transfers between devices: 38.4 us -> 8 us  [exchange(): return lax.all_to_all(x, axis, 0, 0, tiled=True)]
    unnamed x114 -> x39, local copies, waits for them, and re-layouts: 28 us -> 4.11 us
    all_to_all x1, blocking collectives: 9.84 us -> 22.7 us  [exchange(): return lax.all_to_all(x, axis, 0, 0, tiled=True)]
    pallas_call x1 -> x8, Pallas kernels: 1.88 us -> 11.7 us  [the longest x7 6.94 us: kernel_call(): pl.pallas_call(kernel, in_specs=ins, out_specs=[vmem()] * len(outs), out_...]
    ppermute x0 -> x6, waiting for transfers between devices: none -> 9.38 us  [cross(): return lax.ppermute(x, 'chan', [(i, i ^ by) for i in range(peers)])]
    all_gather x3 -> x2, blocking collectives: 20.8 us -> 11.5 us  [the longest x1 6.35 us: shards(): stats = lax.all_gather(part_stats, 'chan')]
    all_to_all x5 -> x3, starting transfers between devices: 22.1 us -> 14.5 us  [exchange(): return lax.all_to_all(x, axis, 0, 0, tiled=True)]
    pallas_call x1, Pallas kernels: 13.7 us -> 8.05 us  [shards(): pl.pallas_call(functools.partial(forward_kernel, micros, seqs, chans, gro...]
  transfers between devices with their start and end apart: 6 -> 9, of which waited for: 3 -> 4; matrix products, arithmetic and copies ran while one was open for 5% -> 0% of each run, Pallas kernels for 8% -> 14%
where the time goes in v2:
time: 105 us
  blocking collectives  34.2 us (33%)
  Pallas kernels  29.6 us (28%)
  starting transfers between devices  18.4 us (18%)
  waiting for transfers between devices  17.4 us (17%)
  local copies, waits for them, and re-layouts  4.11 us (4%)
    all_to_all x1, blocking collectives, exchange(): return lax.all_to_all(x, axis, 0, 0, tiled=True)  22.7 us
    all_to_all x3, starting transfers between devices, exchange(): return lax.all_to_all(x, axis, 0, 0, tiled=True)  14.5 us
    pallas_call x1, Pallas kernels, shards(): pl.pallas_call(functools.partial(backward_kernel, micros, seqs, chans, gr...  9.9 us
    ppermute x6, waiting for transfers between devices, cross(): return lax.ppermute(x, 'chan', [(i, i ^ by) for i in range(peers)])  9.38 us
    pallas_call x1, Pallas kernels, shards(): pl.pallas_call(functools.partial(forward_kernel, micros, seqs, chans, gro...  8.05 us
    all_to_all x3, waiting for transfers between devices, exchange(): return lax.all_to_all(x, axis, 0, 0, tiled=True)  8 us
    pallas_call x7, Pallas kernels, kernel_call(): pl.pallas_call(kernel, in_specs=ins, out_specs=[vmem()] * len(outs), out_...  6.94 us
    all_gather x1, blocking collectives, shards(): stats = lax.all_gather(part_stats, 'chan')  6.35 us
  transfers between devices with their start and end apart: 9, of which 4 were waited for; matrix products, arithmetic and copies ran while one was open for 0% of the time, Pallas kernels for 14%

profile of v2, /device:TPU:0, one launch (start us, length us, event | category | flops | bytes accessed | tf_op | source)
XLA Modules:
  0.0 104.6 jit_solution(12155658550638369613)
XLA Ops:
  0.6 0.0 copy-start.1
  0.7 0.0 copy-start
  0.7 0.0 copy-start.2
  0.7 0.9 copy-done.2
  1.6 0.1 stats.1
  1.7 0.0 copy-start.18
  1.7 0.0 copy-start.5
  1.7 0.0 copy-start.6
  1.7 0.0 copy-start.7
  1.7 0.0 copy-start.8
  1.8 0.0 copy-start.9
  1.8 6.3 %all-gather = f32[32,128]{1,0:T(8,128)S(1)} all-gather(f32[8,128]{1,0:T(8,128)S(1)} %stats.1), channel_id=2, replica_groups=mesh['seq'=8,'chan'=4] {'chan'}, dimensions={0}, use_global_device_ids=true | all-gather | bytes 20480 | tf_op jit(solution)/shard_map/all_gather | solution.py:686
  8.1 0.7 normal.1
  8.9 6.2 %all-to-all-start = ((f32[8,4,16,128]{3,2,1,0:T(8,128)}), f32[8,4,16,128]{3,2,1,0:T(8,128)S(1)}, u32[]{:S(2)}, u32[]{:S(2)}) async-start(f32[8,4,16,128]{3,2,1,0:T(8,128)} %get-tuple-element.42), calls=%async_computation | async-start | bytes 524288 | tf_op jit(solution)/shard_map/all_to_all | solution.py:678
  15.1 0.0 copy-done.1
  15.1 0.0 copy-done
  15.1 0.0 copy-done.4
  15.1 0.0 copy-done.10
  15.1 0.0 copy-done.11
  15.1 0.2 weights.1
  15.3 0.1 collective-permute-start
  15.4 1.6 %collective-permute-start.1 = (bf16[1168,128]{1,0:T(8,128)(2,1)S(1)}, bf16[1168,128]{1,0:T(8,128)(2,1)S(1)}, u32[]{:S(2)}, u32[]{:S(2)}) collective-permute-start(bf16[1168,128]{1,0:T(8,128)(2,1)S(1)} %get-tuple-element.52), channel_id=1, source_target_pairs={{0,2},{1,3},{2,0},{3,1},{4,6},{5,7},{6,4},{7,5},{8,10},{9,11},{10,... | collective-permute-start | bytes 897032 | tf_op jit(solution)/shard_map/ppermute | solution.py:681
  16.9 0.3 collective-permute-start.2
  17.2 0.0 copy-done.18
  17.2 0.1 copy.29.lens_ref
  17.3 0.0 copy-done.5
  17.3 0.0 copy-done.6
  17.3 0.0 copy-done.7
  17.3 0.0 copy-done.8
  17.3 0.0 copy-done.9
  17.3 0.0 copy-start.12
  17.4 0.0 copy-start.13
  17.4 0.0 copy-start.14
  17.4 4.8 %tables.1 = (bf16[16,1024,128]{2,1,0:T(8,128)(2,1)S(1)}, f32[12,16,128]{2,1,0:T(8,128)S(1)}) custom-call(s32[1]{0:T(128)} %bitcast.rank_ref, f32[2,64,128]{2,1,0:T(8,128)S(1)} %bitcast.34, f32[2,64,128]{2,1,0:T(8,128)S(1)} %bitcast.35, f32[2,64,128]{2,1,0:T(8,128)S(1)} %bitcast.36, f32[64,128]{1,0:T(8,128)S(1)} %bitcast.37, f32[64,128]{1,0:T(8,128)S(1)} %bitcast.38), custom_call_target="tpu_custom_call" | custom-call | flops 4000000000 | bytes 12000000 | tf_op jit(solution)/shard_map/tables/pallas_call | solution.py:713
  22.1 0.0 copy-start.15
  22.2 2.0 %copy-done.15 = bf16[16,1024,128]{2,1,0:T(8,128)(2,1)} copy-done((bf16[16,1024,128]{2,1,0:T(8,128)(2,1)}, bf16[16,1024,128]{2,1,0:T(8,128)(2,1)S(1)}, u32[]{:S(2)}) %copy-start.15) | copy-done | bytes 4194328
  24.1 0.3 all-to-all-done
  24.5 0.0 copy-done.12
  24.5 0.0 copy-done.13
  24.5 0.0 copy-done.14
  24.5 8.0 %mixer_forward.1 = (bf16[512,128]{1,0:T(8,128)(2,1)}, f32[16,128,128]{2,1,0:T(8,128)S(1)}) custom-call(s32[1]{0:T(128)} %bitcast.rank_ref, s32[4,1]{1,0:T(4,128)S(1)} %copy.29.lens_ref, f32[128]{0:T(128)S(1)} %copy-done.12, f32[128]{0:T(128)S(1)} %copy-done.13, f32[128]{0:T(128)S(1)} %copy-done.14, f32[512,128]{1,0:T(8,128)S(1)} %bitcast.24, ...), custom_call_target="tpu_custom_call" | custom-call | flops 8000000000 | bytes 24000000 | tf_op jit(solution)/shard_map/mixer_forward/pallas_call | solution.py:734
  32.5 1.0 copy-done.16
  33.6 5.7 %all-to-all-start.1 = ((bf16[32,16,128]{2,1,0:T(8,128)(2,1)}), bf16[32,16,128]{2,1,0:T(8,128)(2,1)S(1)}, u32[]{:S(2)}, u32[]{:S(2)}) async-start(bf16[32,16,128]{2,1,0:T(8,128)(2,1)} %bitcast.10), calls=%async_computation.1 | async-start | bytes 262144 | tf_op jit(solution)/shard_map/all_to_all | solution.py:678
  39.3 0.1 pad_add_fusion.place_ref
  39.3 0.0 collective-permute-done.refs_1_
  39.4 0.0 collective-permute-done.1.refs_2_
  39.4 0.0 collective-permute-done.2.refs_3_
  39.4 7.6 %all-to-all-done.1 = bf16[32,16,128]{2,1,0:T(8,128)(2,1)S(1)} async-done(((bf16[32,16,128]{2,1,0:T(8,128)(2,1)}), bf16[32,16,128]{2,1,0:T(8,128)(2,1)S(1)}, u32[]{:S(2)}, u32[]{:S(2)}) %all-to-all-start.1) | async-done | bytes 131104 | tf_op jit(solution)/shard_map/all_to_all | solution.py:678
  47.0 2.6 %project.1 = f32[512,128]{1,0:T(8,128)} custom-call(s32[2]{0:T(128)S(1)} %pad_add_fusion.place_ref, s32[4,1]{1,0:T(4,128)S(1)} %copy.29.lens_ref, bf16[512,128]{1,0:T(8,128)(2,1)S(1)} %bitcast.27, bf16[1168,128]{1,0:T(8,128)(2,1)S(1)} %get-tuple-element.50.refs_0_, bf16[1168,128]{1,0:T(8,128)(2,1)S(1)} %collective-permute-done.refs_1_, ...), custom_call_target="tpu_custom_call" | custom-call | flops 2000000000 | bytes 6000000 | tf_op jit(solution)/shard_map/project/pallas_call | solution.py:621
  49.6 2.6 %all-to-all-start.2 = ((f32[32,16,128]{2,1,0:T(8,128)}), f32[32,16,128]{2,1,0:T(8,128)S(1)}, u32[]{:S(2)}, u32[]{:S(2)}) async-start(f32[32,16,128]{2,1,0:T(8,128)} %bitcast.13), calls=%async_computation.2 | async-start | bytes 524288 | tf_op jit(solution)/shard_map/all_to_all | solution.py:678
  52.2 1.5 %collective-permute-start.5 = (bf16[512,128]{1,0:T(8,128)(2,1)S(1)}, bf16[512,128]{1,0:T(8,128)(2,1)S(1)}, u32[]{:S(2)}, u32[]{:S(2)}) collective-permute-start(bf16[512,128]{1,0:T(8,128)(2,1)S(1)} %bitcast.28), channel_id=1, source_target_pairs={{0,3},{1,2},{2,1},{3,0},{4,7},{5,6},{6,5},{7,4},{8,11},{9,10},{10,... | collective-permute-start | bytes 393224 | tf_op jit(solution)/shard_map/ppermute | solution.py:681
  53.7 0.4 collective-permute-start.4
  54.0 0.1 collective-permute-start.3
  54.1 5.3 %collective-permute-done.5.refs_3_ = bf16[512,128]{1,0:T(8,128)(2,1)S(1)} collective-permute-done((bf16[512,128]{1,0:T(8,128)(2,1)S(1)}, bf16[512,128]{1,0:T(8,128)(2,1)S(1)}, u32[]{:S(2)}, u32[]{:S(2)}) %collective-permute-start.5) | collective-permute-done | bytes 131104 | tf_op jit(solution)/shard_map/ppermute | solution.py:681
  59.4 4.1 %collective-permute-done.4.refs_2_ = bf16[512,128]{1,0:T(8,128)(2,1)S(1)} collective-permute-done((bf16[512,128]{1,0:T(8,128)(2,1)S(1)}, bf16[512,128]{1,0:T(8,128)(2,1)S(1)}, u32[]{:S(2)}, u32[]{:S(2)}) %collective-permute-start.4) | collective-permute-done | bytes 131104 | tf_op jit(solution)/shard_map/ppermute | solution.py:681
  63.5 0.0 collective-permute-done.3.refs_1_
  63.5 0.0 copy-done.3
  63.5 1.8 %output.1 = (bf16[4,128,128]{2,1,0:T(8,128)(2,1)}, bf16[9,128,128]{2,1,0:T(8,128)(2,1)S(1)}) custom-call(s32[1]{0:T(128)} %bitcast.rank_ref, s32[4,1]{1,0:T(4,128)S(1)} %copy.29.lens_ref, s32[4]{0:T(128)S(1)} %iota_xor_fusion.order_ref, bf16[4,128,128]{2,1,0:T(8,128)(2,1)S(1)} %copy-done.3, bf16[4,128,128]{2,1,0:T(8,128)(2,1)S(1)} %copy-done.4, ...), custom_call_target="tpu_custom_call" | custom-call | flops 3000000000 | bytes 9000000 | tf_op jit(solution)/shard_map/output/pallas_call | solution.py:621
  65.3 0.0 all-to-all-done.2
  65.3 9.9 %mixer_backward.1 = bf16[8,304,128]{2,1,0:T(8,128)(2,1)S(1)} custom-call(s32[1]{0:T(128)} %bitcast.rank_ref, s32[4,1]{1,0:T(4,128)S(1)} %copy.29.lens_ref, f32[128]{0:T(128)S(1)} %copy-done.12, f32[128]{0:T(128)S(1)} %copy-done.13, f32[128]{0:T(128)S(1)} %copy-done.14, f32[512,128]{1,0:T(8,128)S(1)} %bitcast.25, f32[512,128]{1,0:T(8,128)S(1)} %bitcast.26, ...), custom_call_target="tpu_custom_call" | custom-call | flops 8999999488 | bytes 27000000 | tf_op jit(solution)/shard_map/mixer_backward/pallas_call | solution.py:793
  75.2 22.7 %all_to_all.20.got_ref = bf16[8,304,128]{2,1,0:T(8,128)(2,1)S(1)} all-to-all(bf16[8,304,128]{2,1,0:T(8,128)(2,1)S(1)} %mixer_backward.1), channel_id=1, replica_groups=mesh['seq'=8,'chan'=4] {'seq'}, dimensions={0} | all-to-all | bytes 1245184 | tf_op jit(solution)/shard_map/all_to_all | solution.py:678
  97.9 0.1 sums.1
  98.0 5.2 %all-gather.1 = f32[32,128]{1,0:T(8,128)S(1)} all-gather(f32[8,128]{1,0:T(8,128)S(1)} %get-tuple-element.60), channel_id=3, replica_groups=mesh['seq'=8,'chan'=4] {'chan'}, dimensions={0}, use_global_device_ids=true | all-gather | bytes 20480 | tf_op jit(solution)/shard_map/all_gather | solution.py:821
  103.2 1.5 %final.1 = (f32[4,128,128]{2,1,0:T(8,128)}, f32[2,64,128]{2,1,0:T(8,128)}, f32[2,64,128]{2,1,0:T(8,128)}, f32[2,64,128]{2,1,0:T(8,128)}, f32[1,128]{1,0:T(1,128)...) custom-call(s32[1]{0:T(128)} %bitcast.rank_ref, ...), custom_call_target="tpu_custom_call" | custom-call | flops 2000000000 | bytes 6000000 | tf_op jit(solution)/shard_map/final/pallas_call | solution.py:621
  (8 shorter events, 0.0 us)
Async XLA Ops:
  0.6 14.4 %copy-start.1 = (bf16[512,128]{1,0:T(8,128)(2,1)S(1)}, bf16[512,128]{1,0:T(8,128)(2,1)}, u32[]{:S(2)}) copy-start(bf16[512,128]{1,0:T(8,128)(2,1)} %wg_ref.2) | copy-start | bytes 393220
  0.7 14.4 %copy-start = (bf16[512,128]{1,0:T(8,128)(2,1)S(1)}, bf16[512,128]{1,0:T(8,128)(2,1)}, u32[]{:S(2)}) copy-start(bf16[512,128]{1,0:T(8,128)(2,1)} %wv_ref.2) | copy-start | bytes 393220
  0.7 0.9 copy-start.2
  1.6 13.5 %copy-start.4 = (bf16[4,128,128]{2,1,0:T(8,128)(2,1)S(1)}, bf16[4,128,128]{2,1,0:T(8,128)(2,1)}, u32[]{:S(2)}) copy-start(bf16[4,128,128]{2,1,0:T(8,128)(2,1)} %cot_ref.4) | copy-start | bytes 393220
  1.6 13.5 %copy-start.10 = (f32[128]{0:T(128)S(1)}, f32[128]{0:T(128)}, u32[]{:S(2)}) copy-start(f32[128]{0:T(128)} %param.27) | copy-start | bytes 1540
  1.6 13.5 %copy-start.11 = (f32[128]{0:T(128)S(1)}, f32[128]{0:T(128)}, u32[]{:S(2)}) copy-start(f32[128]{0:T(128)} %param.28) | copy-start | bytes 1540
  1.7 15.5 %copy-start.18 = (s32[4,1]{0,1:T(1,128)S(1)}, s32[4,1]{0,1:T(1,128)}, u32[]{:S(2)}) copy-start(s32[4,1]{0,1:T(1,128)} %param.16) | copy-start | bytes 52
  1.7 15.6 %copy-start.5 = (f32[2,128,64]{1,2,0:T(8,128)S(1)}, f32[2,128,64]{1,2,0:T(8,128)}, u32[]{:S(2)}) copy-start(f32[2,128,64]{1,2,0:T(8,128)} %param.19) | copy-start | bytes 196612
  1.7 15.6 %copy-start.6 = (f32[2,128,64]{1,2,0:T(8,128)S(1)}, f32[2,128,64]{1,2,0:T(8,128)}, u32[]{:S(2)}) copy-start(f32[2,128,64]{1,2,0:T(8,128)} %param.20) | copy-start | bytes 196612
  1.7 15.6 %copy-start.7 = (f32[2,128,64]{1,2,0:T(8,128)S(1)}, f32[2,128,64]{1,2,0:T(8,128)}, u32[]{:S(2)}) copy-start(f32[2,128,64]{1,2,0:T(8,128)} %param.21) | copy-start | bytes 196612
  1.7 15.6 %copy-start.8 = (f32[128,64]{0,1:T(8,128)S(1)}, f32[128,64]{0,1:T(8,128)}, u32[]{:S(2)}) copy-start(f32[128,64]{0,1:T(8,128)} %param.23) | copy-start | bytes 98308
  1.8 15.6 %copy-start.9 = (f32[128,64]{0,1:T(8,128)S(1)}, f32[128,64]{0,1:T(8,128)}, u32[]{:S(2)}) copy-start(f32[128,64]{0,1:T(8,128)} %param.24) | copy-start | bytes 98308
  8.9 15.6 %all-to-all-start = ((f32[8,4,16,128]{3,2,1,0:T(8,128)}), f32[8,4,16,128]{3,2,1,0:T(8,128)S(1)}, u32[]{:S(2)}, u32[]{:S(2)}) async-start(f32[8,4,16,128]{3,2,1,0:T(8,128)} %get-tuple-element.42), calls=%async_computation | async-start | bytes 524288 | tf_op jit(solution)/shard_map/all_to_all | solution.py:678
  15.3 24.1 %collective-permute-start = (bf16[1168,128]{1,0:T(8,128)(2,1)S(1)}, bf16[1168,128]{1,0:T(8,128)(2,1)S(1)}, u32[]{:S(2)}, u32[]{:S(2)}) collective-permute-start(bf16[1168,128]{1,0:T(8,128)(2,1)S(1)} %get-tuple-element.51), channel_id=1, source_target_pairs={{0,1},{1,0},{2,3},{3,2},{4,5},{5,4},{6,7},{7,6},{8,9},{9,8},{10,11... | collective-permute-start | bytes 897032 | tf_op jit(solution)/shard_map/ppermute | solution.py:681
  15.4 24.0 %collective-permute-start.1 = (bf16[1168,128]{1,0:T(8,128)(2,1)S(1)}, bf16[1168,128]{1,0:T(8,128)(2,1)S(1)}, u32[]{:S(2)}, u32[]{:S(2)}) collective-permute-start(bf16[1168,128]{1,0:T(8,128)(2,1)S(1)} %get-tuple-element.52), channel_id=1, source_target_pairs={{0,2},{1,3},{2,0},{3,1},{4,6},{5,7},{6,4},{7,5},{8,10},{9,11},{10,... | collective-permute-start | bytes 897032 | tf_op jit(solution)/shard_map/ppermute | solution.py:681
  16.9 22.4 %collective-permute-start.2 = (bf16[1168,128]{1,0:T(8,128)(2,1)S(1)}, bf16[1168,128]{1,0:T(8,128)(2,1)S(1)}, u32[]{:S(2)}, u32[]{:S(2)}) collective-permute-start(bf16[1168,128]{1,0:T(8,128)(2,1)S(1)} %get-tuple-element.53), channel_id=1, source_target_pairs={{0,3},{1,2},{2,1},{3,0},{4,7},{5,6},{6,5},{7,4},{8,11},{9,10},{10,... | collective-permute-start | bytes 897032 | tf_op jit(solution)/shard_map/ppermute | solution.py:681
  17.3 7.1 %copy-start.12 = (f32[128]{0:T(128)S(1)}, f32[128]{0:T(128)}, u32[]{:S(2)}) copy-start(f32[128]{0:T(128)} %gain_ref.3) | copy-start | bytes 1540
  17.4 7.1 %copy-start.13 = (f32[128]{0:T(128)S(1)}, f32[128]{0:T(128)}, u32[]{:S(2)}) copy-start(f32[128]{0:T(128)} %bias_ref.3) | copy-start | bytes 1540
  17.4 7.1 %copy-start.14 = (f32[128]{0:T(128)S(1)}, f32[128]{0:T(128)}, u32[]{:S(2)}) copy-start(f32[128]{0:T(128)} %skip_ref.3) | copy-start | bytes 1540
  22.1 2.0 %copy-start.15 = (bf16[16,1024,128]{2,1,0:T(8,128)(2,1)}, bf16[16,1024,128]{2,1,0:T(8,128)(2,1)S(1)}, u32[]{:S(2)}) copy-start(bf16[16,1024,128]{2,1,0:T(8,128)(2,1)S(1)} %get-tuple-element.43.tab_ref) | copy-start | bytes 12582916
  32.5 1.0 copy-start.16
  33.6 30.0 %copy-start.3 = (bf16[4,128,128]{2,1,0:T(8,128)(2,1)S(1)}, bf16[4,128,128]{2,1,0:T(8,128)(2,1)}, u32[]{:S(2)}) copy-start(bf16[4,128,128]{2,1,0:T(8,128)(2,1)} %tokens_ref.9) | copy-start | bytes 393220
  33.6 13.5 %all-to-all-start.1 = ((bf16[32,16,128]{2,1,0:T(8,128)(2,1)}), bf16[32,16,128]{2,1,0:T(8,128)(2,1)S(1)}, u32[]{:S(2)}, u32[]{:S(2)}) async-start(bf16[32,16,128]{2,1,0:T(8,128)(2,1)} %bitcast.10), calls=%async_computation.1 | async-start | bytes 262144 | tf_op jit(solution)/shard_map/all_to_all | solution.py:678
  49.6 15.7 %all-to-all-start.2 = ((f32[32,16,128]{2,1,0:T(8,128)}), f32[32,16,128]{2,1,0:T(8,128)S(1)}, u32[]{:S(2)}, u32[]{:S(2)}) async-start(f32[32,16,128]{2,1,0:T(8,128)} %bitcast.13), calls=%async_computation.2 | async-start | bytes 524288 | tf_op jit(solution)/shard_map/all_to_all | solution.py:678
  52.2 7.3 %collective-permute-start.5 = (bf16[512,128]{1,0:T(8,128)(2,1)S(1)}, bf16[512,128]{1,0:T(8,128)(2,1)S(1)}, u32[]{:S(2)}, u32[]{:S(2)}) collective-permute-start(bf16[512,128]{1,0:T(8,128)(2,1)S(1)} %bitcast.28), channel_id=1, source_target_pairs={{0,3},{1,2},{2,1},{3,0},{4,7},{5,6},{6,5},{7,4},{8,11},{9,10},{10,... | collective-permute-start | bytes 393224 | tf_op jit(solution)/shard_map/ppermute | solution.py:681
  53.7 9.8 %collective-permute-start.4 = (bf16[512,128]{1,0:T(8,128)(2,1)S(1)}, bf16[512,128]{1,0:T(8,128)(2,1)S(1)}, u32[]{:S(2)}, u32[]{:S(2)}) collective-permute-start(bf16[512,128]{1,0:T(8,128)(2,1)S(1)} %bitcast.29), channel_id=1, source_target_pairs={{0,2},{1,3},{2,0},{3,1},{4,6},{5,7},{6,4},{7,5},{8,10},{9,11},{10,... | collective-permute-start | bytes 393224 | tf_op jit(solution)/shard_map/ppermute | solution.py:681
  54.0 9.5 %collective-permute-start.3 = (bf16[512,128]{1,0:T(8,128)(2,1)S(1)}, bf16[512,128]{1,0:T(8,128)(2,1)S(1)}, u32[]{:S(2)}, u32[]{:S(2)}) collective-permute-start(bf16[512,128]{1,0:T(8,128)(2,1)S(1)} %bitcast.30), channel_id=1, source_target_pairs={{0,1},{1,0},{2,3},{3,2},{4,5},{5,4},{6,7},{7,6},{8,9},{9,8},{10,11... | collective-permute-start | bytes 393224 | tf_op jit(solution)/shard_map/ppermute | solution.py:681
  54.1 11.2 %copy-start.17 = (f32[16,128,128]{2,1,0:T(8,128)S(1)}, f32[16,128,128]{2,1,0:T(8,128)}, u32[]{:S(2)}) copy-start(f32[16,128,128]{2,1,0:T(8,128)} %copy-done.16) | copy-start | bytes 3145732

commit v3 on v2

v3 whole, which is shorter than its diff:
```python
import functools
import math

import jax
import jax.numpy as jnp
from jax import lax
from jax.experimental import pallas as pl
from jax.experimental.pallas import tpu as pltpu
from jax.sharding import PartitionSpec as P

f32 = jnp.float32
bf16 = jnp.bfloat16
epsilon = 1e-05
NN = (((1,), (0,)), ((), ()))
NT = (((1,), (1,)), ((), ()))
TN = (((0,), (0,)), ((), ()))


def mm(left, right, dims=NN):
    return lax.dot_general(left, right, dims, preferred_element_type=f32)


def split(x):
    high = x.astype(bf16)
    return high, (x - high.astype(f32)).astype(bf16)


def swap(x, half):
    return pltpu.roll(x, half, axis=x.ndim - 1)


def lanes(shape):
    return lax.broadcasted_iota(jnp.int32, shape, len(shape) - 1)


def pair(z, half):
    low = lanes(z.shape) < half
    turned = swap(z, half)
    return jnp.where(low, z, turned), jnp.where(low, -turned, z)


def cmul(x, z, half):
    return x * z[0] + swap(x, half) * z[1]


def normal_cdf(y):
    return 0.5 * (1.0 + lax.erf(y * (1.0 / math.sqrt(2.0))))


def mirror(width):
    shape = (width, width)
    at = lanes(shape) + lax.broadcasted_iota(jnp.int32, shape, 0)
    return (at == width - 1).astype(f32).astype(bf16)


def live_rows(lens_ref, micros, chunks, width):
    shape = (chunks, width)
    at = lax.broadcasted_iota(jnp.int32, shape, 0) * width + (width - 1 - lanes(shape))
    rows = [(at < lens_ref[m]).astype(f32) for m in range(micros)]
    return jnp.concatenate(rows, axis=0)


def merge(means, squares, count):
    parts = len(means)
    mean = sum(means[1:], means[0]) * (1.0 / parts)
    square = sum(squares[1:], squares[0])
    for part in means:
        square = square + count * jnp.square(part - mean)
    return mean, lax.rsqrt(square * (1.0 / (parts * count)) + epsilon)


def fetch(copies):
    for copy in copies:
        copy.start()


def shift_chunks(x, by, micros, chunks):
    cube = x.reshape(micros, chunks, x.shape[-1])
    place = lax.broadcasted_iota(jnp.int32, cube.shape, 1)
    if by > 0:
        moved = jnp.where(place >= by, pltpu.roll(cube, by, axis=1), 0.0)
    else:
        moved = jnp.where(place < chunks + by, pltpu.roll(cube, chunks + by, axis=1), 0.0)
    return moved.reshape(x.shape)


def previous(u, micros, chunks):
    width = u.shape[1]
    turned = pltpu.roll(u, width - 1, axis=1)
    return jnp.where(
        lanes(u.shape) == width - 1, shift_chunks(turned, 1, micros, chunks), turned
    )


def following(u, micros, chunks):
    turned = pltpu.roll(u, 1, axis=1)
    return jnp.where(lanes(u.shape) == 0, shift_chunks(turned, -1, micros, chunks), turned)


def hankel(first, width):
    blocks = []
    for k in range(width // 8):
        by = width - 8 - 8 * k
        blocks.append(pltpu.roll(first, by, axis=1) if by else first)
    table = jnp.concatenate(blocks, axis=0)
    at = lanes(table.shape) + lax.broadcasted_iota(jnp.int32, table.shape, 0)
    return split(jnp.where(at >= width - 1, table, 0.0))


def gather_kernel(rank_ref, bv_ref, bg_ref, cot_hbm, wv_hbm, wg_hbm, *refs):
    outs, sems = refs[:-1], refs[-1]
    peers, wide, _ = cot_hbm.shape
    full = wv_hbm.shape[0]
    copies = []
    for k, out in enumerate(outs):
        for source, start, count in (
            (cot_hbm.at[rank_ref[0] ^ k], 0, wide),
            (wv_hbm, wide, full),
            (wg_hbm, wide + full, full),
        ):
            copies.append(
                pltpu.make_async_copy(
                    source, out.at[pl.ds(start, count), :], sems.at[len(copies)]
                )
            )
    fetch(copies)
    pieces = []
    for value in (bv_ref[...], bg_ref[...]):
        for _ in range(3):
            high = value.astype(bf16).astype(f32)
            pieces.append(high)
            value = value - high
    pieces.append(jnp.zeros((10, wide), f32))
    biases = jnp.concatenate(pieces, axis=0).astype(bf16)
    for out in outs:
        out[pl.ds(wide + 2 * full, 16), :] = biases
    for copy in copies:
        copy.wait()


def pack_kernel(seqs, tokens_hbm, send_ref, stats_ref, tokens, sems):
    micros, wide, width = tokens.shape
    chans = wide // seqs
    copies = [
        pltpu.make_async_copy(tokens_hbm.at[m], tokens.at[m], sems.at[m]) for m in range(micros)
    ]
    fetch(copies)
    turn = mirror(width)
    means, squares = [], []
    for m in range(micros):
        copies[m].wait()
        x = tokens[m].astype(f32)
        mean = jnp.sum(x, axis=0, keepdims=True) * (1.0 / wide)
        means.append(mean)
        squares.append(jnp.sum(jnp.square(x - mean), axis=0, keepdims=True))
        turned = mm(tokens[m], turn).astype(bf16)
        send_ref[:, pl.ds(m * chans, chans), :] = turned.reshape(seqs, chans, width)
    stats = jnp.concatenate(means + squares, axis=0)
    stats_ref[...] = stats
    high = stats.astype(bf16).astype(f32)
    tail = jnp.concatenate([high, stats - high], axis=0).astype(bf16)
    tail = mm(tail, turn).astype(bf16)
    for k in range(seqs):
        send_ref[k, pl.ds(micros * chans, 4 * micros), :] = tail


def table_kernel(
    chans,
    seqs,
    width,
    rank_ref,
    lens_ref,
    skip_ref,
    gain_ref,
    bias_ref,
    b_hbm,
    e_hbm,
    c_hbm,
    decay_hbm,
    turn_hbm,
    const_ref,
    power_ref,
    taps_ref,
    live_ref,
    b_ref,
    e_ref,
    c_ref,
    decay_ref,
    turn_ref,
    turned_keep,
    rise,
    coefs,
    steps,
    sems,
):
    half = decay_ref.shape[0]
    loads = [
        pltpu.make_async_copy(source, target, sems.at[k])
        for k, (source, target) in enumerate(
            (
                (b_hbm, b_ref),
                (e_hbm, e_ref),
                (c_hbm, c_ref),
                (decay_hbm, decay_ref),
                (turn_hbm, turn_ref),
            )
        )
    ]
    fetch(loads)
    for load in loads:
        load.wait()
    base = rank_ref[0] * chans
    levels = int(math.log2(width)) - 3
    spans = int(math.log2(seqs))

    def own(value):
        turned_keep[...] = value.T
        return turned_keep[pl.ds(base, chans), :]

    b = own(b_ref[...].reshape(2 * half, -1))
    e = own(e_ref[...].reshape(2 * half, -1))
    c = own(c_ref[...].reshape(2 * half, -1))
    mixed = own(jnp.concatenate([decay_ref[...], turn_ref[...]], axis=0))
    low = lanes(mixed.shape) < half
    other = swap(mixed, half)
    decay = jnp.where(low, mixed, other)
    turn = jnp.where(low, other, mixed)
    turned = jnp.where(low, jnp.cos(turn), jnp.sin(turn))
    a = jnp.exp(-decay) * turned
    inverse = pair(jnp.exp(decay) * jnp.where(low, turned, -turned), half)
    a_pair = pair(a, half)
    power = jnp.where(low, 1.0, 0.0)
    for k in range(8):
        rise[pl.ds(k * chans, chans), :] = power
        power = cmul(power, a_pair, half) if k else a
    for k in range(levels):
        power_pair = pair(power, half)
        steps[2 * k] = power_pair[0]
        steps[2 * k + 1] = power_pair[1]
        power = cmul(power, power_pair, half)
    kept = [pair(b, half), pair(e, half), pair(cmul(a, pair(c, half), half), half)]
    for k in range(spans):
        kept.append(pair(power, half))
        power = cmul(power, kept[-1], half)
    kept += [pair(c, half), a_pair]
    for k, both in enumerate(kept):
        const_ref[2 * k] = both[0]
        const_ref[2 * k + 1] = both[1]
    sign = jnp.where(low, 1.0, -1.0)
    for j in range(2):
        coef = cmul(c, kept[j], half)
        for k in range(7, -1, -1):
            coefs[pl.ds((8 * j + k) * chans, chans), :] = coef * sign
            coef = cmul(coef, inverse, half)

    live_ref[...] = live_rows(lens_ref, lens_ref.shape[0], seqs, width)
    for channel in range(chans):
        for k, ref in enumerate((gain_ref, bias_ref)):
            const_ref[2 * len(kept) + k, channel : channel + 1, :] = jnp.full(
                (1, 2 * half), ref[base + channel], f32
            )
        up = rise[pl.ds(channel, 8, stride=chans), :]
        for k in range(levels):
            by = (
                steps[2 * k, channel : channel + 1, :],
                steps[2 * k + 1, channel : channel + 1, :],
            )
            up = jnp.concatenate([up, cmul(up, by, half)], axis=0)
        high, low_part = split(up)
        power_ref[channel, pl.ds(0, width), :] = high
        power_ref[channel, pl.ds(width, width), :] = low_part
        coef = coefs[pl.ds(channel, 16, stride=chans), :]
        coef_hi = coef.astype(bf16).astype(f32)
        both = jnp.concatenate([coef_hi, coef - coef_hi], axis=0).astype(bf16)
        taps = mm(both, high, NT) + mm(both, low_part, NT)
        taps = taps[:16] + taps[16:]
        at = lanes(taps.shape) + lax.broadcasted_iota(jnp.int32, taps.shape, 0)
        taps_ref[channel] = taps + jnp.where(at == 7, skip_ref[base + channel], 0.0)


def own_rows(keep, at, stride, micros, chunks):
    return jnp.concatenate(
        [keep[pl.ds(at + m, chunks, stride=stride), :] for m in range(micros)], axis=0
    )


def channel_tokens(keep, channel, stride, micros, chunks, chans):
    return jnp.concatenate(
        [keep[pl.ds(m * chans + channel, chunks, stride=stride), :] for m in range(micros)],
        axis=0,
    )


def forward_kernel(
    micros,
    chunks,
    chans,
    peers,
    got_ref,
    const_ref,
    taps_ref,
    live_ref,
    *refs,
):
    stats_refs, refs = refs[: peers - 1], refs[peers - 1 :]
    power_hbm, refs = refs[0], refs[1:]
    act_ref, norm_ref, y_ref, kept_hbm, act_keep, x_keep, stats_keep = refs[:7]
    parts, wide_parts, sent_parts, kept_ref, power_ref, sem = refs[7:]
    load = pltpu.make_async_copy(power_hbm, power_ref, sem.at[0])
    load.start()
    width = got_ref.shape[2]
    half = const_ref.shape[2] // 2
    spans = int(math.log2(chunks))
    rows = micros * chunks
    stride = got_ref.shape[1]
    flip = jnp.where(lanes((1, 2 * half)) < half, 1.0, -1.0)

    def const(channel, k):
        return (
            const_ref[2 * k, channel : channel + 1, :],
            const_ref[2 * k + 1, channel : channel + 1, :],
        )

    live = live_ref[...]
    gain, bias = 2 * (5 + spans), 2 * (5 + spans) + 1
    for k in range(chunks):
        x_keep[pl.ds(k * stride, stride), :] = got_ref[k].astype(f32)
    means, squares = [], []
    for j in range(peers):
        keep, step, at = x_keep, stride, micros * chans
        if j:
            keep, step, at = stats_keep.at[j - 1], 4 * micros, 0
            for k in range(chunks):
                keep[pl.ds(k * step, step), :] = stats_refs[j - 1][k].astype(f32)
        lines = [own_rows(keep, at + q * micros, step, micros, chunks) for q in range(4)]
        means.append(lines[0] + lines[2])
        squares.append(lines[1] + lines[3])
    mean, inverse = merge(means, squares, chans * chunks)
    norm_ref[pl.ds(0, rows), :] = mean
    norm_ref[pl.ds(rows, rows), :] = inverse

    for channel in range(chans):
        x_hat = channel_tokens(x_keep, channel, stride, micros, chunks, chans) - mean
        line = slice(channel, channel + 1)
        u = live * (x_hat * inverse * const_ref[gain, line] + const_ref[bias, line])
        u_hi, u_lo = split(u)
        v_hi, v_lo = split(u * previous(u, micros, chunks))
        for k, part in enumerate((u_hi, v_hi, u_lo, v_lo)):
            parts[channel, k * rows : (k + 1) * rows] = part
        wide_parts[channel, :rows, :width] = u_hi
        wide_parts[channel, :rows, width:] = v_hi
        wide_parts[channel, rows:, :width] = u_lo
        wide_parts[channel, rows:, width:] = v_lo

    for channel in range(chans):
        tables = [hankel(taps_ref[channel, 8 * k : 8 * k + 8], width) for k in range(2)]
        both = wide_parts[channel]
        y = mm(both, jnp.concatenate([tables[0][0], tables[1][0]], axis=0))
        low_part = mm(both[:rows], jnp.concatenate([tables[0][1], tables[1][1]], axis=0))
        y_ref[channel] = y[:rows] + y[rows:] + low_part

    load.wait()
    for channel in range(chans):
        q = mm(parts[channel], power_ref[channel, :width])
        kept_ref[channel, : 2 * rows] = (
            q[: 2 * rows]
            + q[2 * rows :]
            + mm(parts[channel, : 2 * rows], power_ref[channel, width:])
        )

    for channel in range(chans):
        uq, vq = kept_ref[channel, :rows], kept_ref[channel, rows : 2 * rows]
        state = cmul(uq, const(channel, 0), half) + cmul(vq, const(channel, 1), half)
        for k in range(spans):
            moved = shift_chunks(state, 2**k, micros, chunks)
            state = state + cmul(moved, const(channel, 3 + k), half)
        start = shift_chunks(state, 1, micros, chunks)
        kept_ref[channel, 2 * rows :] = start
        high, low_part = split(cmul(start, const(channel, 2), half) * flip)
        sent_parts[channel, :rows] = high
        sent_parts[channel, rows:] = low_part
    store = pltpu.make_async_copy(kept_ref, kept_hbm, sem.at[1])
    store.start()

    for channel in range(chans):
        both = sent_parts[channel]
        cross = mm(both, power_ref[channel, :width], NT)
        y = y_ref[channel] + cross[:rows] + cross[rows:]
        y = y + mm(both[:rows], power_ref[channel, width:], NT)
        y_ref[channel] = y
        act = y * normal_cdf(y)
        for m in range(micros):
            act_keep[pl.ds(m * chunks * chans + channel, chunks, stride=chans), :] = act[
                m * chunks : (m + 1) * chunks
            ]
    act_ref[...] = act_keep[...].astype(bf16)
    store.wait()


def forward_scratch(micros, chunks, chans, peers, width, lane):
    rows = micros * chunks
    return [
        pltpu.VMEM((rows * chans, width), f32),
        pltpu.VMEM((chunks * micros * (chans + 4), width), f32),
        pltpu.VMEM((peers - 1, 4 * rows, width), f32),
        pltpu.VMEM((chans, 4 * rows, width), bf16),
        pltpu.VMEM((chans, 2 * rows, 2 * width), bf16),
        pltpu.VMEM((chans, 2 * rows, lane), bf16),
        pltpu.VMEM((chans, 3 * rows, lane), f32),
        pltpu.VMEM((chans, 2 * width, lane), bf16),
        pltpu.SemaphoreType.DMA((2,)),
    ]


def backward_kernel(
    micros,
    chunks,
    chans,
    got_ref,
    dact_ref,
    norm_ref,
    const_ref,
    taps_ref,
    live_ref,
    y_ref,
    power_hbm,
    kept_hbm,
    send_ref,
    sums_ref,
    sums_keep,
    head,
    x_keep,
    dact_keep,
    u_keep,
    prev_keep,
    dy_parts,
    uv_parts,
    yd_keep,
    duv_keep,
    lag_keep,
    adj_keep,
    sent_parts,
    dots,
    power_ref,
    kept_ref,
    sems,
):
    loads = [
        pltpu.make_async_copy(power_hbm, power_ref, sems.at[0]),
        pltpu.make_async_copy(kept_hbm, kept_ref, sems.at[1]),
    ]
    fetch(loads)
    width = got_ref.shape[2]
    half = const_ref.shape[2] // 2
    spans = int(math.log2(chunks))
    rows = micros * chunks
    stride = head.shape[0] // chunks
    got_stride = got_ref.shape[1]
    shape = (width, width)
    passed = lanes(shape) <= lax.broadcasted_iota(jnp.int32, shape, 0)
    low = lanes((1, 2 * half)) < half
    flip = jnp.where(low, 1.0, -1.0)
    live = live_ref[...]
    gain, bias = 2 * (5 + spans), 2 * (5 + spans) + 1
    for k in range(chunks):
        x_keep[pl.ds(k * got_stride, got_stride), :] = got_ref[k].astype(f32)
    dact_keep[...] = dact_ref[...].astype(f32)
    mean, inverse = norm_ref[:rows], norm_ref[rows:]

    def x_hat_of(channel):
        x = channel_tokens(x_keep, channel, got_stride, micros, chunks, chans)
        return (x - mean) * inverse

    def const(channel, k):
        return (
            const_ref[2 * k, channel : channel + 1, :],
            const_ref[2 * k + 1, channel : channel + 1, :],
        )

    def total(x):
        return jnp.sum(x, axis=0, keepdims=True)

    for channel in range(chans):
        line = slice(channel, channel + 1)
        u = live * (x_hat_of(channel) * const_ref[gain, line] + const_ref[bias, line])
        u_prev = previous(u, micros, chunks)
        u_keep[channel] = u
        prev_keep[channel] = u_prev
        u_hi, u_lo = split(u)
        v_hi, v_lo = split(u * u_prev)
        for k, (left, right) in enumerate(((u_hi, v_hi), (u_hi, v_hi), (u_lo, v_lo))):
            uv_parts[channel, k * rows : (k + 1) * rows, :width] = left
            uv_parts[channel, k * rows : (k + 1) * rows, width:] = right
        y = y_ref[channel]
        density = jnp.exp(-0.5 * y * y) * (1.0 / math.sqrt(2.0 * math.pi))
        d_y = dact_keep[pl.ds(channel, rows, stride=chans), :] * (normal_cdf(y) + y * density)
        high, low_part = split(d_y)
        dy_parts[channel, :rows] = high
        dy_parts[channel, rows : 2 * rows] = low_part
        dy_parts[channel, 2 * rows :] = high

    for channel in range(chans):
        tables = [hankel(taps_ref[channel, 8 * k : 8 * k + 8], width) for k in range(2)]
        both = dy_parts[channel, : 2 * rows]
        duv = mm(both, jnp.concatenate([tables[0][0], tables[1][0]], axis=1))
        low_part = mm(both[:rows], jnp.concatenate([tables[0][1], tables[1][1]], axis=1))
        duv_keep[channel] = duv[:rows] + duv[rows:] + low_part

    for channel in range(chans):
        outer = mm(dy_parts[channel], uv_parts[channel], TN)
        for k in range(2):
            rolled = pltpu.roll(
                outer[:, k * width : (k + 1) * width], 1, axis=1, stride=1, stride_axis=0
            )
            line = total(jnp.where(passed, rolled, 0.0))
            high = line.astype(bf16).astype(f32)
            lag_keep[channel, k : k + 1, :] = high
            lag_keep[channel, 2 + k : 3 + k, :] = line - high
            if k == 0:
                sums_keep[channel : channel + 1, :] = jnp.where(
                    lanes(line.shape) == 0, line, 0.0
                )

    for load in loads:
        load.wait()
    for channel in range(chans):
        both = dy_parts[channel, : 2 * rows]
        yd = mm(both, power_ref[channel, :width])
        low_part = mm(both[:rows], power_ref[channel, width:])
        yd_keep[channel] = yd[:rows] + yd[rows:] + low_part

    for channel in range(chans):
        adj = cmul(yd_keep[channel], const(channel, 2), half)
        for k in range(spans):
            moved = shift_chunks(adj, -(2**k), micros, chunks)
            adj = adj + cmul(moved, const(channel, 3 + k), half)
        adj = shift_chunks(adj, -1, micros, chunks)
        adj_keep[channel] = adj
        sent = jnp.concatenate(
            [cmul(adj, const(channel, 0), half), cmul(adj, const(channel, 1), half)], axis=0
        )
        high, low_part = split(sent * flip)
        sent_parts[channel, : 2 * rows] = high
        sent_parts[channel, 2 * rows :] = low_part

    for channel in range(chans):
        both = sent_parts[channel]
        cross = mm(both, power_ref[channel, :width], NT)
        cross = cross[: 2 * rows] + cross[2 * rows :]
        cross = cross + mm(both[: 2 * rows], power_ref[channel, width:], NT)
        d_v = duv_keep[channel, :, width:] + cross[rows:]
        d_u = duv_keep[channel, :, :width] + cross[:rows] + d_v * prev_keep[channel]
        d_u = d_u + following(d_v * u_keep[channel], micros, chunks)
        d_q = live * d_u
        sums_keep[chans + channel : chans + channel + 1, :] = total(d_q * x_hat_of(channel))
        sums_keep[2 * chans + channel : 2 * chans + channel + 1, :] = total(d_q)
        d_h = d_q * const_ref[gain, channel : channel + 1]
        for m in range(micros):
            head[pl.ds(m * chans + channel, chunks, stride=stride), :] = d_h[
                m * chunks : (m + 1) * chunks
            ]

    lag_keep[:, 4:, :] = jnp.zeros((chans, 12, width), f32)
    for channel in range(chans):
        lags = lag_keep[channel].astype(bf16)
        tops = mm(lags, power_ref[channel, :width]) + mm(lags, power_ref[channel, width:])
        dots[6, channel : channel + 1, :] = tops[0:1] + tops[2:3]
        dots[7, channel : channel + 1, :] = tops[1:2] + tops[3:4]
        adj, yd = adj_keep[channel], yd_keep[channel]
        adj_swap = swap(adj, half)
        uq, vq, start = [kept_ref[channel, k * rows : (k + 1) * rows] for k in range(3)]
        pairs = ((uq, adj), (uq, adj_swap), (vq, adj), (vq, adj_swap), (start, yd))
        for k, (left, right) in enumerate(pairs + ((start, swap(yd, half)),)):
            dots[k, channel : channel + 1, :] = total(left * right)

    def whole_const(k):
        return const_ref[2 * k], const_ref[2 * k + 1]

    def dot(k):
        same, other = dots[k], dots[k + 1]
        return jnp.where(low, same - swap(same, half), other + swap(other, half))

    top_u, top_v = dots[6], dots[7]
    c = whole_const(3 + spans)
    modes = jnp.concatenate(
        [
            flip * (cmul(top_u, c, half) + dot(0)),
            flip * (cmul(top_v, c, half) + dot(2)),
            flip
            * (
                cmul(top_u, whole_const(0), half)
                + cmul(top_v, whole_const(1), half)
                + cmul(dot(4), whole_const(4 + spans), half)
            ),
        ],
        axis=0,
    )
    sums = jnp.sum(sums_keep[...].T, axis=0, keepdims=True)
    sums_ref[:, pl.ds(0, 3 * chans)] = jnp.broadcast_to(sums, (8, 3 * chans))
    cut = micros * chans
    for k in range(chunks):
        head[pl.ds(k * stride + cut, 3 * chans), :] = modes
        send_ref[k] = head[pl.ds(k * stride, stride), :].astype(bf16)


def backward_scratch(micros, chunks, chans, stride, width, lane):
    rows = micros * chunks
    return [
        pltpu.VMEM((3 * chans, lane), f32),
        pltpu.VMEM((chunks * stride, width), f32),
        pltpu.VMEM((chunks * micros * (chans + 4), width), f32),
        pltpu.VMEM((rows * chans, width), f32),
        pltpu.VMEM((chans, rows, width), f32),
        pltpu.VMEM((chans, rows, width), f32),
        pltpu.VMEM((chans, 3 * rows, width), bf16),
        pltpu.VMEM((chans, 3 * rows, 2 * width), bf16),
        pltpu.VMEM((chans, rows, lane), f32),
        pltpu.VMEM((chans, rows, 2 * width), f32),
        pltpu.VMEM((chans, 16, width), f32),
        pltpu.VMEM((chans, rows, lane), f32),
        pltpu.VMEM((chans, 4 * rows, lane), bf16),
        pltpu.VMEM((8, chans, lane), f32),
        pltpu.VMEM((chans, 2 * width, lane), bf16),
        pltpu.VMEM((chans, 3 * rows, lane), f32),
        pltpu.SemaphoreType.DMA((2,)),
    ]


def gated(both, bias, g):
    wide = g.shape[1]
    value = both[:, :wide] + bias[:, :wide]
    gate = jax.nn.sigmoid(both[:, wide:] + bias[:, wide:])
    d_value = g * gate
    return value * gate, jnp.concatenate(
        [d_value.astype(bf16), (d_value * value * (1.0 - gate)).astype(bf16)], axis=1
    )


def project_kernel(width, place_ref, lens_ref, act_ref, *refs):
    refs, (dact_ref, d_keep) = refs[:-2], refs[-2:]
    full, rows = act_ref.shape
    peers = len(refs)
    wide = full // peers
    start = place_ref[1] * rows
    at = place_ref[0] * width + lax.rem(start, width)
    at = at + lax.broadcasted_iota(jnp.int32, (rows, wide), 0)
    live = (at < lens_ref[start // width]).astype(f32)
    act = act_ref[...].T

    def weight(ref):
        return jnp.concatenate(
            [ref[wide : wide + full, :], ref[wide + full : wide + 2 * full, :]], axis=1
        )

    for k, ref in enumerate(refs):
        g = live * ref[:wide, :].T.astype(f32)
        bias = ref[wide + 2 * full :, :].astype(f32)
        bias = jnp.concatenate(
            [bias[0:1] + bias[1:2] + bias[2:3], bias[3:4] + bias[4:5] + bias[5:6]], axis=1
        )
        d_both = gated(mm(act, weight(ref)), bias, g)[1]
        d_keep[:, 2 * k * wide : 2 * (k + 1) * wide] = d_both
    weights = jnp.concatenate([weight(ref) for ref in refs], axis=1)
    dact_ref[...] = mm(weights, d_keep[...], NT).astype(bf16)


def output_kernel(
    seqs,
    rank_ref,
    lens_ref,
    order_ref,
    tokens_ref,
    cot_ref,
    wv_ref,
    wg_ref,
    bv_ref,
    bg_ref,
    *refs,
):
    micros, wide, width = tokens_ref.shape
    acts_in, refs = refs[:micros], refs[micros:]
    sums_ref, head_ref, out_ref, send_hbm, d_keep, grad, sems = refs
    full = wv_ref.shape[0]
    stride = head_ref.shape[1]
    head = pltpu.make_async_copy(head_ref, send_hbm.at[:, pl.ds(0, stride), :], sems.at[0])
    head.start()
    at = rank_ref[0] * width + lax.broadcasted_iota(jnp.int32, (width, wide), 0)
    place = rank_ref[0] * width + lanes((1, width))
    weights = jnp.concatenate([wv_ref[...], wg_ref[...]], axis=1)
    bias = jnp.concatenate([bv_ref[...], bg_ref[...]], axis=1)
    for k in range(micros):
        m = order_ref[k]
        g = (at < lens_ref[m]).astype(f32) * cot_ref[m].T.astype(f32)
        added, d_both = gated(mm(acts_in[k][...].T, weights), bias, g)
        live = (place < lens_ref[m]).astype(f32)
        out_ref[m] = (live * (tokens_ref[m].astype(f32) + added.T)).astype(bf16)
        d_keep[k * width : (k + 1) * width] = d_both
    d_both = d_keep[...]
    acts = jnp.concatenate([ref[...] for ref in acts_in], axis=1)
    grad_w = mm(acts, d_both).astype(bf16)
    grad_b = mm(jnp.ones((8, micros * width), bf16), d_both)
    count = full // seqs
    for k in range(seqs):
        part = grad_w[k * count : (k + 1) * count]
        grad[k, pl.ds(16, count), pl.ds(0, wide)] = part[:, :wide]
        grad[k, pl.ds(16 + count, count), pl.ds(0, wide)] = part[:, wide:]
    rows = [grad_b[0:1, :wide], grad_b[0:1, wide:]]
    if wide < width:
        blank = jnp.zeros((1, width - wide), f32)
        rows = [jnp.concatenate([row, blank], axis=1) for row in rows]
    small = []
    for row in [sums_ref[0:1]] + rows:
        high = row.astype(bf16).astype(f32)
        small += [high, row - high]
    small = jnp.concatenate(small + [jnp.zeros((10, width), f32)], axis=0).astype(bf16)
    for k in range(seqs):
        grad[k, pl.ds(0, 16), :] = small
    tail = pltpu.make_async_copy(
        grad, send_hbm.at[:, pl.ds(stride, 16 + 2 * count), :], sems.at[1]
    )
    tail.start()
    tail.wait()
    head.wait()


def normal(tokens_ref, norm_ref, m):
    micros = tokens_ref.shape[0]
    return (tokens_ref[m].astype(f32) - norm_ref[m : m + 1]) * norm_ref[
        micros + m : micros + m + 1
    ]


def sums_kernel(got_ref, tokens_ref, *refs):
    stats_refs, (out_ref, head_ref, norm_ref) = refs[:-3], refs[-3:]
    micros, wide, width = tokens_ref.shape
    seqs, stride, _ = head_ref.shape
    chans = wide // seqs
    mean, inverse = merge(
        [ref[pl.ds(0, micros), :] for ref in stats_refs],
        [ref[pl.ds(micros, micros), :] for ref in stats_refs],
        wide,
    )
    norm_ref[pl.ds(0, micros), :] = mean
    norm_ref[pl.ds(micros, micros), :] = inverse
    cut = micros * chans
    turned = got_ref[:, pl.ds(0, cut), :].reshape(seqs * cut, width)
    head_ref[:, pl.ds(0, cut), :] = mm(turned, mirror(width)).reshape(seqs, cut, width)
    head_ref[:, pl.ds(cut, stride - cut), :] = got_ref[:, pl.ds(cut, stride - cut), :].astype(f32)
    for m in range(micros):
        d_hat = head_ref[:, pl.ds(m * chans, chans), :].reshape(wide, width)
        x_hat = normal(tokens_ref, norm_ref, m)
        out_ref[pl.ds(m, 1), :] = jnp.sum(d_hat, axis=0, keepdims=True)
        out_ref[pl.ds(micros + m, 1), :] = jnp.sum(d_hat * x_hat, axis=0, keepdims=True)


def final_kernel(
    rank_ref,
    lens_ref,
    got_ref,
    head_ref,
    tokens_ref,
    cot_ref,
    norm_ref,
    *refs,
):
    hat_refs, refs = refs[:-11], refs[-11:]
    d_in_ref, b_ref, e_ref, c_ref, skip_ref, gain_ref, norm_bias_ref = refs[:7]
    wv_ref, wg_ref, bv_ref, bg_ref = refs[7:]
    micros, wide, width = tokens_ref.shape
    seqs, stride, _ = head_ref.shape
    peers = len(hat_refs)
    chans = wide // seqs
    hats = [ref[...] for ref in hat_refs]
    hat = sum(hats[1:], hats[0]) * (1.0 / (peers * wide))
    at = rank_ref[0] * width + lanes((1, width))
    for m in range(micros):
        live = (at < lens_ref[m]).astype(f32)
        d_hat = head_ref[:, pl.ds(m * chans, chans), :].reshape(wide, width)
        x_hat = normal(tokens_ref, norm_ref, m)
        inside = d_hat - hat[m : m + 1] - x_hat * hat[micros + m : micros + m + 1]
        d_in_ref[m] = (
            live * cot_ref[m].astype(f32) + norm_ref[micros + m : micros + m + 1] * inside
        )
    cut = micros * chans
    for k, ref in enumerate((b_ref, e_ref, c_ref)):
        modes = head_ref[:, pl.ds(cut + k * chans, chans), :]
        ref[...] = modes.reshape(wide, -1).T.reshape(ref.shape)
    place = lanes((1, wide)) // chans
    last = stride - 16
    for k, ref in enumerate((skip_ref, gain_ref, norm_bias_ref)):
        line = jnp.zeros((1, wide), f32)
        for s in range(seqs):
            own = head_ref[s, pl.ds(last, 1), :] + head_ref[s, pl.ds(last + 1, 1), :]
            own = pltpu.roll(own, (s - k) * chans % own.shape[1], axis=1)[:, :wide]
            line = jnp.where(place == s, own, line)
        ref[...] = line
    count = wv_ref.shape[0]
    for k, ref in enumerate((wv_ref, wg_ref)):
        parts = got_ref[:, pl.ds(stride + k * count, count), pl.ds(0, wide)]
        ref[...] = jnp.sum(parts.astype(f32), axis=0)
    for k, ref in enumerate((bv_ref, bg_ref)):
        line = jnp.zeros((1, wide), f32)
        for s in range(seqs):
            line = line + head_ref[s, pl.ds(last + 2 + 2 * k, 1), pl.ds(0, wide)]
            line = line + head_ref[s, pl.ds(last + 3 + 2 * k, 1), pl.ds(0, wide)]
        ref[...] = line


def smem():
    return pl.BlockSpec(memory_space=pltpu.SMEM)


def vmem():
    return pl.BlockSpec(memory_space=pltpu.VMEM)


def in_hbm(x):
    return pltpu.with_memory_space_constraint(x, pltpu.HBM)


def shape_of(shape, kind=f32):
    return jax.ShapeDtypeStruct(shape, kind)


def kernel_call(kernel, name, scalars, arrays, outs, micros_of_time, limit=8, **more):
    ins = [smem()] * len(scalars) + [vmem()] * len(arrays)
    return pl.pallas_call(
        kernel,
        in_specs=ins,
        out_specs=[vmem()] * len(outs),
        out_shape=outs,
        compiler_params=pltpu.CompilerParams(vmem_limit_bytes=limit * 1024 * 1024),
        cost_estimate=cost(micros_of_time),
        name=name,
        **more,
    )(*scalars, *arrays)


def cost(micros_of_time):
    return pl.CostEstimate(
        flops=int(micros_of_time * 1e9), bytes_accessed=int(micros_of_time * 3e6), transcendentals=0
    )


def shards(
    tokens,
    lengths,
    ln_gain,
    ln_bias,
    b_coef,
    e_coef,
    c_coef,
    skip_gain,
    decay_rate,
    rotation,
    w_value,
    w_gate,
    bias_value,
    bias_gate,
    out_cotangent,
):
    micros, wide, width = tokens.shape
    modes = decay_rate.shape[1]
    full = w_value.shape[0]
    seqs = lax.axis_size("seq")
    peers = lax.axis_size("chan")
    seq_rank = lax.axis_index("seq").astype(jnp.int32)
    chan_rank = lax.axis_index("chan").astype(jnp.int32)
    chans = wide // seqs
    rows = micros * seqs
    own = micros * width // peers
    parts = width // own
    both = ("chan", "seq")
    lane = 2 * modes
    spans = int(math.log2(seqs))
    levels = int(math.log2(width)) - 3
    rank = seq_rank.reshape(1)
    lens = lengths.reshape(micros)
    place = jnp.stack([seq_rank, chan_rank])
    bias_rows = (bias_value.reshape(1, wide), bias_gate.reshape(1, wide))

    def exchange(x, axis):
        return lax.all_to_all(x, axis, 0, 0, tiled=True)

    def cross(x, by):
        return lax.ppermute(x, "chan", [(i, i ^ by) for i in range(peers)])

    hbm = pl.BlockSpec(memory_space=pltpu.HBM)
    x_send, part_stats = pl.pallas_call(
        functools.partial(pack_kernel, seqs),
        in_specs=[hbm],
        out_specs=[vmem()] * 2,
        out_shape=[
            shape_of((seqs, micros * (chans + 4), width), bf16),
            shape_of((2 * micros, width)),
        ],
        scratch_shapes=[
            pltpu.VMEM(tokens.shape, bf16),
            pltpu.SemaphoreType.DMA((micros,)),
        ],
        compiler_params=pltpu.CompilerParams(vmem_limit_bytes=8 * 1024 * 1024),
        cost_estimate=cost(1),
        name="pack",
    )(in_hbm(tokens))
    x_mine = exchange(x_send, "seq")
    stats = [part_stats] + [cross(part_stats, k) for k in range(1, peers)]

    cot, wv, wg, _ = lax.optimization_barrier((out_cotangent, w_value, w_gate, part_stats))
    cot_own = cot.reshape(micros, wide, parts, own).transpose(0, 2, 1, 3).reshape(peers, wide, own)
    weights = pl.pallas_call(
        gather_kernel,
        in_specs=[smem()] + [vmem()] * 2 + [hbm] * 3,
        out_specs=[vmem()] * peers,
        out_shape=[shape_of((wide + 2 * full + 16, own), bf16)] * peers,
        scratch_shapes=[pltpu.SemaphoreType.DMA((3 * peers,))],
        compiler_params=pltpu.CompilerParams(vmem_limit_bytes=8 * 1024 * 1024),
        cost_estimate=cost(1),
        name="weights",
    )(chan_rank.reshape(1), *bias_rows, in_hbm(cot_own), in_hbm(wv), in_hbm(wg))

    turned = [jnp.transpose(z, (0, 2, 1)) for z in (b_coef, e_coef, c_coef)]
    const, power, taps, live = pl.pallas_call(
        functools.partial(table_kernel, chans, seqs, width),
        in_specs=[smem()] * 5 + [hbm] * 5,
        out_specs=[vmem()] * 4,
        out_shape=[
            shape_of((12 + 2 * spans, chans, lane)),
            pltpu.HBM((chans, 2 * width, lane), bf16),
            shape_of((chans, 16, width)),
            shape_of((rows, width)),
        ],
        scratch_shapes=[pltpu.VMEM(turned[0].shape, f32)] * 3
        + [pltpu.VMEM((modes, wide), f32)] * 2
        + [
            pltpu.VMEM((wide, lane), f32),
            pltpu.VMEM((8 * chans, lane), f32),
            pltpu.VMEM((16 * chans, lane), f32),
            pltpu.VMEM((2 * levels, chans, lane), f32),
            pltpu.SemaphoreType.DMA((5,)),
        ],
        compiler_params=pltpu.CompilerParams(vmem_limit_bytes=8 * 1024 * 1024),
        cost_estimate=cost(2),
        name="tables",
    )(rank, lens, skip_gain, ln_gain, ln_bias, *[in_hbm(z) for z in (*turned, decay_rate.T, rotation.T)])

    x_mine, const, weights = lax.optimization_barrier((x_mine, const, weights))
    x_stats = x_mine[:, micros * chans :]
    x_stats = [cross(x_stats, k) for k in range(1, peers)]
    weights = [weights[0]] + [cross(weights[k], k) for k in range(1, peers)]
    arrays = (x_mine, const, taps, live, *x_stats, in_hbm(power))
    act, norm_mine, y_mine, kept = pl.pallas_call(
        functools.partial(forward_kernel, micros, seqs, chans, peers),
        in_specs=[vmem()] * (len(arrays) - 1) + [hbm],
        out_specs=[vmem()] * 3 + [hbm],
        out_shape=[
            shape_of((rows * chans, width), bf16),
            shape_of((2 * rows, width)),
            shape_of((chans, rows, width)),
            pltpu.HBM((chans, 3 * rows, lane), f32),
        ],
        scratch_shapes=forward_scratch(micros, seqs, chans, peers, width, lane),
        compiler_params=pltpu.CompilerParams(vmem_limit_bytes=16 * 1024 * 1024),
        cost_estimate=cost(5),
        name="mixer_forward",
    )(*arrays)

    act = (
        act.reshape(micros, seqs, chans, parts, own)
        .transpose(0, 3, 1, 2, 4)
        .reshape(peers * seqs, chans, own)
    )
    act = exchange(act, both).reshape(full, own)
    (d_act,) = kernel_call(
        functools.partial(project_kernel, width),
        "project",
        (place, lens),
        (act, *weights),
        [shape_of((full, own), bf16)],
        2,
        limit=12,
        scratch_shapes=[pltpu.VMEM((own, 2 * full), bf16)],
    )

    act, d_act = lax.optimization_barrier((act, d_act))
    acts = [act] + [cross(act, k) for k in range(1, peers)]
    if parts == 1:
        order = chan_rank ^ jnp.arange(peers, dtype=jnp.int32)
    else:
        stacked = jnp.stack(acts)[chan_rank ^ jnp.arange(peers, dtype=jnp.int32)]
        stacked = stacked.reshape(micros, parts, full, own).transpose(0, 2, 1, 3)
        stacked = stacked.reshape(micros, full, width)
        acts = [stacked[m] for m in range(micros)]
        order = jnp.arange(micros, dtype=jnp.int32)

    d_act = exchange(d_act.reshape(peers * seqs, chans, own), both)
    d_act = (
        d_act.reshape(micros, parts, seqs, chans, own)
        .transpose(0, 2, 3, 1, 4)
        .reshape(rows * chans, width)
    )
    count = full // seqs
    stride = -(-(micros + 3) * chans // 16) * 16
    head = shape_of((seqs, stride, width), bf16)
    arrays = (x_mine, d_act, norm_mine, const, taps, live, y_mine, in_hbm(power), in_hbm(kept))
    head, sums = pl.pallas_call(
        functools.partial(backward_kernel, micros, seqs, chans),
        in_specs=[vmem()] * (len(arrays) - 2) + [hbm] * 2,
        out_specs=[vmem()] * 2,
        out_shape=[head, shape_of((8, width))],
        scratch_shapes=backward_scratch(micros, seqs, chans, stride, width, lane),
        compiler_params=pltpu.CompilerParams(vmem_limit_bytes=20 * 1024 * 1024),
        cost_estimate=cost(5),
        name="mixer_backward",
    )(*arrays)
    arrays = (tokens, out_cotangent, w_value, w_gate) + bias_rows + tuple(acts) + (sums, head)
    send_shape = (seqs, stride + 16 + 2 * count, width)
    out, d_hat = pl.pallas_call(
        functools.partial(output_kernel, seqs),
        in_specs=[smem()] * 3 + [vmem()] * len(arrays),
        out_specs=[vmem(), hbm],
        out_shape=[shape_of(tokens.shape, bf16), pltpu.HBM(send_shape, bf16)],
        scratch_shapes=[
            pltpu.VMEM((micros * width, 2 * wide), bf16),
            pltpu.VMEM((seqs, 16 + 2 * count, width), bf16),
            pltpu.SemaphoreType.DMA((2,)),
        ],
        compiler_params=pltpu.CompilerParams(vmem_limit_bytes=12 * 1024 * 1024),
        cost_estimate=cost(2),
        name="output",
    )(rank, lens, order, *arrays)
    stride += 16
    got = exchange(d_hat, "seq")
    own_sums, head, norm = kernel_call(
        sums_kernel,
        "sums",
        (),
        (got, tokens, *stats),
        [
            shape_of((2 * micros, width)),
            shape_of((seqs, stride, width)),
            shape_of((2 * micros, width)),
        ],
        1,
    )
    hat_sums = [own_sums] + [cross(own_sums, k) for k in range(1, peers)]
    mode_grad = shape_of((2, modes, wide))
    d_input, d_b, d_e, d_c, d_skip, d_gain, d_bias, d_wv, d_wg, d_bv, d_bg = kernel_call(
        final_kernel,
        "final",
        (rank, lens),
        (got, head, tokens, out_cotangent, norm, *hat_sums),
        [shape_of(tokens.shape)]
        + [mode_grad] * 3
        + [shape_of((1, wide))] * 3
        + [shape_of((count, wide))] * 2
        + [shape_of((1, wide))] * 2,
        2,
    )
    d_b, d_e, d_c = [jnp.transpose(z, (0, 2, 1)) for z in (d_b, d_e, d_c)]
    d_skip, d_gain, d_bias, d_bv, d_bg = [
        z.reshape(wide) for z in (d_skip, d_gain, d_bias, d_bv, d_bg)
    ]
    return (out, d_input, d_gain, d_bias, d_b, d_e, d_c, d_skip, d_wv, d_wg, d_bv, d_bg)


def solution(mesh):
    chan = P("chan")
    modes = P(None, "chan", None)
    table = P("chan", None)
    weight = P(None, "chan")
    rows = P(None, "chan", "seq")
    spread = P("seq", "chan")
    return jax.shard_map(
        shards,
        mesh=mesh,
        in_specs=(
            rows,
            P(),
            chan,
            chan,
            modes,
            modes,
            modes,
            chan,
            table,
            table,
            weight,
            weight,
            chan,
            chan,
            rows,
        ),
        out_specs=(
            rows,
            rows,
            chan,
            chan,
            modes,
            modes,
            modes,
            chan,
            spread,
            spread,
            chan,
            chan,
        ),
        check_vma=False,
    )
```

time: 105 us -> 83.8 us (0.80)
  blocking collectives: 34.2 us -> 0 us
  waiting for transfers between devices: 17.4 us -> 29.5 us
  starting transfers between devices: 18.4 us -> 28.6 us
  Pallas kernels: 29.6 us -> 22.8 us
  local copies, waits for them, and re-layouts: 4.11 us -> 1.34 us
    all_to_all x1 -> x0, blocking collectives: 22.7 us -> none  [exchange(): return lax.all_to_all(x, axis, 0, 0, tiled=True)]
    all_to_all x3 -> x4, waiting for transfers between devices: 8 us -> 24.7 us  [exchange(): return lax.all_to_all(x, axis, 0, 0, tiled=True)]
    all_gather x2 -> x0, blocking collectives: 11.5 us -> none  [the longest x1 6.35 us: shards(): stats = lax.all_gather(part_stats, 'chan')]
    ppermute x6 -> x15, starting transfers between devices: 3.87 us -> 9.32 us  [cross(): return lax.ppermute(x, 'chan', [(i, i ^ by) for i in range(peers)])]
    all_to_all x3 -> x4, starting transfers between devices: 14.5 us -> 19.2 us  [exchange(): return lax.all_to_all(x, axis, 0, 0, tiled=True)]
    ppermute x6 -> x15, waiting for transfers between devices: 9.38 us -> 4.78 us  [cross(): return lax.ppermute(x, 'chan', [(i, i ^ by) for i in range(peers)])]
    pallas_call x3 -> x6, Pallas kernels: 22.7 us -> 19.2 us  [the longest x1 4.37 us: shards(): pl.pallas_call(functools.partial(backward_kernel, micros, seqs, chans), i...]
    pallas_call x7 -> x3, Pallas kernels: 6.94 us -> 3.6 us  [kernel_call(): pl.pallas_call(kernel, in_specs=ins, out_specs=[vmem()] * len(outs), out_...]
  transfers between devices with their start and end apart: 9 -> 19, of which waited for: 4 -> 10; matrix products, arithmetic and copies ran while one was open for 0% -> 0% of each run, Pallas kernels for 14% -> 17%
where the time goes in v3:
time: 83.8 us; the launch traced here: 83.1 us
  waiting for transfers between devices  29.5 us (35%)
  starting transfers between devices  28.6 us (34%)
  Pallas kernels  22.8 us (27%)
  local copies, waits for them, and re-layouts  1.34 us (2%)
  between operations  0.86 us (1%)
    all_to_all x4, waiting for transfers between devices, exchange(): return lax.all_to_all(x, axis, 0, 0, tiled=True)  24.7 us
    all_to_all x4, starting transfers between devices, exchange(): return lax.all_to_all(x, axis, 0, 0, tiled=True)  19.2 us
    ppermute x15, starting transfers between devices, cross(): return lax.ppermute(x, 'chan', [(i, i ^ by) for i in range(peers)])  9.32 us
    ppermute x15, waiting for transfers between devices, cross(): return lax.ppermute(x, 'chan', [(i, i ^ by) for i in range(peers)])  4.78 us
    pallas_call x1, Pallas kernels, shards(): pl.pallas_call(functools.partial(backward_kernel, micros, seqs, chans), i...  4.37 us
    pallas_call x1, Pallas kernels, shards(): pl.pallas_call(functools.partial(forward_kernel, micros, seqs, chans, pee...  4.35 us
    pallas_call x1, Pallas kernels, shards(): pl.pallas_call(functools.partial(table_kernel, chans, seqs, width), in_sp...  4.34 us
    pallas_call x3, Pallas kernels, kernel_call(): pl.pallas_call(kernel, in_specs=ins, out_specs=[vmem()] * len(outs), out_...  3.6 us
  transfers between devices with their start and end apart: 19, of which 10 were waited for; matrix products, arithmetic and copies ran while one was open for 0% of the time, Pallas kernels for 17%

profile of v3, /device:TPU:0, one launch (start us, length us, event | category | flops | bytes accessed | tf_op | source)
XLA Modules:
  0.0 83.1 jit_solution(13766316825568903883)
XLA Ops:
  0.6 2.1 %pack.1 = (bf16[8,80,128]{2,1,0:T(8,128)(2,1)}, f32[8,128]{1,0:T(8,128)S(1)}) custom-call(bf16[4,128,128]{2,1,0:T(8,128)(2,1)} %tokens_ref.5), custom_call_target="tpu_custom_call" | custom-call | flops 1000000000 | bytes 3000000 | tf_op jit(solution)/shard_map/pack/pallas_call | solution.py:889
  2.7 7.3 %all-to-all-start = ((bf16[8,80,128]{2,1,0:T(8,128)(2,1)}), bf16[8,80,128]{2,1,0:T(8,128)(2,1)S(1)}, u32[]{:S(2)}, u32[]{:S(2)}) async-start(bf16[8,80,128]{2,1,0:T(8,128)(2,1)} %get-tuple-element.55), calls=%async_computation | async-start | bytes 327680 | tf_op jit(solution)/shard_map/all_to_all | solution.py:883
  10.0 0.0 copy-start.7
  10.0 0.0 copy-start.8
  10.0 0.6 copy-done.7
  10.6 0.0 copy-done.8
  10.7 1.5 %weights.1 = (bf16[1168,128]{1,0:T(8,128)(2,1)S(1)}, bf16[1168,128]{1,0:T(8,128)(2,1)S(1)}, bf16[1168,128]{1,0:T(8,128)(2,1)S(1)}, bf16[1168,128]{1,0:T(8,128)(2,1)S(1)}) custom-call(s32[1]{0:T(128)} %bitcast.9.rank_ref, f32[1,128]{1,0:T(1,128)S(1)} %bitcast.28, f32[1,128]{1,0:T(1,128)S(1)} %bitcast.30, bf16[4,128,128]{2,1,0:T(8,128)(2,1)} %cot_ref.3, ...), custom_call_target="tpu_custom_call" | custom-call | flops 1000000000 | bytes 3000000 | tf_op jit(solution)/shard_map/weights/pallas_call | solution.py:910
  12.1 0.0 copy-start.4
  12.1 0.0 copy-start.5
  12.1 0.0 copy-start.6
  12.2 0.0 copy-done.9
  12.2 0.6 copy-done.4
  12.8 0.0 copy-done.5
  12.8 0.0 copy-done.6
  12.8 4.3 %tables.1 = (f32[18,16,128]{2,1,0:T(8,128)S(1)}, bf16[16,256,128]{2,1,0:T(8,128)(2,1)}, f32[16,16,128]{2,1,0:T(8,128)S(1)}, f32[32,128]{1,0:T(8,128)S(1)}) custom-call(s32[1]{0:T(128)} %bitcast.rank_ref, s32[4]{0:T(128)S(1)} %bitcast.32, f32[128]{0:T(128)S(1)} %copy-done.4, f32[128]{0:T(128)S(1)} %copy-done.5, f32[128]{0:T(128)S(1)} %copy-done.6, ...), custom_call_target="tpu_custom_call" | custom-call | flops 2000000000 | bytes 6000000 | tf_op jit(solution)/shard_map/tables/pallas_call | solution.py:922
  17.2 0.4 all-to-all-done.got_ref
  17.6 0.4 collective-permute-start.2
  17.9 1.2 %collective-permute-start.1 = (bf16[8,16,128]{2,1,0:T(8,128)(2,1)S(1)}, bf16[8,16,128]{2,1,0:T(8,128)(2,1)S(1)}, u32[]{:S(2)}, u32[]{:S(2)}) collective-permute-start(bf16[8,16,128]{2,1,0:T(8,128)(2,1)S(1)} %slice.3), channel_id=1, source_target_pairs={{0,2},{1,3},{2,0},{3,1},{4,6},{5,7},{6,4},{7,5},{8,10},{9,11},{10,... | collective-permute-start | bytes 98312 | tf_op jit(solution)/shard_map/ppermute | solution.py:886
  19.1 0.3 collective-permute-start
  19.4 0.2 collective-permute-start.3
  19.6 1.3 %collective-permute-start.4 = (bf16[1168,128]{1,0:T(8,128)(2,1)S(1)}, bf16[1168,128]{1,0:T(8,128)(2,1)S(1)}, u32[]{:S(2)}, u32[]{:S(2)}) collective-permute-start(bf16[1168,128]{1,0:T(8,128)(2,1)S(1)} %get-tuple-element.73), channel_id=1, source_target_pairs={{0,2},{1,3},{2,0},{3,1},{4,6},{5,7},{6,4},{7,5},{8,10},{9,11},{10,... | collective-permute-start | bytes 897032 | tf_op jit(solution)/shard_map/ppermute | solution.py:886
  20.9 0.2 collective-permute-done.2.refs_2_
  21.2 0.1 collective-permute-start.5
  21.3 0.6 collective-permute-done.1.refs_1_
  21.9 0.0 collective-permute-done.refs_0_
  21.9 4.4 %mixer_forward.1 = (bf16[512,128]{1,0:T(8,128)(2,1)}, f32[64,128]{1,0:T(8,128)S(1)}, f32[16,32,128]{2,1,0:T(8,128)S(1)}, f32[16,96,128]{2,1,0:T(8,128)}) custom-call(bf16[8,80,128]{2,1,0:T(8,128)(2,1)S(1)} %all-to-all-done.got_ref, f32[18,16,128]{2,1,0:T(8,128)S(1)} %get-tuple-element.66.const_ref, f32[16,16,128]{2,1,0:T(8,128)S(1)} %get-tuple-element.67.taps_ref, ...), custom_call_target="tpu_custom_call" | custom-call | flops 5000000000 | bytes 15000000 | tf_op jit(solution)/shard_map/mixer_forward/pallas_call | solution.py:951
  26.3 5.4 %all-to-all-start.1 = ((bf16[32,16,128]{2,1,0:T(8,128)(2,1)}), bf16[32,16,128]{2,1,0:T(8,128)(2,1)S(1)}, u32[]{:S(2)}, u32[]{:S(2)}) async-start(bf16[32,16,128]{2,1,0:T(8,128)(2,1)} %bitcast.10), calls=%async_computation.1 | async-start | bytes 262144 | tf_op jit(solution)/shard_map/all_to_all | solution.py:883
  31.7 0.1 pad_add_fusion.place_ref
  31.8 7.7 %all-to-all-done.1 = bf16[32,16,128]{2,1,0:T(8,128)(2,1)S(1)} async-done(((bf16[32,16,128]{2,1,0:T(8,128)(2,1)}), bf16[32,16,128]{2,1,0:T(8,128)(2,1)S(1)}, u32[]{:S(2)}, u32[]{:S(2)}) %all-to-all-start.1) | async-done | bytes 131104 | tf_op jit(solution)/shard_map/all_to_all | solution.py:883
  39.5 0.0 collective-permute-done.3.refs_1_
  39.5 0.0 collective-permute-done.4.refs_2_
  39.5 0.0 collective-permute-done.5.refs_3_
  39.5 2.0 %project.1 = bf16[512,128]{1,0:T(8,128)(2,1)} custom-call(s32[2]{0:T(128)S(1)} %pad_add_fusion.place_ref, s32[4]{0:T(128)S(1)} %bitcast.33, bf16[512,128]{1,0:T(8,128)(2,1)S(1)} %bitcast.22, bf16[1168,128]{1,0:T(8,128)(2,1)S(1)} %get-tuple-element.71.refs_0_, bf16[1168,128]{1,0:T(8,128)(2,1)S(1)} %collective-permute-done.3.refs_1_, ...), custom_call_target="tpu_custom_call" | custom-call | flops 2000000000 | bytes 6000000 | tf_op jit(solution)/shard_map/project/pallas_call | solution.py:827
  41.4 3.0 %all-to-all-start.2 = ((bf16[32,16,128]{2,1,0:T(8,128)(2,1)}), bf16[32,16,128]{2,1,0:T(8,128)(2,1)S(1)}, u32[]{:S(2)}, u32[]{:S(2)}) async-start(bf16[32,16,128]{2,1,0:T(8,128)(2,1)} %bitcast.12), calls=%async_computation.2 | async-start | bytes 262144 | tf_op jit(solution)/shard_map/all_to_all | solution.py:883
  44.5 1.6 %collective-permute-start.8 = (bf16[512,128]{1,0:T(8,128)(2,1)S(1)}, bf16[512,128]{1,0:T(8,128)(2,1)S(1)}, u32[]{:S(2)}, u32[]{:S(2)}) collective-permute-start(bf16[512,128]{1,0:T(8,128)(2,1)S(1)} %bitcast.23), channel_id=1, source_target_pairs={{0,3},{1,2},{2,1},{3,0},{4,7},{5,6},{6,5},{7,4},{8,11},{9,10},{10,... | collective-permute-start | bytes 393224 | tf_op jit(solution)/shard_map/ppermute | solution.py:886
  46.1 0.4 collective-permute-start.7
  46.4 0.0 collective-permute-start.6
  46.4 5.8 %all-to-all-done.2 = bf16[32,16,128]{2,1,0:T(8,128)(2,1)S(1)} async-done(((bf16[32,16,128]{2,1,0:T(8,128)(2,1)}), bf16[32,16,128]{2,1,0:T(8,128)(2,1)S(1)}, u32[]{:S(2)}, u32[]{:S(2)}) %all-to-all-start.2) | async-done | bytes 131104 | tf_op jit(solution)/shard_map/all_to_all | solution.py:883
  52.2 0.0 copy-start
  52.2 4.4 %mixer_backward.1 = (bf16[8,112,128]{2,1,0:T(8,128)(2,1)S(1)}, f32[8,128]{1,0:T(8,128)S(1)}) custom-call(bf16[8,80,128]{2,1,0:T(8,128)(2,1)S(1)} %all-to-all-done.got_ref, bf16[512,128]{1,0:T(8,128)(2,1)S(1)} %bitcast.27, f32[64,128]{1,0:T(8,128)S(1)} %get-tuple-element.77.norm_ref, f32[18,16,128]{2,1,0:T(8,128)S(1)} %get-tuple-element.66.const_ref, ...), custom_call_target="tpu_custom_call" | custom-call | flops 5000000000 | bytes 15000000 | tf_op jit(solution)/shard_map/mixer_backward/pallas_call | solution.py:1005
  56.6 0.0 collective-permute-done.8.refs_3_
  56.6 0.0 collective-permute-done.7.refs_2_
  56.6 0.0 collective-permute-done.6.refs_1_
  56.6 0.0 copy-done
  56.6 0.0 copy-done.1
  56.6 0.0 copy-done.2
  56.7 0.0 copy-done.3
  56.7 2.6 %output.1 = (bf16[4,128,128]{2,1,0:T(8,128)(2,1)}, bf16[8,256,128]{2,1,0:T(8,128)(2,1)}) custom-call(s32[1]{0:T(128)} %bitcast.rank_ref, s32[4]{0:T(128)S(1)} %bitcast.34, s32[4]{0:T(128)S(1)} %iota_xor_fusion.order_ref, bf16[4,128,128]{2,1,0:T(8,128)(2,1)S(1)} %copy-done.2, bf16[4,128,128]{2,1,0:T(8,128)(2,1)S(1)} %copy-done.3, ...), custom_call_target="tpu_custom_call" | custom-call | flops 2000000000 | bytes 6000000 | tf_op jit(solution)/shard_map/output/pallas_call | solution.py:1017
  59.3 3.5 %all-to-all-start.3 = ((bf16[8,256,128]{2,1,0:T(8,128)(2,1)}), bf16[8,256,128]{2,1,0:T(8,128)(2,1)S(1)}, u32[]{:S(2)}, u32[]{:S(2)}) async-start(bf16[8,256,128]{2,1,0:T(8,128)(2,1)} %get-tuple-element.83), calls=%async_computation.3 | async-start | bytes 1048576 | tf_op jit(solution)/shard_map/all_to_all | solution.py:883
  62.8 0.4 collective-permute-start.11
  63.2 1.4 %collective-permute-start.10 = (f32[8,128]{1,0:T(8,128)S(1)}, f32[8,128]{1,0:T(8,128)S(1)}, u32[]{:S(2)}, u32[]{:S(2)}) collective-permute-start(f32[8,128]{1,0:T(8,128)S(1)} %get-tuple-element.57.refs_0_), channel_id=1, source_target_pairs={{0,2},{1,3},{2,0},{3,1},{4,6},{5,7},{6,4},{7,5},{8,10},{9,11},{10,... | collective-permute-start | bytes 12296 | tf_op jit(solution)/shard_map/ppermute | solution.py:886
  64.6 0.1 collective-permute-start.9
  64.7 1.1 %collective-permute-done.11.refs_3_ = f32[8,128]{1,0:T(8,128)S(1)} collective-permute-done((f32[8,128]{1,0:T(8,128)S(1)}, f32[8,128]{1,0:T(8,128)S(1)}, u32[]{:S(2)}, u32[]{:S(2)}) %collective-permute-start.11) | collective-permute-done | bytes 4128 | tf_op jit(solution)/shard_map/ppermute | solution.py:886
  65.9 0.9 %collective-permute-done.10.refs_2_ = f32[8,128]{1,0:T(8,128)S(1)} collective-permute-done((f32[8,128]{1,0:T(8,128)S(1)}, f32[8,128]{1,0:T(8,128)S(1)}, u32[]{:S(2)}, u32[]{:S(2)}) %collective-permute-start.10) | collective-permute-done | bytes 4128 | tf_op jit(solution)/shard_map/ppermute | solution.py:886
  66.8 0.0 collective-permute-done.9.refs_1_
  66.8 10.9 %all-to-all-done.3.got_ref = bf16[8,256,128]{2,1,0:T(8,128)(2,1)S(1)} async-done(((bf16[8,256,128]{2,1,0:T(8,128)(2,1)}), bf16[8,256,128]{2,1,0:T(8,128)(2,1)S(1)}, u32[]{:S(2)}, u32[]{:S(2)}) %all-to-all-start.3) | async-done | bytes 524320 | tf_op jit(solution)/shard_map/all_to_all | solution.py:883
  77.7 0.2 sums.1
  77.9 0.1 collective-permute-start.14
  78.0 0.7 collective-permute-start.13
  78.7 1.1 %collective-permute-start.12 = (f32[8,128]{1,0:T(8,128)S(1)}, f32[8,128]{1,0:T(8,128)S(1)}, u32[]{:S(2)}, u32[]{:S(2)}) collective-permute-start(f32[8,128]{1,0:T(8,128)S(1)} %get-tuple-element.86.refs_0_), channel_id=1, source_target_pairs={{0,1},{1,0},{2,3},{3,2},{4,5},{5,4},{6,7},{7,6},{8,9},{9,8},{10,11... | collective-permute-start | bytes 12296 | tf_op jit(solution)/shard_map/ppermute | solution.py:886
  79.9 1.2 %collective-permute-done.14.refs_3_ = f32[8,128]{1,0:T(8,128)S(1)} collective-permute-done((f32[8,128]{1,0:T(8,128)S(1)}, f32[8,128]{1,0:T(8,128)S(1)}, u32[]{:S(2)}, u32[]{:S(2)}) %collective-permute-start.14) | collective-permute-done | bytes 4128 | tf_op jit(solution)/shard_map/ppermute | solution.py:886
  81.0 0.7 collective-permute-done.13.refs_2_
  81.7 0.0 collective-permute-done.12.refs_1_
  81.7 1.4 %final.1 = (f32[4,128,128]{2,1,0:T(8,128)}, f32[2,64,128]{2,1,0:T(8,128)}, f32[2,64,128]{2,1,0:T(8,128)}, f32[2,64,128]{2,1,0:T(8,128)}, f32[1,128]{1,0:T(1,128)...) custom-call(s32[1]{0:T(128)} %bitcast.rank_ref, ...), custom_call_target="tpu_custom_call" | custom-call | flops 2000000000 | bytes 6000000 | tf_op jit(solution)/shard_map/final/pallas_call | solution.py:827
  (6 shorter events, 0.0 us)
Async XLA Ops:
  2.7 14.8 %all-to-all-start = ((bf16[8,80,128]{2,1,0:T(8,128)(2,1)}), bf16[8,80,128]{2,1,0:T(8,128)(2,1)S(1)}, u32[]{:S(2)}, u32[]{:S(2)}) async-start(bf16[8,80,128]{2,1,0:T(8,128)(2,1)} %get-tuple-element.55), calls=%async_computation | async-start | bytes 327680 | tf_op jit(solution)/shard_map/all_to_all | solution.py:883
  10.0 0.7 copy-start.7
  10.0 0.7 copy-start.8
  10.7 1.5 %copy-start.9 = (s32[4,1]{0,1:T(1,128)S(1)}, s32[4,1]{0,1:T(1,128)}, u32[]{:S(2)}) copy-start(s32[4,1]{0,1:T(1,128)} %param.16) | copy-start | bytes 52
  12.1 0.7 copy-start.4
  12.1 0.7 copy-start.5
  12.1 0.7 copy-start.6
  17.6 3.6 %collective-permute-start.2 = (bf16[8,16,128]{2,1,0:T(8,128)(2,1)S(1)}, bf16[8,16,128]{2,1,0:T(8,128)(2,1)S(1)}, u32[]{:S(2)}, u32[]{:S(2)}) collective-permute-start(bf16[8,16,128]{2,1,0:T(8,128)(2,1)S(1)} %slice.3), channel_id=1, source_target_pairs={{0,3},{1,2},{2,1},{3,0},{4,7},{5,6},{6,5},{7,4},{8,11},{9,10},{10,... | collective-permute-start | bytes 98312 | tf_op jit(solution)/shard_map/ppermute | solution.py:886
  17.9 4.0 %collective-permute-start.1 = (bf16[8,16,128]{2,1,0:T(8,128)(2,1)S(1)}, bf16[8,16,128]{2,1,0:T(8,128)(2,1)S(1)}, u32[]{:S(2)}, u32[]{:S(2)}) collective-permute-start(bf16[8,16,128]{2,1,0:T(8,128)(2,1)S(1)} %slice.3), channel_id=1, source_target_pairs={{0,2},{1,3},{2,0},{3,1},{4,6},{5,7},{6,4},{7,5},{8,10},{9,11},{10,... | collective-permute-start | bytes 98312 | tf_op jit(solution)/shard_map/ppermute | solution.py:886
  19.1 2.8 %collective-permute-start = (bf16[8,16,128]{2,1,0:T(8,128)(2,1)S(1)}, bf16[8,16,128]{2,1,0:T(8,128)(2,1)S(1)}, u32[]{:S(2)}, u32[]{:S(2)}) collective-permute-start(bf16[8,16,128]{2,1,0:T(8,128)(2,1)S(1)} %slice.3), channel_id=1, source_target_pairs={{0,1},{1,0},{2,3},{3,2},{4,5},{5,4},{6,7},{7,6},{8,9},{9,8},{10,11... | collective-permute-start | bytes 98312 | tf_op jit(solution)/shard_map/ppermute | solution.py:886
  19.4 20.0 %collective-permute-start.3 = (bf16[1168,128]{1,0:T(8,128)(2,1)S(1)}, bf16[1168,128]{1,0:T(8,128)(2,1)S(1)}, u32[]{:S(2)}, u32[]{:S(2)}) collective-permute-start(bf16[1168,128]{1,0:T(8,128)(2,1)S(1)} %get-tuple-element.72), channel_id=1, source_target_pairs={{0,1},{1,0},{2,3},{3,2},{4,5},{5,4},{6,7},{7,6},{8,9},{9,8},{10,11... | collective-permute-start | bytes 897032 | tf_op jit(solution)/shard_map/ppermute | solution.py:886
  19.6 19.8 %collective-permute-start.4 = (bf16[1168,128]{1,0:T(8,128)(2,1)S(1)}, bf16[1168,128]{1,0:T(8,128)(2,1)S(1)}, u32[]{:S(2)}, u32[]{:S(2)}) collective-permute-start(bf16[1168,128]{1,0:T(8,128)(2,1)S(1)} %get-tuple-element.73), channel_id=1, source_target_pairs={{0,2},{1,3},{2,0},{3,1},{4,6},{5,7},{6,4},{7,5},{8,10},{9,11},{10,... | collective-permute-start | bytes 897032 | tf_op jit(solution)/shard_map/ppermute | solution.py:886
  21.2 18.3 %collective-permute-start.5 = (bf16[1168,128]{1,0:T(8,128)(2,1)S(1)}, bf16[1168,128]{1,0:T(8,128)(2,1)S(1)}, u32[]{:S(2)}, u32[]{:S(2)}) collective-permute-start(bf16[1168,128]{1,0:T(8,128)(2,1)S(1)} %get-tuple-element.74), channel_id=1, source_target_pairs={{0,3},{1,2},{2,1},{3,0},{4,7},{5,6},{6,5},{7,4},{8,11},{9,10},{10,... | collective-permute-start | bytes 897032 | tf_op jit(solution)/shard_map/ppermute | solution.py:886
  26.3 13.2 %all-to-all-start.1 = ((bf16[32,16,128]{2,1,0:T(8,128)(2,1)}), bf16[32,16,128]{2,1,0:T(8,128)(2,1)S(1)}, u32[]{:S(2)}, u32[]{:S(2)}) async-start(bf16[32,16,128]{2,1,0:T(8,128)(2,1)} %bitcast.10), calls=%async_computation.1 | async-start | bytes 262144 | tf_op jit(solution)/shard_map/all_to_all | solution.py:883
  41.4 10.8 %all-to-all-start.2 = ((bf16[32,16,128]{2,1,0:T(8,128)(2,1)}), bf16[32,16,128]{2,1,0:T(8,128)(2,1)S(1)}, u32[]{:S(2)}, u32[]{:S(2)}) async-start(bf16[32,16,128]{2,1,0:T(8,128)(2,1)} %bitcast.12), calls=%async_computation.2 | async-start | bytes 262144 | tf_op jit(solution)/shard_map/all_to_all | solution.py:883
  44.5 12.1 %collective-permute-start.8 = (bf16[512,128]{1,0:T(8,128)(2,1)S(1)}, bf16[512,128]{1,0:T(8,128)(2,1)S(1)}, u32[]{:S(2)}, u32[]{:S(2)}) collective-permute-start(bf16[512,128]{1,0:T(8,128)(2,1)S(1)} %bitcast.23), channel_id=1, source_target_pairs={{0,3},{1,2},{2,1},{3,0},{4,7},{5,6},{6,5},{7,4},{8,11},{9,10},{10,... | collective-permute-start | bytes 393224 | tf_op jit(solution)/shard_map/ppermute | solution.py:886
  46.1 10.5 %collective-permute-start.7 = (bf16[512,128]{1,0:T(8,128)(2,1)S(1)}, bf16[512,128]{1,0:T(8,128)(2,1)S(1)}, u32[]{:S(2)}, u32[]{:S(2)}) collective-permute-start(bf16[512,128]{1,0:T(8,128)(2,1)S(1)} %bitcast.24), channel_id=1, source_target_pairs={{0,2},{1,3},{2,0},{3,1},{4,6},{5,7},{6,4},{7,5},{8,10},{9,11},{10,... | collective-permute-start | bytes 393224 | tf_op jit(solution)/shard_map/ppermute | solution.py:886
  46.4 10.2 %collective-permute-start.6 = (bf16[512,128]{1,0:T(8,128)(2,1)S(1)}, bf16[512,128]{1,0:T(8,128)(2,1)S(1)}, u32[]{:S(2)}, u32[]{:S(2)}) collective-permute-start(bf16[512,128]{1,0:T(8,128)(2,1)S(1)} %bitcast.25), channel_id=1, source_target_pairs={{0,1},{1,0},{2,3},{3,2},{4,5},{5,4},{6,7},{7,6},{8,9},{9,8},{10,11... | collective-permute-start | bytes 393224 | tf_op jit(solution)/shard_map/ppermute | solution.py:886
  52.2 4.4 %copy-start = (bf16[512,128]{1,0:T(8,128)(2,1)S(1)}, bf16[512,128]{1,0:T(8,128)(2,1)}, u32[]{:S(2)}) copy-start(bf16[512,128]{1,0:T(8,128)(2,1)} %wv_ref.1) | copy-start | bytes 393220
  52.2 4.4 %copy-start.1 = (bf16[512,128]{1,0:T(8,128)(2,1)S(1)}, bf16[512,128]{1,0:T(8,128)(2,1)}, u32[]{:S(2)}) copy-start(bf16[512,128]{1,0:T(8,128)(2,1)} %wg_ref.1) | copy-start | bytes 393220
  52.2 4.4 %copy-start.2 = (bf16[4,128,128]{2,1,0:T(8,128)(2,1)S(1)}, bf16[4,128,128]{2,1,0:T(8,128)(2,1)}, u32[]{:S(2)}) copy-start(bf16[4,128,128]{2,1,0:T(8,128)(2,1)} %tokens_ref.5) | copy-start | bytes 393220
  52.2 4.4 %copy-start.3 = (bf16[4,128,128]{2,1,0:T(8,128)(2,1)S(1)}, bf16[4,128,128]{2,1,0:T(8,128)(2,1)}, u32[]{:S(2)}) copy-start(bf16[4,128,128]{2,1,0:T(8,128)(2,1)} %cot_ref.3) | copy-start | bytes 393220
  59.3 18.5 %all-to-all-start.3 = ((bf16[8,256,128]{2,1,0:T(8,128)(2,1)}), bf16[8,256,128]{2,1,0:T(8,128)(2,1)S(1)}, u32[]{:S(2)}, u32[]{:S(2)}) async-start(bf16[8,256,128]{2,1,0:T(8,128)(2,1)} %get-tuple-element.83), calls=%async_computation.3 | async-start | bytes 1048576 | tf_op jit(solution)/shard_map/all_to_all | solution.py:883
  62.8 3.1 %collective-permute-start.11 = (f32[8,128]{1,0:T(8,128)S(1)}, f32[8,128]{1,0:T(8,128)S(1)}, u32[]{:S(2)}, u32[]{:S(2)}) collective-permute-start(f32[8,128]{1,0:T(8,128)S(1)} %get-tuple-element.57.refs_0_), channel_id=1, source_target_pairs={{0,3},{1,2},{2,1},{3,0},{4,7},{5,6},{6,5},{7,4},{8,11},{9,10},{10,... | collective-permute-start | bytes 12296 | tf_op jit(solution)/shard_map/ppermute | solution.py:886
  63.2 3.6 %collective-permute-start.10 = (f32[8,128]{1,0:T(8,128)S(1)}, f32[8,128]{1,0:T(8,128)S(1)}, u32[]{:S(2)}, u32[]{:S(2)}) collective-permute-start(f32[8,128]{1,0:T(8,128)S(1)} %get-tuple-element.57.refs_0_), channel_id=1, source_target_pairs={{0,2},{1,3},{2,0},{3,1},{4,6},{5,7},{6,4},{7,5},{8,10},{9,11},{10,... | collective-permute-start | bytes 12296 | tf_op jit(solution)/shard_map/ppermute | solution.py:886
  64.6 2.2 %collective-permute-start.9 = (f32[8,128]{1,0:T(8,128)S(1)}, f32[8,128]{1,0:T(8,128)S(1)}, u32[]{:S(2)}, u32[]{:S(2)}) collective-permute-start(f32[8,128]{1,0:T(8,128)S(1)} %get-tuple-element.57.refs_0_), channel_id=1, source_target_pairs={{0,1},{1,0},{2,3},{3,2},{4,5},{5,4},{6,7},{7,6},{8,9},{9,8},{10,11... | collective-permute-start | bytes 12296 | tf_op jit(solution)/shard_map/ppermute | solution.py:886
  77.9 3.1 %collective-permute-start.14 = (f32[8,128]{1,0:T(8,128)S(1)}, f32[8,128]{1,0:T(8,128)S(1)}, u32[]{:S(2)}, u32[]{:S(2)}) collective-permute-start(f32[8,128]{1,0:T(8,128)S(1)} %get-tuple-element.86.refs_0_), channel_id=1, source_target_pairs={{0,3},{1,2},{2,1},{3,0},{4,7},{5,6},{6,5},{7,4},{8,11},{9,10},{10,... | collective-permute-start | bytes 12296 | tf_op jit(solution)/shard_map/ppermute | solution.py:886
  78.0 3.7 %collective-permute-start.13 = (f32[8,128]{1,0:T(8,128)S(1)}, f32[8,128]{1,0:T(8,128)S(1)}, u32[]{:S(2)}, u32[]{:S(2)}) collective-permute-start(f32[8,128]{1,0:T(8,128)S(1)} %get-tuple-element.86.refs_0_), channel_id=1, source_target_pairs={{0,2},{1,3},{2,0},{3,1},{4,6},{5,7},{6,4},{7,5},{8,10},{9,11},{10,... | collective-permute-start | bytes 12296 | tf_op jit(solution)/shard_map/ppermute | solution.py:886
  78.7 3.0 %collective-permute-start.12 = (f32[8,128]{1,0:T(8,128)S(1)}, f32[8,128]{1,0:T(8,128)S(1)}, u32[]{:S(2)}, u32[]{:S(2)}) collective-permute-start(f32[8,128]{1,0:T(8,128)S(1)} %get-tuple-element.86.refs_0_), channel_id=1, source_target_pairs={{0,1},{1,0},{2,3},{3,2},{4,5},{5,4},{6,7},{7,6},{8,9},{9,8},{10,11... | collective-permute-start | bytes 12296 | tf_op jit(solution)/shard_map/ppermute | solution.py:886

commit v4 on v3

--- a/solution.py
+++ b/solution.py
@@ -426,7 +426,6 @@
     power_hbm,
     kept_hbm,
     send_ref,
-    sums_ref,
     sums_keep,
     head,
     x_keep,
@@ -596,10 +595,13 @@
         axis=0,
     )
     sums = jnp.sum(sums_keep[...].T, axis=0, keepdims=True)
-    sums_ref[:, pl.ds(0, 3 * chans)] = jnp.broadcast_to(sums, (8, 3 * chans))
+    sums_hi = sums.astype(bf16).astype(f32)
     cut = micros * chans
     for k in range(chunks):
-        head[pl.ds(k * stride + cut, 3 * chans), :] = modes
+        at = k * stride + cut
+        head[pl.ds(at, 3 * chans), :] = modes
+        head[pl.ds(at + 3 * chans, 1), pl.ds(0, 3 * chans)] = sums_hi
+        head[pl.ds(at + 3 * chans + 1, 1), pl.ds(0, 3 * chans)] = sums - sums_hi
         send_ref[k] = head[pl.ds(k * stride, stride), :].astype(bf16)
 
 
@@ -679,11 +681,8 @@
 ):
     micros, wide, width = tokens_ref.shape
     acts_in, refs = refs[:micros], refs[micros:]
-    sums_ref, head_ref, out_ref, send_hbm, d_keep, grad, sems = refs
+    out_ref, keep_ref, send_ref, d_keep, grad = refs
     full = wv_ref.shape[0]
-    stride = head_ref.shape[1]
-    head = pltpu.make_async_copy(head_ref, send_hbm.at[:, pl.ds(0, stride), :], sems.at[0])
-    head.start()
     at = rank_ref[0] * width + lax.broadcasted_iota(jnp.int32, (width, wide), 0)
     place = rank_ref[0] * width + lanes((1, width))
     weights = jnp.concatenate([wv_ref[...], wg_ref[...]], axis=1)
@@ -697,30 +696,36 @@
         d_keep[k * width : (k + 1) * width] = d_both
     d_both = d_keep[...]
     acts = jnp.concatenate([ref[...] for ref in acts_in], axis=1)
-    grad_w = mm(acts, d_both).astype(bf16)
+    grad_w = mm(acts, d_both)
     grad_b = mm(jnp.ones((8, micros * width), bf16), d_both)
+    row = lax.broadcasted_iota(jnp.int32, (8, wide), 0)
+    small = jnp.where(row == 0, grad_b[:, :wide], grad_b[:, wide:])
     count = full // seqs
     for k in range(seqs):
         part = grad_w[k * count : (k + 1) * count]
-        grad[k, pl.ds(16, count), pl.ds(0, wide)] = part[:, :wide]
-        grad[k, pl.ds(16 + count, count), pl.ds(0, wide)] = part[:, wide:]
-    rows = [grad_b[0:1, :wide], grad_b[0:1, wide:]]
-    if wide < width:
-        blank = jnp.zeros((1, width - wide), f32)
-        rows = [jnp.concatenate([row, blank], axis=1) for row in rows]
-    small = []
-    for row in [sums_ref[0:1]] + rows:
-        high = row.astype(bf16).astype(f32)
-        small += [high, row - high]
-    small = jnp.concatenate(small + [jnp.zeros((10, width), f32)], axis=0).astype(bf16)
-    for k in range(seqs):
-        grad[k, pl.ds(0, 16), :] = small
-    tail = pltpu.make_async_copy(
-        grad, send_hbm.at[:, pl.ds(stride, 16 + 2 * count), :], sems.at[1]
-    )
-    tail.start()
-    tail.wait()
-    head.wait()
+        grad[k, pl.ds(0, count), :] = part[:, :wide]
+        grad[k, pl.ds(count, count), :] = part[:, wide:]
+        grad[k, pl.ds(2 * count, 8), :] = small
+    bit = rank_ref[0] & 1
+    for k in range(seqs // 2):
+        keep_ref[k] = grad[2 * k + bit]
+        send_ref[k] = grad[2 * k + 1 - bit].astype(bf16)
+
+
+def halve_kernel(bit_ref, left_ref, right_ref, keep_ref, send_ref, total):
+    total[...] = left_ref[...] + right_ref[...].astype(f32)
+    for k in range(keep_ref.shape[0]):
+        keep_ref[k] = total[2 * k + bit_ref[0]]
+        send_ref[k] = total[2 * k + 1 - bit_ref[0]].astype(bf16)
+
+
+def last_kernel(left_ref, right_ref, wv_ref, wg_ref, bv_ref, bg_ref):
+    count = wv_ref.shape[0]
+    total = left_ref[0] + right_ref[0].astype(f32)
+    wv_ref[...] = total[:count]
+    wg_ref[...] = total[count : 2 * count]
+    bv_ref[...] = total[2 * count : 2 * count + 1]
+    bg_ref[...] = total[2 * count + 1 : 2 * count + 2]
 
 
 def normal(tokens_ref, norm_ref, m):
@@ -756,16 +761,14 @@
 def final_kernel(
     rank_ref,
     lens_ref,
-    got_ref,
     head_ref,
     tokens_ref,
     cot_ref,
     norm_ref,
     *refs,
 ):
-    hat_refs, refs = refs[:-11], refs[-11:]
-    d_in_ref, b_ref, e_ref, c_ref, skip_ref, gain_ref, norm_bias_ref = refs[:7]
-    wv_ref, wg_ref, bv_ref, bg_ref = refs[7:]
+    hat_refs, refs = refs[:-7], refs[-7:]
+    d_in_ref, b_ref, e_ref, c_ref, skip_ref, gain_ref, norm_bias_ref = refs
     micros, wide, width = tokens_ref.shape
     seqs, stride, _ = head_ref.shape
     peers = len(hat_refs)
@@ -786,23 +789,13 @@
         modes = head_ref[:, pl.ds(cut + k * chans, chans), :]
         ref[...] = modes.reshape(wide, -1).T.reshape(ref.shape)
     place = lanes((1, wide)) // chans
-    last = stride - 16
+    last = cut + 3 * chans
     for k, ref in enumerate((skip_ref, gain_ref, norm_bias_ref)):
         line = jnp.zeros((1, wide), f32)
         for s in range(seqs):
             own = head_ref[s, pl.ds(last, 1), :] + head_ref[s, pl.ds(last + 1, 1), :]
             own = pltpu.roll(own, (s - k) * chans % own.shape[1], axis=1)[:, :wide]
             line = jnp.where(place == s, own, line)
-        ref[...] = line
-    count = wv_ref.shape[0]
-    for k, ref in enumerate((wv_ref, wg_ref)):
-        parts = got_ref[:, pl.ds(stride + k * count, count), pl.ds(0, wide)]
-        ref[...] = jnp.sum(parts.astype(f32), axis=0)
-    for k, ref in enumerate((bv_ref, bg_ref)):
-        line = jnp.zeros((1, wide), f32)
-        for s in range(seqs):
-            line = line + head_ref[s, pl.ds(last + 2 + 2 * k, 1), pl.ds(0, wide)]
-            line = line + head_ref[s, pl.ds(last + 3 + 2 * k, 1), pl.ds(0, wide)]
         ref[...] = line
 
 
@@ -981,7 +974,6 @@
         scratch_shapes=[pltpu.VMEM((own, 2 * full), bf16)],
     )
 
-    act, d_act = lax.optimization_barrier((act, d_act))
     acts = [act] + [cross(act, k) for k in range(1, peers)]
     if parts == 1:
         order = chan_rank ^ jnp.arange(peers, dtype=jnp.int32)
@@ -999,36 +991,59 @@
         .reshape(rows * chans, width)
     )
     count = full // seqs
-    stride = -(-(micros + 3) * chans // 16) * 16
-    head = shape_of((seqs, stride, width), bf16)
+    part = (seqs // 2, 2 * count + 8, wide)
+    out, keep, send = kernel_call(
+        functools.partial(output_kernel, seqs),
+        "output",
+        (rank, lens, order),
+        (tokens, out_cotangent, w_value, w_gate) + bias_rows + tuple(acts),
+        [shape_of(tokens.shape, bf16), shape_of(part), shape_of(part, bf16)],
+        2,
+        limit=12,
+        scratch_shapes=[
+            pltpu.VMEM((micros * width, 2 * wide), bf16),
+            pltpu.VMEM((seqs,) + part[1:], f32),
+        ],
+    )
+    got = lax.ppermute(send, "seq", [(i, i ^ 1) for i in range(seqs)])
+    d_act, keep = lax.optimization_barrier((d_act, keep))
+    stride = -(-((micros + 3) * chans + 2) // 16) * 16
     arrays = (x_mine, d_act, norm_mine, const, taps, live, y_mine, in_hbm(power), in_hbm(kept))
-    head, sums = pl.pallas_call(
+    d_hat = pl.pallas_call(
         functools.partial(backward_kernel, micros, seqs, chans),
         in_specs=[vmem()] * (len(arrays) - 2) + [hbm] * 2,
-        out_specs=[vmem()] * 2,
-        out_shape=[head, shape_of((8, width))],
+        out_specs=vmem(),
+        out_shape=shape_of((seqs, stride, width), bf16),
         scratch_shapes=backward_scratch(micros, seqs, chans, stride, width, lane),
         compiler_params=pltpu.CompilerParams(vmem_limit_bytes=20 * 1024 * 1024),
         cost_estimate=cost(5),
         name="mixer_backward",
     )(*arrays)
-    arrays = (tokens, out_cotangent, w_value, w_gate) + bias_rows + tuple(acts) + (sums, head)
-    send_shape = (seqs, stride + 16 + 2 * count, width)
-    out, d_hat = pl.pallas_call(
-        functools.partial(output_kernel, seqs),
-        in_specs=[smem()] * 3 + [vmem()] * len(arrays),
-        out_specs=[vmem(), hbm],
-        out_shape=[shape_of(tokens.shape, bf16), pltpu.HBM(send_shape, bf16)],
-        scratch_shapes=[
-            pltpu.VMEM((micros * width, 2 * wide), bf16),
-            pltpu.VMEM((seqs, 16 + 2 * count, width), bf16),
-            pltpu.SemaphoreType.DMA((2,)),
-        ],
-        compiler_params=pltpu.CompilerParams(vmem_limit_bytes=12 * 1024 * 1024),
-        cost_estimate=cost(2),
-        name="output",
-    )(rank, lens, order, *arrays)
-    stride += 16
+    d_hat, got = lax.optimization_barrier((d_hat, got))
+    for level in range(spans):
+        by = 1 << level
+        if level:
+            got = lax.ppermute(send, "seq", [(i, i ^ by) for i in range(seqs)])
+        if level == spans - 1:
+            break
+        half_part = (seqs >> (level + 2),) + part[1:]
+        keep, send = kernel_call(
+            halve_kernel,
+            "halve",
+            ((seq_rank.reshape(1) >> (level + 1)) & 1,),
+            (keep, got),
+            [shape_of(half_part), shape_of(half_part, bf16)],
+            1,
+            scratch_shapes=[pltpu.VMEM(keep.shape, f32)],
+        )
+    d_wv, d_wg, d_bv, d_bg = kernel_call(
+        last_kernel,
+        "last",
+        (),
+        (keep, got),
+        [shape_of((count, wide))] * 2 + [shape_of((1, wide))] * 2,
+        1,
+    )
     got = exchange(d_hat, "seq")
     own_sums, head, norm = kernel_call(
         sums_kernel,
@@ -1044,16 +1059,14 @@
     )
     hat_sums = [own_sums] + [cross(own_sums, k) for k in range(1, peers)]
     mode_grad = shape_of((2, modes, wide))
-    d_input, d_b, d_e, d_c, d_skip, d_gain, d_bias, d_wv, d_wg, d_bv, d_bg = kernel_call(
+    d_input, d_b, d_e, d_c, d_skip, d_gain, d_bias = kernel_call(
         final_kernel,
         "final",
         (rank, lens),
-        (got, head, tokens, out_cotangent, norm, *hat_sums),
+        (head, tokens, out_cotangent, norm, *hat_sums),
         [shape_of(tokens.shape)]
         + [mode_grad] * 3
-        + [shape_of((1, wide))] * 3
-        + [shape_of((count, wide))] * 2
-        + [shape_of((1, wide))] * 2,
+        + [shape_of((1, wide))] * 3,
         2,
     )
     d_b, d_e, d_c = [jnp.transpose(z, (0, 2, 1)) for z in (d_b, d_e, d_c)]

time: 83.8 us -> 79.7 us (0.951)
  waiting for transfers between devices: 29.5 us -> 18.6 us
  starting transfers between devices: 28.6 us -> 34.7 us
    all_to_all x4, waiting for transfers between devices: 24.7 us -> 11 us  [exchange(): return lax.all_to_all(x, axis, 0, 0, tiled=True)]
    ppermute x0 -> x3, starting transfers between devices: none -> 6.41 us  [the longest x2 5.19 us: shards(): got = lax.ppermute(send, 'seq', [(i, i ^ by) for i in range(seqs)])]
    ppermute x0 -> x3, waiting for transfers between devices: none -> 3.87 us  [the longest x2 3.86 us: shards(): got = lax.ppermute(send, 'seq', [(i, i ^ by) for i in range(seqs)])]
    pallas_call x1 -> x0, Pallas kernels: 2.59 us -> none  [shards(): pl.pallas_call(functools.partial(output_kernel, seqs), in_specs=[smem()]...]
    pallas_call x3 -> x7, Pallas kernels: 3.6 us -> 6.15 us  [kernel_call(): pl.pallas_call(kernel, in_specs=ins, out_specs=[vmem()] * len(outs), out_...]
    ppermute x15, waiting for transfers between devices: 4.78 us -> 3.79 us  [cross(): return lax.ppermute(x, 'chan', [(i, i ^ by) for i in range(peers)])]
  transfers between devices with their start and end apart: 19 -> 22, of which waited for: 10 -> 9; matrix products, arithmetic and copies ran while one was open for 0% -> 0% of each run, Pallas kernels for 17% -> 25%
where the time goes in v4:
time: 79.7 us; the launch traced here: 79.1 us
  starting transfers between devices  34.7 us (44%)
  Pallas kernels  23.5 us (29%)
  waiting for transfers between devices  18.6 us (23%)
  local copies, waits for them, and re-layouts  1.34 us (2%)
  between operations  0.87 us (1%)
    all_to_all x4, starting transfers between devices, exchange(): return lax.all_to_all(x, axis, 0, 0, tiled=True)  19.1 us
    all_to_all x4, waiting for transfers between devices, exchange(): return lax.all_to_all(x, axis, 0, 0, tiled=True)  11 us
    ppermute x15, starting transfers between devices, cross(): return lax.ppermute(x, 'chan', [(i, i ^ by) for i in range(peers)])  9.16 us
    pallas_call x7, Pallas kernels, kernel_call(): pl.pallas_call(kernel, in_specs=ins, out_specs=[vmem()] * len(outs), out_...  6.15 us
    ppermute x2, starting transfers between devices, shards(): got = lax.ppermute(send, 'seq', [(i, i ^ by) for i in range(seqs)])  5.19 us
    pallas_call x1, Pallas kernels, shards(): pl.pallas_call(functools.partial(backward_kernel, micros, seqs, chans), i...  5.12 us
    pallas_call x1, Pallas kernels, shards(): pl.pallas_call(functools.partial(table_kernel, chans, seqs, width), in_sp...  4.37 us
    pallas_call x1, Pallas kernels, shards(): pl.pallas_call(functools.partial(forward_kernel, micros, seqs, chans, pee...  4.34 us
  transfers between devices with their start and end apart: 22, of which 9 were waited for; matrix products, arithmetic and copies ran while one was open for 0% of the time, Pallas kernels for 25%

profile of v4, /device:TPU:0, one launch (start us, length us, event | category | flops | bytes accessed | tf_op | source)
XLA Modules:
  0.0 79.1 jit_solution(15417446434560926489)
XLA Ops:
  0.6 2.1 %pack.1 = (bf16[8,80,128]{2,1,0:T(8,128)(2,1)}, f32[8,128]{1,0:T(8,128)S(1)}) custom-call(bf16[4,128,128]{2,1,0:T(8,128)(2,1)} %tokens_ref.5), custom_call_target="tpu_custom_call" | custom-call | flops 1000000000 | bytes 3000000 | tf_op jit(solution)/shard_map/pack/pallas_call | solution.py:882
  2.7 7.3 %all-to-all-start = ((bf16[8,80,128]{2,1,0:T(8,128)(2,1)}), bf16[8,80,128]{2,1,0:T(8,128)(2,1)S(1)}, u32[]{:S(2)}, u32[]{:S(2)}) async-start(bf16[8,80,128]{2,1,0:T(8,128)(2,1)} %get-tuple-element.60), calls=%async_computation | async-start | bytes 327680 | tf_op jit(solution)/shard_map/all_to_all | solution.py:876
  10.0 0.0 copy-start.8
  10.0 0.6 copy-done.7
  10.6 0.0 copy-done.8
  10.7 1.5 %weights.1 = (bf16[1168,128]{1,0:T(8,128)(2,1)S(1)}, bf16[1168,128]{1,0:T(8,128)(2,1)S(1)}, bf16[1168,128]{1,0:T(8,128)(2,1)S(1)}, bf16[1168,128]{1,0:T(8,128)(2,1)S(1)}) custom-call(s32[1]{0:T(128)} %bitcast.9.rank_ref, f32[1,128]{1,0:T(1,128)S(1)} %bitcast.28, f32[1,128]{1,0:T(1,128)S(1)} %bitcast.30, bf16[4,128,128]{2,1,0:T(8,128)(2,1)} %cot_ref.3, ...), custom_call_target="tpu_custom_call" | custom-call | flops 1000000000 | bytes 3000000 | tf_op jit(solution)/shard_map/weights/pallas_call | solution.py:903
  12.1 0.0 copy-start.4
  12.1 0.0 copy-start.5
  12.1 0.0 copy-start.6
  12.2 0.6 copy-done.4
  12.8 0.0 copy-done.5
  12.8 0.0 copy-done.6
  12.8 4.4 %tables.1 = (f32[18,16,128]{2,1,0:T(8,128)S(1)}, bf16[16,256,128]{2,1,0:T(8,128)(2,1)}, f32[16,16,128]{2,1,0:T(8,128)S(1)}, f32[32,128]{1,0:T(8,128)S(1)}) custom-call(s32[1]{0:T(128)} %bitcast.rank_ref, s32[4]{0:T(128)S(1)} %bitcast.32, f32[128]{0:T(128)S(1)} %copy-done.4, f32[128]{0:T(128)S(1)} %copy-done.5, f32[128]{0:T(128)S(1)} %copy-done.6, ...), custom_call_target="tpu_custom_call" | custom-call | flops 2000000000 | bytes 6000000 | tf_op jit(solution)/shard_map/tables/pallas_call | solution.py:915
  17.2 0.4 all-to-all-done.got_ref
  17.6 0.4 collective-permute-start.2
  18.0 1.2 %collective-permute-start.1 = (bf16[8,16,128]{2,1,0:T(8,128)(2,1)S(1)}, bf16[8,16,128]{2,1,0:T(8,128)(2,1)S(1)}, u32[]{:S(2)}, u32[]{:S(2)}) collective-permute-start(bf16[8,16,128]{2,1,0:T(8,128)(2,1)S(1)} %slice.3), channel_id=1, source_target_pairs={{0,2},{1,3},{2,0},{3,1},{4,6},{5,7},{6,4},{7,5},{8,10},{9,11},{10,... | collective-permute-start | bytes 98312 | tf_op jit(solution)/shard_map/ppermute | solution.py:879
  19.1 0.3 collective-permute-start
  19.4 0.2 collective-permute-start.6
  19.6 1.3 %collective-permute-start.7 = (bf16[1168,128]{1,0:T(8,128)(2,1)S(1)}, bf16[1168,128]{1,0:T(8,128)(2,1)S(1)}, u32[]{:S(2)}, u32[]{:S(2)}) collective-permute-start(bf16[1168,128]{1,0:T(8,128)(2,1)S(1)} %get-tuple-element.79), channel_id=1, source_target_pairs={{0,2},{1,3},{2,0},{3,1},{4,6},{5,7},{6,4},{7,5},{8,10},{9,11},{10,... | collective-permute-start | bytes 897032 | tf_op jit(solution)/shard_map/ppermute | solution.py:879
  20.9 0.2 collective-permute-done.2.refs_2_
  21.2 0.1 collective-permute-start.8
  21.3 0.7 collective-permute-done.1.refs_1_
  22.0 0.0 collective-permute-done.refs_0_
  22.0 4.3 %mixer_forward.1 = (bf16[512,128]{1,0:T(8,128)(2,1)}, f32[64,128]{1,0:T(8,128)S(1)}, f32[16,32,128]{2,1,0:T(8,128)S(1)}, f32[16,96,128]{2,1,0:T(8,128)}) custom-call(bf16[8,80,128]{2,1,0:T(8,128)(2,1)S(1)} %all-to-all-done.got_ref, f32[18,16,128]{2,1,0:T(8,128)S(1)} %get-tuple-element.71.const_ref, f32[16,16,128]{2,1,0:T(8,128)S(1)} %get-tuple-element.72.taps_ref, ...), custom_call_target="tpu_custom_call" | custom-call | flops 5000000000 | bytes 15000000 | tf_op jit(solution)/shard_map/mixer_forward/pallas_call | solution.py:944
  26.3 5.4 %all-to-all-start.1 = ((bf16[32,16,128]{2,1,0:T(8,128)(2,1)}), bf16[32,16,128]{2,1,0:T(8,128)(2,1)S(1)}, u32[]{:S(2)}, u32[]{:S(2)}) async-start(bf16[32,16,128]{2,1,0:T(8,128)(2,1)} %bitcast.10), calls=%async_computation.1 | async-start | bytes 262144 | tf_op jit(solution)/shard_map/all_to_all | solution.py:876
  31.7 0.1 pad_add_fusion.place_ref
  31.8 7.7 %all-to-all-done.1 = bf16[32,16,128]{2,1,0:T(8,128)(2,1)S(1)} async-done(((bf16[32,16,128]{2,1,0:T(8,128)(2,1)}), bf16[32,16,128]{2,1,0:T(8,128)(2,1)S(1)}, u32[]{:S(2)}, u32[]{:S(2)}) %all-to-all-start.1) | async-done | bytes 131104 | tf_op jit(solution)/shard_map/all_to_all | solution.py:876
  39.5 0.4 collective-permute-start.5
  39.8 1.4 %collective-permute-start.4 = (bf16[512,128]{1,0:T(8,128)(2,1)S(1)}, bf16[512,128]{1,0:T(8,128)(2,1)S(1)}, u32[]{:S(2)}, u32[]{:S(2)}) collective-permute-start(bf16[512,128]{1,0:T(8,128)(2,1)S(1)} %bitcast.23), channel_id=1, source_target_pairs={{0,2},{1,3},{2,0},{3,1},{4,6},{5,7},{6,4},{7,5},{8,10},{9,11},{10,... | collective-permute-start | bytes 393224 | tf_op jit(solution)/shard_map/ppermute | solution.py:879
  41.2 0.0 collective-permute-done.6.refs_1_
  41.2 0.1 collective-permute-start.3
  41.4 0.0 collective-permute-done.7.refs_2_
  41.4 0.0 collective-permute-done.8.refs_3_
  41.4 0.0 copy-start.3
  41.4 2.0 %project.1 = bf16[512,128]{1,0:T(8,128)(2,1)} custom-call(s32[2]{0:T(128)S(1)} %pad_add_fusion.place_ref, s32[4]{0:T(128)S(1)} %bitcast.33, bf16[512,128]{1,0:T(8,128)(2,1)S(1)} %bitcast.25, bf16[1168,128]{1,0:T(8,128)(2,1)S(1)} %get-tuple-element.77.refs_0_, bf16[1168,128]{1,0:T(8,128)(2,1)S(1)} %collective-permute-done.6.refs_1_, ...), custom_call_target="tpu_custom_call" | custom-call | flops 2000000000 | bytes 6000000 | tf_op jit(solution)/shard_map/project/pallas_call | solution.py:820
  43.4 3.0 %all-to-all-start.2 = ((bf16[32,16,128]{2,1,0:T(8,128)(2,1)}), bf16[32,16,128]{2,1,0:T(8,128)(2,1)S(1)}, u32[]{:S(2)}, u32[]{:S(2)}) async-start(bf16[32,16,128]{2,1,0:T(8,128)(2,1)} %bitcast.12), calls=%async_computation.2 | async-start | bytes 262144 | tf_op jit(solution)/shard_map/all_to_all | solution.py:876
  46.4 0.0 collective-permute-done.5.refs_3_
  46.4 1.7 %collective-permute-done.4.refs_2_ = bf16[512,128]{1,0:T(8,128)(2,1)S(1)} collective-permute-done((bf16[512,128]{1,0:T(8,128)(2,1)S(1)}, bf16[512,128]{1,0:T(8,128)(2,1)S(1)}, u32[]{:S(2)}, u32[]{:S(2)}) %collective-permute-start.4) | collective-permute-done | bytes 131104 | tf_op jit(solution)/shard_map/ppermute | solution.py:879
  48.1 0.0 collective-permute-done.3.refs_1_
  48.1 1.9 %output.1 = (bf16[4,128,128]{2,1,0:T(8,128)(2,1)}, f32[4,136,128]{2,1,0:T(8,128)S(1)}, bf16[4,136,128]{2,1,0:T(8,128)(2,1)S(1)}) custom-call(s32[1]{0:T(128)} %bitcast.rank_ref, s32[4]{0:T(128)S(1)} %bitcast.34, s32[4]{0:T(128)S(1)} %iota_xor_fusion.order_ref, bf16[4,128,128]{2,1,0:T(8,128)(2,1)S(1)} %copy-done.2, bf16[4,128,128]{2,1,0:T(8,128)(2,1)S(1)} %copy-done.3, ...), custom_call_target="tpu_custom_call" | custom-call | flops 2000000000 | bytes 6000000 | tf_op jit(solution)/shard_map/output/pallas_call | solution.py:820
  50.0 1.2 %collective-permute-start.9 = (bf16[4,136,128]{2,1,0:T(8,128)(2,1)S(1)}, bf16[4,136,128]{2,1,0:T(8,128)(2,1)S(1)}, u32[]{:S(2)}, u32[]{:S(2)}) collective-permute-start(bf16[4,136,128]{2,1,0:T(8,128)(2,1)S(1)} %get-tuple-element.86), channel_id=1, source_target_pairs={{0,4},{4,0},{8,12},{12,8},{16,20},{20,16},{24,28},{28,24},{1,5},{5... | collective-permute-start | bytes 417800 | tf_op jit(solution)/shard_map/ppermute | solution.py:1008
  51.2 2.9 %all-to-all-done.2 = bf16[32,16,128]{2,1,0:T(8,128)(2,1)S(1)} async-done(((bf16[32,16,128]{2,1,0:T(8,128)(2,1)}), bf16[32,16,128]{2,1,0:T(8,128)(2,1)S(1)}, u32[]{:S(2)}, u32[]{:S(2)}) %all-to-all-start.2) | async-done | bytes 131104 | tf_op jit(solution)/shard_map/all_to_all | solution.py:876
  54.1 5.1 %mixer_backward.1 = bf16[8,128,128]{2,1,0:T(8,128)(2,1)} custom-call(bf16[8,80,128]{2,1,0:T(8,128)(2,1)S(1)} %all-to-all-done.got_ref, bf16[512,128]{1,0:T(8,128)(2,1)S(1)} %bitcast.27, f32[64,128]{1,0:T(8,128)S(1)} %get-tuple-element.83.norm_ref, f32[18,16,128]{2,1,0:T(8,128)S(1)} %get-tuple-element.71.const_ref, ...), custom_call_target="tpu_custom_call" | custom-call | flops 5000000000 | bytes 15000000 | tf_op jit(solution)/shard_map/mixer_backward/pallas_call | solution.py:1012
  59.2 0.0 collective-permute-done.9.right_ref
  59.3 3.4 %all-to-all-start.3 = ((bf16[8,128,128]{2,1,0:T(8,128)(2,1)}), bf16[8,128,128]{2,1,0:T(8,128)(2,1)S(1)}, u32[]{:S(2)}, u32[]{:S(2)}) async-start(bf16[8,128,128]{2,1,0:T(8,128)(2,1)} %mixer_backward.1), calls=%async_computation.3 | async-start | bytes 524288 | tf_op jit(solution)/shard_map/all_to_all | solution.py:876
  62.8 2.0 %collective-permute-start.16 = (bf16[2,136,128]{2,1,0:T(8,128)(2,1)S(1)}, bf16[2,136,128]{2,1,0:T(8,128)(2,1)S(1)}, u32[]{:S(2)}, u32[]{:S(2)}) collective-permute-start(bf16[2,136,128]{2,1,0:T(8,128)(2,1)S(1)} %get-tuple-element.101), channel_id=1, source_target_pairs={{0,8},{4,12},{8,0},{12,4},{16,24},{20,28},{24,16},{28,20},{1,9},{5... | collective-permute-start | bytes 208904 | tf_op jit(solution)/shard_map/ppermute | solution.py:1026
  64.7 0.0 collective-permute-start.12
  64.7 1.2 %collective-permute-start.11 = (f32[8,128]{1,0:T(8,128)S(1)}, f32[8,128]{1,0:T(8,128)S(1)}, u32[]{:S(2)}, u32[]{:S(2)}) collective-permute-start(f32[8,128]{1,0:T(8,128)S(1)} %get-tuple-element.62.refs_0_), channel_id=1, source_target_pairs={{0,2},{1,3},{2,0},{3,1},{4,6},{5,7},{6,4},{7,5},{8,10},{9,11},{10,... | collective-permute-start | bytes 12296 | tf_op jit(solution)/shard_map/ppermute | solution.py:879
  65.9 0.7 collective-permute-start.10
  66.6 3.9 %collective-permute-done.16.right_ref = bf16[2,136,128]{2,1,0:T(8,128)(2,1)S(1)} collective-permute-done((bf16[2,136,128]{2,1,0:T(8,128)(2,1)S(1)}, bf16[2,136,128]{2,1,0:T(8,128)(2,1)S(1)}, u32[]{:S(2)}, u32[]{:S(2)}) %collective-permute-start.16) | collective-permute-done | bytes 69664 | tf_op jit(solution)/shard_map/ppermute | solution.py:1026
  70.5 3.2 %collective-permute-start.17 = (bf16[1,136,128]{2,1,0:T(8,128)(2,1)S(1)}, bf16[1,136,128]{2,1,0:T(8,128)(2,1)S(1)}, u32[]{:S(2)}, u32[]{:S(2)}) collective-permute-start(bf16[1,136,128]{2,1,0:T(8,128)(2,1)S(1)} %get-tuple-element.103), channel_id=1, source_target_pairs={{0,16},{4,20},{8,24},{12,28},{16,0},{20,4},{24,8},{28,12},{1,17},{... | collective-permute-start | bytes 104456 | tf_op jit(solution)/shard_map/ppermute | solution.py:1026
  73.7 0.0 collective-permute-done.12.refs_3_
  73.7 0.0 collective-permute-done.11.refs_2_
  73.7 0.0 collective-permute-done.10.refs_1_
  73.7 0.0 all-to-all-done.3.got_ref
  73.7 0.2 sums.1
  73.9 0.1 collective-permute-start.15
  74.0 0.7 collective-permute-start.14
  74.7 1.1 %collective-permute-start.13 = (f32[8,128]{1,0:T(8,128)S(1)}, f32[8,128]{1,0:T(8,128)S(1)}, u32[]{:S(2)}, u32[]{:S(2)}) collective-permute-start(f32[8,128]{1,0:T(8,128)S(1)} %get-tuple-element.90.refs_0_), channel_id=1, source_target_pairs={{0,1},{1,0},{2,3},{3,2},{4,5},{5,4},{6,7},{7,6},{8,9},{9,8},{10,11... | collective-permute-start | bytes 12296 | tf_op jit(solution)/shard_map/ppermute | solution.py:879
  75.9 0.6 last.1
  76.5 0.5 collective-permute-done.15.refs_3_
  77.0 0.7 collective-permute-done.14.refs_2_
  77.7 0.0 collective-permute-done.13.refs_1_
  77.7 1.4 %final.1 = (f32[4,128,128]{2,1,0:T(8,128)}, f32[2,64,128]{2,1,0:T(8,128)}, f32[2,64,128]{2,1,0:T(8,128)}, f32[2,64,128]{2,1,0:T(8,128)}, f32[1,128]{1,0:T(1,128)}, /*index=5*/f32[1,128]{1,0:T(1,128)}, f32[1,128]{1,0:T(1,128)}) custom-call(s32[1]{0:T(128)} %bitcast.rank_ref, s32[4]{0:T(128)S(1)} %bitcast.35, f32[8,128,128]{2,1,0:T(8,128)S(1)} %get-tuple-element.88.head_ref, ...), custom_call_target="tpu_custom_call" | custom-call | flops 2000000000 | bytes 6000000 | tf_op jit(solution)/shard_map/final/pallas_call | solution.py:820
  (15 shorter events, 0.1 us)
Async XLA Ops:
  2.7 14.8 %all-to-all-start = ((bf16[8,80,128]{2,1,0:T(8,128)(2,1)}), bf16[8,80,128]{2,1,0:T(8,128)(2,1)S(1)}, u32[]{:S(2)}, u32[]{:S(2)}) async-start(bf16[8,80,128]{2,1,0:T(8,128)(2,1)} %get-tuple-element.60), calls=%async_computation | async-start | bytes 327680 | tf_op jit(solution)/shard_map/all_to_all | solution.py:876
  10.0 0.7 copy-start.7
  10.0 0.7 copy-start.8
  10.7 1.5 %copy-start.9 = (s32[4,1]{0,1:T(1,128)S(1)}, s32[4,1]{0,1:T(1,128)}, u32[]{:S(2)}) copy-start(s32[4,1]{0,1:T(1,128)} %param.16) | copy-start | bytes 52
  12.1 0.7 copy-start.4
  12.1 0.7 copy-start.5
  12.1 0.7 copy-start.6
  17.6 3.6 %collective-permute-start.2 = (bf16[8,16,128]{2,1,0:T(8,128)(2,1)S(1)}, bf16[8,16,128]{2,1,0:T(8,128)(2,1)S(1)}, u32[]{:S(2)}, u32[]{:S(2)}) collective-permute-start(bf16[8,16,128]{2,1,0:T(8,128)(2,1)S(1)} %slice.3), channel_id=1, source_target_pairs={{0,3},{1,2},{2,1},{3,0},{4,7},{5,6},{6,5},{7,4},{8,11},{9,10},{10,... | collective-permute-start | bytes 98312 | tf_op jit(solution)/shard_map/ppermute | solution.py:879
  18.0 4.0 %collective-permute-start.1 = (bf16[8,16,128]{2,1,0:T(8,128)(2,1)S(1)}, bf16[8,16,128]{2,1,0:T(8,128)(2,1)S(1)}, u32[]{:S(2)}, u32[]{:S(2)}) collective-permute-start(bf16[8,16,128]{2,1,0:T(8,128)(2,1)S(1)} %slice.3), channel_id=1, source_target_pairs={{0,2},{1,3},{2,0},{3,1},{4,6},{5,7},{6,4},{7,5},{8,10},{9,11},{10,... | collective-permute-start | bytes 98312 | tf_op jit(solution)/shard_map/ppermute | solution.py:879
  19.1 2.8 %collective-permute-start = (bf16[8,16,128]{2,1,0:T(8,128)(2,1)S(1)}, bf16[8,16,128]{2,1,0:T(8,128)(2,1)S(1)}, u32[]{:S(2)}, u32[]{:S(2)}) collective-permute-start(bf16[8,16,128]{2,1,0:T(8,128)(2,1)S(1)} %slice.3), channel_id=1, source_target_pairs={{0,1},{1,0},{2,3},{3,2},{4,5},{5,4},{6,7},{7,6},{8,9},{9,8},{10,11... | collective-permute-start | bytes 98312 | tf_op jit(solution)/shard_map/ppermute | solution.py:879
  19.4 21.8 %collective-permute-start.6 = (bf16[1168,128]{1,0:T(8,128)(2,1)S(1)}, bf16[1168,128]{1,0:T(8,128)(2,1)S(1)}, u32[]{:S(2)}, u32[]{:S(2)}) collective-permute-start(bf16[1168,128]{1,0:T(8,128)(2,1)S(1)} %get-tuple-element.78), channel_id=1, source_target_pairs={{0,1},{1,0},{2,3},{3,2},{4,5},{5,4},{6,7},{7,6},{8,9},{9,8},{10,11... | collective-permute-start | bytes 897032 | tf_op jit(solution)/shard_map/ppermute | solution.py:879
  19.6 21.8 %collective-permute-start.7 = (bf16[1168,128]{1,0:T(8,128)(2,1)S(1)}, bf16[1168,128]{1,0:T(8,128)(2,1)S(1)}, u32[]{:S(2)}, u32[]{:S(2)}) collective-permute-start(bf16[1168,128]{1,0:T(8,128)(2,1)S(1)} %get-tuple-element.79), channel_id=1, source_target_pairs={{0,2},{1,3},{2,0},{3,1},{4,6},{5,7},{6,4},{7,5},{8,10},{9,11},{10,... | collective-permute-start | bytes 897032 | tf_op jit(solution)/shard_map/ppermute | solution.py:879
  21.2 20.2 %collective-permute-start.8 = (bf16[1168,128]{1,0:T(8,128)(2,1)S(1)}, bf16[1168,128]{1,0:T(8,128)(2,1)S(1)}, u32[]{:S(2)}, u32[]{:S(2)}) collective-permute-start(bf16[1168,128]{1,0:T(8,128)(2,1)S(1)} %get-tuple-element.80), channel_id=1, source_target_pairs={{0,3},{1,2},{2,1},{3,0},{4,7},{5,6},{6,5},{7,4},{8,11},{9,10},{10,... | collective-permute-start | bytes 897032 | tf_op jit(solution)/shard_map/ppermute | solution.py:879
  26.3 13.2 %all-to-all-start.1 = ((bf16[32,16,128]{2,1,0:T(8,128)(2,1)}), bf16[32,16,128]{2,1,0:T(8,128)(2,1)S(1)}, u32[]{:S(2)}, u32[]{:S(2)}) async-start(bf16[32,16,128]{2,1,0:T(8,128)(2,1)} %bitcast.10), calls=%async_computation.1 | async-start | bytes 262144 | tf_op jit(solution)/shard_map/all_to_all | solution.py:876
  39.5 6.9 %collective-permute-start.5 = (bf16[512,128]{1,0:T(8,128)(2,1)S(1)}, bf16[512,128]{1,0:T(8,128)(2,1)S(1)}, u32[]{:S(2)}, u32[]{:S(2)}) collective-permute-start(bf16[512,128]{1,0:T(8,128)(2,1)S(1)} %bitcast.22), channel_id=1, source_target_pairs={{0,3},{1,2},{2,1},{3,0},{4,7},{5,6},{6,5},{7,4},{8,11},{9,10},{10,... | collective-permute-start | bytes 393224 | tf_op jit(solution)/shard_map/ppermute | solution.py:879
  39.8 8.2 %collective-permute-start.4 = (bf16[512,128]{1,0:T(8,128)(2,1)S(1)}, bf16[512,128]{1,0:T(8,128)(2,1)S(1)}, u32[]{:S(2)}, u32[]{:S(2)}) collective-permute-start(bf16[512,128]{1,0:T(8,128)(2,1)S(1)} %bitcast.23), channel_id=1, source_target_pairs={{0,2},{1,3},{2,0},{3,1},{4,6},{5,7},{6,4},{7,5},{8,10},{9,11},{10,... | collective-permute-start | bytes 393224 | tf_op jit(solution)/shard_map/ppermute | solution.py:879
  41.2 6.9 %collective-permute-start.3 = (bf16[512,128]{1,0:T(8,128)(2,1)S(1)}, bf16[512,128]{1,0:T(8,128)(2,1)S(1)}, u32[]{:S(2)}, u32[]{:S(2)}) collective-permute-start(bf16[512,128]{1,0:T(8,128)(2,1)S(1)} %bitcast.24), channel_id=1, source_target_pairs={{0,1},{1,0},{2,3},{3,2},{4,5},{5,4},{6,7},{7,6},{8,9},{9,8},{10,11... | collective-permute-start | bytes 393224 | tf_op jit(solution)/shard_map/ppermute | solution.py:879
  41.4 6.7 %copy-start.2 = (bf16[4,128,128]{2,1,0:T(8,128)(2,1)S(1)}, bf16[4,128,128]{2,1,0:T(8,128)(2,1)}, u32[]{:S(2)}) copy-start(bf16[4,128,128]{2,1,0:T(8,128)(2,1)} %tokens_ref.5) | copy-start | bytes 393220
  41.4 6.7 %copy-start.3 = (bf16[4,128,128]{2,1,0:T(8,128)(2,1)S(1)}, bf16[4,128,128]{2,1,0:T(8,128)(2,1)}, u32[]{:S(2)}) copy-start(bf16[4,128,128]{2,1,0:T(8,128)(2,1)} %cot_ref.3) | copy-start | bytes 393220
  43.4 4.7 %copy-start = (bf16[512,128]{1,0:T(8,128)(2,1)S(1)}, bf16[512,128]{1,0:T(8,128)(2,1)}, u32[]{:S(2)}) copy-start(bf16[512,128]{1,0:T(8,128)(2,1)} %wv_ref.1) | copy-start | bytes 393220
  43.4 4.7 %copy-start.1 = (bf16[512,128]{1,0:T(8,128)(2,1)S(1)}, bf16[512,128]{1,0:T(8,128)(2,1)}, u32[]{:S(2)}) copy-start(bf16[512,128]{1,0:T(8,128)(2,1)} %wg_ref.1) | copy-start | bytes 393220
  43.4 10.8 %all-to-all-start.2 = ((bf16[32,16,128]{2,1,0:T(8,128)(2,1)}), bf16[32,16,128]{2,1,0:T(8,128)(2,1)S(1)}, u32[]{:S(2)}, u32[]{:S(2)}) async-start(bf16[32,16,128]{2,1,0:T(8,128)(2,1)} %bitcast.12), calls=%async_computation.2 | async-start | bytes 262144 | tf_op jit(solution)/shard_map/all_to_all | solution.py:876
  50.0 9.3 %collective-permute-start.9 = (bf16[4,136,128]{2,1,0:T(8,128)(2,1)S(1)}, bf16[4,136,128]{2,1,0:T(8,128)(2,1)S(1)}, u32[]{:S(2)}, u32[]{:S(2)}) collective-permute-start(bf16[4,136,128]{2,1,0:T(8,128)(2,1)S(1)} %get-tuple-element.86), channel_id=1, source_target_pairs={{0,4},{4,0},{8,12},{12,8},{16,20},{20,16},{24,28},{28,24},{1,5},{5... | collective-permute-start | bytes 417800 | tf_op jit(solution)/shard_map/ppermute | solution.py:1008
  59.3 14.5 %all-to-all-start.3 = ((bf16[8,128,128]{2,1,0:T(8,128)(2,1)}), bf16[8,128,128]{2,1,0:T(8,128)(2,1)S(1)}, u32[]{:S(2)}, u32[]{:S(2)}) async-start(bf16[8,128,128]{2,1,0:T(8,128)(2,1)} %mixer_backward.1), calls=%async_computation.3 | async-start | bytes 524288 | tf_op jit(solution)/shard_map/all_to_all | solution.py:876
  62.8 7.7 %collective-permute-start.16 = (bf16[2,136,128]{2,1,0:T(8,128)(2,1)S(1)}, bf16[2,136,128]{2,1,0:T(8,128)(2,1)S(1)}, u32[]{:S(2)}, u32[]{:S(2)}) collective-permute-start(bf16[2,136,128]{2,1,0:T(8,128)(2,1)S(1)} %get-tuple-element.101), channel_id=1, source_target_pairs={{0,8},{4,12},{8,0},{12,4},{16,24},{20,28},{24,16},{28,20},{1,9},{5... | collective-permute-start | bytes 208904 | tf_op jit(solution)/shard_map/ppermute | solution.py:1026
  64.7 9.0 %collective-permute-start.12 = (f32[8,128]{1,0:T(8,128)S(1)}, f32[8,128]{1,0:T(8,128)S(1)}, u32[]{:S(2)}, u32[]{:S(2)}) collective-permute-start(f32[8,128]{1,0:T(8,128)S(1)} %get-tuple-element.62.refs_0_), channel_id=1, source_target_pairs={{0,3},{1,2},{2,1},{3,0},{4,7},{5,6},{6,5},{7,4},{8,11},{9,10},{10,... | collective-permute-start | bytes 12296 | tf_op jit(solution)/shard_map/ppermute | solution.py:879
  64.7 9.0 %collective-permute-start.11 = (f32[8,128]{1,0:T(8,128)S(1)}, f32[8,128]{1,0:T(8,128)S(1)}, u32[]{:S(2)}, u32[]{:S(2)}) collective-permute-start(f32[8,128]{1,0:T(8,128)S(1)} %get-tuple-element.62.refs_0_), channel_id=1, source_target_pairs={{0,2},{1,3},{2,0},{3,1},{4,6},{5,7},{6,4},{7,5},{8,10},{9,11},{10,... | collective-permute-start | bytes 12296 | tf_op jit(solution)/shard_map/ppermute | solution.py:879
  65.9 7.8 %collective-permute-start.10 = (f32[8,128]{1,0:T(8,128)S(1)}, f32[8,128]{1,0:T(8,128)S(1)}, u32[]{:S(2)}, u32[]{:S(2)}) collective-permute-start(f32[8,128]{1,0:T(8,128)S(1)} %get-tuple-element.62.refs_0_), channel_id=1, source_target_pairs={{0,1},{1,0},{2,3},{3,2},{4,5},{5,4},{6,7},{7,6},{8,9},{9,8},{10,11... | collective-permute-start | bytes 12296 | tf_op jit(solution)/shard_map/ppermute | solution.py:879
  70.5 5.4 %collective-permute-start.17 = (bf16[1,136,128]{2,1,0:T(8,128)(2,1)S(1)}, bf16[1,136,128]{2,1,0:T(8,128)(2,1)S(1)}, u32[]{:S(2)}, u32[]{:S(2)}) collective-permute-start(bf16[1,136,128]{2,1,0:T(8,128)(2,1)S(1)} %get-tuple-element.103), channel_id=1, source_target_pairs={{0,16},{4,20},{8,24},{12,28},{16,0},{20,4},{24,8},{28,12},{1,17},{... | collective-permute-start | bytes 104456 | tf_op jit(solution)/shard_map/ppermute | solution.py:1026
  73.9 3.1 %collective-permute-start.15 = (f32[8,128]{1,0:T(8,128)S(1)}, f32[8,128]{1,0:T(8,128)S(1)}, u32[]{:S(2)}, u32[]{:S(2)}) collective-permute-start(f32[8,128]{1,0:T(8,128)S(1)} %get-tuple-element.90.refs_0_), channel_id=1, source_target_pairs={{0,3},{1,2},{2,1},{3,0},{4,7},{5,6},{6,5},{7,4},{8,11},{9,10},{10,... | collective-permute-start | bytes 12296 | tf_op jit(solution)/shard_map/ppermute | solution.py:879
  74.0 3.7 %collective-permute-start.14 = (f32[8,128]{1,0:T(8,128)S(1)}, f32[8,128]{1,0:T(8,128)S(1)}, u32[]{:S(2)}, u32[]{:S(2)}) collective-permute-start(f32[8,128]{1,0:T(8,128)S(1)} %get-tuple-element.90.refs_0_), channel_id=1, source_target_pairs={{0,2},{1,3},{2,0},{3,1},{4,6},{5,7},{6,4},{7,5},{8,10},{9,11},{10,... | collective-permute-start | bytes 12296 | tf_op jit(solution)/shard_map/ppermute | solution.py:879
  74.7 3.0 %collective-permute-start.13 = (f32[8,128]{1,0:T(8,128)S(1)}, f32[8,128]{1,0:T(8,128)S(1)}, u32[]{:S(2)}, u32[]{:S(2)}) collective-permute-start(f32[8,128]{1,0:T(8,128)S(1)} %get-tuple-element.90.refs_0_), channel_id=1, source_target_pairs={{0,1},{1,0},{2,3},{3,2},{4,5},{5,4},{6,7},{7,6},{8,9},{9,8},{10,11... | collective-permute-start | bytes 12296 | tf_op jit(solution)/shard_map/ppermute | solution.py:879

commit v5 on v4

--- a/solution.py
+++ b/solution.py
@@ -179,7 +179,7 @@
     decay_hbm,
     turn_hbm,
     const_ref,
-    power_ref,
+    rise,
     taps_ref,
     live_ref,
     b_ref,
@@ -188,9 +188,7 @@
     decay_ref,
     turn_ref,
     turned_keep,
-    rise,
     coefs,
-    steps,
     sems,
 ):
     half = decay_ref.shape[0]
@@ -235,8 +233,8 @@
         power = cmul(power, a_pair, half) if k else a
     for k in range(levels):
         power_pair = pair(power, half)
-        steps[2 * k] = power_pair[0]
-        steps[2 * k + 1] = power_pair[1]
+        rise[pl.ds((8 + 2 * k) * chans, chans), :] = power_pair[0]
+        rise[pl.ds((9 + 2 * k) * chans, chans), :] = power_pair[1]
         power = cmul(power, power_pair, half)
     kept = [pair(b, half), pair(e, half), pair(cmul(a, pair(c, half), half), half)]
     for k in range(spans):
@@ -259,16 +257,7 @@
             const_ref[2 * len(kept) + k, channel : channel + 1, :] = jnp.full(
                 (1, 2 * half), ref[base + channel], f32
             )
-        up = rise[pl.ds(channel, 8, stride=chans), :]
-        for k in range(levels):
-            by = (
-                steps[2 * k, channel : channel + 1, :],
-                steps[2 * k + 1, channel : channel + 1, :],
-            )
-            up = jnp.concatenate([up, cmul(up, by, half)], axis=0)
-        high, low_part = split(up)
-        power_ref[channel, pl.ds(0, width), :] = high
-        power_ref[channel, pl.ds(width, width), :] = low_part
+        high, low_part = mode_powers(rise, channel, chans, levels, half)
         coef = coefs[pl.ds(channel, 16, stride=chans), :]
         coef_hi = coef.astype(bf16).astype(f32)
         both = jnp.concatenate([coef_hi, coef - coef_hi], axis=0).astype(bf16)
@@ -278,6 +267,15 @@
         taps_ref[channel] = taps + jnp.where(at == 7, skip_ref[base + channel], 0.0)
 
 
+def mode_powers(rise_ref, channel, chans, levels, half):
+    up = rise_ref[pl.ds(channel, 8, stride=chans), :]
+    for k in range(levels):
+        at = (8 + 2 * k) * chans + channel
+        by = (rise_ref[at : at + 1, :], rise_ref[at + chans : at + chans + 1, :])
+        up = jnp.concatenate([up, cmul(up, by, half)], axis=0)
+    return split(up)
+
+
 def own_rows(keep, at, stride, micros, chunks):
     return jnp.concatenate(
         [keep[pl.ds(at + m, chunks, stride=stride), :] for m in range(micros)], axis=0
@@ -298,16 +296,14 @@
     peers,
     got_ref,
     const_ref,
+    rise_ref,
     taps_ref,
     live_ref,
     *refs,
 ):
     stats_refs, refs = refs[: peers - 1], refs[peers - 1 :]
-    power_hbm, refs = refs[0], refs[1:]
     act_ref, norm_ref, y_ref, kept_hbm, act_keep, x_keep, stats_keep = refs[:7]
     parts, wide_parts, sent_parts, kept_ref, power_ref, sem = refs[7:]
-    load = pltpu.make_async_copy(power_hbm, power_ref, sem.at[0])
-    load.start()
     width = got_ref.shape[2]
     half = const_ref.shape[2] // 2
     spans = int(math.log2(chunks))
@@ -352,14 +348,12 @@
         wide_parts[channel, rows:, :width] = u_lo
         wide_parts[channel, rows:, width:] = v_lo
 
-    for channel in range(chans):
-        tables = [hankel(taps_ref[channel, 8 * k : 8 * k + 8], width) for k in range(2)]
-        both = wide_parts[channel]
-        y = mm(both, jnp.concatenate([tables[0][0], tables[1][0]], axis=0))
-        low_part = mm(both[:rows], jnp.concatenate([tables[0][1], tables[1][1]], axis=0))
-        y_ref[channel] = y[:rows] + y[rows:] + low_part
-
-    load.wait()
+    levels = int(math.log2(width)) - 3
+    for channel in range(chans):
+        high, low_part = mode_powers(rise_ref, channel, chans, levels, half)
+        power_ref[channel, :width] = high
+        power_ref[channel, width:] = low_part
+
     for channel in range(chans):
         q = mm(parts[channel], power_ref[channel, :width])
         kept_ref[channel, : 2 * rows] = (
@@ -379,8 +373,15 @@
         high, low_part = split(cmul(start, const(channel, 2), half) * flip)
         sent_parts[channel, :rows] = high
         sent_parts[channel, rows:] = low_part
-    store = pltpu.make_async_copy(kept_ref, kept_hbm, sem.at[1])
+    store = pltpu.make_async_copy(kept_ref, kept_hbm, sem)
     store.start()
+
+    for channel in range(chans):
+        tables = [hankel(taps_ref[channel, 8 * k : 8 * k + 8], width) for k in range(2)]
+        both = wide_parts[channel]
+        y = mm(both, jnp.concatenate([tables[0][0], tables[1][0]], axis=0))
+        low_part = mm(both[:rows], jnp.concatenate([tables[0][1], tables[1][1]], axis=0))
+        y_ref[channel] = y[:rows] + y[rows:] + low_part
 
     for channel in range(chans):
         both = sent_parts[channel]
@@ -408,7 +409,7 @@
         pltpu.VMEM((chans, 2 * rows, lane), bf16),
         pltpu.VMEM((chans, 3 * rows, lane), f32),
         pltpu.VMEM((chans, 2 * width, lane), bf16),
-        pltpu.SemaphoreType.DMA((2,)),
+        pltpu.SemaphoreType.DMA(()),
     ]
 
 
@@ -420,10 +421,10 @@
     dact_ref,
     norm_ref,
     const_ref,
+    rise_ref,
     taps_ref,
     live_ref,
     y_ref,
-    power_hbm,
     kept_hbm,
     send_ref,
     sums_keep,
@@ -442,13 +443,10 @@
     dots,
     power_ref,
     kept_ref,
-    sems,
+    sem,
 ):
-    loads = [
-        pltpu.make_async_copy(power_hbm, power_ref, sems.at[0]),
-        pltpu.make_async_copy(kept_hbm, kept_ref, sems.at[1]),
-    ]
-    fetch(loads)
+    load = pltpu.make_async_copy(kept_hbm, kept_ref, sem)
+    load.start()
     width = got_ref.shape[2]
     half = const_ref.shape[2] // 2
     spans = int(math.log2(chunks))
@@ -520,8 +518,12 @@
                     lanes(line.shape) == 0, line, 0.0
                 )
 
-    for load in loads:
-        load.wait()
+    levels = int(math.log2(width)) - 3
+    for channel in range(chans):
+        high, low_part = mode_powers(rise_ref, channel, chans, levels, half)
+        power_ref[channel, :width] = high
+        power_ref[channel, width:] = low_part
+
     for channel in range(chans):
         both = dy_parts[channel, : 2 * rows]
         yd = mm(both, power_ref[channel, :width])
@@ -559,6 +561,7 @@
                 m * chunks : (m + 1) * chunks
             ]
 
+    load.wait()
     lag_keep[:, 4:, :] = jnp.zeros((chans, 12, width), f32)
     for channel in range(chans):
         lags = lag_keep[channel].astype(bf16)
@@ -624,7 +627,7 @@
         pltpu.VMEM((8, chans, lane), f32),
         pltpu.VMEM((chans, 2 * width, lane), bf16),
         pltpu.VMEM((chans, 3 * rows, lane), f32),
-        pltpu.SemaphoreType.DMA((2,)),
+        pltpu.SemaphoreType.DMA(()),
     ]
 
 
@@ -912,13 +915,13 @@
     )(chan_rank.reshape(1), *bias_rows, in_hbm(cot_own), in_hbm(wv), in_hbm(wg))
 
     turned = [jnp.transpose(z, (0, 2, 1)) for z in (b_coef, e_coef, c_coef)]
-    const, power, taps, live = pl.pallas_call(
+    const, rise, taps, live = pl.pallas_call(
         functools.partial(table_kernel, chans, seqs, width),
         in_specs=[smem()] * 5 + [hbm] * 5,
         out_specs=[vmem()] * 4,
         out_shape=[
             shape_of((12 + 2 * spans, chans, lane)),
-            pltpu.HBM((chans, 2 * width, lane), bf16),
+            shape_of(((8 + 2 * levels) * chans, lane)),
             shape_of((chans, 16, width)),
             shape_of((rows, width)),
         ],
@@ -926,9 +929,7 @@
         + [pltpu.VMEM((modes, wide), f32)] * 2
         + [
             pltpu.VMEM((wide, lane), f32),
-            pltpu.VMEM((8 * chans, lane), f32),
             pltpu.VMEM((16 * chans, lane), f32),
-            pltpu.VMEM((2 * levels, chans, lane), f32),
             pltpu.SemaphoreType.DMA((5,)),
         ],
         compiler_params=pltpu.CompilerParams(vmem_limit_bytes=8 * 1024 * 1024),
@@ -940,10 +941,10 @@
     x_stats = x_mine[:, micros * chans :]
     x_stats = [cross(x_stats, k) for k in range(1, peers)]
     weights = [weights[0]] + [cross(weights[k], k) for k in range(1, peers)]
-    arrays = (x_mine, const, taps, live, *x_stats, in_hbm(power))
+    arrays = (x_mine, const, rise, taps, live, *x_stats)
     act, norm_mine, y_mine, kept = pl.pallas_call(
         functools.partial(forward_kernel, micros, seqs, chans, peers),
-        in_specs=[vmem()] * (len(arrays) - 1) + [hbm],
+        in_specs=[vmem()] * len(arrays),
         out_specs=[vmem()] * 3 + [hbm],
         out_shape=[
             shape_of((rows * chans, width), bf16),
@@ -1006,12 +1007,12 @@
         ],
     )
     got = lax.ppermute(send, "seq", [(i, i ^ 1) for i in range(seqs)])
-    d_act, keep = lax.optimization_barrier((d_act, keep))
+    d_act, keep, *stats = lax.optimization_barrier((d_act, keep, *stats))
     stride = -(-((micros + 3) * chans + 2) // 16) * 16
-    arrays = (x_mine, d_act, norm_mine, const, taps, live, y_mine, in_hbm(power), in_hbm(kept))
+    arrays = (x_mine, d_act, norm_mine, const, rise, taps, live, y_mine, in_hbm(kept))
     d_hat = pl.pallas_call(
         functools.partial(backward_kernel, micros, seqs, chans),
-        in_specs=[vmem()] * (len(arrays) - 2) + [hbm] * 2,
+        in_specs=[vmem()] * (len(arrays) - 1) + [hbm],
         out_specs=vmem(),
         out_shape=shape_of((seqs, stride, width), bf16),
         scratch_shapes=backward_scratch(micros, seqs, chans, stride, width, lane),

time: 79.7 us -> 78.4 us (0.984)
  Pallas kernels: 23.5 us -> 21.7 us
    ppermute x2, waiting for transfers between devices: 3.86 us -> 5.71 us  [shards(): got = lax.ppermute(send, 'seq', [(i, i ^ by) for i in range(seqs)])]
    ppermute x15, waiting for transfers between devices: 3.79 us -> 2.59 us  [cross(): return lax.ppermute(x, 'chan', [(i, i ^ by) for i in range(peers)])]
    pallas_call x1, Pallas kernels: 4.37 us -> 3.52 us  [shards(): pl.pallas_call(functools.partial(table_kernel, chans, seqs, width), in_sp...]
  transfers between devices with their start and end apart: 22 -> 22, of which waited for: 9 -> 9; matrix products, arithmetic and copies ran while one was open for 0% -> 0% of each run, Pallas kernels for 25% -> 23%
where the time goes in v5:
time: 78.4 us; the launch traced here: 77.8 us
  starting transfers between devices  35.2 us (45%)
  Pallas kernels  21.7 us (28%)
  waiting for transfers between devices  18.6 us (24%)
  local copies, waits for them, and re-layouts  1.34 us (2%)
  between operations  0.85 us (1%)
    all_to_all x4, starting transfers between devices, exchange(): return lax.all_to_all(x, axis, 0, 0, tiled=True)  19.2 us
    all_to_all x4, waiting for transfers between devices, exchange(): return lax.all_to_all(x, axis, 0, 0, tiled=True)  10.3 us
    ppermute x15, starting transfers between devices, cross(): return lax.ppermute(x, 'chan', [(i, i ^ by) for i in range(peers)])  9.56 us
    pallas_call x7, Pallas kernels, kernel_call(): pl.pallas_call(kernel, in_specs=ins, out_specs=[vmem()] * len(outs), out_...  6.15 us
    ppermute x2, waiting for transfers between devices, shards(): got = lax.ppermute(send, 'seq', [(i, i ^ by) for i in range(seqs)])  5.71 us
    ppermute x2, starting transfers between devices, shards(): got = lax.ppermute(send, 'seq', [(i, i ^ by) for i in range(seqs)])  5.2 us
    pallas_call x1, Pallas kernels, shards(): pl.pallas_call(functools.partial(backward_kernel, micros, seqs, chans), i...  4.6 us
    pallas_call x1, Pallas kernels, shards(): pl.pallas_call(functools.partial(forward_kernel, micros, seqs, chans, pee...  3.87 us
  transfers between devices with their start and end apart: 22, of which 9 were waited for; matrix products, arithmetic and copies ran while one was open for 0% of the time, Pallas kernels for 23%

profile of v5, /device:TPU:0, one launch (start us, length us, event | category | flops | bytes accessed | tf_op | source)
XLA Modules:
  0.0 77.8 jit_solution(12906025988523961925)
XLA Ops:
  0.6 2.1 %pack.1 = (bf16[8,80,128]{2,1,0:T(8,128)(2,1)}, f32[8,128]{1,0:T(8,128)S(1)}) custom-call(bf16[4,128,128]{2,1,0:T(8,128)(2,1)} %tokens_ref.5), custom_call_target="tpu_custom_call" | custom-call | flops 1000000000 | bytes 3000000 | tf_op jit(solution)/shard_map/pack/pallas_call | solution.py:885
  2.7 7.3 %all-to-all-start = ((bf16[8,80,128]{2,1,0:T(8,128)(2,1)}), bf16[8,80,128]{2,1,0:T(8,128)(2,1)S(1)}, u32[]{:S(2)}, u32[]{:S(2)}) async-start(bf16[8,80,128]{2,1,0:T(8,128)(2,1)} %get-tuple-element.64), calls=%async_computation | async-start | bytes 327680 | tf_op jit(solution)/shard_map/all_to_all | solution.py:879
  10.0 0.0 copy-start.8
  10.0 0.6 copy-done.7
  10.6 0.0 copy-done.8
  10.7 1.5 %weights.1 = (bf16[1168,128]{1,0:T(8,128)(2,1)S(1)}, bf16[1168,128]{1,0:T(8,128)(2,1)S(1)}, bf16[1168,128]{1,0:T(8,128)(2,1)S(1)}, bf16[1168,128]{1,0:T(8,128)(2,1)S(1)}) custom-call(s32[1]{0:T(128)} %bitcast.9.rank_ref, f32[1,128]{1,0:T(1,128)S(1)} %bitcast.28, f32[1,128]{1,0:T(1,128)S(1)} %bitcast.30, bf16[4,128,128]{2,1,0:T(8,128)(2,1)} %cot_ref.3, ...), custom_call_target="tpu_custom_call" | custom-call | flops 1000000000 | bytes 3000000 | tf_op jit(solution)/shard_map/weights/pallas_call | solution.py:906
  12.2 0.0 copy-start.4
  12.2 0.0 copy-start.5
  12.2 0.0 copy-start.6
  12.2 0.6 copy-done.4
  12.8 0.0 copy-done.5
  12.8 0.0 copy-done.6
  12.9 3.5 %tables.1 = (f32[18,16,128]{2,1,0:T(8,128)S(1)}, f32[256,128]{1,0:T(8,128)S(1)}, f32[16,16,128]{2,1,0:T(8,128)S(1)}, f32[32,128]{1,0:T(8,128)S(1)}) custom-call(s32[1]{0:T(128)} %bitcast.rank_ref, s32[4]{0:T(128)S(1)} %bitcast.32, f32[128]{0:T(128)S(1)} %copy-done.4, f32[128]{0:T(128)S(1)} %copy-done.5, f32[128]{0:T(128)S(1)} %copy-done.6, ...), custom_call_target="tpu_custom_call" | custom-call | flops 2000000000 | bytes 6000000 | tf_op jit(solution)/shard_map/tables/pallas_call | solution.py:918
  16.4 1.2 %all-to-all-done.got_ref = bf16[8,80,128]{2,1,0:T(8,128)(2,1)S(1)} async-done(((bf16[8,80,128]{2,1,0:T(8,128)(2,1)}), bf16[8,80,128]{2,1,0:T(8,128)(2,1)S(1)}, u32[]{:S(2)}, u32[]{:S(2)}) %all-to-all-start) | async-done | bytes 163872 | tf_op jit(solution)/shard_map/all_to_all | solution.py:879
  17.6 0.0 collective-permute-start.2
  17.6 1.5 %collective-permute-start.1 = (bf16[8,16,128]{2,1,0:T(8,128)(2,1)S(1)}, bf16[8,16,128]{2,1,0:T(8,128)(2,1)S(1)}, u32[]{:S(2)}, u32[]{:S(2)}) collective-permute-start(bf16[8,16,128]{2,1,0:T(8,128)(2,1)S(1)} %slice.3), channel_id=1, source_target_pairs={{0,2},{1,3},{2,0},{3,1},{4,6},{5,7},{6,4},{7,5},{8,10},{9,11},{10,... | collective-permute-start | bytes 98312 | tf_op jit(solution)/shard_map/ppermute | solution.py:882
  19.1 0.3 collective-permute-start
  19.4 0.2 collective-permute-start.6
  19.6 1.3 %collective-permute-start.7 = (bf16[1168,128]{1,0:T(8,128)(2,1)S(1)}, bf16[1168,128]{1,0:T(8,128)(2,1)S(1)}, u32[]{:S(2)}, u32[]{:S(2)}) collective-permute-start(bf16[1168,128]{1,0:T(8,128)(2,1)S(1)} %get-tuple-element.83), channel_id=1, source_target_pairs={{0,2},{1,3},{2,0},{3,1},{4,6},{5,7},{6,4},{7,5},{8,10},{9,11},{10,... | collective-permute-start | bytes 897032 | tf_op jit(solution)/shard_map/ppermute | solution.py:882
  20.9 0.2 collective-permute-done.2.refs_2_
  21.2 0.1 collective-permute-start.8
  21.3 0.3 collective-permute-done.1.refs_1_
  21.6 0.0 collective-permute-done.refs_0_
  21.6 3.9 %mixer_forward.1 = (bf16[512,128]{1,0:T(8,128)(2,1)}, f32[64,128]{1,0:T(8,128)S(1)}, f32[16,32,128]{2,1,0:T(8,128)S(1)}, f32[16,96,128]{2,1,0:T(8,128)}) custom-call(bf16[8,80,128]{2,1,0:T(8,128)(2,1)S(1)} %all-to-all-done.got_ref, f32[18,16,128]{2,1,0:T(8,128)S(1)} %get-tuple-element.75.const_ref, f32[256,128]{1,0:T(8,128)S(1)} %get-tuple-element.76.rise_ref, ...), custom_call_target="tpu_custom_call" | custom-call | flops 5000000000 | bytes 15000000 | tf_op jit(solution)/shard_map/mixer_forward/pallas_call | solution.py:945
  25.5 5.0 %all-to-all-start.1 = ((bf16[32,16,128]{2,1,0:T(8,128)(2,1)}), bf16[32,16,128]{2,1,0:T(8,128)(2,1)S(1)}, u32[]{:S(2)}, u32[]{:S(2)}) async-start(bf16[32,16,128]{2,1,0:T(8,128)(2,1)} %bitcast.10), calls=%async_computation.1 | async-start | bytes 262144 | tf_op jit(solution)/shard_map/all_to_all | solution.py:879
  30.5 1.6 %collective-permute-start.11 = (f32[8,128]{1,0:T(8,128)S(1)}, f32[8,128]{1,0:T(8,128)S(1)}, u32[]{:S(2)}, u32[]{:S(2)}) collective-permute-start(f32[8,128]{1,0:T(8,128)S(1)} %get-tuple-element.92.refs_0_), channel_id=1, source_target_pairs={{0,3},{1,2},{2,1},{3,0},{4,7},{5,6},{6,5},{7,4},{8,11},{9,10},{10,... | collective-permute-start | bytes 12296 | tf_op jit(solution)/shard_map/ppermute | solution.py:882
  32.0 0.4 collective-permute-start.10
  32.4 0.1 pad_add_fusion.place_ref
  32.5 5.7 %all-to-all-done.1 = bf16[32,16,128]{2,1,0:T(8,128)(2,1)S(1)} async-done(((bf16[32,16,128]{2,1,0:T(8,128)(2,1)}), bf16[32,16,128]{2,1,0:T(8,128)(2,1)S(1)}, u32[]{:S(2)}, u32[]{:S(2)}) %all-to-all-start.1) | async-done | bytes 131104 | tf_op jit(solution)/shard_map/all_to_all | solution.py:879
  38.2 0.0 collective-permute-done.6.refs_1_
  38.2 0.4 collective-permute-start.5
  38.6 0.0 collective-permute-done.7.refs_2_
  38.6 1.4 %collective-permute-start.4 = (bf16[512,128]{1,0:T(8,128)(2,1)S(1)}, bf16[512,128]{1,0:T(8,128)(2,1)S(1)}, u32[]{:S(2)}, u32[]{:S(2)}) collective-permute-start(bf16[512,128]{1,0:T(8,128)(2,1)S(1)} %bitcast.23), channel_id=1, source_target_pairs={{0,2},{1,3},{2,0},{3,1},{4,6},{5,7},{6,4},{7,5},{8,10},{9,11},{10,... | collective-permute-start | bytes 393224 | tf_op jit(solution)/shard_map/ppermute | solution.py:882
  40.0 0.0 collective-permute-done.8.refs_3_
  40.0 0.1 collective-permute-start.3
  40.1 2.0 %project.1 = bf16[512,128]{1,0:T(8,128)(2,1)} custom-call(s32[2]{0:T(128)S(1)} %pad_add_fusion.place_ref, s32[4]{0:T(128)S(1)} %bitcast.33, bf16[512,128]{1,0:T(8,128)(2,1)S(1)} %bitcast.25, bf16[1168,128]{1,0:T(8,128)(2,1)S(1)} %get-tuple-element.81.refs_0_, bf16[1168,128]{1,0:T(8,128)(2,1)S(1)} %collective-permute-done.6.refs_1_, ...), custom_call_target="tpu_custom_call" | custom-call | flops 2000000000 | bytes 6000000 | tf_op jit(solution)/shard_map/project/pallas_call | solution.py:823
  42.1 3.6 %all-to-all-start.2 = ((bf16[32,16,128]{2,1,0:T(8,128)(2,1)}), bf16[32,16,128]{2,1,0:T(8,128)(2,1)S(1)}, u32[]{:S(2)}, u32[]{:S(2)}) async-start(bf16[32,16,128]{2,1,0:T(8,128)(2,1)} %bitcast.12), calls=%async_computation.2 | async-start | bytes 262144 | tf_op jit(solution)/shard_map/all_to_all | solution.py:879
  45.7 0.0 collective-permute-done.5.refs_3_
  45.7 0.3 collective-permute-start.9
  46.0 0.8 %collective-permute-done.4.refs_2_ = bf16[512,128]{1,0:T(8,128)(2,1)S(1)} collective-permute-done((bf16[512,128]{1,0:T(8,128)(2,1)S(1)}, bf16[512,128]{1,0:T(8,128)(2,1)S(1)}, u32[]{:S(2)}, u32[]{:S(2)}) %collective-permute-start.4) | collective-permute-done | bytes 131104 | tf_op jit(solution)/shard_map/ppermute | solution.py:882
  46.8 0.0 collective-permute-done.3.refs_1_
  46.8 1.9 %output.1 = (bf16[4,128,128]{2,1,0:T(8,128)(2,1)}, f32[4,136,128]{2,1,0:T(8,128)S(1)}, bf16[4,136,128]{2,1,0:T(8,128)(2,1)S(1)}) custom-call(s32[1]{0:T(128)} %bitcast.rank_ref, s32[4]{0:T(128)S(1)} %bitcast.34, s32[4]{0:T(128)S(1)} %iota_xor_fusion.order_ref, bf16[4,128,128]{2,1,0:T(8,128)(2,1)S(1)} %copy-done.2, bf16[4,128,128]{2,1,0:T(8,128)(2,1)S(1)} %copy-done.3, ...), custom_call_target="tpu_custom_call" | custom-call | flops 2000000000 | bytes 6000000 | tf_op jit(solution)/shard_map/output/pallas_call | solution.py:823
  48.7 1.2 %collective-permute-start.12 = (bf16[4,136,128]{2,1,0:T(8,128)(2,1)S(1)}, bf16[4,136,128]{2,1,0:T(8,128)(2,1)S(1)}, u32[]{:S(2)}, u32[]{:S(2)}) collective-permute-start(bf16[4,136,128]{2,1,0:T(8,128)(2,1)S(1)} %get-tuple-element.90), channel_id=1, source_target_pairs={{0,4},{4,0},{8,12},{12,8},{16,20},{20,16},{24,28},{28,24},{1,5},{5... | collective-permute-start | bytes 417800 | tf_op jit(solution)/shard_map/ppermute | solution.py:1009
  49.9 0.0 collective-permute-done.11.refs_3_
  49.9 0.0 collective-permute-done.10.refs_2_
  49.9 0.0 collective-permute-done.9.refs_1_
  49.9 3.4 %all-to-all-done.2 = bf16[32,16,128]{2,1,0:T(8,128)(2,1)S(1)} async-done(((bf16[32,16,128]{2,1,0:T(8,128)(2,1)}), bf16[32,16,128]{2,1,0:T(8,128)(2,1)S(1)}, u32[]{:S(2)}, u32[]{:S(2)}) %all-to-all-start.2) | async-done | bytes 131104 | tf_op jit(solution)/shard_map/all_to_all | solution.py:879
  53.4 4.6 %mixer_backward.1 = bf16[8,128,128]{2,1,0:T(8,128)(2,1)} custom-call(bf16[8,80,128]{2,1,0:T(8,128)(2,1)S(1)} %all-to-all-done.got_ref, bf16[512,128]{1,0:T(8,128)(2,1)S(1)} %bitcast.27, f32[64,128]{1,0:T(8,128)S(1)} %get-tuple-element.87.norm_ref, f32[18,16,128]{2,1,0:T(8,128)S(1)} %get-tuple-element.75.const_ref, ...), custom_call_target="tpu_custom_call" | custom-call | flops 5000000000 | bytes 15000000 | tf_op jit(solution)/shard_map/mixer_backward/pallas_call | solution.py:1013
  58.0 0.0 collective-permute-done.12.right_ref
  58.0 3.4 %all-to-all-start.3 = ((bf16[8,128,128]{2,1,0:T(8,128)(2,1)}), bf16[8,128,128]{2,1,0:T(8,128)(2,1)S(1)}, u32[]{:S(2)}, u32[]{:S(2)}) async-start(bf16[8,128,128]{2,1,0:T(8,128)(2,1)} %mixer_backward.1), calls=%async_computation.3 | async-start | bytes 524288 | tf_op jit(solution)/shard_map/all_to_all | solution.py:879
  61.4 0.1 halve.2
  61.5 2.0 %collective-permute-start.16 = (bf16[2,136,128]{2,1,0:T(8,128)(2,1)S(1)}, bf16[2,136,128]{2,1,0:T(8,128)(2,1)S(1)}, u32[]{:S(2)}, u32[]{:S(2)}) collective-permute-start(bf16[2,136,128]{2,1,0:T(8,128)(2,1)S(1)} %get-tuple-element.109), channel_id=1, source_target_pairs={{0,8},{4,12},{8,0},{12,4},{16,24},{20,28},{24,16},{28,20},{1,9},{5... | collective-permute-start | bytes 208904 | tf_op jit(solution)/shard_map/ppermute | solution.py:1027
  63.5 5.7 %collective-permute-done.16.right_ref = bf16[2,136,128]{2,1,0:T(8,128)(2,1)S(1)} collective-permute-done((bf16[2,136,128]{2,1,0:T(8,128)(2,1)S(1)}, bf16[2,136,128]{2,1,0:T(8,128)(2,1)S(1)}, u32[]{:S(2)}, u32[]{:S(2)}) %collective-permute-start.16) | collective-permute-done | bytes 69664 | tf_op jit(solution)/shard_map/ppermute | solution.py:1027
  69.2 3.2 %collective-permute-start.17 = (bf16[1,136,128]{2,1,0:T(8,128)(2,1)S(1)}, bf16[1,136,128]{2,1,0:T(8,128)(2,1)S(1)}, u32[]{:S(2)}, u32[]{:S(2)}) collective-permute-start(bf16[1,136,128]{2,1,0:T(8,128)(2,1)S(1)} %get-tuple-element.111), channel_id=1, source_target_pairs={{0,16},{4,20},{8,24},{12,28},{16,0},{20,4},{24,8},{28,12},{1,17},{... | collective-permute-start | bytes 104456 | tf_op jit(solution)/shard_map/ppermute | solution.py:1027
  72.4 0.2 sums.1
  72.6 0.1 collective-permute-start.15
  72.7 0.7 collective-permute-start.14
  73.4 1.1 %collective-permute-start.13 = (f32[8,128]{1,0:T(8,128)S(1)}, f32[8,128]{1,0:T(8,128)S(1)}, u32[]{:S(2)}, u32[]{:S(2)}) collective-permute-start(f32[8,128]{1,0:T(8,128)S(1)} %get-tuple-element.98.refs_0_), channel_id=1, source_target_pairs={{0,1},{1,0},{2,3},{3,2},{4,5},{5,4},{6,7},{7,6},{8,9},{9,8},{10,11... | collective-permute-start | bytes 12296 | tf_op jit(solution)/shard_map/ppermute | solution.py:882
  74.6 0.0 collective-permute-done.17.right_ref
  74.6 0.6 last.1
  75.2 0.5 collective-permute-done.15.refs_3_
  75.7 0.7 collective-permute-done.14.refs_2_
  76.4 0.0 collective-permute-done.13.refs_1_
  76.4 1.4 %final.1 = (f32[4,128,128]{2,1,0:T(8,128)}, f32[2,64,128]{2,1,0:T(8,128)}, f32[2,64,128]{2,1,0:T(8,128)}, f32[2,64,128]{2,1,0:T(8,128)}, f32[1,128]{1,0:T(1,128)}, /*index=5*/f32[1,128]{1,0:T(1,128)}, f32[1,128]{1,0:T(1,128)}) custom-call(s32[1]{0:T(128)} %bitcast.rank_ref, s32[4]{0:T(128)S(1)} %bitcast.35, f32[8,128,128]{2,1,0:T(8,128)S(1)} %get-tuple-element.96.head_ref, ...), custom_call_target="tpu_custom_call" | custom-call | flops 2000000000 | bytes 6000000 | tf_op jit(solution)/shard_map/final/pallas_call | solution.py:823
  (15 shorter events, 0.1 us)
Async XLA Ops:
  2.7 14.8 %all-to-all-start = ((bf16[8,80,128]{2,1,0:T(8,128)(2,1)}), bf16[8,80,128]{2,1,0:T(8,128)(2,1)S(1)}, u32[]{:S(2)}, u32[]{:S(2)}) async-start(bf16[8,80,128]{2,1,0:T(8,128)(2,1)} %get-tuple-element.64), calls=%async_computation | async-start | bytes 327680 | tf_op jit(solution)/shard_map/all_to_all | solution.py:879
  10.0 0.7 copy-start.7
  10.0 0.7 copy-start.8
  10.7 1.5 %copy-start.9 = (s32[4,1]{0,1:T(1,128)S(1)}, s32[4,1]{0,1:T(1,128)}, u32[]{:S(2)}) copy-start(s32[4,1]{0,1:T(1,128)} %param.16) | copy-start | bytes 52
  12.2 0.7 copy-start.4
  12.2 0.7 copy-start.5
  12.2 0.7 copy-start.6
  17.6 3.6 %collective-permute-start.2 = (bf16[8,16,128]{2,1,0:T(8,128)(2,1)S(1)}, bf16[8,16,128]{2,1,0:T(8,128)(2,1)S(1)}, u32[]{:S(2)}, u32[]{:S(2)}) collective-permute-start(bf16[8,16,128]{2,1,0:T(8,128)(2,1)S(1)} %slice.3), channel_id=1, source_target_pairs={{0,3},{1,2},{2,1},{3,0},{4,7},{5,6},{6,5},{7,4},{8,11},{9,10},{10,... | collective-permute-start | bytes 98312 | tf_op jit(solution)/shard_map/ppermute | solution.py:882
  17.6 4.0 %collective-permute-start.1 = (bf16[8,16,128]{2,1,0:T(8,128)(2,1)S(1)}, bf16[8,16,128]{2,1,0:T(8,128)(2,1)S(1)}, u32[]{:S(2)}, u32[]{:S(2)}) collective-permute-start(bf16[8,16,128]{2,1,0:T(8,128)(2,1)S(1)} %slice.3), channel_id=1, source_target_pairs={{0,2},{1,3},{2,0},{3,1},{4,6},{5,7},{6,4},{7,5},{8,10},{9,11},{10,... | collective-permute-start | bytes 98312 | tf_op jit(solution)/shard_map/ppermute | solution.py:882
  19.1 2.5 %collective-permute-start = (bf16[8,16,128]{2,1,0:T(8,128)(2,1)S(1)}, bf16[8,16,128]{2,1,0:T(8,128)(2,1)S(1)}, u32[]{:S(2)}, u32[]{:S(2)}) collective-permute-start(bf16[8,16,128]{2,1,0:T(8,128)(2,1)S(1)} %slice.3), channel_id=1, source_target_pairs={{0,1},{1,0},{2,3},{3,2},{4,5},{5,4},{6,7},{7,6},{8,9},{9,8},{10,11... | collective-permute-start | bytes 98312 | tf_op jit(solution)/shard_map/ppermute | solution.py:882
  19.4 18.8 %collective-permute-start.6 = (bf16[1168,128]{1,0:T(8,128)(2,1)S(1)}, bf16[1168,128]{1,0:T(8,128)(2,1)S(1)}, u32[]{:S(2)}, u32[]{:S(2)}) collective-permute-start(bf16[1168,128]{1,0:T(8,128)(2,1)S(1)} %get-tuple-element.82), channel_id=1, source_target_pairs={{0,1},{1,0},{2,3},{3,2},{4,5},{5,4},{6,7},{7,6},{8,9},{9,8},{10,11... | collective-permute-start | bytes 897032 | tf_op jit(solution)/shard_map/ppermute | solution.py:882
  19.6 18.9 %collective-permute-start.7 = (bf16[1168,128]{1,0:T(8,128)(2,1)S(1)}, bf16[1168,128]{1,0:T(8,128)(2,1)S(1)}, u32[]{:S(2)}, u32[]{:S(2)}) collective-permute-start(bf16[1168,128]{1,0:T(8,128)(2,1)S(1)} %get-tuple-element.83), channel_id=1, source_target_pairs={{0,2},{1,3},{2,0},{3,1},{4,6},{5,7},{6,4},{7,5},{8,10},{9,11},{10,... | collective-permute-start | bytes 897032 | tf_op jit(solution)/shard_map/ppermute | solution.py:882
  21.2 18.8 %collective-permute-start.8 = (bf16[1168,128]{1,0:T(8,128)(2,1)S(1)}, bf16[1168,128]{1,0:T(8,128)(2,1)S(1)}, u32[]{:S(2)}, u32[]{:S(2)}) collective-permute-start(bf16[1168,128]{1,0:T(8,128)(2,1)S(1)} %get-tuple-element.84), channel_id=1, source_target_pairs={{0,3},{1,2},{2,1},{3,0},{4,7},{5,6},{6,5},{7,4},{8,11},{9,10},{10,... | collective-permute-start | bytes 897032 | tf_op jit(solution)/shard_map/ppermute | solution.py:882
  25.5 12.7 %all-to-all-start.1 = ((bf16[32,16,128]{2,1,0:T(8,128)(2,1)}), bf16[32,16,128]{2,1,0:T(8,128)(2,1)S(1)}, u32[]{:S(2)}, u32[]{:S(2)}) async-start(bf16[32,16,128]{2,1,0:T(8,128)(2,1)} %bitcast.10), calls=%async_computation.1 | async-start | bytes 262144 | tf_op jit(solution)/shard_map/all_to_all | solution.py:879
  30.5 19.5 %collective-permute-start.11 = (f32[8,128]{1,0:T(8,128)S(1)}, f32[8,128]{1,0:T(8,128)S(1)}, u32[]{:S(2)}, u32[]{:S(2)}) collective-permute-start(f32[8,128]{1,0:T(8,128)S(1)} %get-tuple-element.92.refs_0_), channel_id=1, source_target_pairs={{0,3},{1,2},{2,1},{3,0},{4,7},{5,6},{6,5},{7,4},{8,11},{9,10},{10,... | collective-permute-start | bytes 12296 | tf_op jit(solution)/shard_map/ppermute | solution.py:882
  32.0 17.9 %collective-permute-start.10 = (f32[8,128]{1,0:T(8,128)S(1)}, f32[8,128]{1,0:T(8,128)S(1)}, u32[]{:S(2)}, u32[]{:S(2)}) collective-permute-start(f32[8,128]{1,0:T(8,128)S(1)} %get-tuple-element.92.refs_0_), channel_id=1, source_target_pairs={{0,2},{1,3},{2,0},{3,1},{4,6},{5,7},{6,4},{7,5},{8,10},{9,11},{10,... | collective-permute-start | bytes 12296 | tf_op jit(solution)/shard_map/ppermute | solution.py:882
  38.2 7.5 %collective-permute-start.5 = (bf16[512,128]{1,0:T(8,128)(2,1)S(1)}, bf16[512,128]{1,0:T(8,128)(2,1)S(1)}, u32[]{:S(2)}, u32[]{:S(2)}) collective-permute-start(bf16[512,128]{1,0:T(8,128)(2,1)S(1)} %bitcast.22), channel_id=1, source_target_pairs={{0,3},{1,2},{2,1},{3,0},{4,7},{5,6},{6,5},{7,4},{8,11},{9,10},{10,... | collective-permute-start | bytes 393224 | tf_op jit(solution)/shard_map/ppermute | solution.py:882
  38.6 8.2 %collective-permute-start.4 = (bf16[512,128]{1,0:T(8,128)(2,1)S(1)}, bf16[512,128]{1,0:T(8,128)(2,1)S(1)}, u32[]{:S(2)}, u32[]{:S(2)}) collective-permute-start(bf16[512,128]{1,0:T(8,128)(2,1)S(1)} %bitcast.23), channel_id=1, source_target_pairs={{0,2},{1,3},{2,0},{3,1},{4,6},{5,7},{6,4},{7,5},{8,10},{9,11},{10,... | collective-permute-start | bytes 393224 | tf_op jit(solution)/shard_map/ppermute | solution.py:882
  40.0 6.9 %collective-permute-start.3 = (bf16[512,128]{1,0:T(8,128)(2,1)S(1)}, bf16[512,128]{1,0:T(8,128)(2,1)S(1)}, u32[]{:S(2)}, u32[]{:S(2)}) collective-permute-start(bf16[512,128]{1,0:T(8,128)(2,1)S(1)} %bitcast.24), channel_id=1, source_target_pairs={{0,1},{1,0},{2,3},{3,2},{4,5},{5,4},{6,7},{7,6},{8,9},{9,8},{10,11... | collective-permute-start | bytes 393224 | tf_op jit(solution)/shard_map/ppermute | solution.py:882
  40.1 6.7 %copy-start.2 = (bf16[4,128,128]{2,1,0:T(8,128)(2,1)S(1)}, bf16[4,128,128]{2,1,0:T(8,128)(2,1)}, u32[]{:S(2)}) copy-start(bf16[4,128,128]{2,1,0:T(8,128)(2,1)} %tokens_ref.5) | copy-start | bytes 393220
  40.1 6.7 %copy-start.3 = (bf16[4,128,128]{2,1,0:T(8,128)(2,1)S(1)}, bf16[4,128,128]{2,1,0:T(8,128)(2,1)}, u32[]{:S(2)}) copy-start(bf16[4,128,128]{2,1,0:T(8,128)(2,1)} %cot_ref.3) | copy-start | bytes 393220
  42.1 4.8 %copy-start = (bf16[512,128]{1,0:T(8,128)(2,1)S(1)}, bf16[512,128]{1,0:T(8,128)(2,1)}, u32[]{:S(2)}) copy-start(bf16[512,128]{1,0:T(8,128)(2,1)} %wv_ref.1) | copy-start | bytes 393220
  42.1 4.8 %copy-start.1 = (bf16[512,128]{1,0:T(8,128)(2,1)S(1)}, bf16[512,128]{1,0:T(8,128)(2,1)}, u32[]{:S(2)}) copy-start(bf16[512,128]{1,0:T(8,128)(2,1)} %wg_ref.1) | copy-start | bytes 393220
  42.1 11.3 %all-to-all-start.2 = ((bf16[32,16,128]{2,1,0:T(8,128)(2,1)}), bf16[32,16,128]{2,1,0:T(8,128)(2,1)S(1)}, u32[]{:S(2)}, u32[]{:S(2)}) async-start(bf16[32,16,128]{2,1,0:T(8,128)(2,1)} %bitcast.12), calls=%async_computation.2 | async-start | bytes 262144 | tf_op jit(solution)/shard_map/all_to_all | solution.py:879
  45.7 4.3 %collective-permute-start.9 = (f32[8,128]{1,0:T(8,128)S(1)}, f32[8,128]{1,0:T(8,128)S(1)}, u32[]{:S(2)}, u32[]{:S(2)}) collective-permute-start(f32[8,128]{1,0:T(8,128)S(1)} %get-tuple-element.92.refs_0_), channel_id=1, source_target_pairs={{0,1},{1,0},{2,3},{3,2},{4,5},{5,4},{6,7},{7,6},{8,9},{9,8},{10,11... | collective-permute-start | bytes 12296 | tf_op jit(solution)/shard_map/ppermute | solution.py:882
  48.7 9.3 %collective-permute-start.12 = (bf16[4,136,128]{2,1,0:T(8,128)(2,1)S(1)}, bf16[4,136,128]{2,1,0:T(8,128)(2,1)S(1)}, u32[]{:S(2)}, u32[]{:S(2)}) collective-permute-start(bf16[4,136,128]{2,1,0:T(8,128)(2,1)S(1)} %get-tuple-element.90), channel_id=1, source_target_pairs={{0,4},{4,0},{8,12},{12,8},{16,20},{20,16},{24,28},{28,24},{1,5},{5... | collective-permute-start | bytes 417800 | tf_op jit(solution)/shard_map/ppermute | solution.py:1009
  58.0 14.4 %all-to-all-start.3 = ((bf16[8,128,128]{2,1,0:T(8,128)(2,1)}), bf16[8,128,128]{2,1,0:T(8,128)(2,1)S(1)}, u32[]{:S(2)}, u32[]{:S(2)}) async-start(bf16[8,128,128]{2,1,0:T(8,128)(2,1)} %mixer_backward.1), calls=%async_computation.3 | async-start | bytes 524288 | tf_op jit(solution)/shard_map/all_to_all | solution.py:879
  61.5 7.7 %collective-permute-start.16 = (bf16[2,136,128]{2,1,0:T(8,128)(2,1)S(1)}, bf16[2,136,128]{2,1,0:T(8,128)(2,1)S(1)}, u32[]{:S(2)}, u32[]{:S(2)}) collective-permute-start(bf16[2,136,128]{2,1,0:T(8,128)(2,1)S(1)} %get-tuple-element.109), channel_id=1, source_target_pairs={{0,8},{4,12},{8,0},{12,4},{16,24},{20,28},{24,16},{28,20},{1,9},{5... | collective-permute-start | bytes 208904 | tf_op jit(solution)/shard_map/ppermute | solution.py:1027
  69.2 5.4 %collective-permute-start.17 = (bf16[1,136,128]{2,1,0:T(8,128)(2,1)S(1)}, bf16[1,136,128]{2,1,0:T(8,128)(2,1)S(1)}, u32[]{:S(2)}, u32[]{:S(2)}) collective-permute-start(bf16[1,136,128]{2,1,0:T(8,128)(2,1)S(1)} %get-tuple-element.111), channel_id=1, source_target_pairs={{0,16},{4,20},{8,24},{12,28},{16,0},{20,4},{24,8},{28,12},{1,17},{... | collective-permute-start | bytes 104456 | tf_op jit(solution)/shard_map/ppermute | solution.py:1027
  72.6 3.1 %collective-permute-start.15 = (f32[8,128]{1,0:T(8,128)S(1)}, f32[8,128]{1,0:T(8,128)S(1)}, u32[]{:S(2)}, u32[]{:S(2)}) collective-permute-start(f32[8,128]{1,0:T(8,128)S(1)} %get-tuple-element.98.refs_0_), channel_id=1, source_target_pairs={{0,3},{1,2},{2,1},{3,0},{4,7},{5,6},{6,5},{7,4},{8,11},{9,10},{10,... | collective-permute-start | bytes 12296 | tf_op jit(solution)/shard_map/ppermute | solution.py:882
  72.7 3.7 %collective-permute-start.14 = (f32[8,128]{1,0:T(8,128)S(1)}, f32[8,128]{1,0:T(8,128)S(1)}, u32[]{:S(2)}, u32[]{:S(2)}) collective-permute-start(f32[8,128]{1,0:T(8,128)S(1)} %get-tuple-element.98.refs_0_), channel_id=1, source_target_pairs={{0,2},{1,3},{2,0},{3,1},{4,6},{5,7},{6,4},{7,5},{8,10},{9,11},{10,... | collective-permute-start | bytes 12296 | tf_op jit(solution)/shard_map/ppermute | solution.py:882
  73.4 3.0 %collective-permute-start.13 = (f32[8,128]{1,0:T(8,128)S(1)}, f32[8,128]{1,0:T(8,128)S(1)}, u32[]{:S(2)}, u32[]{:S(2)}) collective-permute-start(f32[8,128]{1,0:T(8,128)S(1)} %get-tuple-element.98.refs_0_), channel_id=1, source_target_pairs={{0,1},{1,0},{2,3},{3,2},{4,5},{5,4},{6,7},{7,6},{8,9},{9,8},{10,11... | collective-permute-start | bytes 12296 | tf_op jit(solution)/shard_map/ppermute | solution.py:882

commit v6 on v5

--- a/solution.py
+++ b/solution.py
@@ -684,7 +684,8 @@
 ):
     micros, wide, width = tokens_ref.shape
     acts_in, refs = refs[:micros], refs[micros:]
-    out_ref, keep_ref, send_ref, d_keep, grad = refs
+    out_ref, keep_ref, send_refs = refs[0], refs[1], refs[2:-2]
+    d_keep, grad = refs[-2:]
     full = wv_ref.shape[0]
     at = rank_ref[0] * width + lax.broadcasted_iota(jnp.int32, (width, wide), 0)
     place = rank_ref[0] * width + lanes((1, width))
@@ -709,22 +710,26 @@
         grad[k, pl.ds(0, count), :] = part[:, :wide]
         grad[k, pl.ds(count, count), :] = part[:, wide:]
         grad[k, pl.ds(2 * count, 8), :] = small
-    bit = rank_ref[0] & 1
-    for k in range(seqs // 2):
-        keep_ref[k] = grad[2 * k + bit]
-        send_ref[k] = grad[2 * k + 1 - bit].astype(bf16)
-
-
-def halve_kernel(bit_ref, left_ref, right_ref, keep_ref, send_ref, total):
-    total[...] = left_ref[...] + right_ref[...].astype(f32)
-    for k in range(keep_ref.shape[0]):
-        keep_ref[k] = total[2 * k + bit_ref[0]]
-        send_ref[k] = total[2 * k + 1 - bit_ref[0]].astype(bf16)
+    place = rank_ref[0] >> 1
+    for j in range(2):
+        keep_ref[j] = grad[2 * place + j]
+        for k, ref in enumerate(send_refs):
+            ref[j] = grad[2 * (place ^ (k + 1)) + j].astype(bf16)
+
+
+def parts_kernel(bit_ref, keep_in_ref, *refs):
+    got_refs, (keep_ref, send_ref, total) = refs[:-3], refs[-3:]
+    value = keep_in_ref[...]
+    for ref in got_refs:
+        value = value + ref[...].astype(f32)
+    total[...] = value
+    keep_ref[...] = total[bit_ref[0]]
+    send_ref[...] = total[1 - bit_ref[0]].astype(bf16)
 
 
 def last_kernel(left_ref, right_ref, wv_ref, wg_ref, bv_ref, bg_ref):
     count = wv_ref.shape[0]
-    total = left_ref[0] + right_ref[0].astype(f32)
+    total = left_ref[...] + right_ref[...].astype(f32)
     wv_ref[...] = total[:count]
     wg_ref[...] = total[count : 2 * count]
     bv_ref[...] = total[2 * count : 2 * count + 1]
@@ -992,13 +997,13 @@
         .reshape(rows * chans, width)
     )
     count = full // seqs
-    part = (seqs // 2, 2 * count + 8, wide)
-    out, keep, send = kernel_call(
+    part = (2, 2 * count + 8, wide)
+    out, keep, *blocks = kernel_call(
         functools.partial(output_kernel, seqs),
         "output",
         (rank, lens, order),
         (tokens, out_cotangent, w_value, w_gate) + bias_rows + tuple(acts),
-        [shape_of(tokens.shape, bf16), shape_of(part), shape_of(part, bf16)],
+        [shape_of(tokens.shape, bf16), shape_of(part)] + [shape_of(part, bf16)] * (seqs // 2 - 1),
         2,
         limit=12,
         scratch_shapes=[
@@ -1006,7 +1011,10 @@
             pltpu.VMEM((seqs,) + part[1:], f32),
         ],
     )
-    got = lax.ppermute(send, "seq", [(i, i ^ 1) for i in range(seqs)])
+    blocks = [
+        lax.ppermute(block, "seq", [(i, i ^ ((k + 1) << 1)) for i in range(seqs)])
+        for k, block in enumerate(blocks)
+    ]
     d_act, keep, *stats = lax.optimization_barrier((d_act, keep, *stats))
     stride = -(-((micros + 3) * chans + 2) // 16) * 16
     arrays = (x_mine, d_act, norm_mine, const, rise, taps, live, y_mine, in_hbm(kept))
@@ -1020,23 +1028,17 @@
         cost_estimate=cost(5),
         name="mixer_backward",
     )(*arrays)
-    d_hat, got = lax.optimization_barrier((d_hat, got))
-    for level in range(spans):
-        by = 1 << level
-        if level:
-            got = lax.ppermute(send, "seq", [(i, i ^ by) for i in range(seqs)])
-        if level == spans - 1:
-            break
-        half_part = (seqs >> (level + 2),) + part[1:]
-        keep, send = kernel_call(
-            halve_kernel,
-            "halve",
-            ((seq_rank.reshape(1) >> (level + 1)) & 1,),
-            (keep, got),
-            [shape_of(half_part), shape_of(half_part, bf16)],
-            1,
-            scratch_shapes=[pltpu.VMEM(keep.shape, f32)],
-        )
+    d_hat, *blocks = lax.optimization_barrier((d_hat, *blocks))
+    keep, send = kernel_call(
+        parts_kernel,
+        "parts",
+        (seq_rank.reshape(1) & 1,),
+        (keep, *blocks),
+        [shape_of(part[1:]), shape_of(part[1:], bf16)],
+        1,
+        scratch_shapes=[pltpu.VMEM(part, f32)],
+    )
+    got = lax.ppermute(send, "seq", [(i, i ^ 1) for i in range(seqs)])
     d_wv, d_wg, d_bv, d_bg = kernel_call(
         last_kernel,
         "last",

time: 78.4 us -> 77.3 us (0.986)
  waiting for transfers between devices: 18.6 us -> 16.4 us
  starting transfers between devices: 35.2 us -> 36.5 us
    ppermute x2 -> x3, waiting for transfers between devices: 5.71 us -> 0.18 us  [shards(): lax.ppermute(block, 'seq', [(i, i ^ k + 1 << 1) for i in range(seqs)])]
    all_to_all x4, waiting for transfers between devices: 10.3 us -> 13.6 us  [exchange(): return lax.all_to_all(x, axis, 0, 0, tiled=True)]
    all_to_all x4, starting transfers between devices: 19.2 us -> 20.5 us  [exchange(): return lax.all_to_all(x, axis, 0, 0, tiled=True)]
    ppermute x1, starting transfers between devices: 1.22 us -> 2.09 us  [shards(): got = lax.ppermute(send, 'seq', [(i, i ^ 1) for i in range(seqs)])]
    ppermute x2 -> x3, starting transfers between devices: 5.2 us -> 4.39 us  [shards(): lax.ppermute(block, 'seq', [(i, i ^ k + 1 << 1) for i in range(seqs)])]
    pallas_call x7 -> x6, Pallas kernels: 6.15 us -> 6.06 us  [kernel_call(): pl.pallas_call(kernel, in_specs=ins, out_specs=[vmem()] * len(outs), out_...]
  transfers between devices with their start and end apart: 22 -> 23, of which waited for: 9 -> 10; matrix products, arithmetic and copies ran while one was open for 0% -> 0% of each run, Pallas kernels for 23% -> 24%
where the time goes in v6:
time: 77.3 us; the launch traced here: 76.7 us
  starting transfers between devices  36.5 us (47%)
  Pallas kernels  21.6 us (28%)
  waiting for transfers between devices  16.4 us (21%)
  local copies, waits for them, and re-layouts  1.34 us (2%)
  between operations  0.83 us (1%)
    all_to_all x4, starting transfers between devices, exchange(): return lax.all_to_all(x, axis, 0, 0, tiled=True)  20.5 us
    all_to_all x4, waiting for transfers between devices, exchange(): return lax.all_to_all(x, axis, 0, 0, tiled=True)  13.6 us
    ppermute x15, starting transfers between devices, cross(): return lax.ppermute(x, 'chan', [(i, i ^ by) for i in range(peers)])  9.56 us
    pallas_call x6, Pallas kernels, kernel_call(): pl.pallas_call(kernel, in_specs=ins, out_specs=[vmem()] * len(outs), out_...  6.06 us
    pallas_call x1, Pallas kernels, shards(): pl.pallas_call(functools.partial(backward_kernel, micros, seqs, chans), i...  4.6 us
    ppermute x3, starting transfers between devices, shards(): lax.ppermute(block, 'seq', [(i, i ^ k + 1 << 1) for i in range(seqs)])  4.39 us
    pallas_call x1, Pallas kernels, shards(): pl.pallas_call(functools.partial(forward_kernel, micros, seqs, chans, pee...  3.87 us
    pallas_call x1, Pallas kernels, shards(): pl.pallas_call(functools.partial(table_kernel, chans, seqs, width), in_sp...  3.52 us
  transfers between devices with their start and end apart: 23, of which 10 were waited for; matrix products, arithmetic and copies ran while one was open for 0% of the time, Pallas kernels for 24%

profile of v6, /device:TPU:0, one launch (start us, length us, event | category | flops | bytes accessed | tf_op | source)
XLA Modules:
  0.0 76.7 jit_solution(3036679063177686317)
XLA Ops:
  0.6 2.1 %pack.1 = (bf16[8,80,128]{2,1,0:T(8,128)(2,1)}, f32[8,128]{1,0:T(8,128)S(1)}) custom-call(bf16[4,128,128]{2,1,0:T(8,128)(2,1)} %tokens_ref.5), custom_call_target="tpu_custom_call" | custom-call | flops 1000000000 | bytes 3000000 | tf_op jit(solution)/shard_map/pack/pallas_call | solution.py:890
  2.7 7.3 %all-to-all-start = ((bf16[8,80,128]{2,1,0:T(8,128)(2,1)}), bf16[8,80,128]{2,1,0:T(8,128)(2,1)S(1)}, u32[]{:S(2)}, u32[]{:S(2)}) async-start(bf16[8,80,128]{2,1,0:T(8,128)(2,1)} %get-tuple-element.66), calls=%async_computation | async-start | bytes 327680 | tf_op jit(solution)/shard_map/all_to_all | solution.py:884
  10.0 0.0 copy-start.8
  10.0 0.6 copy-done.7
  10.6 0.0 copy-done.8
  10.7 1.5 %weights.1 = (bf16[1168,128]{1,0:T(8,128)(2,1)S(1)}, bf16[1168,128]{1,0:T(8,128)(2,1)S(1)}, bf16[1168,128]{1,0:T(8,128)(2,1)S(1)}, bf16[1168,128]{1,0:T(8,128)(2,1)S(1)}) custom-call(s32[1]{0:T(128)} %bitcast.9.rank_ref, f32[1,128]{1,0:T(1,128)S(1)} %bitcast.28, f32[1,128]{1,0:T(1,128)S(1)} %bitcast.30, bf16[4,128,128]{2,1,0:T(8,128)(2,1)} %cot_ref.3, ...), custom_call_target="tpu_custom_call" | custom-call | flops 1000000000 | bytes 3000000 | tf_op jit(solution)/shard_map/weights/pallas_call | solution.py:911
  12.2 0.0 copy-start.4
  12.2 0.0 copy-start.5
  12.2 0.0 copy-start.6
  12.2 0.6 copy-done.4
  12.8 0.0 copy-done.5
  12.8 0.0 copy-done.6
  12.9 3.5 %tables.1 = (f32[18,16,128]{2,1,0:T(8,128)S(1)}, f32[256,128]{1,0:T(8,128)S(1)}, f32[16,16,128]{2,1,0:T(8,128)S(1)}, f32[32,128]{1,0:T(8,128)S(1)}) custom-call(s32[1]{0:T(128)} %bitcast.rank_ref, s32[4]{0:T(128)S(1)} %bitcast.32, f32[128]{0:T(128)S(1)} %copy-done.4, f32[128]{0:T(128)S(1)} %copy-done.5, f32[128]{0:T(128)S(1)} %copy-done.6, ...), custom_call_target="tpu_custom_call" | custom-call | flops 2000000000 | bytes 6000000 | tf_op jit(solution)/shard_map/tables/pallas_call | solution.py:923
  16.4 1.2 %all-to-all-done.got_ref = bf16[8,80,128]{2,1,0:T(8,128)(2,1)S(1)} async-done(((bf16[8,80,128]{2,1,0:T(8,128)(2,1)}), bf16[8,80,128]{2,1,0:T(8,128)(2,1)S(1)}, u32[]{:S(2)}, u32[]{:S(2)}) %all-to-all-start) | async-done | bytes 163872 | tf_op jit(solution)/shard_map/all_to_all | solution.py:884
  17.6 0.0 collective-permute-start.2
  17.6 1.5 %collective-permute-start.1 = (bf16[8,16,128]{2,1,0:T(8,128)(2,1)S(1)}, bf16[8,16,128]{2,1,0:T(8,128)(2,1)S(1)}, u32[]{:S(2)}, u32[]{:S(2)}) collective-permute-start(bf16[8,16,128]{2,1,0:T(8,128)(2,1)S(1)} %slice.3), channel_id=1, source_target_pairs={{0,2},{1,3},{2,0},{3,1},{4,6},{5,7},{6,4},{7,5},{8,10},{9,11},{10,... | collective-permute-start | bytes 98312 | tf_op jit(solution)/shard_map/ppermute | solution.py:887
  19.1 0.3 collective-permute-start
  19.4 0.2 collective-permute-start.6
  19.6 1.3 %collective-permute-start.7 = (bf16[1168,128]{1,0:T(8,128)(2,1)S(1)}, bf16[1168,128]{1,0:T(8,128)(2,1)S(1)}, u32[]{:S(2)}, u32[]{:S(2)}) collective-permute-start(bf16[1168,128]{1,0:T(8,128)(2,1)S(1)} %get-tuple-element.85), channel_id=1, source_target_pairs={{0,2},{1,3},{2,0},{3,1},{4,6},{5,7},{6,4},{7,5},{8,10},{9,11},{10,... | collective-permute-start | bytes 897032 | tf_op jit(solution)/shard_map/ppermute | solution.py:887
  20.9 0.2 collective-permute-done.2.refs_2_
  21.2 0.1 collective-permute-start.8
  21.3 0.3 collective-permute-done.1.refs_1_
  21.6 0.0 collective-permute-done.refs_0_
  21.6 3.9 %mixer_forward.1 = (bf16[512,128]{1,0:T(8,128)(2,1)}, f32[64,128]{1,0:T(8,128)S(1)}, f32[16,32,128]{2,1,0:T(8,128)S(1)}, f32[16,96,128]{2,1,0:T(8,128)}) custom-call(bf16[8,80,128]{2,1,0:T(8,128)(2,1)S(1)} %all-to-all-done.got_ref, f32[18,16,128]{2,1,0:T(8,128)S(1)} %get-tuple-element.77.const_ref, f32[256,128]{1,0:T(8,128)S(1)} %get-tuple-element.78.rise_ref, ...), custom_call_target="tpu_custom_call" | custom-call | flops 5000000000 | bytes 15000000 | tf_op jit(solution)/shard_map/mixer_forward/pallas_call | solution.py:950
  25.5 5.0 %all-to-all-start.1 = ((bf16[32,16,128]{2,1,0:T(8,128)(2,1)}), bf16[32,16,128]{2,1,0:T(8,128)(2,1)S(1)}, u32[]{:S(2)}, u32[]{:S(2)}) async-start(bf16[32,16,128]{2,1,0:T(8,128)(2,1)} %bitcast.10), calls=%async_computation.1 | async-start | bytes 262144 | tf_op jit(solution)/shard_map/all_to_all | solution.py:884
  30.5 1.6 %collective-permute-start.11 = (f32[8,128]{1,0:T(8,128)S(1)}, f32[8,128]{1,0:T(8,128)S(1)}, u32[]{:S(2)}, u32[]{:S(2)}) collective-permute-start(f32[8,128]{1,0:T(8,128)S(1)} %get-tuple-element.96.refs_0_), channel_id=1, source_target_pairs={{0,3},{1,2},{2,1},{3,0},{4,7},{5,6},{6,5},{7,4},{8,11},{9,10},{10,... | collective-permute-start | bytes 12296 | tf_op jit(solution)/shard_map/ppermute | solution.py:887
  32.0 0.4 collective-permute-start.10
  32.4 0.1 pad_add_fusion.place_ref
  32.5 5.7 %all-to-all-done.1 = bf16[32,16,128]{2,1,0:T(8,128)(2,1)S(1)} async-done(((bf16[32,16,128]{2,1,0:T(8,128)(2,1)}), bf16[32,16,128]{2,1,0:T(8,128)(2,1)S(1)}, u32[]{:S(2)}, u32[]{:S(2)}) %all-to-all-start.1) | async-done | bytes 131104 | tf_op jit(solution)/shard_map/all_to_all | solution.py:884
  38.2 0.0 collective-permute-done.6.refs_1_
  38.2 0.4 collective-permute-start.5
  38.6 0.0 collective-permute-done.7.refs_2_
  38.6 1.4 %collective-permute-start.4 = (bf16[512,128]{1,0:T(8,128)(2,1)S(1)}, bf16[512,128]{1,0:T(8,128)(2,1)S(1)}, u32[]{:S(2)}, u32[]{:S(2)}) collective-permute-start(bf16[512,128]{1,0:T(8,128)(2,1)S(1)} %bitcast.23), channel_id=1, source_target_pairs={{0,2},{1,3},{2,0},{3,1},{4,6},{5,7},{6,4},{7,5},{8,10},{9,11},{10,... | collective-permute-start | bytes 393224 | tf_op jit(solution)/shard_map/ppermute | solution.py:887
  40.0 0.0 collective-permute-done.8.refs_3_
  40.0 0.1 collective-permute-start.3
  40.1 2.0 %project.1 = bf16[512,128]{1,0:T(8,128)(2,1)} custom-call(s32[2]{0:T(128)S(1)} %pad_add_fusion.place_ref, s32[4]{0:T(128)S(1)} %bitcast.33, bf16[512,128]{1,0:T(8,128)(2,1)S(1)} %bitcast.25, bf16[1168,128]{1,0:T(8,128)(2,1)S(1)} %get-tuple-element.83.refs_0_, bf16[1168,128]{1,0:T(8,128)(2,1)S(1)} %collective-permute-done.6.refs_1_, ...), custom_call_target="tpu_custom_call" | custom-call | flops 2000000000 | bytes 6000000 | tf_op jit(solution)/shard_map/project/pallas_call | solution.py:828
  42.1 3.6 %all-to-all-start.2 = ((bf16[32,16,128]{2,1,0:T(8,128)(2,1)}), bf16[32,16,128]{2,1,0:T(8,128)(2,1)S(1)}, u32[]{:S(2)}, u32[]{:S(2)}) async-start(bf16[32,16,128]{2,1,0:T(8,128)(2,1)} %bitcast.12), calls=%async_computation.2 | async-start | bytes 262144 | tf_op jit(solution)/shard_map/all_to_all | solution.py:884
  45.7 0.0 collective-permute-done.5.refs_3_
  45.7 0.3 collective-permute-start.9
  46.0 0.8 %collective-permute-done.4.refs_2_ = bf16[512,128]{1,0:T(8,128)(2,1)S(1)} collective-permute-done((bf16[512,128]{1,0:T(8,128)(2,1)S(1)}, bf16[512,128]{1,0:T(8,128)(2,1)S(1)}, u32[]{:S(2)}, u32[]{:S(2)}) %collective-permute-start.4) | collective-permute-done | bytes 131104 | tf_op jit(solution)/shard_map/ppermute | solution.py:887
  46.8 0.0 collective-permute-done.3.refs_1_
  46.8 1.8 %output.1 = (bf16[4,128,128]{2,1,0:T(8,128)(2,1)}, f32[2,136,128]{2,1,0:T(8,128)S(1)}, bf16[2,136,128]{2,1,0:T(8,128)(2,1)S(1)}, bf16[2,136,128]{2,1,0:T(8,128)(2,1)S(1)}, bf16[2,136,128]{2,1,0:T(8,128)(2,1)S(1)}) custom-call(s32[1]{0:T(128)} %bitcast.rank_ref, s32[4]{0:T(128)S(1)} %bitcast.34, s32[4]{0:T(128)S(1)} %iota_xor_fusion.order_ref, ...), custom_call_target="tpu_custom_call" | custom-call | flops 2000000000 | bytes 6000000 | tf_op jit(solution)/shard_map/output/pallas_call | solution.py:828
  48.6 0.9 %collective-permute-start.12 = (bf16[2,136,128]{2,1,0:T(8,128)(2,1)S(1)}, bf16[2,136,128]{2,1,0:T(8,128)(2,1)S(1)}, u32[]{:S(2)}, u32[]{:S(2)}) collective-permute-start(bf16[2,136,128]{2,1,0:T(8,128)(2,1)S(1)} %get-tuple-element.92), channel_id=1, source_target_pairs={{0,8},{4,12},{8,0},{12,4},{16,24},{20,28},{24,16},{28,20},{1,9},{5... | collective-permute-start | bytes 208904 | tf_op jit(solution)/shard_map/ppermute | solution.py:1015
  49.5 2.4 %collective-permute-start.13 = (bf16[2,136,128]{2,1,0:T(8,128)(2,1)S(1)}, bf16[2,136,128]{2,1,0:T(8,128)(2,1)S(1)}, u32[]{:S(2)}, u32[]{:S(2)}) collective-permute-start(bf16[2,136,128]{2,1,0:T(8,128)(2,1)S(1)} %get-tuple-element.93), channel_id=1, source_target_pairs={{0,16},{4,20},{8,24},{12,28},{16,0},{20,4},{24,8},{28,12},{1,17},{... | collective-permute-start | bytes 208904 | tf_op jit(solution)/shard_map/ppermute | solution.py:1015
  51.9 0.0 collective-permute-done.11.refs_3_
  51.9 1.1 %collective-permute-start.14 = (bf16[2,136,128]{2,1,0:T(8,128)(2,1)S(1)}, bf16[2,136,128]{2,1,0:T(8,128)(2,1)S(1)}, u32[]{:S(2)}, u32[]{:S(2)}) collective-permute-start(bf16[2,136,128]{2,1,0:T(8,128)(2,1)S(1)} %get-tuple-element.94), channel_id=1, source_target_pairs={{0,24},{4,28},{8,16},{12,20},{16,8},{20,12},{24,0},{28,4},{1,25},{... | collective-permute-start | bytes 208904 | tf_op jit(solution)/shard_map/ppermute | solution.py:1015
  53.0 0.0 collective-permute-done.10.refs_2_
  53.0 0.0 collective-permute-done.9.refs_1_
  53.0 0.3 all-to-all-done.2
  53.4 4.6 %mixer_backward.1 = bf16[8,128,128]{2,1,0:T(8,128)(2,1)} custom-call(bf16[8,80,128]{2,1,0:T(8,128)(2,1)S(1)} %all-to-all-done.got_ref, bf16[512,128]{1,0:T(8,128)(2,1)S(1)} %bitcast.27, f32[64,128]{1,0:T(8,128)S(1)} %get-tuple-element.89.norm_ref, f32[18,16,128]{2,1,0:T(8,128)S(1)} %get-tuple-element.77.const_ref, ...), custom_call_target="tpu_custom_call" | custom-call | flops 5000000000 | bytes 15000000 | tf_op jit(solution)/shard_map/mixer_backward/pallas_call | solution.py:1021
  58.0 0.0 collective-permute-done.12.refs_0_
  58.0 0.2 collective-permute-done.13.refs_1_
  58.2 4.7 %all-to-all-start.3 = ((bf16[8,128,128]{2,1,0:T(8,128)(2,1)}), bf16[8,128,128]{2,1,0:T(8,128)(2,1)S(1)}, u32[]{:S(2)}, u32[]{:S(2)}) async-start(bf16[8,128,128]{2,1,0:T(8,128)(2,1)} %mixer_backward.1), calls=%async_computation.3 | async-start | bytes 524288 | tf_op jit(solution)/shard_map/all_to_all | solution.py:884
  62.9 2.1 %collective-permute-start.18 = (bf16[136,128]{1,0:T(8,128)(2,1)S(1)}, bf16[136,128]{1,0:T(8,128)(2,1)S(1)}, u32[]{:S(2)}, u32[]{:S(2)}) collective-permute-start(bf16[136,128]{1,0:T(8,128)(2,1)S(1)} %get-tuple-element.115), channel_id=1, source_target_pairs={{0,4},{4,0},{8,12},{12,8},{16,20},{20,16},{24,28},{28,24},{1,5},{5... | collective-permute-start | bytes 104456 | tf_op jit(solution)/shard_map/ppermute | solution.py:1041
  65.0 6.4 %all-to-all-done.3.got_ref = bf16[8,128,128]{2,1,0:T(8,128)(2,1)S(1)} async-done(((bf16[8,128,128]{2,1,0:T(8,128)(2,1)}), bf16[8,128,128]{2,1,0:T(8,128)(2,1)S(1)}, u32[]{:S(2)}, u32[]{:S(2)}) %all-to-all-start.3) | async-done | bytes 262176 | tf_op jit(solution)/shard_map/all_to_all | solution.py:884
  71.4 0.2 sums.1
  71.6 0.1 collective-permute-start.17
  71.6 1.6 %collective-permute-start.16 = (f32[8,128]{1,0:T(8,128)S(1)}, f32[8,128]{1,0:T(8,128)S(1)}, u32[]{:S(2)}, u32[]{:S(2)}) collective-permute-start(f32[8,128]{1,0:T(8,128)S(1)} %get-tuple-element.102.refs_0_), channel_id=1, source_target_pairs={{0,2},{1,3},{2,0},{3,1},{4,6},{5,7},{6,4},{7,5},{8,10},{9,11},{10,... | collective-permute-start | bytes 12296 | tf_op jit(solution)/shard_map/ppermute | solution.py:887
  73.2 0.3 collective-permute-start.15
  73.5 0.0 collective-permute-done.18.right_ref
  73.5 0.6 last.1
  74.1 0.5 collective-permute-done.17.refs_3_
  74.7 0.7 collective-permute-done.16.refs_2_
  75.3 1.4 %final.1 = (f32[4,128,128]{2,1,0:T(8,128)}, f32[2,64,128]{2,1,0:T(8,128)}, f32[2,64,128]{2,1,0:T(8,128)}, f32[2,64,128]{2,1,0:T(8,128)}, f32[1,128]{1,0:T(1,128)}, /*index=5*/f32[1,128]{1,0:T(1,128)}, f32[1,128]{1,0:T(1,128)}) custom-call(s32[1]{0:T(128)} %bitcast.rank_ref, s32[4]{0:T(128)S(1)} %bitcast.35, f32[8,128,128]{2,1,0:T(8,128)S(1)} %get-tuple-element.100.head_ref, ...), custom_call_target="tpu_custom_call" | custom-call | flops 2000000000 | bytes 6000000 | tf_op jit(solution)/shard_map/final/pallas_call | solution.py:828
  (16 shorter events, 0.1 us)
Async XLA Ops:
  2.7 14.8 %all-to-all-start = ((bf16[8,80,128]{2,1,0:T(8,128)(2,1)}), bf16[8,80,128]{2,1,0:T(8,128)(2,1)S(1)}, u32[]{:S(2)}, u32[]{:S(2)}) async-start(bf16[8,80,128]{2,1,0:T(8,128)(2,1)} %get-tuple-element.66), calls=%async_computation | async-start | bytes 327680 | tf_op jit(solution)/shard_map/all_to_all | solution.py:884
  10.0 0.7 copy-start.7
  10.0 0.7 copy-start.8
  10.7 1.5 %copy-start.9 = (s32[4,1]{0,1:T(1,128)S(1)}, s32[4,1]{0,1:T(1,128)}, u32[]{:S(2)}) copy-start(s32[4,1]{0,1:T(1,128)} %param.16) | copy-start | bytes 52
  12.2 0.7 copy-start.4
  12.2 0.7 copy-start.5
  12.2 0.7 copy-start.6
  17.6 3.6 %collective-permute-start.2 = (bf16[8,16,128]{2,1,0:T(8,128)(2,1)S(1)}, bf16[8,16,128]{2,1,0:T(8,128)(2,1)S(1)}, u32[]{:S(2)}, u32[]{:S(2)}) collective-permute-start(bf16[8,16,128]{2,1,0:T(8,128)(2,1)S(1)} %slice.3), channel_id=1, source_target_pairs={{0,3},{1,2},{2,1},{3,0},{4,7},{5,6},{6,5},{7,4},{8,11},{9,10},{10,... | collective-permute-start | bytes 98312 | tf_op jit(solution)/shard_map/ppermute | solution.py:887
  17.6 4.0 %collective-permute-start.1 = (bf16[8,16,128]{2,1,0:T(8,128)(2,1)S(1)}, bf16[8,16,128]{2,1,0:T(8,128)(2,1)S(1)}, u32[]{:S(2)}, u32[]{:S(2)}) collective-permute-start(bf16[8,16,128]{2,1,0:T(8,128)(2,1)S(1)} %slice.3), channel_id=1, source_target_pairs={{0,2},{1,3},{2,0},{3,1},{4,6},{5,7},{6,4},{7,5},{8,10},{9,11},{10,... | collective-permute-start | bytes 98312 | tf_op jit(solution)/shard_map/ppermute | solution.py:887
  19.1 2.5 %collective-permute-start = (bf16[8,16,128]{2,1,0:T(8,128)(2,1)S(1)}, bf16[8,16,128]{2,1,0:T(8,128)(2,1)S(1)}, u32[]{:S(2)}, u32[]{:S(2)}) collective-permute-start(bf16[8,16,128]{2,1,0:T(8,128)(2,1)S(1)} %slice.3), channel_id=1, source_target_pairs={{0,1},{1,0},{2,3},{3,2},{4,5},{5,4},{6,7},{7,6},{8,9},{9,8},{10,11... | collective-permute-start | bytes 98312 | tf_op jit(solution)/shard_map/ppermute | solution.py:887
  19.4 18.8 %collective-permute-start.6 = (bf16[1168,128]{1,0:T(8,128)(2,1)S(1)}, bf16[1168,128]{1,0:T(8,128)(2,1)S(1)}, u32[]{:S(2)}, u32[]{:S(2)}) collective-permute-start(bf16[1168,128]{1,0:T(8,128)(2,1)S(1)} %get-tuple-element.84), channel_id=1, source_target_pairs={{0,1},{1,0},{2,3},{3,2},{4,5},{5,4},{6,7},{7,6},{8,9},{9,8},{10,11... | collective-permute-start | bytes 897032 | tf_op jit(solution)/shard_map/ppermute | solution.py:887
  19.6 18.9 %collective-permute-start.7 = (bf16[1168,128]{1,0:T(8,128)(2,1)S(1)}, bf16[1168,128]{1,0:T(8,128)(2,1)S(1)}, u32[]{:S(2)}, u32[]{:S(2)}) collective-permute-start(bf16[1168,128]{1,0:T(8,128)(2,1)S(1)} %get-tuple-element.85), channel_id=1, source_target_pairs={{0,2},{1,3},{2,0},{3,1},{4,6},{5,7},{6,4},{7,5},{8,10},{9,11},{10,... | collective-permute-start | bytes 897032 | tf_op jit(solution)/shard_map/ppermute | solution.py:887
  21.2 18.8 %collective-permute-start.8 = (bf16[1168,128]{1,0:T(8,128)(2,1)S(1)}, bf16[1168,128]{1,0:T(8,128)(2,1)S(1)}, u32[]{:S(2)}, u32[]{:S(2)}) collective-permute-start(bf16[1168,128]{1,0:T(8,128)(2,1)S(1)} %get-tuple-element.86), channel_id=1, source_target_pairs={{0,3},{1,2},{2,1},{3,0},{4,7},{5,6},{6,5},{7,4},{8,11},{9,10},{10,... | collective-permute-start | bytes 897032 | tf_op jit(solution)/shard_map/ppermute | solution.py:887
  25.5 12.7 %all-to-all-start.1 = ((bf16[32,16,128]{2,1,0:T(8,128)(2,1)}), bf16[32,16,128]{2,1,0:T(8,128)(2,1)S(1)}, u32[]{:S(2)}, u32[]{:S(2)}) async-start(bf16[32,16,128]{2,1,0:T(8,128)(2,1)} %bitcast.10), calls=%async_computation.1 | async-start | bytes 262144 | tf_op jit(solution)/shard_map/all_to_all | solution.py:884
  30.5 21.5 %collective-permute-start.11 = (f32[8,128]{1,0:T(8,128)S(1)}, f32[8,128]{1,0:T(8,128)S(1)}, u32[]{:S(2)}, u32[]{:S(2)}) collective-permute-start(f32[8,128]{1,0:T(8,128)S(1)} %get-tuple-element.96.refs_0_), channel_id=1, source_target_pairs={{0,3},{1,2},{2,1},{3,0},{4,7},{5,6},{6,5},{7,4},{8,11},{9,10},{10,... | collective-permute-start | bytes 12296 | tf_op jit(solution)/shard_map/ppermute | solution.py:887
  32.0 21.0 %collective-permute-start.10 = (f32[8,128]{1,0:T(8,128)S(1)}, f32[8,128]{1,0:T(8,128)S(1)}, u32[]{:S(2)}, u32[]{:S(2)}) collective-permute-start(f32[8,128]{1,0:T(8,128)S(1)} %get-tuple-element.96.refs_0_), channel_id=1, source_target_pairs={{0,2},{1,3},{2,0},{3,1},{4,6},{5,7},{6,4},{7,5},{8,10},{9,11},{10,... | collective-permute-start | bytes 12296 | tf_op jit(solution)/shard_map/ppermute | solution.py:887
  38.2 7.5 %collective-permute-start.5 = (bf16[512,128]{1,0:T(8,128)(2,1)S(1)}, bf16[512,128]{1,0:T(8,128)(2,1)S(1)}, u32[]{:S(2)}, u32[]{:S(2)}) collective-permute-start(bf16[512,128]{1,0:T(8,128)(2,1)S(1)} %bitcast.22), channel_id=1, source_target_pairs={{0,3},{1,2},{2,1},{3,0},{4,7},{5,6},{6,5},{7,4},{8,11},{9,10},{10,... | collective-permute-start | bytes 393224 | tf_op jit(solution)/shard_map/ppermute | solution.py:887
  38.6 8.2 %collective-permute-start.4 = (bf16[512,128]{1,0:T(8,128)(2,1)S(1)}, bf16[512,128]{1,0:T(8,128)(2,1)S(1)}, u32[]{:S(2)}, u32[]{:S(2)}) collective-permute-start(bf16[512,128]{1,0:T(8,128)(2,1)S(1)} %bitcast.23), channel_id=1, source_target_pairs={{0,2},{1,3},{2,0},{3,1},{4,6},{5,7},{6,4},{7,5},{8,10},{9,11},{10,... | collective-permute-start | bytes 393224 | tf_op jit(solution)/shard_map/ppermute | solution.py:887
  40.0 6.9 %collective-permute-start.3 = (bf16[512,128]{1,0:T(8,128)(2,1)S(1)}, bf16[512,128]{1,0:T(8,128)(2,1)S(1)}, u32[]{:S(2)}, u32[]{:S(2)}) collective-permute-start(bf16[512,128]{1,0:T(8,128)(2,1)S(1)} %bitcast.24), channel_id=1, source_target_pairs={{0,1},{1,0},{2,3},{3,2},{4,5},{5,4},{6,7},{7,6},{8,9},{9,8},{10,11... | collective-permute-start | bytes 393224 | tf_op jit(solution)/shard_map/ppermute | solution.py:887
  40.1 6.7 %copy-start.2 = (bf16[4,128,128]{2,1,0:T(8,128)(2,1)S(1)}, bf16[4,128,128]{2,1,0:T(8,128)(2,1)}, u32[]{:S(2)}) copy-start(bf16[4,128,128]{2,1,0:T(8,128)(2,1)} %tokens_ref.5) | copy-start | bytes 393220
  40.1 6.7 %copy-start.3 = (bf16[4,128,128]{2,1,0:T(8,128)(2,1)S(1)}, bf16[4,128,128]{2,1,0:T(8,128)(2,1)}, u32[]{:S(2)}) copy-start(bf16[4,128,128]{2,1,0:T(8,128)(2,1)} %cot_ref.3) | copy-start | bytes 393220
  42.1 4.8 %copy-start = (bf16[512,128]{1,0:T(8,128)(2,1)S(1)}, bf16[512,128]{1,0:T(8,128)(2,1)}, u32[]{:S(2)}) copy-start(bf16[512,128]{1,0:T(8,128)(2,1)} %wv_ref.1) | copy-start | bytes 393220
  42.1 4.8 %copy-start.1 = (bf16[512,128]{1,0:T(8,128)(2,1)S(1)}, bf16[512,128]{1,0:T(8,128)(2,1)}, u32[]{:S(2)}) copy-start(bf16[512,128]{1,0:T(8,128)(2,1)} %wg_ref.1) | copy-start | bytes 393220
  42.1 11.3 %all-to-all-start.2 = ((bf16[32,16,128]{2,1,0:T(8,128)(2,1)}), bf16[32,16,128]{2,1,0:T(8,128)(2,1)S(1)}, u32[]{:S(2)}, u32[]{:S(2)}) async-start(bf16[32,16,128]{2,1,0:T(8,128)(2,1)} %bitcast.12), calls=%async_computation.2 | async-start | bytes 262144 | tf_op jit(solution)/shard_map/all_to_all | solution.py:884
  45.7 7.4 %collective-permute-start.9 = (f32[8,128]{1,0:T(8,128)S(1)}, f32[8,128]{1,0:T(8,128)S(1)}, u32[]{:S(2)}, u32[]{:S(2)}) collective-permute-start(f32[8,128]{1,0:T(8,128)S(1)} %get-tuple-element.96.refs_0_), channel_id=1, source_target_pairs={{0,1},{1,0},{2,3},{3,2},{4,5},{5,4},{6,7},{7,6},{8,9},{9,8},{10,11... | collective-permute-start | bytes 12296 | tf_op jit(solution)/shard_map/ppermute | solution.py:887
  48.6 9.3 %collective-permute-start.12 = (bf16[2,136,128]{2,1,0:T(8,128)(2,1)S(1)}, bf16[2,136,128]{2,1,0:T(8,128)(2,1)S(1)}, u32[]{:S(2)}, u32[]{:S(2)}) collective-permute-start(bf16[2,136,128]{2,1,0:T(8,128)(2,1)S(1)} %get-tuple-element.92), channel_id=1, source_target_pairs={{0,8},{4,12},{8,0},{12,4},{16,24},{20,28},{24,16},{28,20},{1,9},{5... | collective-permute-start | bytes 208904 | tf_op jit(solution)/shard_map/ppermute | solution.py:1015
  49.5 8.7 %collective-permute-start.13 = (bf16[2,136,128]{2,1,0:T(8,128)(2,1)S(1)}, bf16[2,136,128]{2,1,0:T(8,128)(2,1)S(1)}, u32[]{:S(2)}, u32[]{:S(2)}) collective-permute-start(bf16[2,136,128]{2,1,0:T(8,128)(2,1)S(1)} %get-tuple-element.93), channel_id=1, source_target_pairs={{0,16},{4,20},{8,24},{12,28},{16,0},{20,4},{24,8},{28,12},{1,17},{... | collective-permute-start | bytes 208904 | tf_op jit(solution)/shard_map/ppermute | solution.py:1015
  51.9 6.2 %collective-permute-start.14 = (bf16[2,136,128]{2,1,0:T(8,128)(2,1)S(1)}, bf16[2,136,128]{2,1,0:T(8,128)(2,1)S(1)}, u32[]{:S(2)}, u32[]{:S(2)}) collective-permute-start(bf16[2,136,128]{2,1,0:T(8,128)(2,1)S(1)} %get-tuple-element.94), channel_id=1, source_target_pairs={{0,24},{4,28},{8,16},{12,20},{16,8},{20,12},{24,0},{28,4},{1,25},{... | collective-permute-start | bytes 208904 | tf_op jit(solution)/shard_map/ppermute | solution.py:1015
  58.2 13.2 %all-to-all-start.3 = ((bf16[8,128,128]{2,1,0:T(8,128)(2,1)}), bf16[8,128,128]{2,1,0:T(8,128)(2,1)S(1)}, u32[]{:S(2)}, u32[]{:S(2)}) async-start(bf16[8,128,128]{2,1,0:T(8,128)(2,1)} %mixer_backward.1), calls=%async_computation.3 | async-start | bytes 524288 | tf_op jit(solution)/shard_map/all_to_all | solution.py:884
  62.9 10.6 %collective-permute-start.18 = (bf16[136,128]{1,0:T(8,128)(2,1)S(1)}, bf16[136,128]{1,0:T(8,128)(2,1)S(1)}, u32[]{:S(2)}, u32[]{:S(2)}) collective-permute-start(bf16[136,128]{1,0:T(8,128)(2,1)S(1)} %get-tuple-element.115), channel_id=1, source_target_pairs={{0,4},{4,0},{8,12},{12,8},{16,20},{20,16},{24,28},{28,24},{1,5},{5... | collective-permute-start | bytes 104456 | tf_op jit(solution)/shard_map/ppermute | solution.py:1041
  71.6 3.1 %collective-permute-start.17 = (f32[8,128]{1,0:T(8,128)S(1)}, f32[8,128]{1,0:T(8,128)S(1)}, u32[]{:S(2)}, u32[]{:S(2)}) collective-permute-start(f32[8,128]{1,0:T(8,128)S(1)} %get-tuple-element.102.refs_0_), channel_id=1, source_target_pairs={{0,3},{1,2},{2,1},{3,0},{4,7},{5,6},{6,5},{7,4},{8,11},{9,10},{10,... | collective-permute-start | bytes 12296 | tf_op jit(solution)/shard_map/ppermute | solution.py:887
  71.6 3.7 %collective-permute-start.16 = (f32[8,128]{1,0:T(8,128)S(1)}, f32[8,128]{1,0:T(8,128)S(1)}, u32[]{:S(2)}, u32[]{:S(2)}) collective-permute-start(f32[8,128]{1,0:T(8,128)S(1)} %get-tuple-element.102.refs_0_), channel_id=1, source_target_pairs={{0,2},{1,3},{2,0},{3,1},{4,6},{5,7},{6,4},{7,5},{8,10},{9,11},{10,... | collective-permute-start | bytes 12296 | tf_op jit(solution)/shard_map/ppermute | solution.py:887
  73.2 2.1 %collective-permute-start.15 = (f32[8,128]{1,0:T(8,128)S(1)}, f32[8,128]{1,0:T(8,128)S(1)}, u32[]{:S(2)}, u32[]{:S(2)}) collective-permute-start(f32[8,128]{1,0:T(8,128)S(1)} %get-tuple-element.102.refs_0_), channel_id=1, source_target_pairs={{0,1},{1,0},{2,3},{3,2},{4,5},{5,4},{6,7},{7,6},{8,9},{9,8},{10,11... | collective-permute-start | bytes 12296 | tf_op jit(solution)/shard_map/ppermute | solution.py:887

commit v7 on v6

--- a/solution.py
+++ b/solution.py
@@ -147,8 +147,9 @@
     fetch(copies)
     turn = mirror(width)
     means, squares = [], []
+    for copy in copies:
+        copy.wait()
     for m in range(micros):
-        copies[m].wait()
         x = tokens[m].astype(f32)
         mean = jnp.sum(x, axis=0, keepdims=True) * (1.0 / wide)
         means.append(mean)
@@ -302,8 +303,8 @@
     *refs,
 ):
     stats_refs, refs = refs[: peers - 1], refs[peers - 1 :]
-    act_ref, norm_ref, y_ref, kept_hbm, act_keep, x_keep, stats_keep = refs[:7]
-    parts, wide_parts, sent_parts, kept_ref, power_ref, sem = refs[7:]
+    act_ref, norm_ref, y_ref, start_ref, act_keep, x_keep, stats_keep = refs[:7]
+    parts, wide_parts, sent_parts, kept_ref, power_ref = refs[7:]
     width = got_ref.shape[2]
     half = const_ref.shape[2] // 2
     spans = int(math.log2(chunks))
@@ -369,12 +370,10 @@
             moved = shift_chunks(state, 2**k, micros, chunks)
             state = state + cmul(moved, const(channel, 3 + k), half)
         start = shift_chunks(state, 1, micros, chunks)
-        kept_ref[channel, 2 * rows :] = start
+        start_ref[channel] = start
         high, low_part = split(cmul(start, const(channel, 2), half) * flip)
         sent_parts[channel, :rows] = high
         sent_parts[channel, rows:] = low_part
-    store = pltpu.make_async_copy(kept_ref, kept_hbm, sem)
-    store.start()
 
     for channel in range(chans):
         tables = [hankel(taps_ref[channel, 8 * k : 8 * k + 8], width) for k in range(2)]
@@ -395,7 +394,6 @@
                 m * chunks : (m + 1) * chunks
             ]
     act_ref[...] = act_keep[...].astype(bf16)
-    store.wait()
 
 
 def forward_scratch(micros, chunks, chans, peers, width, lane):
@@ -407,9 +405,8 @@
         pltpu.VMEM((chans, 4 * rows, width), bf16),
         pltpu.VMEM((chans, 2 * rows, 2 * width), bf16),
         pltpu.VMEM((chans, 2 * rows, lane), bf16),
-        pltpu.VMEM((chans, 3 * rows, lane), f32),
+        pltpu.VMEM((chans, 2 * rows, lane), f32),
         pltpu.VMEM((chans, 2 * width, lane), bf16),
-        pltpu.SemaphoreType.DMA(()),
     ]
 
 
@@ -425,7 +422,7 @@
     taps_ref,
     live_ref,
     y_ref,
-    kept_hbm,
+    start_ref,
     send_ref,
     sums_keep,
     head,
@@ -442,11 +439,7 @@
     sent_parts,
     dots,
     power_ref,
-    kept_ref,
-    sem,
 ):
-    load = pltpu.make_async_copy(kept_hbm, kept_ref, sem)
-    load.start()
     width = got_ref.shape[2]
     half = const_ref.shape[2] // 2
     spans = int(math.log2(chunks))
@@ -561,7 +554,6 @@
                 m * chunks : (m + 1) * chunks
             ]
 
-    load.wait()
     lag_keep[:, 4:, :] = jnp.zeros((chans, 12, width), f32)
     for channel in range(chans):
         lags = lag_keep[channel].astype(bf16)
@@ -570,7 +562,13 @@
         dots[7, channel : channel + 1, :] = tops[1:2] + tops[3:4]
         adj, yd = adj_keep[channel], yd_keep[channel]
         adj_swap = swap(adj, half)
-        uq, vq, start = [kept_ref[channel, k * rows : (k + 1) * rows] for k in range(3)]
+        high, low_part = uv_parts[channel, :rows], uv_parts[channel, 2 * rows :]
+        parts = jnp.concatenate(
+            [high[:, :width], high[:, width:], low_part[:, :width], low_part[:, width:]], axis=0
+        )
+        q = mm(parts, power_ref[channel, :width])
+        q = q[: 2 * rows] + q[2 * rows :] + mm(parts[: 2 * rows], power_ref[channel, width:])
+        uq, vq, start = q[:rows], q[rows:], start_ref[channel]
         pairs = ((uq, adj), (uq, adj_swap), (vq, adj), (vq, adj_swap), (start, yd))
         for k, (left, right) in enumerate(pairs + ((start, swap(yd, half)),)):
             dots[k, channel : channel + 1, :] = total(left * right)
@@ -626,8 +624,6 @@
         pltpu.VMEM((chans, 4 * rows, lane), bf16),
         pltpu.VMEM((8, chans, lane), f32),
         pltpu.VMEM((chans, 2 * width, lane), bf16),
-        pltpu.VMEM((chans, 3 * rows, lane), f32),
-        pltpu.SemaphoreType.DMA(()),
     ]
 
 
@@ -947,15 +943,15 @@
     x_stats = [cross(x_stats, k) for k in range(1, peers)]
     weights = [weights[0]] + [cross(weights[k], k) for k in range(1, peers)]
     arrays = (x_mine, const, rise, taps, live, *x_stats)
-    act, norm_mine, y_mine, kept = pl.pallas_call(
+    act, norm_mine, y_mine, start_mine = pl.pallas_call(
         functools.partial(forward_kernel, micros, seqs, chans, peers),
         in_specs=[vmem()] * len(arrays),
-        out_specs=[vmem()] * 3 + [hbm],
+        out_specs=[vmem()] * 4,
         out_shape=[
             shape_of((rows * chans, width), bf16),
             shape_of((2 * rows, width)),
             shape_of((chans, rows, width)),
-            pltpu.HBM((chans, 3 * rows, lane), f32),
+            shape_of((chans, rows, lane)),
         ],
         scratch_shapes=forward_scratch(micros, seqs, chans, peers, width, lane),
         compiler_params=pltpu.CompilerParams(vmem_limit_bytes=16 * 1024 * 1024),
@@ -1017,10 +1013,10 @@
     ]
     d_act, keep, *stats = lax.optimization_barrier((d_act, keep, *stats))
     stride = -(-((micros + 3) * chans + 2) // 16) * 16
-    arrays = (x_mine, d_act, norm_mine, const, rise, taps, live, y_mine, in_hbm(kept))
+    arrays = (x_mine, d_act, norm_mine, const, rise, taps, live, y_mine, start_mine)
     d_hat = pl.pallas_call(
         functools.partial(backward_kernel, micros, seqs, chans),
-        in_specs=[vmem()] * (len(arrays) - 1) + [hbm],
+        in_specs=[vmem()] * len(arrays),
         out_specs=vmem(),
         out_shape=shape_of((seqs, stride, width), bf16),
         scratch_shapes=backward_scratch(micros, seqs, chans, stride, width, lane),

time: 77.3 us -> 76.9 us (level)
  Pallas kernels: 21.6 us -> 20.5 us
  transfers between devices with their start and end apart: 23 -> 23, of which waited for: 10 -> 10; matrix products, arithmetic and copies ran while one was open for 0% -> 0% of each run, Pallas kernels for 24% -> 23%
where the time goes in v7:
time: 76.9 us; the launch traced here: 76.3 us
  starting transfers between devices  37.2 us (48%)
  Pallas kernels  20.5 us (27%)
  waiting for transfers between devices  16.4 us (21%)
  local copies, waits for them, and re-layouts  1.35 us (2%)
  between operations  0.82 us (1%)
    all_to_all x4, starting transfers between devices, exchange(): return lax.all_to_all(x, axis, 0, 0, tiled=True)  21.1 us
    all_to_all x4, waiting for transfers between devices, exchange(): return lax.all_to_all(x, axis, 0, 0, tiled=True)  14.1 us
    ppermute x15, starting transfers between devices, cross(): return lax.ppermute(x, 'chan', [(i, i ^ by) for i in range(peers)])  9.56 us
    pallas_call x6, Pallas kernels, kernel_call(): pl.pallas_call(kernel, in_specs=ins, out_specs=[vmem()] * len(outs), out_...  6.05 us
    pallas_call x1, Pallas kernels, shards(): pl.pallas_call(functools.partial(backward_kernel, micros, seqs, chans), i...  4.49 us
    ppermute x3, starting transfers between devices, shards(): lax.ppermute(block, 'seq', [(i, i ^ k + 1 << 1) for i in range(seqs)])  4.39 us
    pallas_call x1, Pallas kernels, shards(): pl.pallas_call(functools.partial(table_kernel, chans, seqs, width), in_sp...  3.52 us
    pallas_call x1, Pallas kernels, shards(): pl.pallas_call(functools.partial(forward_kernel, micros, seqs, chans, pee...  3.23 us
  transfers between devices with their start and end apart: 23, of which 10 were waited for; matrix products, arithmetic and copies ran while one was open for 0% of the time, Pallas kernels for 23%

profile of v7, /device:TPU:0, one launch (start us, length us, event | category | flops | bytes accessed | tf_op | source)
XLA Modules:
  0.0 76.3 jit_solution(17859164778110018438)
XLA Ops:
  0.6 1.7 %pack.1 = (bf16[8,80,128]{2,1,0:T(8,128)(2,1)}, f32[8,128]{1,0:T(8,128)S(1)}) custom-call(bf16[4,128,128]{2,1,0:T(8,128)(2,1)} %tokens_ref.5), custom_call_target="tpu_custom_call" | custom-call | flops 1000000000 | bytes 3000000 | tf_op jit(solution)/shard_map/pack/pallas_call | solution.py:886
  2.4 7.3 %all-to-all-start = ((bf16[8,80,128]{2,1,0:T(8,128)(2,1)}), bf16[8,80,128]{2,1,0:T(8,128)(2,1)S(1)}, u32[]{:S(2)}, u32[]{:S(2)}) async-start(bf16[8,80,128]{2,1,0:T(8,128)(2,1)} %get-tuple-element.66), calls=%async_computation | async-start | bytes 327680 | tf_op jit(solution)/shard_map/all_to_all | solution.py:880
  9.6 0.0 copy-start.8
  9.7 0.6 copy-done.7
  10.3 0.0 copy-done.8
  10.3 1.5 %weights.1 = (bf16[1168,128]{1,0:T(8,128)(2,1)S(1)}, bf16[1168,128]{1,0:T(8,128)(2,1)S(1)}, bf16[1168,128]{1,0:T(8,128)(2,1)S(1)}, bf16[1168,128]{1,0:T(8,128)(2,1)S(1)}) custom-call(s32[1]{0:T(128)} %bitcast.9.rank_ref, f32[1,128]{1,0:T(1,128)S(1)} %bitcast.28, f32[1,128]{1,0:T(1,128)S(1)} %bitcast.30, bf16[4,128,128]{2,1,0:T(8,128)(2,1)} %cot_ref.3, ...), custom_call_target="tpu_custom_call" | custom-call | flops 1000000000 | bytes 3000000 | tf_op jit(solution)/shard_map/weights/pallas_call | solution.py:907
  11.8 0.0 copy-start.4
  11.8 0.0 copy-start.5
  11.8 0.0 copy-start.6
  11.9 0.6 copy-done.4
  12.5 0.0 copy-done.5
  12.5 0.0 copy-done.6
  12.5 3.5 %tables.1 = (f32[18,16,128]{2,1,0:T(8,128)S(1)}, f32[256,128]{1,0:T(8,128)S(1)}, f32[16,16,128]{2,1,0:T(8,128)S(1)}, f32[32,128]{1,0:T(8,128)S(1)}) custom-call(s32[1]{0:T(128)} %bitcast.rank_ref, s32[4]{0:T(128)S(1)} %bitcast.32, f32[128]{0:T(128)S(1)} %copy-done.4, f32[128]{0:T(128)S(1)} %copy-done.5, f32[128]{0:T(128)S(1)} %copy-done.6, ...), custom_call_target="tpu_custom_call" | custom-call | flops 2000000000 | bytes 6000000 | tf_op jit(solution)/shard_map/tables/pallas_call | solution.py:919
  16.0 1.2 %all-to-all-done.got_ref = bf16[8,80,128]{2,1,0:T(8,128)(2,1)S(1)} async-done(((bf16[8,80,128]{2,1,0:T(8,128)(2,1)}), bf16[8,80,128]{2,1,0:T(8,128)(2,1)S(1)}, u32[]{:S(2)}, u32[]{:S(2)}) %all-to-all-start) | async-done | bytes 163872 | tf_op jit(solution)/shard_map/all_to_all | solution.py:880
  17.2 0.0 collective-permute-start.2
  17.2 1.5 %collective-permute-start.1 = (bf16[8,16,128]{2,1,0:T(8,128)(2,1)S(1)}, bf16[8,16,128]{2,1,0:T(8,128)(2,1)S(1)}, u32[]{:S(2)}, u32[]{:S(2)}) collective-permute-start(bf16[8,16,128]{2,1,0:T(8,128)(2,1)S(1)} %slice.3), channel_id=1, source_target_pairs={{0,2},{1,3},{2,0},{3,1},{4,6},{5,7},{6,4},{7,5},{8,10},{9,11},{10,... | collective-permute-start | bytes 98312 | tf_op jit(solution)/shard_map/ppermute | solution.py:883
  18.8 0.3 collective-permute-start
  19.1 0.2 collective-permute-start.6
  19.3 1.3 %collective-permute-start.7 = (bf16[1168,128]{1,0:T(8,128)(2,1)S(1)}, bf16[1168,128]{1,0:T(8,128)(2,1)S(1)}, u32[]{:S(2)}, u32[]{:S(2)}) collective-permute-start(bf16[1168,128]{1,0:T(8,128)(2,1)S(1)} %get-tuple-element.85), channel_id=1, source_target_pairs={{0,2},{1,3},{2,0},{3,1},{4,6},{5,7},{6,4},{7,5},{8,10},{9,11},{10,... | collective-permute-start | bytes 897032 | tf_op jit(solution)/shard_map/ppermute | solution.py:883
  20.6 0.2 collective-permute-done.2.refs_2_
  20.8 0.1 collective-permute-start.8
  20.9 0.3 collective-permute-done.1.refs_1_
  21.3 0.0 collective-permute-done.refs_0_
  21.3 3.2 %mixer_forward.1 = (bf16[512,128]{1,0:T(8,128)(2,1)}, f32[64,128]{1,0:T(8,128)S(1)}, f32[16,32,128]{2,1,0:T(8,128)S(1)}, f32[16,32,128]{2,1,0:T(8,128)S(1)}) custom-call(bf16[8,80,128]{2,1,0:T(8,128)(2,1)S(1)} %all-to-all-done.got_ref, f32[18,16,128]{2,1,0:T(8,128)S(1)} %get-tuple-element.77.const_ref, f32[256,128]{1,0:T(8,128)S(1)} %get-tuple-element.78.rise_ref, ...), custom_call_target="tpu_custom_call" | custom-call | flops 5000000000 | bytes 15000000 | tf_op jit(solution)/shard_map/mixer_forward/pallas_call | solution.py:946
  24.5 5.0 %all-to-all-start.1 = ((bf16[32,16,128]{2,1,0:T(8,128)(2,1)}), bf16[32,16,128]{2,1,0:T(8,128)(2,1)S(1)}, u32[]{:S(2)}, u32[]{:S(2)}) async-start(bf16[32,16,128]{2,1,0:T(8,128)(2,1)} %bitcast.10), calls=%async_computation.1 | async-start | bytes 262144 | tf_op jit(solution)/shard_map/all_to_all | solution.py:880
  29.5 1.6 %collective-permute-start.11 = (f32[8,128]{1,0:T(8,128)S(1)}, f32[8,128]{1,0:T(8,128)S(1)}, u32[]{:S(2)}, u32[]{:S(2)}) collective-permute-start(f32[8,128]{1,0:T(8,128)S(1)} %get-tuple-element.96.refs_0_), channel_id=1, source_target_pairs={{0,3},{1,2},{2,1},{3,0},{4,7},{5,6},{6,5},{7,4},{8,11},{9,10},{10,... | collective-permute-start | bytes 12296 | tf_op jit(solution)/shard_map/ppermute | solution.py:883
  31.1 0.4 collective-permute-start.10
  31.4 0.1 pad_add_fusion.place_ref
  31.5 5.7 %all-to-all-done.1 = bf16[32,16,128]{2,1,0:T(8,128)(2,1)S(1)} async-done(((bf16[32,16,128]{2,1,0:T(8,128)(2,1)}), bf16[32,16,128]{2,1,0:T(8,128)(2,1)S(1)}, u32[]{:S(2)}, u32[]{:S(2)}) %all-to-all-start.1) | async-done | bytes 131104 | tf_op jit(solution)/shard_map/all_to_all | solution.py:880
  37.2 0.0 collective-permute-done.6.refs_1_
  37.2 0.4 collective-permute-start.5
  37.6 0.0 collective-permute-done.7.refs_2_
  37.6 1.3 %collective-permute-start.4 = (bf16[512,128]{1,0:T(8,128)(2,1)S(1)}, bf16[512,128]{1,0:T(8,128)(2,1)S(1)}, u32[]{:S(2)}, u32[]{:S(2)}) collective-permute-start(bf16[512,128]{1,0:T(8,128)(2,1)S(1)} %bitcast.23), channel_id=1, source_target_pairs={{0,2},{1,3},{2,0},{3,1},{4,6},{5,7},{6,4},{7,5},{8,10},{9,11},{10,... | collective-permute-start | bytes 393224 | tf_op jit(solution)/shard_map/ppermute | solution.py:883
  39.0 0.0 collective-permute-done.8.refs_3_
  39.0 0.1 collective-permute-start.3
  39.1 1.9 %project.1 = bf16[512,128]{1,0:T(8,128)(2,1)} custom-call(s32[2]{0:T(128)S(1)} %pad_add_fusion.place_ref, s32[4]{0:T(128)S(1)} %bitcast.33, bf16[512,128]{1,0:T(8,128)(2,1)S(1)} %bitcast.25, bf16[1168,128]{1,0:T(8,128)(2,1)S(1)} %get-tuple-element.83.refs_0_, bf16[1168,128]{1,0:T(8,128)(2,1)S(1)} %collective-permute-done.6.refs_1_, ...), custom_call_target="tpu_custom_call" | custom-call | flops 2000000000 | bytes 6000000 | tf_op jit(solution)/shard_map/project/pallas_call | solution.py:824
  41.1 4.2 %all-to-all-start.2 = ((bf16[32,16,128]{2,1,0:T(8,128)(2,1)}), bf16[32,16,128]{2,1,0:T(8,128)(2,1)S(1)}, u32[]{:S(2)}, u32[]{:S(2)}) async-start(bf16[32,16,128]{2,1,0:T(8,128)(2,1)} %bitcast.12), calls=%async_computation.2 | async-start | bytes 262144 | tf_op jit(solution)/shard_map/all_to_all | solution.py:880
  45.3 0.0 copy-start.11
  45.3 0.0 collective-permute-done.5.refs_3_
  45.3 0.3 collective-permute-start.9
  45.6 0.2 collective-permute-done.4.refs_2_
  45.8 0.0 collective-permute-done.3.refs_1_
  45.8 1.8 %output.1 = (bf16[4,128,128]{2,1,0:T(8,128)(2,1)}, f32[2,136,128]{2,1,0:T(8,128)S(1)}, bf16[2,136,128]{2,1,0:T(8,128)(2,1)S(1)}, bf16[2,136,128]{2,1,0:T(8,128)(2,1)S(1)}, bf16[2,136,128]{2,1,0:T(8,128)(2,1)S(1)}) custom-call(s32[1]{0:T(128)} %bitcast.rank_ref, s32[4]{0:T(128)S(1)} %bitcast.34, s32[4]{0:T(128)S(1)} %iota_xor_fusion.order_ref, ...), custom_call_target="tpu_custom_call" | custom-call | flops 2000000000 | bytes 6000000 | tf_op jit(solution)/shard_map/output/pallas_call | solution.py:824
  47.6 1.5 %collective-permute-start.12 = (bf16[2,136,128]{2,1,0:T(8,128)(2,1)S(1)}, bf16[2,136,128]{2,1,0:T(8,128)(2,1)S(1)}, u32[]{:S(2)}, u32[]{:S(2)}) collective-permute-start(bf16[2,136,128]{2,1,0:T(8,128)(2,1)S(1)} %get-tuple-element.92), channel_id=1, source_target_pairs={{0,8},{4,12},{8,0},{12,4},{16,24},{20,28},{24,16},{28,20},{1,9},{5... | collective-permute-start | bytes 208904 | tf_op jit(solution)/shard_map/ppermute | solution.py:1011
  49.2 2.4 %collective-permute-start.13 = (bf16[2,136,128]{2,1,0:T(8,128)(2,1)S(1)}, bf16[2,136,128]{2,1,0:T(8,128)(2,1)S(1)}, u32[]{:S(2)}, u32[]{:S(2)}) collective-permute-start(bf16[2,136,128]{2,1,0:T(8,128)(2,1)S(1)} %get-tuple-element.93), channel_id=1, source_target_pairs={{0,16},{4,20},{8,24},{12,28},{16,0},{20,4},{24,8},{28,12},{1,17},{... | collective-permute-start | bytes 208904 | tf_op jit(solution)/shard_map/ppermute | solution.py:1011
  51.6 0.0 collective-permute-done.11.refs_3_
  51.6 0.4 collective-permute-start.14
  52.0 0.0 collective-permute-done.10.refs_2_
  52.0 1.0 %all-to-all-done.2 = bf16[32,16,128]{2,1,0:T(8,128)(2,1)S(1)} async-done(((bf16[32,16,128]{2,1,0:T(8,128)(2,1)}), bf16[32,16,128]{2,1,0:T(8,128)(2,1)S(1)}, u32[]{:S(2)}, u32[]{:S(2)}) %all-to-all-start.2) | async-done | bytes 131104 | tf_op jit(solution)/shard_map/all_to_all | solution.py:880
  53.0 4.5 %mixer_backward.1 = bf16[8,128,128]{2,1,0:T(8,128)(2,1)} custom-call(bf16[8,80,128]{2,1,0:T(8,128)(2,1)S(1)} %all-to-all-done.got_ref, bf16[512,128]{1,0:T(8,128)(2,1)S(1)} %bitcast.27, f32[64,128]{1,0:T(8,128)S(1)} %get-tuple-element.89.norm_ref, f32[18,16,128]{2,1,0:T(8,128)S(1)} %get-tuple-element.77.const_ref, ...), custom_call_target="tpu_custom_call" | custom-call | flops 5000000000 | bytes 15000000 | tf_op jit(solution)/shard_map/mixer_backward/pallas_call | solution.py:1017
  57.5 0.3 collective-permute-done.13.refs_1_
  57.8 0.0 collective-permute-done.14.refs_2_
  57.8 4.7 %all-to-all-start.3 = ((bf16[8,128,128]{2,1,0:T(8,128)(2,1)}), bf16[8,128,128]{2,1,0:T(8,128)(2,1)S(1)}, u32[]{:S(2)}, u32[]{:S(2)}) async-start(bf16[8,128,128]{2,1,0:T(8,128)(2,1)} %mixer_backward.1), calls=%async_computation.3 | async-start | bytes 524288 | tf_op jit(solution)/shard_map/all_to_all | solution.py:880
  62.6 2.1 %collective-permute-start.18 = (bf16[136,128]{1,0:T(8,128)(2,1)S(1)}, bf16[136,128]{1,0:T(8,128)(2,1)S(1)}, u32[]{:S(2)}, u32[]{:S(2)}) collective-permute-start(bf16[136,128]{1,0:T(8,128)(2,1)S(1)} %get-tuple-element.115), channel_id=1, source_target_pairs={{0,4},{4,0},{8,12},{12,8},{16,20},{20,16},{24,28},{28,24},{1,5},{5... | collective-permute-start | bytes 104456 | tf_op jit(solution)/shard_map/ppermute | solution.py:1037
  64.6 6.2 %all-to-all-done.3.got_ref = bf16[8,128,128]{2,1,0:T(8,128)(2,1)S(1)} async-done(((bf16[8,128,128]{2,1,0:T(8,128)(2,1)}), bf16[8,128,128]{2,1,0:T(8,128)(2,1)S(1)}, u32[]{:S(2)}, u32[]{:S(2)}) %all-to-all-start.3) | async-done | bytes 262176 | tf_op jit(solution)/shard_map/all_to_all | solution.py:880
  70.9 0.2 sums.1
  71.1 0.1 collective-permute-start.17
  71.2 1.6 %collective-permute-start.16 = (f32[8,128]{1,0:T(8,128)S(1)}, f32[8,128]{1,0:T(8,128)S(1)}, u32[]{:S(2)}, u32[]{:S(2)}) collective-permute-start(f32[8,128]{1,0:T(8,128)S(1)} %get-tuple-element.102.refs_0_), channel_id=1, source_target_pairs={{0,2},{1,3},{2,0},{3,1},{4,6},{5,7},{6,4},{7,5},{8,10},{9,11},{10,... | collective-permute-start | bytes 12296 | tf_op jit(solution)/shard_map/ppermute | solution.py:883
  72.7 0.3 collective-permute-start.15
  73.0 0.6 last.1
  73.7 0.5 collective-permute-done.17.refs_3_
  74.2 0.7 collective-permute-done.16.refs_2_
  74.8 0.0 collective-permute-done.15.refs_1_
  74.8 1.4 %final.1 = (f32[4,128,128]{2,1,0:T(8,128)}, f32[2,64,128]{2,1,0:T(8,128)}, f32[2,64,128]{2,1,0:T(8,128)}, f32[2,64,128]{2,1,0:T(8,128)}, f32[1,128]{1,0:T(1,128)}, /*index=5*/f32[1,128]{1,0:T(1,128)}, f32[1,128]{1,0:T(1,128)}) custom-call(s32[1]{0:T(128)} %bitcast.rank_ref, s32[4]{0:T(128)S(1)} %bitcast.35, f32[8,128,128]{2,1,0:T(8,128)S(1)} %get-tuple-element.100.head_ref, ...), custom_call_target="tpu_custom_call" | custom-call | flops 2000000000 | bytes 6000000 | tf_op jit(solution)/shard_map/final/pallas_call | solution.py:824
  (20 shorter events, 0.1 us)
Async XLA Ops:
  2.4 14.8 %all-to-all-start = ((bf16[8,80,128]{2,1,0:T(8,128)(2,1)}), bf16[8,80,128]{2,1,0:T(8,128)(2,1)S(1)}, u32[]{:S(2)}, u32[]{:S(2)}) async-start(bf16[8,80,128]{2,1,0:T(8,128)(2,1)} %get-tuple-element.66), calls=%async_computation | async-start | bytes 327680 | tf_op jit(solution)/shard_map/all_to_all | solution.py:880
  9.6 0.7 copy-start.7
  9.6 0.7 copy-start.8
  10.3 1.5 %copy-start.9 = (s32[4,1]{0,1:T(1,128)S(1)}, s32[4,1]{0,1:T(1,128)}, u32[]{:S(2)}) copy-start(s32[4,1]{0,1:T(1,128)} %param.16) | copy-start | bytes 52
  11.8 0.7 copy-start.4
  11.8 0.7 copy-start.5
  11.8 0.7 copy-start.6
  17.2 3.6 %collective-permute-start.2 = (bf16[8,16,128]{2,1,0:T(8,128)(2,1)S(1)}, bf16[8,16,128]{2,1,0:T(8,128)(2,1)S(1)}, u32[]{:S(2)}, u32[]{:S(2)}) collective-permute-start(bf16[8,16,128]{2,1,0:T(8,128)(2,1)S(1)} %slice.3), channel_id=1, source_target_pairs={{0,3},{1,2},{2,1},{3,0},{4,7},{5,6},{6,5},{7,4},{8,11},{9,10},{10,... | collective-permute-start | bytes 98312 | tf_op jit(solution)/shard_map/ppermute | solution.py:883
  17.2 4.0 %collective-permute-start.1 = (bf16[8,16,128]{2,1,0:T(8,128)(2,1)S(1)}, bf16[8,16,128]{2,1,0:T(8,128)(2,1)S(1)}, u32[]{:S(2)}, u32[]{:S(2)}) collective-permute-start(bf16[8,16,128]{2,1,0:T(8,128)(2,1)S(1)} %slice.3), channel_id=1, source_target_pairs={{0,2},{1,3},{2,0},{3,1},{4,6},{5,7},{6,4},{7,5},{8,10},{9,11},{10,... | collective-permute-start | bytes 98312 | tf_op jit(solution)/shard_map/ppermute | solution.py:883
  18.8 2.5 %collective-permute-start = (bf16[8,16,128]{2,1,0:T(8,128)(2,1)S(1)}, bf16[8,16,128]{2,1,0:T(8,128)(2,1)S(1)}, u32[]{:S(2)}, u32[]{:S(2)}) collective-permute-start(bf16[8,16,128]{2,1,0:T(8,128)(2,1)S(1)} %slice.3), channel_id=1, source_target_pairs={{0,1},{1,0},{2,3},{3,2},{4,5},{5,4},{6,7},{7,6},{8,9},{9,8},{10,11... | collective-permute-start | bytes 98312 | tf_op jit(solution)/shard_map/ppermute | solution.py:883
  19.1 18.1 %collective-permute-start.6 = (bf16[1168,128]{1,0:T(8,128)(2,1)S(1)}, bf16[1168,128]{1,0:T(8,128)(2,1)S(1)}, u32[]{:S(2)}, u32[]{:S(2)}) collective-permute-start(bf16[1168,128]{1,0:T(8,128)(2,1)S(1)} %get-tuple-element.84), channel_id=1, source_target_pairs={{0,1},{1,0},{2,3},{3,2},{4,5},{5,4},{6,7},{7,6},{8,9},{9,8},{10,11... | collective-permute-start | bytes 897032 | tf_op jit(solution)/shard_map/ppermute | solution.py:883
  19.3 18.4 %collective-permute-start.7 = (bf16[1168,128]{1,0:T(8,128)(2,1)S(1)}, bf16[1168,128]{1,0:T(8,128)(2,1)S(1)}, u32[]{:S(2)}, u32[]{:S(2)}) collective-permute-start(bf16[1168,128]{1,0:T(8,128)(2,1)S(1)} %get-tuple-element.85), channel_id=1, source_target_pairs={{0,2},{1,3},{2,0},{3,1},{4,6},{5,7},{6,4},{7,5},{8,10},{9,11},{10,... | collective-permute-start | bytes 897032 | tf_op jit(solution)/shard_map/ppermute | solution.py:883
  20.8 18.1 %collective-permute-start.8 = (bf16[1168,128]{1,0:T(8,128)(2,1)S(1)}, bf16[1168,128]{1,0:T(8,128)(2,1)S(1)}, u32[]{:S(2)}, u32[]{:S(2)}) collective-permute-start(bf16[1168,128]{1,0:T(8,128)(2,1)S(1)} %get-tuple-element.86), channel_id=1, source_target_pairs={{0,3},{1,2},{2,1},{3,0},{4,7},{5,6},{6,5},{7,4},{8,11},{9,10},{10,... | collective-permute-start | bytes 897032 | tf_op jit(solution)/shard_map/ppermute | solution.py:883
  24.5 13.2 %copy-start.10 = (f32[16,32,128]{2,1,0:T(8,128)}, f32[16,32,128]{2,1,0:T(8,128)S(1)}, u32[]{:S(2)}) copy-start(f32[16,32,128]{2,1,0:T(8,128)S(1)} %get-tuple-element.91.start_ref) | copy-start | bytes 786436
  24.5 12.7 %all-to-all-start.1 = ((bf16[32,16,128]{2,1,0:T(8,128)(2,1)}), bf16[32,16,128]{2,1,0:T(8,128)(2,1)S(1)}, u32[]{:S(2)}, u32[]{:S(2)}) async-start(bf16[32,16,128]{2,1,0:T(8,128)(2,1)} %bitcast.10), calls=%async_computation.1 | async-start | bytes 262144 | tf_op jit(solution)/shard_map/all_to_all | solution.py:880
  29.5 22.1 %collective-permute-start.11 = (f32[8,128]{1,0:T(8,128)S(1)}, f32[8,128]{1,0:T(8,128)S(1)}, u32[]{:S(2)}, u32[]{:S(2)}) collective-permute-start(f32[8,128]{1,0:T(8,128)S(1)} %get-tuple-element.96.refs_0_), channel_id=1, source_target_pairs={{0,3},{1,2},{2,1},{3,0},{4,7},{5,6},{6,5},{7,4},{8,11},{9,10},{10,... | collective-permute-start | bytes 12296 | tf_op jit(solution)/shard_map/ppermute | solution.py:883
  31.1 21.0 %collective-permute-start.10 = (f32[8,128]{1,0:T(8,128)S(1)}, f32[8,128]{1,0:T(8,128)S(1)}, u32[]{:S(2)}, u32[]{:S(2)}) collective-permute-start(f32[8,128]{1,0:T(8,128)S(1)} %get-tuple-element.96.refs_0_), channel_id=1, source_target_pairs={{0,2},{1,3},{2,0},{3,1},{4,6},{5,7},{6,4},{7,5},{8,10},{9,11},{10,... | collective-permute-start | bytes 12296 | tf_op jit(solution)/shard_map/ppermute | solution.py:883
  37.2 8.1 %collective-permute-start.5 = (bf16[512,128]{1,0:T(8,128)(2,1)S(1)}, bf16[512,128]{1,0:T(8,128)(2,1)S(1)}, u32[]{:S(2)}, u32[]{:S(2)}) collective-permute-start(bf16[512,128]{1,0:T(8,128)(2,1)S(1)} %bitcast.22), channel_id=1, source_target_pairs={{0,3},{1,2},{2,1},{3,0},{4,7},{5,6},{6,5},{7,4},{8,11},{9,10},{10,... | collective-permute-start | bytes 393224 | tf_op jit(solution)/shard_map/ppermute | solution.py:883
  37.6 8.2 %collective-permute-start.4 = (bf16[512,128]{1,0:T(8,128)(2,1)S(1)}, bf16[512,128]{1,0:T(8,128)(2,1)S(1)}, u32[]{:S(2)}, u32[]{:S(2)}) collective-permute-start(bf16[512,128]{1,0:T(8,128)(2,1)S(1)} %bitcast.23), channel_id=1, source_target_pairs={{0,2},{1,3},{2,0},{3,1},{4,6},{5,7},{6,4},{7,5},{8,10},{9,11},{10,... | collective-permute-start | bytes 393224 | tf_op jit(solution)/shard_map/ppermute | solution.py:883
  39.0 6.9 %collective-permute-start.3 = (bf16[512,128]{1,0:T(8,128)(2,1)S(1)}, bf16[512,128]{1,0:T(8,128)(2,1)S(1)}, u32[]{:S(2)}, u32[]{:S(2)}) collective-permute-start(bf16[512,128]{1,0:T(8,128)(2,1)S(1)} %bitcast.24), channel_id=1, source_target_pairs={{0,1},{1,0},{2,3},{3,2},{4,5},{5,4},{6,7},{7,6},{8,9},{9,8},{10,11... | collective-permute-start | bytes 393224 | tf_op jit(solution)/shard_map/ppermute | solution.py:883
  39.1 6.7 %copy-start.2 = (bf16[4,128,128]{2,1,0:T(8,128)(2,1)S(1)}, bf16[4,128,128]{2,1,0:T(8,128)(2,1)}, u32[]{:S(2)}) copy-start(bf16[4,128,128]{2,1,0:T(8,128)(2,1)} %tokens_ref.5) | copy-start | bytes 393220
  39.1 6.7 %copy-start.3 = (bf16[4,128,128]{2,1,0:T(8,128)(2,1)S(1)}, bf16[4,128,128]{2,1,0:T(8,128)(2,1)}, u32[]{:S(2)}) copy-start(bf16[4,128,128]{2,1,0:T(8,128)(2,1)} %cot_ref.3) | copy-start | bytes 393220
  41.1 4.8 %copy-start = (bf16[512,128]{1,0:T(8,128)(2,1)S(1)}, bf16[512,128]{1,0:T(8,128)(2,1)}, u32[]{:S(2)}) copy-start(bf16[512,128]{1,0:T(8,128)(2,1)} %wv_ref.1) | copy-start | bytes 393220
  41.1 4.8 %copy-start.1 = (bf16[512,128]{1,0:T(8,128)(2,1)S(1)}, bf16[512,128]{1,0:T(8,128)(2,1)}, u32[]{:S(2)}) copy-start(bf16[512,128]{1,0:T(8,128)(2,1)} %wg_ref.1) | copy-start | bytes 393220
  41.1 12.0 %all-to-all-start.2 = ((bf16[32,16,128]{2,1,0:T(8,128)(2,1)}), bf16[32,16,128]{2,1,0:T(8,128)(2,1)S(1)}, u32[]{:S(2)}, u32[]{:S(2)}) async-start(bf16[32,16,128]{2,1,0:T(8,128)(2,1)} %bitcast.12), calls=%async_computation.2 | async-start | bytes 262144 | tf_op jit(solution)/shard_map/all_to_all | solution.py:880
  45.3 7.7 %copy-start.11 = (f32[16,32,128]{2,1,0:T(8,128)S(1)}, f32[16,32,128]{2,1,0:T(8,128)}, u32[]{:S(2)}) copy-start(f32[16,32,128]{2,1,0:T(8,128)} %copy-done.10) | copy-start | bytes 786436
  45.3 6.7 %collective-permute-start.9 = (f32[8,128]{1,0:T(8,128)S(1)}, f32[8,128]{1,0:T(8,128)S(1)}, u32[]{:S(2)}, u32[]{:S(2)}) collective-permute-start(f32[8,128]{1,0:T(8,128)S(1)} %get-tuple-element.96.refs_0_), channel_id=1, source_target_pairs={{0,1},{1,0},{2,3},{3,2},{4,5},{5,4},{6,7},{7,6},{8,9},{9,8},{10,11... | collective-permute-start | bytes 12296 | tf_op jit(solution)/shard_map/ppermute | solution.py:883
  47.6 9.9 %collective-permute-start.12 = (bf16[2,136,128]{2,1,0:T(8,128)(2,1)S(1)}, bf16[2,136,128]{2,1,0:T(8,128)(2,1)S(1)}, u32[]{:S(2)}, u32[]{:S(2)}) collective-permute-start(bf16[2,136,128]{2,1,0:T(8,128)(2,1)S(1)} %get-tuple-element.92), channel_id=1, source_target_pairs={{0,8},{4,12},{8,0},{12,4},{16,24},{20,28},{24,16},{28,20},{1,9},{5... | collective-permute-start | bytes 208904 | tf_op jit(solution)/shard_map/ppermute | solution.py:1011
  49.2 8.7 %collective-permute-start.13 = (bf16[2,136,128]{2,1,0:T(8,128)(2,1)S(1)}, bf16[2,136,128]{2,1,0:T(8,128)(2,1)S(1)}, u32[]{:S(2)}, u32[]{:S(2)}) collective-permute-start(bf16[2,136,128]{2,1,0:T(8,128)(2,1)S(1)} %get-tuple-element.93), channel_id=1, source_target_pairs={{0,16},{4,20},{8,24},{12,28},{16,0},{20,4},{24,8},{28,12},{1,17},{... | collective-permute-start | bytes 208904 | tf_op jit(solution)/shard_map/ppermute | solution.py:1011
  51.6 6.2 %collective-permute-start.14 = (bf16[2,136,128]{2,1,0:T(8,128)(2,1)S(1)}, bf16[2,136,128]{2,1,0:T(8,128)(2,1)S(1)}, u32[]{:S(2)}, u32[]{:S(2)}) collective-permute-start(bf16[2,136,128]{2,1,0:T(8,128)(2,1)S(1)} %get-tuple-element.94), channel_id=1, source_target_pairs={{0,24},{4,28},{8,16},{12,20},{16,8},{20,12},{24,0},{28,4},{1,25},{... | collective-permute-start | bytes 208904 | tf_op jit(solution)/shard_map/ppermute | solution.py:1011
  57.8 13.0 %all-to-all-start.3 = ((bf16[8,128,128]{2,1,0:T(8,128)(2,1)}), bf16[8,128,128]{2,1,0:T(8,128)(2,1)S(1)}, u32[]{:S(2)}, u32[]{:S(2)}) async-start(bf16[8,128,128]{2,1,0:T(8,128)(2,1)} %mixer_backward.1), calls=%async_computation.3 | async-start | bytes 524288 | tf_op jit(solution)/shard_map/all_to_all | solution.py:880
  62.6 10.5 %collective-permute-start.18 = (bf16[136,128]{1,0:T(8,128)(2,1)S(1)}, bf16[136,128]{1,0:T(8,128)(2,1)S(1)}, u32[]{:S(2)}, u32[]{:S(2)}) collective-permute-start(bf16[136,128]{1,0:T(8,128)(2,1)S(1)} %get-tuple-element.115), channel_id=1, source_target_pairs={{0,4},{4,0},{8,12},{12,8},{16,20},{20,16},{24,28},{28,24},{1,5},{5... | collective-permute-start | bytes 104456 | tf_op jit(solution)/shard_map/ppermute | solution.py:1037
  71.1 3.1 %collective-permute-start.17 = (f32[8,128]{1,0:T(8,128)S(1)}, f32[8,128]{1,0:T(8,128)S(1)}, u32[]{:S(2)}, u32[]{:S(2)}) collective-permute-start(f32[8,128]{1,0:T(8,128)S(1)} %get-tuple-element.102.refs_0_), channel_id=1, source_target_pairs={{0,3},{1,2},{2,1},{3,0},{4,7},{5,6},{6,5},{7,4},{8,11},{9,10},{10,... | collective-permute-start | bytes 12296 | tf_op jit(solution)/shard_map/ppermute | solution.py:883
  71.2 3.7 %collective-permute-start.16 = (f32[8,128]{1,0:T(8,128)S(1)}, f32[8,128]{1,0:T(8,128)S(1)}, u32[]{:S(2)}, u32[]{:S(2)}) collective-permute-start(f32[8,128]{1,0:T(8,128)S(1)} %get-tuple-element.102.refs_0_), channel_id=1, source_target_pairs={{0,2},{1,3},{2,0},{3,1},{4,6},{5,7},{6,4},{7,5},{8,10},{9,11},{10,... | collective-permute-start | bytes 12296 | tf_op jit(solution)/shard_map/ppermute | solution.py:883
  72.7 2.1 %collective-permute-start.15 = (f32[8,128]{1,0:T(8,128)S(1)}, f32[8,128]{1,0:T(8,128)S(1)}, u32[]{:S(2)}, u32[]{:S(2)}) collective-permute-start(f32[8,128]{1,0:T(8,128)S(1)} %get-tuple-element.102.refs_0_), channel_id=1, source_target_pairs={{0,1},{1,0},{2,3},{3,2},{4,5},{5,4},{6,7},{7,6},{8,9},{9,8},{10,11... | collective-permute-start | bytes 12296 | tf_op jit(solution)/shard_map/ppermute | solution.py:883

commit v8 on v7

--- a/solution.py
+++ b/solution.py
@@ -158,11 +158,15 @@
         send_ref[:, pl.ds(m * chans, chans), :] = turned.reshape(seqs, chans, width)
     stats = jnp.concatenate(means + squares, axis=0)
     stats_ref[...] = stats
-    high = stats.astype(bf16).astype(f32)
-    tail = jnp.concatenate([high, stats - high], axis=0).astype(bf16)
+    rest, lines = stats, []
+    for _ in range(3):
+        high = rest.astype(bf16).astype(f32)
+        lines.append(high)
+        rest = rest - high
+    tail = jnp.concatenate(lines, axis=0).astype(bf16)
     tail = mm(tail, turn).astype(bf16)
     for k in range(seqs):
-        send_ref[k, pl.ds(micros * chans, 4 * micros), :] = tail
+        send_ref[k, pl.ds(micros * chans, 6 * micros), :] = tail
 
 
 def table_kernel(
@@ -326,11 +330,11 @@
     for j in range(peers):
         keep, step, at = x_keep, stride, micros * chans
         if j:
-            keep, step, at = stats_keep.at[j - 1], 4 * micros, 0
+            keep, step, at = stats_keep.at[j - 1], 6 * micros, 0
             for k in range(chunks):
                 keep[pl.ds(k * step, step), :] = stats_refs[j - 1][k].astype(f32)
-        lines = [own_rows(keep, at + q * micros, step, micros, chunks) for q in range(4)]
-        means.append(lines[0] + lines[2])
+        lines = [own_rows(keep, at + q * micros, step, micros, chunks) for q in range(5)]
+        means.append(lines[0] + lines[2] + lines[4])
         squares.append(lines[1] + lines[3])
     mean, inverse = merge(means, squares, chans * chunks)
     norm_ref[pl.ds(0, rows), :] = mean
@@ -400,8 +404,8 @@
     rows = micros * chunks
     return [
         pltpu.VMEM((rows * chans, width), f32),
-        pltpu.VMEM((chunks * micros * (chans + 4), width), f32),
-        pltpu.VMEM((peers - 1, 4 * rows, width), f32),
+        pltpu.VMEM((chunks * micros * (chans + 6), width), f32),
+        pltpu.VMEM((peers - 1, 6 * rows, width), f32),
         pltpu.VMEM((chans, 4 * rows, width), bf16),
         pltpu.VMEM((chans, 2 * rows, 2 * width), bf16),
         pltpu.VMEM((chans, 2 * rows, lane), bf16),
@@ -611,7 +615,7 @@
     return [
         pltpu.VMEM((3 * chans, lane), f32),
         pltpu.VMEM((chunks * stride, width), f32),
-        pltpu.VMEM((chunks * micros * (chans + 4), width), f32),
+        pltpu.VMEM((chunks * micros * (chans + 6), width), f32),
         pltpu.VMEM((rows * chans, width), f32),
         pltpu.VMEM((chans, rows, width), f32),
         pltpu.VMEM((chans, rows, width), f32),
@@ -888,7 +892,7 @@
         in_specs=[hbm],
         out_specs=[vmem()] * 2,
         out_shape=[
-            shape_of((seqs, micros * (chans + 4), width), bf16),
+            shape_of((seqs, micros * (chans + 6), width), bf16),
             shape_of((2 * micros, width)),
         ],
         scratch_shapes=[

time: 76.9 us -> 76.8 us (level)
  starting transfers between devices: 37.2 us -> 36.1 us
  waiting for transfers between devices: 16.4 us -> 17.4 us
    ppermute x15, waiting for transfers between devices: 1.93 us -> 3.37 us  [cross(): return lax.ppermute(x, 'chan', [(i, i ^ by) for i in range(peers)])]
    all_to_all x4, starting transfers between devices: 21.1 us -> 20.2 us  [exchange(): return lax.all_to_all(x, axis, 0, 0, tiled=True)]
where the time goes in v8:
time: 76.8 us; the launch traced here: 76.2 us
  starting transfers between devices  36.1 us (47%)
  Pallas kernels  20.4 us (27%)
  waiting for transfers between devices  17.4 us (23%)
  local copies, waits for them, and re-layouts  1.35 us (2%)
  between operations  0.82 us (1%)
    all_to_all x4, starting transfers between devices, exchange(): return lax.all_to_all(x, axis, 0, 0, tiled=True)  20.2 us
    all_to_all x4, waiting for transfers between devices, exchange(): return lax.all_to_all(x, axis, 0, 0, tiled=True)  13.7 us
    ppermute x15, starting transfers between devices, cross(): return lax.ppermute(x, 'chan', [(i, i ^ by) for i in range(peers)])  9.45 us
    pallas_call x6, Pallas kernels, kernel_call(): pl.pallas_call(kernel, in_specs=ins, out_specs=[vmem()] * len(outs), out_...  6.06 us
    pallas_call x1, Pallas kernels, shards(): pl.pallas_call(functools.partial(backward_kernel, micros, seqs, chans), i...  4.44 us
    ppermute x3, starting transfers between devices, shards(): lax.ppermute(block, 'seq', [(i, i ^ k + 1 << 1) for i in range(seqs)])  4.39 us
    pallas_call x1, Pallas kernels, shards(): pl.pallas_call(functools.partial(table_kernel, chans, seqs, width), in_sp...  3.52 us
    ppermute x15, waiting for transfers between devices, cross(): return lax.ppermute(x, 'chan', [(i, i ^ by) for i in range(peers)])  3.37 us
  transfers between devices with their start and end apart: 23, of which 10 were waited for; matrix products, arithmetic and copies ran while one was open for 0% of the time, Pallas kernels for 23%

profile of v8, /device:TPU:0, one launch (start us, length us, event | category | flops | bytes accessed | tf_op | source)
XLA Modules:
  0.0 76.2 jit_solution(9284961986716647783)
XLA Ops:
  0.6 1.7 %pack.1 = (bf16[8,88,128]{2,1,0:T(8,128)(2,1)}, f32[8,128]{1,0:T(8,128)S(1)}) custom-call(bf16[4,128,128]{2,1,0:T(8,128)(2,1)} %tokens_ref.5), custom_call_target="tpu_custom_call" | custom-call | flops 1000000000 | bytes 3000000 | tf_op jit(solution)/shard_map/pack/pallas_call | solution.py:890
  2.4 7.3 %all-to-all-start = ((bf16[8,88,128]{2,1,0:T(8,128)(2,1)}), bf16[8,88,128]{2,1,0:T(8,128)(2,1)S(1)}, u32[]{:S(2)}, u32[]{:S(2)}) async-start(bf16[8,88,128]{2,1,0:T(8,128)(2,1)} %get-tuple-element.66), calls=%async_computation | async-start | bytes 360448 | tf_op jit(solution)/shard_map/all_to_all | solution.py:884
  9.7 0.0 copy-start.8
  9.7 0.6 copy-done.7
  10.3 0.0 copy-done.8
  10.3 1.5 %weights.1 = (bf16[1168,128]{1,0:T(8,128)(2,1)S(1)}, bf16[1168,128]{1,0:T(8,128)(2,1)S(1)}, bf16[1168,128]{1,0:T(8,128)(2,1)S(1)}, bf16[1168,128]{1,0:T(8,128)(2,1)S(1)}) custom-call(s32[1]{0:T(128)} %bitcast.9.rank_ref, f32[1,128]{1,0:T(1,128)S(1)} %bitcast.28, f32[1,128]{1,0:T(1,128)S(1)} %bitcast.30, bf16[4,128,128]{2,1,0:T(8,128)(2,1)} %cot_ref.3, ...), custom_call_target="tpu_custom_call" | custom-call | flops 1000000000 | bytes 3000000 | tf_op jit(solution)/shard_map/weights/pallas_call | solution.py:911
  11.8 0.0 copy-start.4
  11.8 0.0 copy-start.5
  11.9 0.0 copy-start.6
  11.9 0.6 copy-done.4
  12.5 0.0 copy-done.5
  12.5 0.0 copy-done.6
  12.5 3.5 %tables.1 = (f32[18,16,128]{2,1,0:T(8,128)S(1)}, f32[256,128]{1,0:T(8,128)S(1)}, f32[16,16,128]{2,1,0:T(8,128)S(1)}, f32[32,128]{1,0:T(8,128)S(1)}) custom-call(s32[1]{0:T(128)} %bitcast.rank_ref, s32[4]{0:T(128)S(1)} %bitcast.32, f32[128]{0:T(128)S(1)} %copy-done.4, f32[128]{0:T(128)S(1)} %copy-done.5, f32[128]{0:T(128)S(1)} %copy-done.6, ...), custom_call_target="tpu_custom_call" | custom-call | flops 2000000000 | bytes 6000000 | tf_op jit(solution)/shard_map/tables/pallas_call | solution.py:923
  16.0 1.3 %all-to-all-done.got_ref = bf16[8,88,128]{2,1,0:T(8,128)(2,1)S(1)} async-done(((bf16[8,88,128]{2,1,0:T(8,128)(2,1)}), bf16[8,88,128]{2,1,0:T(8,128)(2,1)S(1)}, u32[]{:S(2)}, u32[]{:S(2)}) %all-to-all-start) | async-done | bytes 180256 | tf_op jit(solution)/shard_map/all_to_all | solution.py:884
  17.4 0.0 collective-permute-start.2
  17.4 1.6 %collective-permute-start.1 = (bf16[8,24,128]{2,1,0:T(8,128)(2,1)S(1)}, bf16[8,24,128]{2,1,0:T(8,128)(2,1)S(1)}, u32[]{:S(2)}, u32[]{:S(2)}) collective-permute-start(bf16[8,24,128]{2,1,0:T(8,128)(2,1)S(1)} %slice.3), channel_id=1, source_target_pairs={{0,2},{1,3},{2,0},{3,1},{4,6},{5,7},{6,4},{7,5},{8,10},{9,11},{10,... | collective-permute-start | bytes 147464 | tf_op jit(solution)/shard_map/ppermute | solution.py:887
  19.0 0.3 collective-permute-start
  19.2 0.2 collective-permute-start.6
  19.5 1.3 %collective-permute-start.7 = (bf16[1168,128]{1,0:T(8,128)(2,1)S(1)}, bf16[1168,128]{1,0:T(8,128)(2,1)S(1)}, u32[]{:S(2)}, u32[]{:S(2)}) collective-permute-start(bf16[1168,128]{1,0:T(8,128)(2,1)S(1)} %get-tuple-element.85), channel_id=1, source_target_pairs={{0,2},{1,3},{2,0},{3,1},{4,6},{5,7},{6,4},{7,5},{8,10},{9,11},{10,... | collective-permute-start | bytes 897032 | tf_op jit(solution)/shard_map/ppermute | solution.py:887
  20.7 0.6 collective-permute-done.2.refs_2_
  21.3 0.9 %collective-permute-done.1.refs_1_ = bf16[8,24,128]{2,1,0:T(8,128)(2,1)S(1)} collective-permute-done((bf16[8,24,128]{2,1,0:T(8,128)(2,1)S(1)}, bf16[8,24,128]{2,1,0:T(8,128)(2,1)S(1)}, u32[]{:S(2)}, u32[]{:S(2)}) %collective-permute-start.1) | collective-permute-done | bytes 49184 | tf_op jit(solution)/shard_map/ppermute | solution.py:887
  22.2 0.0 collective-permute-done.refs_0_
  22.2 3.2 %mixer_forward.1 = (bf16[512,128]{1,0:T(8,128)(2,1)}, f32[64,128]{1,0:T(8,128)S(1)}, f32[16,32,128]{2,1,0:T(8,128)S(1)}, f32[16,32,128]{2,1,0:T(8,128)S(1)}) custom-call(bf16[8,88,128]{2,1,0:T(8,128)(2,1)S(1)} %all-to-all-done.got_ref, f32[18,16,128]{2,1,0:T(8,128)S(1)} %get-tuple-element.77.const_ref, f32[256,128]{1,0:T(8,128)S(1)} %get-tuple-element.78.rise_ref, ...), custom_call_target="tpu_custom_call" | custom-call | flops 5000000000 | bytes 15000000 | tf_op jit(solution)/shard_map/mixer_forward/pallas_call | solution.py:950
  25.4 4.5 %all-to-all-start.1 = ((bf16[32,16,128]{2,1,0:T(8,128)(2,1)}), bf16[32,16,128]{2,1,0:T(8,128)(2,1)S(1)}, u32[]{:S(2)}, u32[]{:S(2)}) async-start(bf16[32,16,128]{2,1,0:T(8,128)(2,1)} %bitcast.10), calls=%async_computation.1 | async-start | bytes 262144 | tf_op jit(solution)/shard_map/all_to_all | solution.py:884
  30.0 1.6 %collective-permute-start.11 = (f32[8,128]{1,0:T(8,128)S(1)}, f32[8,128]{1,0:T(8,128)S(1)}, u32[]{:S(2)}, u32[]{:S(2)}) collective-permute-start(f32[8,128]{1,0:T(8,128)S(1)} %get-tuple-element.96.refs_0_), channel_id=1, source_target_pairs={{0,3},{1,2},{2,1},{3,0},{4,7},{5,6},{6,5},{7,4},{8,11},{9,10},{10,... | collective-permute-start | bytes 12296 | tf_op jit(solution)/shard_map/ppermute | solution.py:887
  31.6 0.4 collective-permute-start.10
  31.9 0.1 pad_add_fusion.place_ref
  32.0 0.0 collective-permute-done.6.refs_1_
  32.0 5.7 %all-to-all-done.1 = bf16[32,16,128]{2,1,0:T(8,128)(2,1)S(1)} async-done(((bf16[32,16,128]{2,1,0:T(8,128)(2,1)}), bf16[32,16,128]{2,1,0:T(8,128)(2,1)S(1)}, u32[]{:S(2)}, u32[]{:S(2)}) %all-to-all-start.1) | async-done | bytes 131104 | tf_op jit(solution)/shard_map/all_to_all | solution.py:884
  37.7 0.4 collective-permute-start.5
  38.1 0.0 collective-permute-done.7.refs_2_
  38.1 1.4 %collective-permute-start.4 = (bf16[512,128]{1,0:T(8,128)(2,1)S(1)}, bf16[512,128]{1,0:T(8,128)(2,1)S(1)}, u32[]{:S(2)}, u32[]{:S(2)}) collective-permute-start(bf16[512,128]{1,0:T(8,128)(2,1)S(1)} %bitcast.23), channel_id=1, source_target_pairs={{0,2},{1,3},{2,0},{3,1},{4,6},{5,7},{6,4},{7,5},{8,10},{9,11},{10,... | collective-permute-start | bytes 393224 | tf_op jit(solution)/shard_map/ppermute | solution.py:887
  39.5 0.0 collective-permute-done.8.refs_3_
  39.5 0.1 collective-permute-start.3
  39.6 2.0 %project.1 = bf16[512,128]{1,0:T(8,128)(2,1)} custom-call(s32[2]{0:T(128)S(1)} %pad_add_fusion.place_ref, s32[4]{0:T(128)S(1)} %bitcast.33, bf16[512,128]{1,0:T(8,128)(2,1)S(1)} %bitcast.25, bf16[1168,128]{1,0:T(8,128)(2,1)S(1)} %get-tuple-element.83.refs_0_, bf16[1168,128]{1,0:T(8,128)(2,1)S(1)} %collective-permute-done.6.refs_1_, ...), custom_call_target="tpu_custom_call" | custom-call | flops 2000000000 | bytes 6000000 | tf_op jit(solution)/shard_map/project/pallas_call | solution.py:828
  41.6 3.7 %all-to-all-start.2 = ((bf16[32,16,128]{2,1,0:T(8,128)(2,1)}), bf16[32,16,128]{2,1,0:T(8,128)(2,1)S(1)}, u32[]{:S(2)}, u32[]{:S(2)}) async-start(bf16[32,16,128]{2,1,0:T(8,128)(2,1)} %bitcast.12), calls=%async_computation.2 | async-start | bytes 262144 | tf_op jit(solution)/shard_map/all_to_all | solution.py:884
  45.3 0.0 copy-start.11
  45.3 0.0 collective-permute-done.5.refs_3_
  45.3 0.3 collective-permute-start.9
  45.7 0.7 collective-permute-done.4.refs_2_
  46.3 0.0 collective-permute-done.3.refs_1_
  46.4 1.8 %output.1 = (bf16[4,128,128]{2,1,0:T(8,128)(2,1)}, f32[2,136,128]{2,1,0:T(8,128)S(1)}, bf16[2,136,128]{2,1,0:T(8,128)(2,1)S(1)}, bf16[2,136,128]{2,1,0:T(8,128)(2,1)S(1)}, bf16[2,136,128]{2,1,0:T(8,128)(2,1)S(1)}) custom-call(s32[1]{0:T(128)} %bitcast.rank_ref, s32[4]{0:T(128)S(1)} %bitcast.34, s32[4]{0:T(128)S(1)} %iota_xor_fusion.order_ref, ...), custom_call_target="tpu_custom_call" | custom-call | flops 2000000000 | bytes 6000000 | tf_op jit(solution)/shard_map/output/pallas_call | solution.py:828
  48.2 1.0 %collective-permute-start.12 = (bf16[2,136,128]{2,1,0:T(8,128)(2,1)S(1)}, bf16[2,136,128]{2,1,0:T(8,128)(2,1)S(1)}, u32[]{:S(2)}, u32[]{:S(2)}) collective-permute-start(bf16[2,136,128]{2,1,0:T(8,128)(2,1)S(1)} %get-tuple-element.92), channel_id=1, source_target_pairs={{0,8},{4,12},{8,0},{12,4},{16,24},{20,28},{24,16},{28,20},{1,9},{5... | collective-permute-start | bytes 208904 | tf_op jit(solution)/shard_map/ppermute | solution.py:1015
  49.2 2.4 %collective-permute-start.13 = (bf16[2,136,128]{2,1,0:T(8,128)(2,1)S(1)}, bf16[2,136,128]{2,1,0:T(8,128)(2,1)S(1)}, u32[]{:S(2)}, u32[]{:S(2)}) collective-permute-start(bf16[2,136,128]{2,1,0:T(8,128)(2,1)S(1)} %get-tuple-element.93), channel_id=1, source_target_pairs={{0,16},{4,20},{8,24},{12,28},{16,0},{20,4},{24,8},{28,12},{1,17},{... | collective-permute-start | bytes 208904 | tf_op jit(solution)/shard_map/ppermute | solution.py:1015
  51.6 0.0 collective-permute-done.11.refs_3_
  51.6 0.9 %collective-permute-start.14 = (bf16[2,136,128]{2,1,0:T(8,128)(2,1)S(1)}, bf16[2,136,128]{2,1,0:T(8,128)(2,1)S(1)}, u32[]{:S(2)}, u32[]{:S(2)}) collective-permute-start(bf16[2,136,128]{2,1,0:T(8,128)(2,1)S(1)} %get-tuple-element.94), channel_id=1, source_target_pairs={{0,24},{4,28},{8,16},{12,20},{16,8},{20,12},{24,0},{28,4},{1,25},{... | collective-permute-start | bytes 208904 | tf_op jit(solution)/shard_map/ppermute | solution.py:1015
  52.5 0.0 collective-permute-done.10.refs_2_
  52.6 0.0 collective-permute-done.9.refs_1_
  52.6 0.5 all-to-all-done.2
  53.0 4.4 %mixer_backward.1 = bf16[8,128,128]{2,1,0:T(8,128)(2,1)} custom-call(bf16[8,88,128]{2,1,0:T(8,128)(2,1)S(1)} %all-to-all-done.got_ref, bf16[512,128]{1,0:T(8,128)(2,1)S(1)} %bitcast.27, f32[64,128]{1,0:T(8,128)S(1)} %get-tuple-element.89.norm_ref, f32[18,16,128]{2,1,0:T(8,128)S(1)} %get-tuple-element.77.const_ref, ...), custom_call_target="tpu_custom_call" | custom-call | flops 5000000000 | bytes 15000000 | tf_op jit(solution)/shard_map/mixer_backward/pallas_call | solution.py:1021
  57.5 0.0 collective-permute-done.12.refs_0_
  57.5 0.4 collective-permute-done.13.refs_1_
  57.8 4.7 %all-to-all-start.3 = ((bf16[8,128,128]{2,1,0:T(8,128)(2,1)}), bf16[8,128,128]{2,1,0:T(8,128)(2,1)S(1)}, u32[]{:S(2)}, u32[]{:S(2)}) async-start(bf16[8,128,128]{2,1,0:T(8,128)(2,1)} %mixer_backward.1), calls=%async_computation.3 | async-start | bytes 524288 | tf_op jit(solution)/shard_map/all_to_all | solution.py:884
  62.6 2.1 %collective-permute-start.18 = (bf16[136,128]{1,0:T(8,128)(2,1)S(1)}, bf16[136,128]{1,0:T(8,128)(2,1)S(1)}, u32[]{:S(2)}, u32[]{:S(2)}) collective-permute-start(bf16[136,128]{1,0:T(8,128)(2,1)S(1)} %get-tuple-element.115), channel_id=1, source_target_pairs={{0,4},{4,0},{8,12},{12,8},{16,20},{20,16},{24,28},{28,24},{1,5},{5... | collective-permute-start | bytes 104456 | tf_op jit(solution)/shard_map/ppermute | solution.py:1041
  64.6 6.2 %all-to-all-done.3.got_ref = bf16[8,128,128]{2,1,0:T(8,128)(2,1)S(1)} async-done(((bf16[8,128,128]{2,1,0:T(8,128)(2,1)}), bf16[8,128,128]{2,1,0:T(8,128)(2,1)S(1)}, u32[]{:S(2)}, u32[]{:S(2)}) %all-to-all-start.3) | async-done | bytes 262176 | tf_op jit(solution)/shard_map/all_to_all | solution.py:884
  70.8 0.2 sums.1
  71.1 0.1 collective-permute-start.17
  71.1 1.6 %collective-permute-start.16 = (f32[8,128]{1,0:T(8,128)S(1)}, f32[8,128]{1,0:T(8,128)S(1)}, u32[]{:S(2)}, u32[]{:S(2)}) collective-permute-start(f32[8,128]{1,0:T(8,128)S(1)} %get-tuple-element.102.refs_0_), channel_id=1, source_target_pairs={{0,2},{1,3},{2,0},{3,1},{4,6},{5,7},{6,4},{7,5},{8,10},{9,11},{10,... | collective-permute-start | bytes 12296 | tf_op jit(solution)/shard_map/ppermute | solution.py:887
  72.7 0.3 collective-permute-start.15
  73.0 0.6 last.1
  73.6 0.5 collective-permute-done.17.refs_3_
  74.1 0.7 collective-permute-done.16.refs_2_
  74.8 0.0 collective-permute-done.15.refs_1_
  74.8 1.4 %final.1 = (f32[4,128,128]{2,1,0:T(8,128)}, f32[2,64,128]{2,1,0:T(8,128)}, f32[2,64,128]{2,1,0:T(8,128)}, f32[2,64,128]{2,1,0:T(8,128)}, f32[1,128]{1,0:T(1,128)}, /*index=5*/f32[1,128]{1,0:T(1,128)}, f32[1,128]{1,0:T(1,128)}) custom-call(s32[1]{0:T(128)} %bitcast.rank_ref, s32[4]{0:T(128)S(1)} %bitcast.35, f32[8,128,128]{2,1,0:T(8,128)S(1)} %get-tuple-element.100.head_ref, ...), custom_call_target="tpu_custom_call" | custom-call | flops 2000000000 | bytes 6000000 | tf_op jit(solution)/shard_map/final/pallas_call | solution.py:828
  (20 shorter events, 0.1 us)
Async XLA Ops:
  2.4 15.0 %all-to-all-start = ((bf16[8,88,128]{2,1,0:T(8,128)(2,1)}), bf16[8,88,128]{2,1,0:T(8,128)(2,1)S(1)}, u32[]{:S(2)}, u32[]{:S(2)}) async-start(bf16[8,88,128]{2,1,0:T(8,128)(2,1)} %get-tuple-element.66), calls=%async_computation | async-start | bytes 360448 | tf_op jit(solution)/shard_map/all_to_all | solution.py:884
  9.7 0.7 copy-start.7
  9.7 0.7 copy-start.8
  10.3 1.5 %copy-start.9 = (s32[4,1]{0,1:T(1,128)S(1)}, s32[4,1]{0,1:T(1,128)}, u32[]{:S(2)}) copy-start(s32[4,1]{0,1:T(1,128)} %param.16) | copy-start | bytes 52
  11.8 0.7 copy-start.4
  11.8 0.7 copy-start.5
  11.9 0.7 copy-start.6
  17.4 4.0 %collective-permute-start.2 = (bf16[8,24,128]{2,1,0:T(8,128)(2,1)S(1)}, bf16[8,24,128]{2,1,0:T(8,128)(2,1)S(1)}, u32[]{:S(2)}, u32[]{:S(2)}) collective-permute-start(bf16[8,24,128]{2,1,0:T(8,128)(2,1)S(1)} %slice.3), channel_id=1, source_target_pairs={{0,3},{1,2},{2,1},{3,0},{4,7},{5,6},{6,5},{7,4},{8,11},{9,10},{10,... | collective-permute-start | bytes 147464 | tf_op jit(solution)/shard_map/ppermute | solution.py:887
  17.4 4.9 %collective-permute-start.1 = (bf16[8,24,128]{2,1,0:T(8,128)(2,1)S(1)}, bf16[8,24,128]{2,1,0:T(8,128)(2,1)S(1)}, u32[]{:S(2)}, u32[]{:S(2)}) collective-permute-start(bf16[8,24,128]{2,1,0:T(8,128)(2,1)S(1)} %slice.3), channel_id=1, source_target_pairs={{0,2},{1,3},{2,0},{3,1},{4,6},{5,7},{6,4},{7,5},{8,10},{9,11},{10,... | collective-permute-start | bytes 147464 | tf_op jit(solution)/shard_map/ppermute | solution.py:887
  19.0 3.3 %collective-permute-start = (bf16[8,24,128]{2,1,0:T(8,128)(2,1)S(1)}, bf16[8,24,128]{2,1,0:T(8,128)(2,1)S(1)}, u32[]{:S(2)}, u32[]{:S(2)}) collective-permute-start(bf16[8,24,128]{2,1,0:T(8,128)(2,1)S(1)} %slice.3), channel_id=1, source_target_pairs={{0,1},{1,0},{2,3},{3,2},{4,5},{5,4},{6,7},{7,6},{8,9},{9,8},{10,11... | collective-permute-start | bytes 147464 | tf_op jit(solution)/shard_map/ppermute | solution.py:887
  19.2 12.8 %collective-permute-start.6 = (bf16[1168,128]{1,0:T(8,128)(2,1)S(1)}, bf16[1168,128]{1,0:T(8,128)(2,1)S(1)}, u32[]{:S(2)}, u32[]{:S(2)}) collective-permute-start(bf16[1168,128]{1,0:T(8,128)(2,1)S(1)} %get-tuple-element.84), channel_id=1, source_target_pairs={{0,1},{1,0},{2,3},{3,2},{4,5},{5,4},{6,7},{7,6},{8,9},{9,8},{10,11... | collective-permute-start | bytes 897032 | tf_op jit(solution)/shard_map/ppermute | solution.py:887
  19.5 18.6 %collective-permute-start.7 = (bf16[1168,128]{1,0:T(8,128)(2,1)S(1)}, bf16[1168,128]{1,0:T(8,128)(2,1)S(1)}, u32[]{:S(2)}, u32[]{:S(2)}) collective-permute-start(bf16[1168,128]{1,0:T(8,128)(2,1)S(1)} %get-tuple-element.85), channel_id=1, source_target_pairs={{0,2},{1,3},{2,0},{3,1},{4,6},{5,7},{6,4},{7,5},{8,10},{9,11},{10,... | collective-permute-start | bytes 897032 | tf_op jit(solution)/shard_map/ppermute | solution.py:887
  21.3 18.1 %collective-permute-start.8 = (bf16[1168,128]{1,0:T(8,128)(2,1)S(1)}, bf16[1168,128]{1,0:T(8,128)(2,1)S(1)}, u32[]{:S(2)}, u32[]{:S(2)}) collective-permute-start(bf16[1168,128]{1,0:T(8,128)(2,1)S(1)} %get-tuple-element.86), channel_id=1, source_target_pairs={{0,3},{1,2},{2,1},{3,0},{4,7},{5,6},{6,5},{7,4},{8,11},{9,10},{10,... | collective-permute-start | bytes 897032 | tf_op jit(solution)/shard_map/ppermute | solution.py:887
  25.4 12.6 %copy-start.10 = (f32[16,32,128]{2,1,0:T(8,128)}, f32[16,32,128]{2,1,0:T(8,128)S(1)}, u32[]{:S(2)}) copy-start(f32[16,32,128]{2,1,0:T(8,128)S(1)} %get-tuple-element.91.start_ref) | copy-start | bytes 786436
  25.4 12.3 %all-to-all-start.1 = ((bf16[32,16,128]{2,1,0:T(8,128)(2,1)}), bf16[32,16,128]{2,1,0:T(8,128)(2,1)S(1)}, u32[]{:S(2)}, u32[]{:S(2)}) async-start(bf16[32,16,128]{2,1,0:T(8,128)(2,1)} %bitcast.10), calls=%async_computation.1 | async-start | bytes 262144 | tf_op jit(solution)/shard_map/all_to_all | solution.py:884
  30.0 21.6 %collective-permute-start.11 = (f32[8,128]{1,0:T(8,128)S(1)}, f32[8,128]{1,0:T(8,128)S(1)}, u32[]{:S(2)}, u32[]{:S(2)}) collective-permute-start(f32[8,128]{1,0:T(8,128)S(1)} %get-tuple-element.96.refs_0_), channel_id=1, source_target_pairs={{0,3},{1,2},{2,1},{3,0},{4,7},{5,6},{6,5},{7,4},{8,11},{9,10},{10,... | collective-permute-start | bytes 12296 | tf_op jit(solution)/shard_map/ppermute | solution.py:887
  31.6 21.0 %collective-permute-start.10 = (f32[8,128]{1,0:T(8,128)S(1)}, f32[8,128]{1,0:T(8,128)S(1)}, u32[]{:S(2)}, u32[]{:S(2)}) collective-permute-start(f32[8,128]{1,0:T(8,128)S(1)} %get-tuple-element.96.refs_0_), channel_id=1, source_target_pairs={{0,2},{1,3},{2,0},{3,1},{4,6},{5,7},{6,4},{7,5},{8,10},{9,11},{10,... | collective-permute-start | bytes 12296 | tf_op jit(solution)/shard_map/ppermute | solution.py:887
  37.7 7.6 %collective-permute-start.5 = (bf16[512,128]{1,0:T(8,128)(2,1)S(1)}, bf16[512,128]{1,0:T(8,128)(2,1)S(1)}, u32[]{:S(2)}, u32[]{:S(2)}) collective-permute-start(bf16[512,128]{1,0:T(8,128)(2,1)S(1)} %bitcast.22), channel_id=1, source_target_pairs={{0,3},{1,2},{2,1},{3,0},{4,7},{5,6},{6,5},{7,4},{8,11},{9,10},{10,... | collective-permute-start | bytes 393224 | tf_op jit(solution)/shard_map/ppermute | solution.py:887
  38.1 8.2 %collective-permute-start.4 = (bf16[512,128]{1,0:T(8,128)(2,1)S(1)}, bf16[512,128]{1,0:T(8,128)(2,1)S(1)}, u32[]{:S(2)}, u32[]{:S(2)}) collective-permute-start(bf16[512,128]{1,0:T(8,128)(2,1)S(1)} %bitcast.23), channel_id=1, source_target_pairs={{0,2},{1,3},{2,0},{3,1},{4,6},{5,7},{6,4},{7,5},{8,10},{9,11},{10,... | collective-permute-start | bytes 393224 | tf_op jit(solution)/shard_map/ppermute | solution.py:887
  39.5 6.9 %collective-permute-start.3 = (bf16[512,128]{1,0:T(8,128)(2,1)S(1)}, bf16[512,128]{1,0:T(8,128)(2,1)S(1)}, u32[]{:S(2)}, u32[]{:S(2)}) collective-permute-start(bf16[512,128]{1,0:T(8,128)(2,1)S(1)} %bitcast.24), channel_id=1, source_target_pairs={{0,1},{1,0},{2,3},{3,2},{4,5},{5,4},{6,7},{7,6},{8,9},{9,8},{10,11... | collective-permute-start | bytes 393224 | tf_op jit(solution)/shard_map/ppermute | solution.py:887
  39.6 6.7 %copy-start.2 = (bf16[4,128,128]{2,1,0:T(8,128)(2,1)S(1)}, bf16[4,128,128]{2,1,0:T(8,128)(2,1)}, u32[]{:S(2)}) copy-start(bf16[4,128,128]{2,1,0:T(8,128)(2,1)} %tokens_ref.5) | copy-start | bytes 393220
  39.6 6.7 %copy-start.3 = (bf16[4,128,128]{2,1,0:T(8,128)(2,1)S(1)}, bf16[4,128,128]{2,1,0:T(8,128)(2,1)}, u32[]{:S(2)}) copy-start(bf16[4,128,128]{2,1,0:T(8,128)(2,1)} %cot_ref.3) | copy-start | bytes 393220
  41.6 4.8 %copy-start = (bf16[512,128]{1,0:T(8,128)(2,1)S(1)}, bf16[512,128]{1,0:T(8,128)(2,1)}, u32[]{:S(2)}) copy-start(bf16[512,128]{1,0:T(8,128)(2,1)} %wv_ref.1) | copy-start | bytes 393220
  41.6 4.8 %copy-start.1 = (bf16[512,128]{1,0:T(8,128)(2,1)S(1)}, bf16[512,128]{1,0:T(8,128)(2,1)}, u32[]{:S(2)}) copy-start(bf16[512,128]{1,0:T(8,128)(2,1)} %wg_ref.1) | copy-start | bytes 393220
  41.6 11.5 %all-to-all-start.2 = ((bf16[32,16,128]{2,1,0:T(8,128)(2,1)}), bf16[32,16,128]{2,1,0:T(8,128)(2,1)S(1)}, u32[]{:S(2)}, u32[]{:S(2)}) async-start(bf16[32,16,128]{2,1,0:T(8,128)(2,1)} %bitcast.12), calls=%async_computation.2 | async-start | bytes 262144 | tf_op jit(solution)/shard_map/all_to_all | solution.py:884
  45.3 7.7 %copy-start.11 = (f32[16,32,128]{2,1,0:T(8,128)S(1)}, f32[16,32,128]{2,1,0:T(8,128)}, u32[]{:S(2)}) copy-start(f32[16,32,128]{2,1,0:T(8,128)} %copy-done.10) | copy-start | bytes 786436
  45.3 7.2 %collective-permute-start.9 = (f32[8,128]{1,0:T(8,128)S(1)}, f32[8,128]{1,0:T(8,128)S(1)}, u32[]{:S(2)}, u32[]{:S(2)}) collective-permute-start(f32[8,128]{1,0:T(8,128)S(1)} %get-tuple-element.96.refs_0_), channel_id=1, source_target_pairs={{0,1},{1,0},{2,3},{3,2},{4,5},{5,4},{6,7},{7,6},{8,9},{9,8},{10,11... | collective-permute-start | bytes 12296 | tf_op jit(solution)/shard_map/ppermute | solution.py:887
  48.2 9.3 %collective-permute-start.12 = (bf16[2,136,128]{2,1,0:T(8,128)(2,1)S(1)}, bf16[2,136,128]{2,1,0:T(8,128)(2,1)S(1)}, u32[]{:S(2)}, u32[]{:S(2)}) collective-permute-start(bf16[2,136,128]{2,1,0:T(8,128)(2,1)S(1)} %get-tuple-element.92), channel_id=1, source_target_pairs={{0,8},{4,12},{8,0},{12,4},{16,24},{20,28},{24,16},{28,20},{1,9},{5... | collective-permute-start | bytes 208904 | tf_op jit(solution)/shard_map/ppermute | solution.py:1015
  49.2 8.7 %collective-permute-start.13 = (bf16[2,136,128]{2,1,0:T(8,128)(2,1)S(1)}, bf16[2,136,128]{2,1,0:T(8,128)(2,1)S(1)}, u32[]{:S(2)}, u32[]{:S(2)}) collective-permute-start(bf16[2,136,128]{2,1,0:T(8,128)(2,1)S(1)} %get-tuple-element.93), channel_id=1, source_target_pairs={{0,16},{4,20},{8,24},{12,28},{16,0},{20,4},{24,8},{28,12},{1,17},{... | collective-permute-start | bytes 208904 | tf_op jit(solution)/shard_map/ppermute | solution.py:1015
  51.6 6.2 %collective-permute-start.14 = (bf16[2,136,128]{2,1,0:T(8,128)(2,1)S(1)}, bf16[2,136,128]{2,1,0:T(8,128)(2,1)S(1)}, u32[]{:S(2)}, u32[]{:S(2)}) collective-permute-start(bf16[2,136,128]{2,1,0:T(8,128)(2,1)S(1)} %get-tuple-element.94), channel_id=1, source_target_pairs={{0,24},{4,28},{8,16},{12,20},{16,8},{20,12},{24,0},{28,4},{1,25},{... | collective-permute-start | bytes 208904 | tf_op jit(solution)/shard_map/ppermute | solution.py:1015
  57.8 13.0 %all-to-all-start.3 = ((bf16[8,128,128]{2,1,0:T(8,128)(2,1)}), bf16[8,128,128]{2,1,0:T(8,128)(2,1)S(1)}, u32[]{:S(2)}, u32[]{:S(2)}) async-start(bf16[8,128,128]{2,1,0:T(8,128)(2,1)} %mixer_backward.1), calls=%async_computation.3 | async-start | bytes 524288 | tf_op jit(solution)/shard_map/all_to_all | solution.py:884
  62.6 10.4 %collective-permute-start.18 = (bf16[136,128]{1,0:T(8,128)(2,1)S(1)}, bf16[136,128]{1,0:T(8,128)(2,1)S(1)}, u32[]{:S(2)}, u32[]{:S(2)}) collective-permute-start(bf16[136,128]{1,0:T(8,128)(2,1)S(1)} %get-tuple-element.115), channel_id=1, source_target_pairs={{0,4},{4,0},{8,12},{12,8},{16,20},{20,16},{24,28},{28,24},{1,5},{5... | collective-permute-start | bytes 104456 | tf_op jit(solution)/shard_map/ppermute | solution.py:1041
  71.1 3.1 %collective-permute-start.17 = (f32[8,128]{1,0:T(8,128)S(1)}, f32[8,128]{1,0:T(8,128)S(1)}, u32[]{:S(2)}, u32[]{:S(2)}) collective-permute-start(f32[8,128]{1,0:T(8,128)S(1)} %get-tuple-element.102.refs_0_), channel_id=1, source_target_pairs={{0,3},{1,2},{2,1},{3,0},{4,7},{5,6},{6,5},{7,4},{8,11},{9,10},{10,... | collective-permute-start | bytes 12296 | tf_op jit(solution)/shard_map/ppermute | solution.py:887
  71.1 3.7 %collective-permute-start.16 = (f32[8,128]{1,0:T(8,128)S(1)}, f32[8,128]{1,0:T(8,128)S(1)}, u32[]{:S(2)}, u32[]{:S(2)}) collective-permute-start(f32[8,128]{1,0:T(8,128)S(1)} %get-tuple-element.102.refs_0_), channel_id=1, source_target_pairs={{0,2},{1,3},{2,0},{3,1},{4,6},{5,7},{6,4},{7,5},{8,10},{9,11},{10,... | collective-permute-start | bytes 12296 | tf_op jit(solution)/shard_map/ppermute | solution.py:887
  72.7 2.1 %collective-permute-start.15 = (f32[8,128]{1,0:T(8,128)S(1)}, f32[8,128]{1,0:T(8,128)S(1)}, u32[]{:S(2)}, u32[]{:S(2)}) collective-permute-start(f32[8,128]{1,0:T(8,128)S(1)} %get-tuple-element.102.refs_0_), channel_id=1, source_target_pairs={{0,1},{1,0},{2,3},{3,2},{4,5},{5,4},{6,7},{7,6},{8,9},{9,8},{10,11... | collective-permute-start | bytes 12296 | tf_op jit(solution)/shard_map/ppermute | solution.py:887

commit v9 on v8

--- a/solution.py
+++ b/solution.py
@@ -397,15 +397,15 @@
             act_keep[pl.ds(m * chunks * chans + channel, chunks, stride=chans), :] = act[
                 m * chunks : (m + 1) * chunks
             ]
-    act_ref[...] = act_keep[...].astype(bf16)
+    act_ref[...] = act_keep[: rows * chans].astype(bf16)
 
 
 def forward_scratch(micros, chunks, chans, peers, width, lane):
     rows = micros * chunks
     return [
-        pltpu.VMEM((rows * chans, width), f32),
-        pltpu.VMEM((chunks * micros * (chans + 6), width), f32),
-        pltpu.VMEM((peers - 1, 6 * rows, width), f32),
+        pltpu.VMEM(((rows + 1) * chans, width), f32),
+        pltpu.VMEM(((chunks + 1) * micros * (chans + 6), width), f32),
+        pltpu.VMEM((peers - 1, 6 * (rows + micros), width), f32),
         pltpu.VMEM((chans, 4 * rows, width), bf16),
         pltpu.VMEM((chans, 2 * rows, 2 * width), bf16),
         pltpu.VMEM((chans, 2 * rows, lane), bf16),
@@ -448,7 +448,7 @@
     half = const_ref.shape[2] // 2
     spans = int(math.log2(chunks))
     rows = micros * chunks
-    stride = head.shape[0] // chunks
+    stride = send_ref.shape[1]
     got_stride = got_ref.shape[1]
     shape = (width, width)
     passed = lanes(shape) <= lax.broadcasted_iota(jnp.int32, shape, 0)
@@ -458,7 +458,7 @@
     gain, bias = 2 * (5 + spans), 2 * (5 + spans) + 1
     for k in range(chunks):
         x_keep[pl.ds(k * got_stride, got_stride), :] = got_ref[k].astype(f32)
-    dact_keep[...] = dact_ref[...].astype(f32)
+    dact_keep[: rows * chans] = dact_ref[...].astype(f32)
     mean, inverse = norm_ref[:rows], norm_ref[rows:]
 
     def x_hat_of(channel):
@@ -614,9 +614,9 @@
     rows = micros * chunks
     return [
         pltpu.VMEM((3 * chans, lane), f32),
-        pltpu.VMEM((chunks * stride, width), f32),
-        pltpu.VMEM((chunks * micros * (chans + 6), width), f32),
-        pltpu.VMEM((rows * chans, width), f32),
+        pltpu.VMEM(((chunks + 1) * stride, width), f32),
+        pltpu.VMEM(((chunks + 1) * micros * (chans + 6), width), f32),
+        pltpu.VMEM(((rows + 1) * chans, width), f32),
         pltpu.VMEM((chans, rows, width), f32),
         pltpu.VMEM((chans, rows, width), f32),
         pltpu.VMEM((chans, 3 * rows, width), bf16),
@@ -934,7 +934,7 @@
         + [pltpu.VMEM((modes, wide), f32)] * 2
         + [
             pltpu.VMEM((wide, lane), f32),
-            pltpu.VMEM((16 * chans, lane), f32),
+            pltpu.VMEM((17 * chans, lane), f32),
             pltpu.SemaphoreType.DMA((5,)),
         ],
         compiler_params=pltpu.CompilerParams(vmem_limit_bytes=8 * 1024 * 1024),

time: 76.8 us -> 76.8 us (level)
  no operation moved by 1% of the time
where the time goes in v9:
time: 76.8 us; the launch traced here: 76.3 us
  starting transfers between devices  36.1 us (47%)
  Pallas kernels  20.5 us (27%)
  waiting for transfers between devices  17.4 us (23%)
  local copies, waits for them, and re-layouts  1.35 us (2%)
  between operations  0.82 us (1%)
    all_to_all x4, starting transfers between devices, exchange(): return lax.all_to_all(x, axis, 0, 0, tiled=True)  20.2 us
    all_to_all x4, waiting for transfers between devices, exchange(): return lax.all_to_all(x, axis, 0, 0, tiled=True)  13.7 us
    ppermute x15, starting transfers between devices, cross(): return lax.ppermute(x, 'chan', [(i, i ^ by) for i in range(peers)])  9.45 us
    pallas_call x6, Pallas kernels, kernel_call(): pl.pallas_call(kernel, in_specs=ins, out_specs=[vmem()] * len(outs), out_...  6.05 us
    pallas_call x1, Pallas kernels, shards(): pl.pallas_call(functools.partial(backward_kernel, micros, seqs, chans), i...  4.46 us
    ppermute x3, starting transfers between devices, shards(): lax.ppermute(block, 'seq', [(i, i ^ k + 1 << 1) for i in range(seqs)])  4.39 us
    pallas_call x1, Pallas kernels, shards(): pl.pallas_call(functools.partial(table_kernel, chans, seqs, width), in_sp...  3.52 us
    ppermute x15, waiting for transfers between devices, cross(): return lax.ppermute(x, 'chan', [(i, i ^ by) for i in range(peers)])  3.36 us
  transfers between devices with their start and end apart: 23, of which 10 were waited for; matrix products, arithmetic and copies ran while one was open for 0% of the time, Pallas kernels for 23%

profile of v9, /device:TPU:0, one launch (start us, length us, event | category | flops | bytes accessed | tf_op | source)
XLA Modules:
  0.0 76.3 jit_solution(2866637898953276865)
XLA Ops:
  0.6 1.7 %pack.1 = (bf16[8,88,128]{2,1,0:T(8,128)(2,1)}, f32[8,128]{1,0:T(8,128)S(1)}) custom-call(bf16[4,128,128]{2,1,0:T(8,128)(2,1)} %tokens_ref.5), custom_call_target="tpu_custom_call" | custom-call | flops 1000000000 | bytes 3000000 | tf_op jit(solution)/shard_map/pack/pallas_call | solution.py:890
  2.4 7.3 %all-to-all-start = ((bf16[8,88,128]{2,1,0:T(8,128)(2,1)}), bf16[8,88,128]{2,1,0:T(8,128)(2,1)S(1)}, u32[]{:S(2)}, u32[]{:S(2)}) async-start(bf16[8,88,128]{2,1,0:T(8,128)(2,1)} %get-tuple-element.66), calls=%async_computation | async-start | bytes 360448 | tf_op jit(solution)/shard_map/all_to_all | solution.py:884
  9.7 0.0 copy-start.8
  9.7 0.6 copy-done.7
  10.3 0.0 copy-done.8
  10.3 1.5 %weights.1 = (bf16[1168,128]{1,0:T(8,128)(2,1)S(1)}, bf16[1168,128]{1,0:T(8,128)(2,1)S(1)}, bf16[1168,128]{1,0:T(8,128)(2,1)S(1)}, bf16[1168,128]{1,0:T(8,128)(2,1)S(1)}) custom-call(s32[1]{0:T(128)} %bitcast.9.rank_ref, f32[1,128]{1,0:T(1,128)S(1)} %bitcast.28, f32[1,128]{1,0:T(1,128)S(1)} %bitcast.30, bf16[4,128,128]{2,1,0:T(8,128)(2,1)} %cot_ref.3, ...), custom_call_target="tpu_custom_call" | custom-call | flops 1000000000 | bytes 3000000 | tf_op jit(solution)/shard_map/weights/pallas_call | solution.py:911
  11.8 0.0 copy-start.4
  11.8 0.0 copy-start.5
  11.9 0.0 copy-start.6
  11.9 0.6 copy-done.4
  12.5 0.0 copy-done.5
  12.5 0.0 copy-done.6
  12.5 3.5 %tables.1 = (f32[18,16,128]{2,1,0:T(8,128)S(1)}, f32[256,128]{1,0:T(8,128)S(1)}, f32[16,16,128]{2,1,0:T(8,128)S(1)}, f32[32,128]{1,0:T(8,128)S(1)}) custom-call(s32[1]{0:T(128)} %bitcast.rank_ref, s32[4]{0:T(128)S(1)} %bitcast.32, f32[128]{0:T(128)S(1)} %copy-done.4, f32[128]{0:T(128)S(1)} %copy-done.5, f32[128]{0:T(128)S(1)} %copy-done.6, ...), custom_call_target="tpu_custom_call" | custom-call | flops 2000000000 | bytes 6000000 | tf_op jit(solution)/shard_map/tables/pallas_call | solution.py:923
  16.0 1.3 %all-to-all-done.got_ref = bf16[8,88,128]{2,1,0:T(8,128)(2,1)S(1)} async-done(((bf16[8,88,128]{2,1,0:T(8,128)(2,1)}), bf16[8,88,128]{2,1,0:T(8,128)(2,1)S(1)}, u32[]{:S(2)}, u32[]{:S(2)}) %all-to-all-start) | async-done | bytes 180256 | tf_op jit(solution)/shard_map/all_to_all | solution.py:884
  17.4 0.0 collective-permute-start.2
  17.4 1.6 %collective-permute-start.1 = (bf16[8,24,128]{2,1,0:T(8,128)(2,1)S(1)}, bf16[8,24,128]{2,1,0:T(8,128)(2,1)S(1)}, u32[]{:S(2)}, u32[]{:S(2)}) collective-permute-start(bf16[8,24,128]{2,1,0:T(8,128)(2,1)S(1)} %slice.3), channel_id=1, source_target_pairs={{0,2},{1,3},{2,0},{3,1},{4,6},{5,7},{6,4},{7,5},{8,10},{9,11},{10,... | collective-permute-start | bytes 147464 | tf_op jit(solution)/shard_map/ppermute | solution.py:887
  19.0 0.3 collective-permute-start
  19.2 0.2 collective-permute-start.6
  19.5 1.3 %collective-permute-start.7 = (bf16[1168,128]{1,0:T(8,128)(2,1)S(1)}, bf16[1168,128]{1,0:T(8,128)(2,1)S(1)}, u32[]{:S(2)}, u32[]{:S(2)}) collective-permute-start(bf16[1168,128]{1,0:T(8,128)(2,1)S(1)} %get-tuple-element.85), channel_id=1, source_target_pairs={{0,2},{1,3},{2,0},{3,1},{4,6},{5,7},{6,4},{7,5},{8,10},{9,11},{10,... | collective-permute-start | bytes 897032 | tf_op jit(solution)/shard_map/ppermute | solution.py:887
  20.7 0.6 collective-permute-done.2.refs_2_
  21.3 0.0 collective-permute-start.8
  21.3 0.9 %collective-permute-done.1.refs_1_ = bf16[8,24,128]{2,1,0:T(8,128)(2,1)S(1)} collective-permute-done((bf16[8,24,128]{2,1,0:T(8,128)(2,1)S(1)}, bf16[8,24,128]{2,1,0:T(8,128)(2,1)S(1)}, u32[]{:S(2)}, u32[]{:S(2)}) %collective-permute-start.1) | collective-permute-done | bytes 49184 | tf_op jit(solution)/shard_map/ppermute | solution.py:887
  22.2 0.0 collective-permute-done.refs_0_
  22.2 3.2 %mixer_forward.1 = (bf16[512,128]{1,0:T(8,128)(2,1)}, f32[64,128]{1,0:T(8,128)S(1)}, f32[16,32,128]{2,1,0:T(8,128)S(1)}, f32[16,32,128]{2,1,0:T(8,128)S(1)}) custom-call(bf16[8,88,128]{2,1,0:T(8,128)(2,1)S(1)} %all-to-all-done.got_ref, f32[18,16,128]{2,1,0:T(8,128)S(1)} %get-tuple-element.77.const_ref, f32[256,128]{1,0:T(8,128)S(1)} %get-tuple-element.78.rise_ref, ...), custom_call_target="tpu_custom_call" | custom-call | flops 5000000000 | bytes 15000000 | tf_op jit(solution)/shard_map/mixer_forward/pallas_call | solution.py:950
  25.4 4.5 %all-to-all-start.1 = ((bf16[32,16,128]{2,1,0:T(8,128)(2,1)}), bf16[32,16,128]{2,1,0:T(8,128)(2,1)S(1)}, u32[]{:S(2)}, u32[]{:S(2)}) async-start(bf16[32,16,128]{2,1,0:T(8,128)(2,1)} %bitcast.10), calls=%async_computation.1 | async-start | bytes 262144 | tf_op jit(solution)/shard_map/all_to_all | solution.py:884
  30.0 1.6 %collective-permute-start.11 = (f32[8,128]{1,0:T(8,128)S(1)}, f32[8,128]{1,0:T(8,128)S(1)}, u32[]{:S(2)}, u32[]{:S(2)}) collective-permute-start(f32[8,128]{1,0:T(8,128)S(1)} %get-tuple-element.96.refs_0_), channel_id=1, source_target_pairs={{0,3},{1,2},{2,1},{3,0},{4,7},{5,6},{6,5},{7,4},{8,11},{9,10},{10,... | collective-permute-start | bytes 12296 | tf_op jit(solution)/shard_map/ppermute | solution.py:887
  31.6 0.4 collective-permute-start.10
  31.9 0.1 pad_add_fusion.place_ref
  32.0 0.0 collective-permute-done.6.refs_1_
  32.0 5.7 %all-to-all-done.1 = bf16[32,16,128]{2,1,0:T(8,128)(2,1)S(1)} async-done(((bf16[32,16,128]{2,1,0:T(8,128)(2,1)}), bf16[32,16,128]{2,1,0:T(8,128)(2,1)S(1)}, u32[]{:S(2)}, u32[]{:S(2)}) %all-to-all-start.1) | async-done | bytes 131104 | tf_op jit(solution)/shard_map/all_to_all | solution.py:884
  37.7 0.4 collective-permute-start.5
  38.1 0.0 collective-permute-done.7.refs_2_
  38.1 1.4 %collective-permute-start.4 = (bf16[512,128]{1,0:T(8,128)(2,1)S(1)}, bf16[512,128]{1,0:T(8,128)(2,1)S(1)}, u32[]{:S(2)}, u32[]{:S(2)}) collective-permute-start(bf16[512,128]{1,0:T(8,128)(2,1)S(1)} %bitcast.23), channel_id=1, source_target_pairs={{0,2},{1,3},{2,0},{3,1},{4,6},{5,7},{6,4},{7,5},{8,10},{9,11},{10,... | collective-permute-start | bytes 393224 | tf_op jit(solution)/shard_map/ppermute | solution.py:887
  39.5 0.0 collective-permute-done.8.refs_3_
  39.5 0.1 collective-permute-start.3
  39.6 1.9 %project.1 = bf16[512,128]{1,0:T(8,128)(2,1)} custom-call(s32[2]{0:T(128)S(1)} %pad_add_fusion.place_ref, s32[4]{0:T(128)S(1)} %bitcast.33, bf16[512,128]{1,0:T(8,128)(2,1)S(1)} %bitcast.25, bf16[1168,128]{1,0:T(8,128)(2,1)S(1)} %get-tuple-element.83.refs_0_, bf16[1168,128]{1,0:T(8,128)(2,1)S(1)} %collective-permute-done.6.refs_1_, ...), custom_call_target="tpu_custom_call" | custom-call | flops 2000000000 | bytes 6000000 | tf_op jit(solution)/shard_map/project/pallas_call | solution.py:828
  41.6 3.7 %all-to-all-start.2 = ((bf16[32,16,128]{2,1,0:T(8,128)(2,1)}), bf16[32,16,128]{2,1,0:T(8,128)(2,1)S(1)}, u32[]{:S(2)}, u32[]{:S(2)}) async-start(bf16[32,16,128]{2,1,0:T(8,128)(2,1)} %bitcast.12), calls=%async_computation.2 | async-start | bytes 262144 | tf_op jit(solution)/shard_map/all_to_all | solution.py:884
  45.3 0.0 copy-start.11
  45.3 0.0 collective-permute-done.5.refs_3_
  45.3 0.3 collective-permute-start.9
  45.7 0.7 collective-permute-done.4.refs_2_
  46.3 1.8 %output.1 = (bf16[4,128,128]{2,1,0:T(8,128)(2,1)}, f32[2,136,128]{2,1,0:T(8,128)S(1)}, bf16[2,136,128]{2,1,0:T(8,128)(2,1)S(1)}, bf16[2,136,128]{2,1,0:T(8,128)(2,1)S(1)}, bf16[2,136,128]{2,1,0:T(8,128)(2,1)S(1)}) custom-call(s32[1]{0:T(128)} %bitcast.rank_ref, s32[4]{0:T(128)S(1)} %bitcast.34, s32[4]{0:T(128)S(1)} %iota_xor_fusion.order_ref, ...), custom_call_target="tpu_custom_call" | custom-call | flops 2000000000 | bytes 6000000 | tf_op jit(solution)/shard_map/output/pallas_call | solution.py:828
  48.1 1.0 %collective-permute-start.12 = (bf16[2,136,128]{2,1,0:T(8,128)(2,1)S(1)}, bf16[2,136,128]{2,1,0:T(8,128)(2,1)S(1)}, u32[]{:S(2)}, u32[]{:S(2)}) collective-permute-start(bf16[2,136,128]{2,1,0:T(8,128)(2,1)S(1)} %get-tuple-element.92), channel_id=1, source_target_pairs={{0,8},{4,12},{8,0},{12,4},{16,24},{20,28},{24,16},{28,20},{1,9},{5... | collective-permute-start | bytes 208904 | tf_op jit(solution)/shard_map/ppermute | solution.py:1015
  49.2 2.4 %collective-permute-start.13 = (bf16[2,136,128]{2,1,0:T(8,128)(2,1)S(1)}, bf16[2,136,128]{2,1,0:T(8,128)(2,1)S(1)}, u32[]{:S(2)}, u32[]{:S(2)}) collective-permute-start(bf16[2,136,128]{2,1,0:T(8,128)(2,1)S(1)} %get-tuple-element.93), channel_id=1, source_target_pairs={{0,16},{4,20},{8,24},{12,28},{16,0},{20,4},{24,8},{28,12},{1,17},{... | collective-permute-start | bytes 208904 | tf_op jit(solution)/shard_map/ppermute | solution.py:1015
  51.6 0.0 collective-permute-done.11.refs_3_
  51.6 0.9 %collective-permute-start.14 = (bf16[2,136,128]{2,1,0:T(8,128)(2,1)S(1)}, bf16[2,136,128]{2,1,0:T(8,128)(2,1)S(1)}, u32[]{:S(2)}, u32[]{:S(2)}) collective-permute-start(bf16[2,136,128]{2,1,0:T(8,128)(2,1)S(1)} %get-tuple-element.94), channel_id=1, source_target_pairs={{0,24},{4,28},{8,16},{12,20},{16,8},{20,12},{24,0},{28,4},{1,25},{... | collective-permute-start | bytes 208904 | tf_op jit(solution)/shard_map/ppermute | solution.py:1015
  52.5 0.0 collective-permute-done.10.refs_2_
  52.5 0.0 collective-permute-done.9.refs_1_
  52.5 0.5 all-to-all-done.2
  53.0 4.5 %mixer_backward.1 = bf16[8,128,128]{2,1,0:T(8,128)(2,1)} custom-call(bf16[8,88,128]{2,1,0:T(8,128)(2,1)S(1)} %all-to-all-done.got_ref, bf16[512,128]{1,0:T(8,128)(2,1)S(1)} %bitcast.27, f32[64,128]{1,0:T(8,128)S(1)} %get-tuple-element.89.norm_ref, f32[18,16,128]{2,1,0:T(8,128)S(1)} %get-tuple-element.77.const_ref, ...), custom_call_target="tpu_custom_call" | custom-call | flops 5000000000 | bytes 15000000 | tf_op jit(solution)/shard_map/mixer_backward/pallas_call | solution.py:1021
  57.5 0.0 collective-permute-done.12.refs_0_
  57.5 0.3 collective-permute-done.13.refs_1_
  57.8 4.7 %all-to-all-start.3 = ((bf16[8,128,128]{2,1,0:T(8,128)(2,1)}), bf16[8,128,128]{2,1,0:T(8,128)(2,1)S(1)}, u32[]{:S(2)}, u32[]{:S(2)}) async-start(bf16[8,128,128]{2,1,0:T(8,128)(2,1)} %mixer_backward.1), calls=%async_computation.3 | async-start | bytes 524288 | tf_op jit(solution)/shard_map/all_to_all | solution.py:884
  62.6 2.1 %collective-permute-start.18 = (bf16[136,128]{1,0:T(8,128)(2,1)S(1)}, bf16[136,128]{1,0:T(8,128)(2,1)S(1)}, u32[]{:S(2)}, u32[]{:S(2)}) collective-permute-start(bf16[136,128]{1,0:T(8,128)(2,1)S(1)} %get-tuple-element.115), channel_id=1, source_target_pairs={{0,4},{4,0},{8,12},{12,8},{16,20},{20,16},{24,28},{28,24},{1,5},{5... | collective-permute-start | bytes 104456 | tf_op jit(solution)/shard_map/ppermute | solution.py:1041
  64.6 6.2 %all-to-all-done.3.got_ref = bf16[8,128,128]{2,1,0:T(8,128)(2,1)S(1)} async-done(((bf16[8,128,128]{2,1,0:T(8,128)(2,1)}), bf16[8,128,128]{2,1,0:T(8,128)(2,1)S(1)}, u32[]{:S(2)}, u32[]{:S(2)}) %all-to-all-start.3) | async-done | bytes 262176 | tf_op jit(solution)/shard_map/all_to_all | solution.py:884
  70.9 0.2 sums.1
  71.1 0.1 collective-permute-start.17
  71.2 1.6 %collective-permute-start.16 = (f32[8,128]{1,0:T(8,128)S(1)}, f32[8,128]{1,0:T(8,128)S(1)}, u32[]{:S(2)}, u32[]{:S(2)}) collective-permute-start(f32[8,128]{1,0:T(8,128)S(1)} %get-tuple-element.102.refs_0_), channel_id=1, source_target_pairs={{0,2},{1,3},{2,0},{3,1},{4,6},{5,7},{6,4},{7,5},{8,10},{9,11},{10,... | collective-permute-start | bytes 12296 | tf_op jit(solution)/shard_map/ppermute | solution.py:887
  72.7 0.3 collective-permute-start.15
  73.0 0.0 collective-permute-done.18.right_ref
  73.0 0.6 last.1
  73.7 0.5 collective-permute-done.17.refs_3_
  74.2 0.7 collective-permute-done.16.refs_2_
  74.8 1.4 %final.1 = (f32[4,128,128]{2,1,0:T(8,128)}, f32[2,64,128]{2,1,0:T(8,128)}, f32[2,64,128]{2,1,0:T(8,128)}, f32[2,64,128]{2,1,0:T(8,128)}, f32[1,128]{1,0:T(1,128)}, /*index=5*/f32[1,128]{1,0:T(1,128)}, f32[1,128]{1,0:T(1,128)}) custom-call(s32[1]{0:T(128)} %bitcast.rank_ref, s32[4]{0:T(128)S(1)} %bitcast.35, f32[8,128,128]{2,1,0:T(8,128)S(1)} %get-tuple-element.100.head_ref, ...), custom_call_target="tpu_custom_call" | custom-call | flops 2000000000 | bytes 6000000 | tf_op jit(solution)/shard_map/final/pallas_call | solution.py:828
  (20 shorter events, 0.1 us)
Async XLA Ops:
  2.4 15.0 %all-to-all-start = ((bf16[8,88,128]{2,1,0:T(8,128)(2,1)}), bf16[8,88,128]{2,1,0:T(8,128)(2,1)S(1)}, u32[]{:S(2)}, u32[]{:S(2)}) async-start(bf16[8,88,128]{2,1,0:T(8,128)(2,1)} %get-tuple-element.66), calls=%async_computation | async-start | bytes 360448 | tf_op jit(solution)/shard_map/all_to_all | solution.py:884
  9.7 0.7 copy-start.7
  9.7 0.7 copy-start.8
  10.3 1.5 %copy-start.9 = (s32[4,1]{0,1:T(1,128)S(1)}, s32[4,1]{0,1:T(1,128)}, u32[]{:S(2)}) copy-start(s32[4,1]{0,1:T(1,128)} %param.16) | copy-start | bytes 52
  11.8 0.7 copy-start.4
  11.8 0.7 copy-start.5
  11.9 0.7 copy-start.6
  17.4 4.0 %collective-permute-start.2 = (bf16[8,24,128]{2,1,0:T(8,128)(2,1)S(1)}, bf16[8,24,128]{2,1,0:T(8,128)(2,1)S(1)}, u32[]{:S(2)}, u32[]{:S(2)}) collective-permute-start(bf16[8,24,128]{2,1,0:T(8,128)(2,1)S(1)} %slice.3), channel_id=1, source_target_pairs={{0,3},{1,2},{2,1},{3,0},{4,7},{5,6},{6,5},{7,4},{8,11},{9,10},{10,... | collective-permute-start | bytes 147464 | tf_op jit(solution)/shard_map/ppermute | solution.py:887
  17.4 4.9 %collective-permute-start.1 = (bf16[8,24,128]{2,1,0:T(8,128)(2,1)S(1)}, bf16[8,24,128]{2,1,0:T(8,128)(2,1)S(1)}, u32[]{:S(2)}, u32[]{:S(2)}) collective-permute-start(bf16[8,24,128]{2,1,0:T(8,128)(2,1)S(1)} %slice.3), channel_id=1, source_target_pairs={{0,2},{1,3},{2,0},{3,1},{4,6},{5,7},{6,4},{7,5},{8,10},{9,11},{10,... | collective-permute-start | bytes 147464 | tf_op jit(solution)/shard_map/ppermute | solution.py:887
  19.0 3.3 %collective-permute-start = (bf16[8,24,128]{2,1,0:T(8,128)(2,1)S(1)}, bf16[8,24,128]{2,1,0:T(8,128)(2,1)S(1)}, u32[]{:S(2)}, u32[]{:S(2)}) collective-permute-start(bf16[8,24,128]{2,1,0:T(8,128)(2,1)S(1)} %slice.3), channel_id=1, source_target_pairs={{0,1},{1,0},{2,3},{3,2},{4,5},{5,4},{6,7},{7,6},{8,9},{9,8},{10,11... | collective-permute-start | bytes 147464 | tf_op jit(solution)/shard_map/ppermute | solution.py:887
  19.2 12.8 %collective-permute-start.6 = (bf16[1168,128]{1,0:T(8,128)(2,1)S(1)}, bf16[1168,128]{1,0:T(8,128)(2,1)S(1)}, u32[]{:S(2)}, u32[]{:S(2)}) collective-permute-start(bf16[1168,128]{1,0:T(8,128)(2,1)S(1)} %get-tuple-element.84), channel_id=1, source_target_pairs={{0,1},{1,0},{2,3},{3,2},{4,5},{5,4},{6,7},{7,6},{8,9},{9,8},{10,11... | collective-permute-start | bytes 897032 | tf_op jit(solution)/shard_map/ppermute | solution.py:887
  19.5 18.6 %collective-permute-start.7 = (bf16[1168,128]{1,0:T(8,128)(2,1)S(1)}, bf16[1168,128]{1,0:T(8,128)(2,1)S(1)}, u32[]{:S(2)}, u32[]{:S(2)}) collective-permute-start(bf16[1168,128]{1,0:T(8,128)(2,1)S(1)} %get-tuple-element.85), channel_id=1, source_target_pairs={{0,2},{1,3},{2,0},{3,1},{4,6},{5,7},{6,4},{7,5},{8,10},{9,11},{10,... | collective-permute-start | bytes 897032 | tf_op jit(solution)/shard_map/ppermute | solution.py:887
  21.3 18.1 %collective-permute-start.8 = (bf16[1168,128]{1,0:T(8,128)(2,1)S(1)}, bf16[1168,128]{1,0:T(8,128)(2,1)S(1)}, u32[]{:S(2)}, u32[]{:S(2)}) collective-permute-start(bf16[1168,128]{1,0:T(8,128)(2,1)S(1)} %get-tuple-element.86), channel_id=1, source_target_pairs={{0,3},{1,2},{2,1},{3,0},{4,7},{5,6},{6,5},{7,4},{8,11},{9,10},{10,... | collective-permute-start | bytes 897032 | tf_op jit(solution)/shard_map/ppermute | solution.py:887
  25.4 12.6 %copy-start.10 = (f32[16,32,128]{2,1,0:T(8,128)}, f32[16,32,128]{2,1,0:T(8,128)S(1)}, u32[]{:S(2)}) copy-start(f32[16,32,128]{2,1,0:T(8,128)S(1)} %get-tuple-element.91.start_ref) | copy-start | bytes 786436
  25.4 12.3 %all-to-all-start.1 = ((bf16[32,16,128]{2,1,0:T(8,128)(2,1)}), bf16[32,16,128]{2,1,0:T(8,128)(2,1)S(1)}, u32[]{:S(2)}, u32[]{:S(2)}) async-start(bf16[32,16,128]{2,1,0:T(8,128)(2,1)} %bitcast.10), calls=%async_computation.1 | async-start | bytes 262144 | tf_op jit(solution)/shard_map/all_to_all | solution.py:884
  30.0 21.6 %collective-permute-start.11 = (f32[8,128]{1,0:T(8,128)S(1)}, f32[8,128]{1,0:T(8,128)S(1)}, u32[]{:S(2)}, u32[]{:S(2)}) collective-permute-start(f32[8,128]{1,0:T(8,128)S(1)} %get-tuple-element.96.refs_0_), channel_id=1, source_target_pairs={{0,3},{1,2},{2,1},{3,0},{4,7},{5,6},{6,5},{7,4},{8,11},{9,10},{10,... | collective-permute-start | bytes 12296 | tf_op jit(solution)/shard_map/ppermute | solution.py:887
  31.6 21.0 %collective-permute-start.10 = (f32[8,128]{1,0:T(8,128)S(1)}, f32[8,128]{1,0:T(8,128)S(1)}, u32[]{:S(2)}, u32[]{:S(2)}) collective-permute-start(f32[8,128]{1,0:T(8,128)S(1)} %get-tuple-element.96.refs_0_), channel_id=1, source_target_pairs={{0,2},{1,3},{2,0},{3,1},{4,6},{5,7},{6,4},{7,5},{8,10},{9,11},{10,... | collective-permute-start | bytes 12296 | tf_op jit(solution)/shard_map/ppermute | solution.py:887
  37.7 7.6 %collective-permute-start.5 = (bf16[512,128]{1,0:T(8,128)(2,1)S(1)}, bf16[512,128]{1,0:T(8,128)(2,1)S(1)}, u32[]{:S(2)}, u32[]{:S(2)}) collective-permute-start(bf16[512,128]{1,0:T(8,128)(2,1)S(1)} %bitcast.22), channel_id=1, source_target_pairs={{0,3},{1,2},{2,1},{3,0},{4,7},{5,6},{6,5},{7,4},{8,11},{9,10},{10,... | collective-permute-start | bytes 393224 | tf_op jit(solution)/shard_map/ppermute | solution.py:887
  38.1 8.2 %collective-permute-start.4 = (bf16[512,128]{1,0:T(8,128)(2,1)S(1)}, bf16[512,128]{1,0:T(8,128)(2,1)S(1)}, u32[]{:S(2)}, u32[]{:S(2)}) collective-permute-start(bf16[512,128]{1,0:T(8,128)(2,1)S(1)} %bitcast.23), channel_id=1, source_target_pairs={{0,2},{1,3},{2,0},{3,1},{4,6},{5,7},{6,4},{7,5},{8,10},{9,11},{10,... | collective-permute-start | bytes 393224 | tf_op jit(solution)/shard_map/ppermute | solution.py:887
  39.5 6.9 %collective-permute-start.3 = (bf16[512,128]{1,0:T(8,128)(2,1)S(1)}, bf16[512,128]{1,0:T(8,128)(2,1)S(1)}, u32[]{:S(2)}, u32[]{:S(2)}) collective-permute-start(bf16[512,128]{1,0:T(8,128)(2,1)S(1)} %bitcast.24), channel_id=1, source_target_pairs={{0,1},{1,0},{2,3},{3,2},{4,5},{5,4},{6,7},{7,6},{8,9},{9,8},{10,11... | collective-permute-start | bytes 393224 | tf_op jit(solution)/shard_map/ppermute | solution.py:887
  39.6 6.7 %copy-start.2 = (bf16[4,128,128]{2,1,0:T(8,128)(2,1)S(1)}, bf16[4,128,128]{2,1,0:T(8,128)(2,1)}, u32[]{:S(2)}) copy-start(bf16[4,128,128]{2,1,0:T(8,128)(2,1)} %tokens_ref.5) | copy-start | bytes 393220
  39.6 6.7 %copy-start.3 = (bf16[4,128,128]{2,1,0:T(8,128)(2,1)S(1)}, bf16[4,128,128]{2,1,0:T(8,128)(2,1)}, u32[]{:S(2)}) copy-start(bf16[4,128,128]{2,1,0:T(8,128)(2,1)} %cot_ref.3) | copy-start | bytes 393220
  41.6 4.8 %copy-start = (bf16[512,128]{1,0:T(8,128)(2,1)S(1)}, bf16[512,128]{1,0:T(8,128)(2,1)}, u32[]{:S(2)}) copy-start(bf16[512,128]{1,0:T(8,128)(2,1)} %wv_ref.1) | copy-start | bytes 393220
  41.6 4.8 %copy-start.1 = (bf16[512,128]{1,0:T(8,128)(2,1)S(1)}, bf16[512,128]{1,0:T(8,128)(2,1)}, u32[]{:S(2)}) copy-start(bf16[512,128]{1,0:T(8,128)(2,1)} %wg_ref.1) | copy-start | bytes 393220
  41.6 11.5 %all-to-all-start.2 = ((bf16[32,16,128]{2,1,0:T(8,128)(2,1)}), bf16[32,16,128]{2,1,0:T(8,128)(2,1)S(1)}, u32[]{:S(2)}, u32[]{:S(2)}) async-start(bf16[32,16,128]{2,1,0:T(8,128)(2,1)} %bitcast.12), calls=%async_computation.2 | async-start | bytes 262144 | tf_op jit(solution)/shard_map/all_to_all | solution.py:884
  45.3 7.7 %copy-start.11 = (f32[16,32,128]{2,1,0:T(8,128)S(1)}, f32[16,32,128]{2,1,0:T(8,128)}, u32[]{:S(2)}) copy-start(f32[16,32,128]{2,1,0:T(8,128)} %copy-done.10) | copy-start | bytes 786436
  45.3 7.2 %collective-permute-start.9 = (f32[8,128]{1,0:T(8,128)S(1)}, f32[8,128]{1,0:T(8,128)S(1)}, u32[]{:S(2)}, u32[]{:S(2)}) collective-permute-start(f32[8,128]{1,0:T(8,128)S(1)} %get-tuple-element.96.refs_0_), channel_id=1, source_target_pairs={{0,1},{1,0},{2,3},{3,2},{4,5},{5,4},{6,7},{7,6},{8,9},{9,8},{10,11... | collective-permute-start | bytes 12296 | tf_op jit(solution)/shard_map/ppermute | solution.py:887
  48.1 9.4 %collective-permute-start.12 = (bf16[2,136,128]{2,1,0:T(8,128)(2,1)S(1)}, bf16[2,136,128]{2,1,0:T(8,128)(2,1)S(1)}, u32[]{:S(2)}, u32[]{:S(2)}) collective-permute-start(bf16[2,136,128]{2,1,0:T(8,128)(2,1)S(1)} %get-tuple-element.92), channel_id=1, source_target_pairs={{0,8},{4,12},{8,0},{12,4},{16,24},{20,28},{24,16},{28,20},{1,9},{5... | collective-permute-start | bytes 208904 | tf_op jit(solution)/shard_map/ppermute | solution.py:1015
  49.2 8.7 %collective-permute-start.13 = (bf16[2,136,128]{2,1,0:T(8,128)(2,1)S(1)}, bf16[2,136,128]{2,1,0:T(8,128)(2,1)S(1)}, u32[]{:S(2)}, u32[]{:S(2)}) collective-permute-start(bf16[2,136,128]{2,1,0:T(8,128)(2,1)S(1)} %get-tuple-element.93), channel_id=1, source_target_pairs={{0,16},{4,20},{8,24},{12,28},{16,0},{20,4},{24,8},{28,12},{1,17},{... | collective-permute-start | bytes 208904 | tf_op jit(solution)/shard_map/ppermute | solution.py:1015
  51.6 6.2 %collective-permute-start.14 = (bf16[2,136,128]{2,1,0:T(8,128)(2,1)S(1)}, bf16[2,136,128]{2,1,0:T(8,128)(2,1)S(1)}, u32[]{:S(2)}, u32[]{:S(2)}) collective-permute-start(bf16[2,136,128]{2,1,0:T(8,128)(2,1)S(1)} %get-tuple-element.94), channel_id=1, source_target_pairs={{0,24},{4,28},{8,16},{12,20},{16,8},{20,12},{24,0},{28,4},{1,25},{... | collective-permute-start | bytes 208904 | tf_op jit(solution)/shard_map/ppermute | solution.py:1015
  57.8 13.0 %all-to-all-start.3 = ((bf16[8,128,128]{2,1,0:T(8,128)(2,1)}), bf16[8,128,128]{2,1,0:T(8,128)(2,1)S(1)}, u32[]{:S(2)}, u32[]{:S(2)}) async-start(bf16[8,128,128]{2,1,0:T(8,128)(2,1)} %mixer_backward.1), calls=%async_computation.3 | async-start | bytes 524288 | tf_op jit(solution)/shard_map/all_to_all | solution.py:884
  62.6 10.4 %collective-permute-start.18 = (bf16[136,128]{1,0:T(8,128)(2,1)S(1)}, bf16[136,128]{1,0:T(8,128)(2,1)S(1)}, u32[]{:S(2)}, u32[]{:S(2)}) collective-permute-start(bf16[136,128]{1,0:T(8,128)(2,1)S(1)} %get-tuple-element.115), channel_id=1, source_target_pairs={{0,4},{4,0},{8,12},{12,8},{16,20},{20,16},{24,28},{28,24},{1,5},{5... | collective-permute-start | bytes 104456 | tf_op jit(solution)/shard_map/ppermute | solution.py:1041
  71.1 3.1 %collective-permute-start.17 = (f32[8,128]{1,0:T(8,128)S(1)}, f32[8,128]{1,0:T(8,128)S(1)}, u32[]{:S(2)}, u32[]{:S(2)}) collective-permute-start(f32[8,128]{1,0:T(8,128)S(1)} %get-tuple-element.102.refs_0_), channel_id=1, source_target_pairs={{0,3},{1,2},{2,1},{3,0},{4,7},{5,6},{6,5},{7,4},{8,11},{9,10},{10,... | collective-permute-start | bytes 12296 | tf_op jit(solution)/shard_map/ppermute | solution.py:887
  71.2 3.7 %collective-permute-start.16 = (f32[8,128]{1,0:T(8,128)S(1)}, f32[8,128]{1,0:T(8,128)S(1)}, u32[]{:S(2)}, u32[]{:S(2)}) collective-permute-start(f32[8,128]{1,0:T(8,128)S(1)} %get-tuple-element.102.refs_0_), channel_id=1, source_target_pairs={{0,2},{1,3},{2,0},{3,1},{4,6},{5,7},{6,4},{7,5},{8,10},{9,11},{10,... | collective-permute-start | bytes 12296 | tf_op jit(solution)/shard_map/ppermute | solution.py:887
  72.7 2.1 %collective-permute-start.15 = (f32[8,128]{1,0:T(8,128)S(1)}, f32[8,128]{1,0:T(8,128)S(1)}, u32[]{:S(2)}, u32[]{:S(2)}) collective-permute-start(f32[8,128]{1,0:T(8,128)S(1)} %get-tuple-element.102.refs_0_), channel_id=1, source_target_pairs={{0,1},{1,0},{2,3},{3,2},{4,5},{5,4},{6,7},{7,6},{8,9},{9,8},{10,11... | collective-permute-start | bytes 12296 | tf_op jit(solution)/shard_map/ppermute | solution.py:887
